TPU v7x, 32 devices: a whole 2x2x4 slice. The times are simulated.
32 devices in a mesh: gx: 2 (over x), gy: 4 (over z), gz: 4 (over y, core).
Axes of the slice: x: 2, y: 2, z: 4, core: 2. Of those that a mesh axis runs over, the one named last changes fastest.
Arguments:
- features: bfloat16 [2, 4, 4, 768, 256], P('gx', 'gy', 'gz'), may hold values from -6 to 6
- weight: bfloat16 [27, 256, 256], replicated, may hold values from -0.078125 to 0.078125
- upstream: bfloat16 [2, 4, 4, 768, 256], P('gx', 'gy', 'gz'), may hold values from -6 to 6
- send_rows: int32 [2, 4, 4, 6, 96], P('gx', 'gy', 'gz'), may hold values from 0 to 767
- in_rows: int32 [2, 4, 4, 27, 768], P('gx', 'gy', 'gz'), may hold values from 0 to 1343, as said below
- out_rows: int32 [2, 4, 4, 27, 768], P('gx', 'gy', 'gz'), may hold values from 0 to 767, each once within a row
- tap_pair_exists: int32 [2, 4, 4, 27, 768], P('gx', 'gy', 'gz'), may hold values from 0 to 1, as said below
Outputs:
- activated: bfloat16 [2, 4, 4, 768, 256], P('gx', 'gy', 'gz')
- grad_features: bfloat16 [2, 4, 4, 768, 256], P('gx', 'gy', 'gz')
- grad_weight: bfloat16 [27, 256, 256], replicated
Inputs may be any that keep to these rules, and one draw needn't show every extreme that they name: `in_rows`: rows below 768 are a device's own; row 768 + d * 96 + f is row f of face d of the extended rows. For each device and tap the 768 rows are distinct. `out_rows`: for each device and tap, every row appears exactly once. `tap_pair_exists`: the share of existing pairs differs from device to device and from tap to tap.
All inputs are finite; a program needn't handle non-finite values.
Results may differ from a plain program's by a relative error of at most 0.0053.
Values may be sent and summed in bfloat16 or wider, within the bound.
No kernel may reach another device: no remote copies, remote signals or barrier semaphores. Data moves between devices by JAX's collectives and lax.ppermute only.
A program may use at most 128 MiB of HBM per device.

v0:
```python
import jax
import jax.numpy as jnp
from jax import lax
from jax.sharding import PartitionSpec as P


def extended(cells, sides, width):
    for axis, dim in sides:
        count = lax.axis_size(axis)
        ends = count - 1
        head = lax.slice_in_dim(cells, 0, width, axis=dim)
        tail = lax.slice_in_dim(cells, cells.shape[dim] - width, cells.shape[dim], axis=dim)
        cells = jnp.concatenate(
            [
                lax.ppermute(tail, axis, [(i, (i + 1) % count) for i in range(ends)]),
                cells,
                lax.ppermute(head, axis, [((i + 1) % count, i) for i in range(ends)]),
            ],
            axis=dim,
        )
    return cells


def trade(stacked):
    along_x = extended(stacked[0:2], (("gx", 0),), 1)
    along_y = extended(stacked[2:4], (("gy", 0),), 1)
    along_z = extended(stacked[4:6], (("gz", 0),), 1)
    return jnp.stack([along_x[0], along_x[3], along_y[0], along_y[3], along_z[0], along_z[3]])


def pairing_tables(source_voxels, target_voxels, occupancy_flags, extended_rows):
    tap_count, own_rows = source_voxels.shape
    tap_index = jnp.arange(tap_count, dtype=jnp.int32)[:, None]
    pair_index = jnp.broadcast_to(
        jnp.arange(own_rows, dtype=jnp.int32)[None, :], (tap_count, own_rows)
    )
    inverse_out = (
        jnp.zeros((tap_count, own_rows), jnp.int32).at[tap_index, target_voxels].set(pair_index)
    )
    live_at_out = jnp.take_along_axis(occupancy_flags, inverse_out, axis=1)
    source_at_out = jnp.take_along_axis(source_voxels, inverse_out, axis=1)
    forward_source = jnp.where(live_at_out > 0, source_at_out, extended_rows)
    live_target = jnp.where(occupancy_flags > 0, target_voxels, own_rows)
    backward_target = (
        jnp.full((tap_count, extended_rows), own_rows, jnp.int32)
        .at[tap_index, source_voxels]
        .set(live_target)
    )
    return (forward_source, backward_target)


def convolution_forward_step(padded_zero, forward_source, weight, group_length):
    tap_count, own_rows = forward_source.shape
    channels = weight.shape[2]
    source_by_row = forward_source.T

    def advance(group_index, running):
        leading_tap = group_index * group_length
        picks = lax.dynamic_slice_in_dim(source_by_row, leading_tap, group_length, 1)
        kernels = lax.dynamic_slice_in_dim(weight, leading_tap, group_length, 0).reshape(
            group_length * channels, channels
        )

        def accumulate(current):
            gathered = padded_zero[picks].reshape(own_rows, group_length * channels)
            return current + jnp.dot(gathered, kernels, preferred_element_type=jnp.float32)

        return accumulate(running)

    start = jnp.zeros((own_rows, channels), jnp.float32)
    return lax.fori_loop(0, tap_count // group_length, advance, start)


def convolution_backward_step(
    padded_features, backward_target, weight, gradient_zero, group_length
):
    tap_count, extended_rows = backward_target.shape
    channels = weight.shape[2]
    target_by_row = backward_target.T
    flipped = jnp.transpose(weight, (0, 2, 1))

    def advance(group_index, carried):
        leading_tap = group_index * group_length
        places = lax.dynamic_slice_in_dim(target_by_row, leading_tap, group_length, 1)
        kernels = lax.dynamic_slice_in_dim(flipped, leading_tap, group_length, 0).reshape(
            group_length * channels, channels
        )

        def accumulate(current):
            grad_rows, grad_kernel = current
            chosen = gradient_zero[places].reshape(extended_rows, group_length * channels)
            grad_rows = grad_rows + jnp.dot(chosen, kernels, preferred_element_type=jnp.float32)
            kernel_term = lax.dot_general(
                padded_features,
                chosen,
                (((0,), (0,)), ((), ())),
                preferred_element_type=jnp.float32,
            )
            kernel_term = jnp.transpose(
                kernel_term.reshape(channels, group_length, channels), (1, 0, 2)
            )
            grad_kernel = lax.dynamic_update_slice_in_dim(grad_kernel, kernel_term, leading_tap, 0)
            return (grad_rows, grad_kernel)

        return accumulate(carried)

    start = (
        jnp.zeros((extended_rows, channels), jnp.float32),
        jnp.zeros((tap_count, channels, channels), jnp.float32),
    )
    return lax.fori_loop(0, tap_count // group_length, advance, start)


def shards(features, weight, upstream, send_rows, in_rows, out_rows, tap_pair_exists):
    own_features = features[0, 0, 0]
    own_rows, channels = own_features.shape
    sends = send_rows[0, 0, 0]
    face_rows = sends.shape[1]
    source_voxels = in_rows[0, 0, 0]
    target_voxels = out_rows[0, 0, 0]
    occupancy_flags = tap_pair_exists[0, 0, 0]
    sent = own_features[sends]
    incoming = trade(sent)
    padded_features = jnp.concatenate(
        [own_features, incoming.reshape(6 * face_rows, channels)], axis=0
    )
    extended_rows = padded_features.shape[0]
    padded_zero = jnp.concatenate([padded_features, jnp.zeros((1, channels), jnp.bfloat16)], axis=0)
    forward_source, backward_target = pairing_tables(
        source_voxels, target_voxels, occupancy_flags, extended_rows
    )
    group_length, skip_dead = (9, False)
    linear_response = convolution_forward_step(padded_zero, forward_source, weight, group_length)
    sigmoid = jax.nn.sigmoid(linear_response)
    activated = (linear_response * sigmoid).astype(jnp.bfloat16)
    derivative = sigmoid * (1.0 + linear_response * (1.0 - sigmoid))
    preactivation_gradient = (upstream[0, 0, 0].astype(jnp.float32) * derivative).astype(
        jnp.bfloat16
    )
    gradient_zero = jnp.concatenate(
        [preactivation_gradient, jnp.zeros((1, channels), jnp.bfloat16)], axis=0
    )
    grad_extended, weight_partial = convolution_backward_step(
        padded_features, backward_target, weight, gradient_zero, group_length
    )
    devices_all = lax.axis_size("gx") * lax.axis_size("gy") * lax.axis_size("gz")
    scaling = float(devices_all * own_rows) ** (-0.5)
    summed = lax.psum(weight_partial, ("gx", "gy", "gz"))
    grad_weight = (summed * scaling).astype(jnp.bfloat16)
    faces_back = grad_extended[own_rows:].astype(jnp.bfloat16).reshape(6, face_rows, channels)
    returned = trade(faces_back)
    grad_features = (
        grad_extended[:own_rows]
        .at[sends.reshape(-1)]
        .add(returned.reshape(-1, channels).astype(jnp.float32))
    )
    activated = activated[None, None, None]
    grad_features = grad_features.astype(jnp.bfloat16)[None, None, None]
    return (activated, grad_features, grad_weight)


def solution(mesh):
    return jax.shard_map(
        shards,
        mesh=mesh,
        in_specs=(
            P("gx", "gy", "gz", None, None),
            P(),
            P("gx", "gy", "gz", None, None),
            P("gx", "gy", "gz", None, None),
            P("gx", "gy", "gz", None, None),
            P("gx", "gy", "gz", None, None),
            P("gx", "gy", "gz", None, None),
        ),
        out_specs=(P("gx", "gy", "gz", None, None), P("gx", "gy", "gz", None, None), P()),
        check_vma=False,
    )
```

profile of v0, /device:TPU:0, one launch (start us, length us, event | category | flops | bytes accessed | tf_op | source)
XLA Modules:
  0.0 1032.5 jit_solution(6745703560755910110)
XLA Ops:
  8.0 3.2 gather_fusion.2
  11.2 1.3 collective-permute-start.5
  12.5 3.0 collective-permute-start.4
  15.6 1.3 collective-permute-start.3
  16.9 5.6 collective-permute-start.2
  22.5 3.8 collective-permute-start
  26.3 1.0 compare_select_fusion.2
  28.2 1.0 compare_select_fusion.3
  29.2 1.4 and_reduce_fusion
  30.6 1.3 multiply_reduce_fusion
  32.9 76.2 %scatter_custom_fusion.1 = s32[20736]{0:T(1024)S(1)} fusion(s32[20736]{0:T(1024)S(1)} %reshape.225, s32[20736]{0:T(1024)S(1)} %reshape.227, s32[]{:T(128)} %constant.100.clone.1), kind=kCustom, calls=%fused_computation.70 | custom fusion | bytes 82948
  109.2 156.1 %gather_fusion.4 = s32[20736]{0:T(1024)S(1)} fusion(s32[27,768]{1,0:T(8,128)S(1)} %bitcast.88, s32[20736]{0:T(1024)S(1)} %reshape.270), kind=kCustom, calls=%fused_computation.3.clone | custom fusion | bytes 331776 | tf_op jit(solution)/shard_map/jit(take_along_axis)/gather | solution.py:41
  265.4 156.1 %gather_fusion.3 = s32[20736]{0:T(1024)S(1)} fusion(s32[27,768]{1,0:T(8,128)S(1)} %bitcast.89, s32[20736]{0:T(1024)S(1)} %reshape.270), kind=kCustom, calls=%fused_computation.clone | custom fusion | bytes 331776 | tf_op jit(solution)/shard_map/jit(take_along_axis)/gather | solution.py:40
  421.7 76.3 %scatter_custom_fusion.2 = s32[36288]{0:T(1024)S(1)} fusion(s32[20736]{0:T(1024)S(1)} %reshape.231, s32[20736]{0:T(1024)S(1)} %reshape.233, s32[]{:T(128)} %constant.102.clone.1), kind=kCustom, calls=%fused_computation.54 | custom fusion | bytes 145156
  498.1 5.7 copy.22
  503.9 1.3 collective-permute-start.1
  505.2 4.7 collective-permute-done.1
  511.2 100.8 %while.30 = (s32[]{:T(128)}, f32[768,256]{1,0:T(8,128)S(1)}, s32[768,27]{0,1:T(8,128)S(1)}, bf16[1345,256]{1,0:T(8,128)(2,1)S(1)}, bf16[27,256,256]{2,1,0:T(8,12...) while((s32[]{:T(128)}, f32[768,256]{1,0:T(8,128)S(1)}, s32[768,27]{0,1:T(8,128)S(1)}, ...), condition=%wide.region_2.4_spmd.clone, body=%wide.region_1.3_spmd.clone.sunk | while | flops 906390784 | bytes 23505060 | solution.py:71
  511.8 20.0 %gather_fusion = bf16[6912,256]{1,0:T(8,128)(2,1)} fusion(bf16[1345,256]{1,0:T(8,128)(2,1)S(1)} %get-tuple-element.424, s32[7168]{0:T(1024)S(1)} %pad_clamp_fusion.5), kind=kCustom, calls=%fused_computation.1.clone.clone.1 | custom fusion | bytes 7105536 | tf_op jit(solution)/shard_map/while/body/eval_jaxpr/gather | solution.py:65
  531.7 7.8 reshape.303
  539.5 5.3 fusion.45
  545.3 20.0 %gather_fusion = bf16[6912,256]{1,0:T(8,128)(2,1)} fusion(bf16[1345,256]{1,0:T(8,128)(2,1)S(1)} %get-tuple-element.424, s32[7168]{0:T(1024)S(1)} %pad_clamp_fusion.5), kind=kCustom, calls=%fused_computation.1.clone.clone.1 | custom fusion | bytes 7105536 | tf_op jit(solution)/shard_map/while/body/eval_jaxpr/gather | solution.py:65
  565.3 7.8 reshape.303
  573.1 5.3 fusion.45
  578.9 20.0 %gather_fusion = bf16[6912,256]{1,0:T(8,128)(2,1)} fusion(bf16[1345,256]{1,0:T(8,128)(2,1)S(1)} %get-tuple-element.424, s32[7168]{0:T(1024)S(1)} %pad_clamp_fusion.5), kind=kCustom, calls=%fused_computation.1.clone.clone.1 | custom fusion | bytes 7105536 | tf_op jit(solution)/shard_map/while/body/eval_jaxpr/gather | solution.py:65
  598.9 7.8 reshape.303
  606.7 5.3 fusion.45
  611.9 1.1 fusion.20
  613.1 3.7 broadcast_in_dim.69.clone
  616.8 238.7 %while.31 = (s32[]{:T(128)}, f32[1344,256]{1,0:T(8,128)}, f32[27,256,256]{2,1,0:T(8,128)}, s32[1344,27]{0,1:T(8,128)S(1)}, bf16[769,256]{1,0:T(8,128)(2,1)S(1)},...) while((s32[]{:T(128)}, f32[1344,256]{1,0:T(8,128)}, ...), condition=%wide.region_5.7_spmd.clone, body=%wide.region_4.6_spmd.clone.sunk | while | flops 3171630592 | bytes 85074704 | solution.py:111
  617.6 34.7 %gather_fusion.1 = bf16[12096,256]{1,0:T(8,128)(2,1)} fusion(bf16[769,256]{1,0:T(8,128)(2,1)S(1)} %get-tuple-element.456, s32[12288]{0:T(1024)S(1)} %pad_clamp_fusion.6), kind=kCustom, calls=%fused_computation.2.clone.clone.1 | custom fusion | bytes 12434688 | tf_op jit(solution)/shard_map/while/body/eval_jaxpr/gather | solution.py:91
  652.3 11.9 %reshape.308 = bf16[1344,2304]{1,0:T(8,128)(2,1)} reshape(bf16[12096,256]{1,0:T(8,128)(2,1)} %gather_fusion.1) | data formatting | bytes 12386304 | tf_op jit(solution)/shard_map/while/body/eval_jaxpr/reshape | solution.py:91
  664.2 6.2 fusion.51
  670.5 2.0 copy.60
  672.5 1.6 constant_dynamic-update-slice_fusion.14
  674.2 12.8 %reshape.307 = bf16[1344,9,256]{2,1,0:T(8,128)(2,1)} reshape(bf16[12096,256]{1,0:T(8,128)(2,1)} %gather_fusion.1) | data formatting | bytes 12386304 | tf_op jit(solution)/shard_map/while/body/eval_jaxpr/gather | solution.py:91
  686.9 8.3 fusion.50
  695.2 1.2 copy-done.2
  697.2 34.7 %gather_fusion.1 = bf16[12096,256]{1,0:T(8,128)(2,1)} fusion(bf16[769,256]{1,0:T(8,128)(2,1)S(1)} %get-tuple-element.456, s32[12288]{0:T(1024)S(1)} %pad_clamp_fusion.6), kind=kCustom, calls=%fused_computation.2.clone.clone.1 | custom fusion | bytes 12434688 | tf_op jit(solution)/shard_map/while/body/eval_jaxpr/gather | solution.py:91
  731.9 11.9 %reshape.308 = bf16[1344,2304]{1,0:T(8,128)(2,1)} reshape(bf16[12096,256]{1,0:T(8,128)(2,1)} %gather_fusion.1) | data formatting | bytes 12386304 | tf_op jit(solution)/shard_map/while/body/eval_jaxpr/reshape | solution.py:91
  743.8 6.2 fusion.51
  750.1 2.0 copy.60
  752.1 1.5 constant_dynamic-update-slice_fusion.14
  753.7 12.8 %reshape.307 = bf16[1344,9,256]{2,1,0:T(8,128)(2,1)} reshape(bf16[12096,256]{1,0:T(8,128)(2,1)} %gather_fusion.1) | data formatting | bytes 12386304 | tf_op jit(solution)/shard_map/while/body/eval_jaxpr/gather | solution.py:91
  766.4 8.3 fusion.50
  774.7 1.2 copy-done.2
  776.7 34.7 %gather_fusion.1 = bf16[12096,256]{1,0:T(8,128)(2,1)} fusion(bf16[769,256]{1,0:T(8,128)(2,1)S(1)} %get-tuple-element.456, s32[12288]{0:T(1024)S(1)} %pad_clamp_fusion.6), kind=kCustom, calls=%fused_computation.2.clone.clone.1 | custom fusion | bytes 12434688 | tf_op jit(solution)/shard_map/while/body/eval_jaxpr/gather | solution.py:91
  811.4 11.9 %reshape.308 = bf16[1344,2304]{1,0:T(8,128)(2,1)} reshape(bf16[12096,256]{1,0:T(8,128)(2,1)} %gather_fusion.1) | data formatting | bytes 12386304 | tf_op jit(solution)/shard_map/while/body/eval_jaxpr/reshape | solution.py:91
  823.4 6.2 fusion.51
  829.6 2.0 copy.60
  831.6 1.6 constant_dynamic-update-slice_fusion.14
  833.2 12.8 %reshape.307 = bf16[1344,9,256]{2,1,0:T(8,128)(2,1)} reshape(bf16[12096,256]{1,0:T(8,128)(2,1)} %gather_fusion.1) | data formatting | bytes 12386304 | tf_op jit(solution)/shard_map/while/body/eval_jaxpr/gather | solution.py:91
  845.9 8.3 fusion.50
  854.3 1.2 copy-done.2
  856.9 1.6 collective-permute-start.6
  858.6 1.3 collective-permute-start.11
  859.9 3.0 collective-permute-start.10
  862.9 1.3 collective-permute-start.9
  864.2 4.5 collective-permute-start.8
  868.8 1.3 collective-permute-start.7
  870.1 4.8 collective-permute-done.7
  875.0 6.7 scatter_custom_fusion
  882.5 137.4 %all-reduce.3.cloned.1.call-done = f32[27,256,256]{2,1,0:T(8,128)} async-done(((f32[27,256,256]{2,1,0:T(8,128)}), f32[27,256,256]{2,1,0:T(8,128)}) %all-reduce.3.cloned.1.call-update) | async-done | bytes 7077904 | tf_op jit(solution)/shard_map/psum | solution.py:148
  1019.9 5.7 multiply_convert_fusion
  (115 shorter events, 10.8 us)
Async XLA Ops:
  7.2 1012.7 %all-reduce.3.cloned.1.call-start = ((), (), s32[]{:S(2)}) async-start(), calls=%async_computation | async-start | bytes 14155776 | tf_op jit(solution)/shard_map/psum | solution.py:148
  11.2 498.7 %collective-permute-start.5 = (bf16[1,96,256]{2,1,0:T(8,128)(2,1)S(1)}, bf16[1,96,256]{2,1,0:T(8,128)(2,1)S(1)}, u32[]{:S(2)}, u32[]{:S(2)}) collective-permute-start(bf16[1,96,256]{2,1,0:T(8,128)(2,1)S(1)} %get-tuple-element.321), channel_id=1, source_target_pairs={{1,0},{2,1},{3,2},{5,4},{6,5},{7,6},{9,8},{10,9},{11,10},{13,12},{... | collective-permute-start | bytes 147464 | tf_op jit(solution)/shard_map/ppermute | solution.py:17
  12.5 497.3 %collective-permute-start.4 = (bf16[1,96,256]{2,1,0:T(8,128)(2,1)S(1)}, bf16[1,96,256]{2,1,0:T(8,128)(2,1)S(1)}, u32[]{:S(2)}, u32[]{:S(2)}) collective-permute-start(bf16[1,96,256]{2,1,0:T(8,128)(2,1)S(1)} %get-tuple-element.322), channel_id=1, source_target_pairs={{0,1},{1,2},{2,3},{4,5},{5,6},{6,7},{8,9},{9,10},{10,11},{12,13},{... | collective-permute-start | bytes 147464 | tf_op jit(solution)/shard_map/ppermute | solution.py:15
  15.6 494.3 %collective-permute-start.3 = (bf16[1,96,256]{2,1,0:T(8,128)(2,1)S(1)}, bf16[1,96,256]{2,1,0:T(8,128)(2,1)S(1)}, u32[]{:S(2)}, u32[]{:S(2)}) collective-permute-start(bf16[1,96,256]{2,1,0:T(8,128)(2,1)S(1)} %get-tuple-element.323), channel_id=1, source_target_pairs={{4,0},{8,4},{12,8},{5,1},{9,5},{13,9},{6,2},{10,6},{14,10},{7,3},{... | collective-permute-start | bytes 147464 | tf_op jit(solution)/shard_map/ppermute | solution.py:17
  16.9 493.0 %collective-permute-start.2 = (bf16[1,96,256]{2,1,0:T(8,128)(2,1)S(1)}, bf16[1,96,256]{2,1,0:T(8,128)(2,1)S(1)}, u32[]{:S(2)}, u32[]{:S(2)}) collective-permute-start(bf16[1,96,256]{2,1,0:T(8,128)(2,1)S(1)} %get-tuple-element.324), channel_id=1, source_target_pairs={{0,4},{4,8},{8,12},{1,5},{5,9},{9,13},{2,6},{6,10},{10,14},{3,7},{... | collective-permute-start | bytes 147464 | tf_op jit(solution)/shard_map/ppermute | solution.py:15
  22.5 481.4 %collective-permute-start = (bf16[1,96,256]{2,1,0:T(8,128)(2,1)S(1)}, bf16[1,96,256]{2,1,0:T(8,128)(2,1)S(1)}, u32[]{:S(2)}, u32[]{:S(2)}) collective-permute-start(bf16[1,96,256]{2,1,0:T(8,128)(2,1)S(1)} %get-tuple-element.326), channel_id=1, source_target_pairs={{0,16},{1,17},{2,18},{3,19},{4,20},{5,21},{6,22},{7,23},{8,24},{9,... | collective-permute-start | bytes 147464 | tf_op jit(solution)/shard_map/ppermute | solution.py:15
  265.3 156.2 %copy-start.6 = (s32[1,1,1,27,768]{4,2,3,1,0:T(1,128)S(1)}, s32[1,1,1,27,768]{4,2,3,1,0:T(1,128)}, u32[]{:S(2)}) copy-start(s32[1,1,1,27,768]{4,2,3,1,0:T(1,128)} %param.18) | copy-start | bytes 248836
  265.4 156.2 %copy-start.7 = (s32[1,1,1,27,768]{4,2,3,1,0:T(1,128)S(1)}, s32[1,1,1,27,768]{4,2,3,1,0:T(1,128)}, u32[]{:S(2)}) copy-start(s32[1,1,1,27,768]{4,2,3,1,0:T(1,128)} %param.19) | copy-start | bytes 248836
  421.5 88.4 %copy-start = (bf16[1,1,1,768,256]{4,3,2,1,0:T(8,128)(2,1)S(1)}, bf16[1,1,1,768,256]{4,3,2,1,0:T(8,128)(2,1)}, u32[]{:S(2)}) copy-start(bf16[1,1,1,768,256]{4,3,2,1,0:T(8,128)(2,1)} %param.13) | copy-start | bytes 1179652
  503.9 6.0 collective-permute-start.1
  511.2 100.8 %copy-start.5 = (bf16[1,1,1,768,256]{4,3,2,1,0:T(8,128)(2,1)S(1)}, bf16[1,1,1,768,256]{4,3,2,1,0:T(8,128)(2,1)}, u32[]{:S(2)}) copy-start(bf16[1,1,1,768,256]{4,3,2,1,0:T(8,128)(2,1)} %param.15) | copy-start | bytes 1179652
  652.3 11.9 %copy-start.4 = (bf16[1344,256]{1,0:T(8,128)(2,1)S(1)}, bf16[1344,256]{1,0:T(8,128)(2,1)}, u32[]{:S(2)}) copy-start(bf16[1344,256]{1,0:T(8,128)(2,1)} %get-tuple-element.458) | copy-start | bytes 2064388 | tf_op jit(solution)/shard_map/while
  674.1 12.8 %copy-start.1 = (f32[1344,256]{1,0:T(8,128)S(1)}, f32[1344,256]{1,0:T(8,128)}, u32[]{:S(2)}) copy-start(f32[1344,256]{1,0:T(8,128)} %get-tuple-element.442) | copy-start | bytes 4128772 | tf_op jit(solution)/shard_map/while
  695.2 1.2 copy-start.2
  731.9 11.9 %copy-start.4 = (bf16[1344,256]{1,0:T(8,128)(2,1)S(1)}, bf16[1344,256]{1,0:T(8,128)(2,1)}, u32[]{:S(2)}) copy-start(bf16[1344,256]{1,0:T(8,128)(2,1)} %get-tuple-element.458) | copy-start | bytes 2064388 | tf_op jit(solution)/shard_map/while
  753.7 12.8 %copy-start.1 = (f32[1344,256]{1,0:T(8,128)S(1)}, f32[1344,256]{1,0:T(8,128)}, u32[]{:S(2)}) copy-start(f32[1344,256]{1,0:T(8,128)} %get-tuple-element.442) | copy-start | bytes 4128772 | tf_op jit(solution)/shard_map/while
  774.7 1.2 copy-start.2
  811.4 11.9 %copy-start.4 = (bf16[1344,256]{1,0:T(8,128)(2,1)S(1)}, bf16[1344,256]{1,0:T(8,128)(2,1)}, u32[]{:S(2)}) copy-start(bf16[1344,256]{1,0:T(8,128)(2,1)} %get-tuple-element.458) | copy-start | bytes 2064388 | tf_op jit(solution)/shard_map/while
  833.2 12.8 %copy-start.1 = (f32[1344,256]{1,0:T(8,128)S(1)}, f32[1344,256]{1,0:T(8,128)}, u32[]{:S(2)}) copy-start(f32[1344,256]{1,0:T(8,128)} %get-tuple-element.442) | copy-start | bytes 4128772 | tf_op jit(solution)/shard_map/while
  854.2 1.2 copy-start.2
  855.4 0.7 copy-start.8
  855.4 1.4 copy-start.3
  856.9 11.9 %collective-permute-start.6 = (bf16[1,96,256]{2,1,0:T(8,128)(2,1)S(1)}, bf16[1,96,256]{2,1,0:T(8,128)(2,1)S(1)}, u32[]{:S(2)}, u32[]{:S(2)}) collective-permute-start(bf16[1,96,256]{2,1,0:T(8,128)(2,1)S(1)} %get-tuple-element.320), channel_id=1, source_target_pairs={{0,16},{1,17},{2,18},{3,19},{4,20},{5,21},{6,22},{7,23},{8,24},{9,... | collective-permute-start | bytes 147464 | tf_op jit(solution)/shard_map/ppermute | solution.py:15
  858.6 16.4 %collective-permute-start.11 = (bf16[1,96,256]{2,1,0:T(8,128)(2,1)S(1)}, bf16[1,96,256]{2,1,0:T(8,128)(2,1)S(1)}, u32[]{:S(2)}, u32[]{:S(2)}) collective-permute-start(bf16[1,96,256]{2,1,0:T(8,128)(2,1)S(1)} %get-tuple-element.315), channel_id=1, source_target_pairs={{1,0},{2,1},{3,2},{5,4},{6,5},{7,6},{9,8},{10,9},{11,10},{13,12},{... | collective-permute-start | bytes 147464 | tf_op jit(solution)/shard_map/ppermute | solution.py:17
  859.9 15.1 %collective-permute-start.10 = (bf16[1,96,256]{2,1,0:T(8,128)(2,1)S(1)}, bf16[1,96,256]{2,1,0:T(8,128)(2,1)S(1)}, u32[]{:S(2)}, u32[]{:S(2)}) collective-permute-start(bf16[1,96,256]{2,1,0:T(8,128)(2,1)S(1)} %get-tuple-element.316), channel_id=1, source_target_pairs={{0,1},{1,2},{2,3},{4,5},{5,6},{6,7},{8,9},{9,10},{10,11},{12,13},{... | collective-permute-start | bytes 147464 | tf_op jit(solution)/shard_map/ppermute | solution.py:15
  862.9 12.0 %collective-permute-start.9 = (bf16[1,96,256]{2,1,0:T(8,128)(2,1)S(1)}, bf16[1,96,256]{2,1,0:T(8,128)(2,1)S(1)}, u32[]{:S(2)}, u32[]{:S(2)}) collective-permute-start(bf16[1,96,256]{2,1,0:T(8,128)(2,1)S(1)} %get-tuple-element.317), channel_id=1, source_target_pairs={{4,0},{8,4},{12,8},{5,1},{9,5},{13,9},{6,2},{10,6},{14,10},{7,3},{... | collective-permute-start | bytes 147464 | tf_op jit(solution)/shard_map/ppermute | solution.py:17
  864.2 10.7 %collective-permute-start.8 = (bf16[1,96,256]{2,1,0:T(8,128)(2,1)S(1)}, bf16[1,96,256]{2,1,0:T(8,128)(2,1)S(1)}, u32[]{:S(2)}, u32[]{:S(2)}) collective-permute-start(bf16[1,96,256]{2,1,0:T(8,128)(2,1)S(1)} %get-tuple-element.318), channel_id=1, source_target_pairs={{0,4},{4,8},{8,12},{1,5},{5,9},{9,13},{2,6},{6,10},{10,14},{3,7},{... | collective-permute-start | bytes 147464 | tf_op jit(solution)/shard_map/ppermute | solution.py:15
  868.8 6.1 collective-permute-start.7
Sparse Core Ops, SparseCore 0:
  855.6 164.2 all-reduce.2
where the time goes:
time: 1040 us; the launch traced here: 1030 us
  local copies, waits for them, and re-layouts  760 us (73%)
  waiting for transfers between devices  147 us (14%)
  matrix products  59.3 us (6%)
  starting transfers between devices  29.4 us (3%)
  other arithmetic  21.6 us (2%)
  between operations  14.6 us (1%)
    unnamed x29, local copies, waits for them, and re-layouts  161 us
    gather x3, local copies, waits for them, and re-layouts, pairing_tables(): live_at_out = jnp.take_along_axis(occupancy_flags, inverse_out, axis=1)  156 us
    gather x2, local copies, waits for them, and re-layouts, pairing_tables(): source_at_out = jnp.take_along_axis(source_voxels, inverse_out, axis=1)  156 us
    gather x6, local copies, waits for them, and re-layouts, accumulate(): gradient_zero[places].reshape(extended_rows, group_length * channels)  142 us
    psum x1, waiting for transfers between devices, shards(): summed = lax.psum(weight_partial, ('gx', 'gy', 'gz'))  137 us
    gather x6, local copies, waits for them, and re-layouts, accumulate(): gathered = padded_zero[picks].reshape(own_rows, group_length * channels)  83.2 us
    reshape x3, local copies, waits for them, and re-layouts, accumulate(): gradient_zero[places].reshape(extended_rows, group_length * channels)  35.8 us
    dot_general x3, matrix products, accumulate(): jnp.dot(chosen, kernels, preferred_element_type=jnp.float32)  24.9 us
  transfers between devices with their start and end apart: 13, of which 3 were waited for; matrix products, arithmetic and copies ran while one was open for 47% of the time, Pallas kernels for 0%

commit v1 on v0

v1 whole, which is shorter than its diff:
```python
import jax
import jax.numpy as jnp
from jax import lax
from jax.experimental import pallas as pl
from jax.experimental.pallas import tpu as pltpu
from jax.sharding import PartitionSpec as P

BF = jnp.bfloat16
F32 = jnp.float32
NT = (((1,), (1,)), ((), ()))
NN = (((1,), (0,)), ((), ()))
TN = (((0,), (0,)), ((), ()))
LIMIT = 56 << 20
AXES = ("gx", "gy", "gz")


def dot(a, b, dims=NN):
    return lax.dot_general(a, b, dims, preferred_element_type=F32)


def one_hot(mask):
    return jnp.where(mask, jnp.ones((), F32), jnp.zeros((), F32)).astype(BF)


def whole(shape):
    return pl.BlockSpec(shape, lambda k: (0,) * len(shape))


def send_kernel(rows_ref, own_ref, sent_ref):
    directions, face = rows_ref.shape
    own = own_ref.shape[0]
    places = lax.broadcasted_iota(jnp.int32, (own, face), 0)
    for d in range(directions):
        hot = one_hot(places == rows_ref[d : d + 1, :])
        sent_ref[d] = dot(hot, own_ref[...], TN).astype(BF)


def send(rows, own_features):
    directions, face = rows.shape
    return pl.pallas_call(
        send_kernel,
        out_shape=jax.ShapeDtypeStruct((directions, face, own_features.shape[1]), BF),
        compiler_params=pltpu.CompilerParams(vmem_limit_bytes=LIMIT),
        name="send",
    )(rows, own_features)


def invert_kernel(block, missing, in_ref, out_ref, live_ref, col_ref, row_ref):
    taps, own = in_ref.shape
    lows = lax.broadcasted_iota(jnp.int32, (block, own), 0)
    ranks = lax.broadcasted_iota(jnp.int32, (8, own), 0)
    for k in range(taps):
        target = out_ref[pl.ds(k, 1), :]
        source = jnp.where(live_ref[pl.ds(k, 1), :] > 0, in_ref[pl.ds(k, 1), :], missing)
        high = target // block
        hot = one_hot(lows == target - high * block)
        big = (source // 16) * 16
        spread = jnp.where(ranks == high, big, jnp.where(ranks - 4 == high, source - big, 0))
        spread = spread.astype(F32).astype(BF)
        col_ref[k] = dot(hot, spread, NT)
        row_ref[k] = dot(spread, hot, NT)


def invert(in_rows, out_rows, live, missing, block):
    taps, own = in_rows.shape
    return pl.pallas_call(
        lambda *refs: invert_kernel(block, missing, *refs),
        out_shape=(
            jax.ShapeDtypeStruct((taps, block, 8), F32),
            jax.ShapeDtypeStruct((taps, 8, block), F32),
        ),
        compiler_params=pltpu.CompilerParams(vmem_limit_bytes=LIMIT),
        name="invert",
    )(in_rows, out_rows, live)


def forward_kernel(
    taps, block, parts, odd_ref, col_ref, own_ref, face_ref, w_ref, up_ref,
    act_ref, gp_ref, keep_ref, give_ref, ext, acc, gt, turned,
):
    k = pl.program_id(0)
    own, ch = own_ref.shape
    rows = ext.shape[0]
    half = ch // 2

    @pl.when(k == 0)
    def _():
        ext[pl.ds(0, own), :] = own_ref[...]
        ext[pl.ds(own, rows - own), :] = face_ref[...]
        acc[...] = jnp.zeros_like(acc)

    lanes = lax.broadcasted_iota(jnp.int32, (block, rows), 1)
    for h in range(parts):
        place = (col_ref[0, :, h : h + 1] + col_ref[0, :, h + 4 : h + 5]).astype(jnp.int32)
        got = dot(one_hot(lanes == place), ext[...]).astype(BF)
        gt[pl.ds(pl.multiple_of(k * ch, ch), ch), pl.ds(h * block, block)] = got.T
        acc[pl.ds(h * block, block), :] += dot(got, w_ref[0])

    @pl.when(k == taps - 1)
    def _():
        v = acc[...]
        s = jax.nn.sigmoid(v)
        act_ref[...] = (v * s).astype(BF)
        g = up_ref[...].astype(F32) * (s * (1.0 + v * (1.0 - s)))
        gp_ref[...] = g.astype(BF)
        first = jnp.where(odd_ref[0] > 0, g[:, half:], g[:, :half])
        second = jnp.where(odd_ref[0] > 0, g[:, :half], g[:, half:])
        turned[:, :half] = first.astype(BF)
        turned[:, half:] = second.astype(BF)

        def one(t, carried):
            at = pl.multiple_of(t * ch, ch)
            r = dot(gt[pl.ds(at, ch), :], turned[...]).astype(BF)
            keep_ref[pl.ds(at, ch), :] = r[:, :half]
            give_ref[pl.ds(at, ch), :] = r[:, half:]
            return carried

        lax.fori_loop(0, taps, one, 0, unroll=3)


def forward(odd, col, own_features, faces, weight, upstream):
    taps, block, _ = col.shape
    own, ch = own_features.shape
    rows = own + faces.shape[0]
    like = jax.ShapeDtypeStruct
    return pl.pallas_call(
        lambda *refs: forward_kernel(taps, block, own // block, *refs),
        grid=(taps,),
        in_specs=[
            pl.BlockSpec(memory_space=pltpu.SMEM),
            pl.BlockSpec((1, block, 8), lambda k: (k, 0, 0)),
            whole((own, ch)),
            whole(faces.shape),
            pl.BlockSpec((1, ch, ch), lambda k: (k, 0, 0)),
            whole((own, ch)),
        ],
        out_specs=[whole((own, ch)), whole((own, ch)), whole((taps * ch, ch // 2)), whole((taps * ch, ch // 2))],
        out_shape=[
            like((own, ch), BF),
            like((own, ch), BF),
            like((taps * ch, ch // 2), BF),
            like((taps * ch, ch // 2), BF),
        ],
        scratch_shapes=[
            pltpu.VMEM((rows, ch), BF),
            pltpu.VMEM((own, ch), F32),
            pltpu.VMEM((taps * ch, own), BF),
            pltpu.VMEM((own, ch), BF),
        ],
        compiler_params=pltpu.CompilerParams(vmem_limit_bytes=LIMIT),
        name="forward",
    )(odd, col, own_features, faces, weight, upstream)


def backward_kernel(parts, step, row_ref, gp_ref, w_ref, *rest):
    out_ref = rest[-1]
    k = pl.program_id(0)
    rows = out_ref.shape[0]
    block = row_ref.shape[2]

    @pl.when(k == 0)
    def _():
        out_ref[...] = rest[0][...] if len(rest) > 1 else jnp.zeros_like(out_ref)

    for r in range(0, rows, step):
        size = min(step, rows - r)
        lines = lax.broadcasted_iota(jnp.int32, (size, block), 0) + r
        hots = []
        for h in range(parts):
            place = (row_ref[0, h : h + 1, :] + row_ref[0, h + 4 : h + 5, :]).astype(jnp.int32)
            hots.append(one_hot(lines == place))
        got = dot(jnp.concatenate(hots, axis=1), gp_ref[...]).astype(BF)
        out_ref[pl.ds(r, size), :] += dot(got, w_ref[0], NT)


def backward(row, gp, weight, first, count, before, rows):
    block = row.shape[2]
    own, ch = gp.shape
    specs = [
        pl.BlockSpec((1, 8, block), lambda k: (k + first, 0, 0)),
        whole((own, ch)),
        pl.BlockSpec((1, ch, ch), lambda k: (k + first, 0, 0)),
    ]
    args = [row, gp, weight]
    if before is not None:
        specs.append(whole((rows, ch)))
        args.append(before)
    return pl.pallas_call(
        lambda *refs: backward_kernel(own // block, 448, *refs),
        grid=(count,),
        in_specs=specs,
        out_specs=whole((rows, ch)),
        out_shape=jax.ShapeDtypeStruct((rows, ch), F32),
        compiler_params=pltpu.CompilerParams(vmem_limit_bytes=LIMIT),
        name="backward",
    )(*args)


def finish_kernel(rows_ref, grad_ref, back_ref, out_ref):
    directions, face = rows_ref.shape
    own = out_ref.shape[0]
    places = lax.broadcasted_iota(jnp.int32, (own, face), 0)
    total = grad_ref[...]
    for d in range(directions):
        hot = one_hot(places == rows_ref[d : d + 1, :])
        total = total + dot(hot, back_ref[d])
    out_ref[...] = total.astype(BF)


def finish(rows, grad_extended, returned, own):
    ch = grad_extended.shape[1]
    return pl.pallas_call(
        finish_kernel,
        grid=(1,),
        in_specs=[whole(rows.shape), whole((own, ch)), whole(returned.shape)],
        out_specs=whole((own, ch)),
        out_shape=jax.ShapeDtypeStruct((own, ch), BF),
        compiler_params=pltpu.CompilerParams(vmem_limit_bytes=LIMIT),
        name="finish",
    )(rows, grad_extended, returned)


def trade(faces):
    got = [None] * 6
    for i, axis in enumerate(AXES):
        lower, upper = 2 * i, 2 * i + 1
        n = lax.axis_size(axis)
        if n == 2:
            last = lax.axis_index(axis) == 1
            moved = lax.ppermute(jnp.where(last, faces[lower], faces[upper]), axis, [(0, 1), (1, 0)])
            blank = jnp.zeros_like(moved)
            got[lower] = jnp.where(last, moved, blank)
            got[upper] = jnp.where(last, blank, moved)
        else:
            got[lower] = lax.ppermute(faces[upper], axis, [(j, j + 1) for j in range(n - 1)])
            got[upper] = lax.ppermute(faces[lower], axis, [(j + 1, j) for j in range(n - 1)])
    return jnp.stack(got)


def add(a, b):
    return (a.astype(F32) + b.astype(F32)).astype(BF)


def swap(x, axis, bit):
    n = lax.axis_size(axis)
    return lax.ppermute(x, axis, [(j, j ^ (1 << bit)) for j in range(n)])


def side(axis, bit):
    return (lax.axis_index(axis) >> bit) & 1


def cut(x, which):
    half = x.shape[0] // 2
    return lax.dynamic_slice_in_dim(x, which * half, half, 0)


def join(mine, other, which):
    half = mine.shape[0]
    out = jnp.zeros((2 * half,) + mine.shape[1:], mine.dtype)
    out = lax.dynamic_update_slice_in_dim(out, mine, which * half, 0)
    return lax.dynamic_update_slice_in_dim(out, other, (1 - which) * half, 0)


def reduce_all(keep, give, scaling):
    bits = lambda axis, low: [(axis, b) for b in range(low, lax.axis_size(axis).bit_length() - 1)]
    plane = [bits("gx", 0) + bits("gz", 1), bits("gz", 1) + bits("gx", 0)]
    x = add(keep, swap(give, "gz", 0))
    rows, ch = x.shape
    pieces = [x[: rows // 2], x[rows // 2 :]]
    for turn in range(len(plane[0])):
        for i in range(2):
            axis, bit = plane[i][turn]
            mine = side(axis, bit)
            pieces[i] = add(cut(pieces[i], mine), swap(cut(pieces[i], 1 - mine), axis, bit))
    n = lax.axis_size("gy")
    at = lax.axis_index("gy")
    joint = jnp.concatenate([p.reshape(n, -1, ch) for p in pieces], axis=1)
    slot = lambda s: lax.dynamic_index_in_dim(joint, (at + s) % n, 0, keepdims=False)
    turn_by = lambda y, s: lax.ppermute(y, "gy", [(j, (j + s) % n) for j in range(n)])
    total = slot(0).astype(F32)
    for s in range(1, n):
        total = total + turn_by(slot(s), s).astype(F32)
    mine = (total * scaling).astype(BF)
    full = jnp.zeros_like(joint)
    full = lax.dynamic_update_index_in_dim(full, mine, at, 0)
    for s in range(1, n):
        full = lax.dynamic_update_index_in_dim(full, turn_by(mine, s), (at - s) % n, 0)
    size = full.shape[1] // 2
    pieces = [full[:, :size].reshape(-1, ch), full[:, size:].reshape(-1, ch)]
    for turn in reversed(range(len(plane[0]))):
        for i in range(2):
            axis, bit = plane[i][turn]
            pieces[i] = join(pieces[i], swap(pieces[i], axis, bit), side(axis, bit))
    mine = jnp.concatenate(pieces, axis=0)
    other = swap(mine, "gz", 0)
    odd = side("gz", 0) == 1
    return jnp.concatenate([jnp.where(odd, other, mine), jnp.where(odd, mine, other)], axis=1)


def shards(features, weight, upstream, send_rows, in_rows, out_rows, tap_pair_exists):
    own_features = features[0, 0, 0]
    own, ch = own_features.shape
    sends = send_rows[0, 0, 0]
    taps = weight.shape[0]
    block = 256
    sent = send(sends, own_features)
    faces = trade([sent[d] for d in range(6)]).reshape(-1, ch)
    rows = own + faces.shape[0]
    col, row = invert(in_rows[0, 0, 0], out_rows[0, 0, 0], tap_pair_exists[0, 0, 0], 2000, block)
    odd = side("gz", 0).reshape(1)
    activated, gp, keep, give = forward(odd, col, own_features, faces, weight, upstream[0, 0, 0])
    devices = lax.axis_size("gx") * lax.axis_size("gy") * lax.axis_size("gz")
    grad_weight = reduce_all(keep, give, float(devices * own) ** -0.5).reshape(weight.shape)
    grad = None
    for first in range(0, taps, 9):
        grad = backward(row, gp, weight, first, 9, grad, rows)
    back = grad[own:].astype(BF).reshape(6, -1, ch)
    returned = trade([back[d] for d in range(6)])
    grad_features = finish(sends, grad, returned, own)
    return activated[None, None, None], grad_features[None, None, None], grad_weight


def solution(mesh):
    part = P("gx", "gy", "gz", None, None)
    return jax.shard_map(
        shards,
        mesh=mesh,
        in_specs=(part, P(), part, part, part, part, part),
        out_specs=(part, part, P()),
        check_vma=False,
    )
```

time: 1040 us -> 229 us (0.22)
  local copies, waits for them, and re-layouts: 760 us -> 6.99 us
  Pallas kernels: 0 us -> 117 us
  waiting for transfers between devices: 147 us -> 46.3 us
  matrix products: 59.3 us -> 0 us
  starting transfers between devices: 29.4 us -> 43.9 us
  between operations: 14.6 us -> 1.02 us
  other arithmetic: 21.6 us -> 10.5 us
    gather x18 -> x0, local copies, waits for them, and re-layouts: 541 us -> none  [the longest x3 156 us: pairing_tables(): live_at_out = jnp.take_along_axis(occupancy_flags, inverse_out, axis=1)]
    unnamed x29 -> x13, local copies, waits for them, and re-layouts: 161 us -> 5.87 us
    psum x1 -> x0, waiting for transfers between devices: 137 us -> none  [shards(): summed = lax.psum(weight_partial, ('gx', 'gy', 'gz'))]
    pallas_call x0 -> x7, Pallas kernels: none -> 117 us  [the longest x1 55.9 us: forward(): pl.pallas_call(lambda *refs: forward_kernel(taps, block, own // block, *r...]
    dot_general x9 -> x0, matrix products: 59.3 us -> none  [the longest x3 24.9 us: accumulate(): jnp.dot(chosen, kernels, preferred_element_type=jnp.float32)]
    ppermute x12 -> x26, waiting for transfers between devices: 9.5 us -> 46.3 us  [the longest x10 33.3 us: swap(): return lax.ppermute(x, axis, [(j, j ^ 1 << bit) for j in range(n)])]
    reshape x3 -> x0, local copies, waits for them, and re-layouts: 35.8 us -> none  [accumulate(): gradient_zero[places].reshape(extended_rows, group_length * channels)]
    ppermute x12 -> x26, starting transfers between devices: 29.3 us -> 43.9 us  [the longest x10 12.5 us: swap(): return lax.ppermute(x, axis, [(j, j ^ 1 << bit) for j in range(n)])]
  transfers between devices with their start and end apart: 13 -> 26, of which waited for: 3 -> 14; matrix products, arithmetic and copies ran while one was open for 47% -> 3% of each run, Pallas kernels for 0% -> 26%
where the time goes in v1:
time: 229 us; the launch traced here: 225 us
  Pallas kernels  117 us (51%)
  waiting for transfers between devices  46.3 us (20%)
  starting transfers between devices  43.9 us (19%)
  other arithmetic  10.5 us (5%)
  local copies, waits for them, and re-layouts  6.99 us (3%)
    pallas_call x1, Pallas kernels, forward(): pl.pallas_call(lambda *refs: forward_kernel(taps, block, own // block, *r...  55.9 us
    pallas_call x3, Pallas kernels, backward(): pl.pallas_call(lambda *refs: backward_kernel(own // block, 448, *refs), g...  47.4 us
    ppermute x10, waiting for transfers between devices, swap(): return lax.ppermute(x, axis, [(j, j ^ 1 << bit) for j in range(n)])  33.3 us
    ppermute x10, starting transfers between devices, swap(): return lax.ppermute(x, axis, [(j, j ^ 1 << bit) for j in range(n)])  12.5 us
    ppermute x4, starting transfers between devices, trade(): lax.ppermute(faces[upper], axis, [(j, j + 1) for j in range(n - 1)])  11.6 us
    ppermute x6, starting transfers between devices, reduce_all(): lax.ppermute(y, 'gy', [(j, (j + s) % n) for j in range(n)])  11.3 us
    ppermute x6, waiting for transfers between devices, reduce_all(): lax.ppermute(y, 'gy', [(j, (j + s) % n) for j in range(n)])  11 us
    pallas_call x1, Pallas kernels, invert(): pl.pallas_call(lambda *refs: invert_kernel(block, missing, *refs), out_sh...  8.48 us
  transfers between devices with their start and end apart: 26, of which 14 were waited for; matrix products, arithmetic and copies ran while one was open for 3% of the time, Pallas kernels for 26%

profile of v1, /device:TPU:0, one launch (start us, length us, event | category | flops | bytes accessed | tf_op | source)
XLA Modules:
  0.0 225.4 jit_solution(5960952258200624704)
XLA Ops:
  0.6 1.3 copy.19
  1.9 2.3 %send.1 = bf16[6,96,256]{2,1,0:T(8,128)(2,1)} custom-call(s32[6,96]{1,0:T(8,128)} %bitcast.90, bf16[768,256]{1,0:T(8,128)(2,1)} %bitcast.80), custom_call_target="tpu_custom_call" | custom-call | tf_op jit(solution)/shard_map/send/pallas_call | solution.py:40
  4.2 0.9 slice_bitcast_fusion
  5.1 3.0 %collective-permute-start = (bf16[96,256]{1,0:T(8,128)(2,1)S(1)}, bf16[96,256]{1,0:T(8,128)(2,1)S(1)}, u32[]{:S(2)}, u32[]{:S(2)}) collective-permute-start(bf16[96,256]{1,0:T(8,128)(2,1)S(1)} %get-tuple-element.35), channel_id=1, source_target_pairs={{0,16},{16,0},{1,17},{17,1},{2,18},{18,2},{3,19},{19,3},{4,20},{20... | collective-permute-start | bytes 147464 | tf_op jit(solution)/shard_map/ppermute | solution.py:230
  8.1 3.5 %collective-permute-start.1 = (bf16[96,256]{1,0:T(8,128)(2,1)S(1)}, bf16[96,256]{1,0:T(8,128)(2,1)S(1)}, u32[]{:S(2)}, u32[]{:S(2)}) collective-permute-start(bf16[96,256]{1,0:T(8,128)(2,1)S(1)} %get-tuple-element.34), channel_id=1, source_target_pairs={{0,4},{4,8},{8,12},{1,5},{5,9},{9,13},{2,6},{6,10},{10,14},{3,7},{... | collective-permute-start | bytes 147464 | tf_op jit(solution)/shard_map/ppermute | solution.py:235
  11.6 1.3 collective-permute-start.2
  12.9 1.3 collective-permute-start.3
  14.2 1.3 collective-permute-start.4
  15.5 1.6 copy_bitcast_fusion
  17.1 1.5 copy.18
  18.7 8.5 %invert.1 = (f32[27,256,8]{2,1,0:T(8,128)}, f32[27,8,256]{2,1,0:T(8,128)}) custom-call(s32[27,768]{1,0:T(8,128)} %bitcast.88, s32[27,768]{1,0:T(8,128)} %get-tuple-element.37.refs_1_, s32[27,768]{1,0:T(8,128)} %get-tuple-element.36.refs_2_), custom_call_target="tpu_custom_call" | custom-call | tf_op jit(solution)/shard_map/invert/pallas_call | solution.py:66
  27.3 0.7 copy-done
  28.0 55.9 %forward.1 = (bf16[768,256]{1,0:T(8,128)(2,1)}, bf16[768,256]{1,0:T(8,128)(2,1)}, bf16[6912,128]{1,0:T(8,128)(2,1)}, bf16[6912,128]{1,0:T(8,128)(2,1)}) custom-call(s32[1]{0:T(128)} %bitcast.refs_0_, f32[27,256,8]{2,1,0:T(8,128)} %get-tuple-element.9.refs_1_, bf16[768,256]{1,0:T(8,128)(2,1)} %bitcast.81, bf16[576,256]{1,0:T(8,128)(2,1)} %bitcast.86, ...), custom_call_target="tpu_custom_call" | custom-call | tf_op jit(solution)/shard_map/forward/pallas_call | solution.py:126
  83.9 2.9 %collective-permute-start.10 = (bf16[6912,128]{1,0:T(8,128)(2,1)}, bf16[6912,128]{1,0:T(8,128)(2,1)S(1)}, u32[]{:S(2)}, u32[]{:S(2)}) collective-permute-start(bf16[6912,128]{1,0:T(8,128)(2,1)} %get-tuple-element.14), channel_id=1, source_target_pairs={{0,1},{1,0},{2,3},{3,2},{4,5},{5,4},{6,7},{7,6},{8,9},{9,8},{10,11... | collective-permute-start | bytes 5308424 | tf_op jit(solution)/shard_map/ppermute | solution.py:246
  86.7 3.5 %collective-permute-done.10 = bf16[6912,128]{1,0:T(8,128)(2,1)S(1)} collective-permute-done((bf16[6912,128]{1,0:T(8,128)(2,1)}, bf16[6912,128]{1,0:T(8,128)(2,1)S(1)}, u32[]{:S(2)}, u32[]{:S(2)}) %collective-permute-start.10) | collective-permute-done | bytes 1769504 | tf_op jit(solution)/shard_map/ppermute | solution.py:246
  90.3 1.9 add_convert_fusion
  92.2 0.1 fusion.14
  92.4 2.1 collective-permute-start.13
  94.5 0.6 collective-permute-start.11
  95.1 9.8 %collective-permute-done.13 = bf16[1728,128]{1,0:T(8,128)(2,1)S(1)} collective-permute-done((bf16[1728,128]{1,0:T(8,128)(2,1)S(1)}, bf16[1728,128]{1,0:T(8,128)(2,1)S(1)}, u32[]{:S(2)}, u32[]{:S(2)}) %collective-permute-start.13) | collective-permute-done | bytes 442400 | tf_op jit(solution)/shard_map/ppermute | solution.py:246
  104.9 0.1 add_convert_fusion.1
  105.1 0.6 collective-permute-start.14
  105.7 0.8 collective-permute-done.11
  106.5 0.1 add_convert_fusion.2
  106.6 1.0 collective-permute-start.12
  107.6 4.4 %collective-permute-done.14 = bf16[864,128]{1,0:T(8,128)(2,1)S(1)} collective-permute-done((bf16[864,128]{1,0:T(8,128)(2,1)S(1)}, bf16[864,128]{1,0:T(8,128)(2,1)S(1)}, u32[]{:S(2)}, u32[]{:S(2)}) %collective-permute-start.14) | collective-permute-done | bytes 221216 | tf_op jit(solution)/shard_map/ppermute | solution.py:246
  112.1 0.9 collective-permute-done.12
  113.1 2.7 %collective-permute-start.15 = (bf16[432,128]{1,0:T(8,128)(2,1)S(1)}, bf16[432,128]{1,0:T(8,128)(2,1)S(1)}, u32[]{:S(2)}, u32[]{:S(2)}) collective-permute-start(bf16[432,128]{1,0:T(8,128)(2,1)S(1)} %get-tuple-element.28), channel_id=1, source_target_pairs={{0,4},{4,8},{8,12},{12,0},{1,5},{5,9},{9,13},{13,1},{2,6},{6,10},{... | collective-permute-start | bytes 331784 | tf_op jit(solution)/shard_map/ppermute | solution.py:280
  115.8 2.6 %collective-permute-start.16 = (bf16[432,128]{1,0:T(8,128)(2,1)S(1)}, bf16[432,128]{1,0:T(8,128)(2,1)S(1)}, u32[]{:S(2)}, u32[]{:S(2)}) collective-permute-start(bf16[432,128]{1,0:T(8,128)(2,1)S(1)} %get-tuple-element.29), channel_id=1, source_target_pairs={{0,8},{4,12},{8,0},{12,4},{1,9},{5,13},{9,1},{13,5},{2,10},{6,14},... | collective-permute-start | bytes 331784 | tf_op jit(solution)/shard_map/ppermute | solution.py:280
  118.4 1.4 collective-permute-start.17
  119.7 2.0 collective-permute-done.15
  121.7 3.0 %collective-permute-done.16 = bf16[432,128]{1,0:T(8,128)(2,1)S(1)} collective-permute-done((bf16[432,128]{1,0:T(8,128)(2,1)S(1)}, bf16[432,128]{1,0:T(8,128)(2,1)S(1)}, u32[]{:S(2)}, u32[]{:S(2)}) %collective-permute-start.16) | collective-permute-done | bytes 110624 | tf_op jit(solution)/shard_map/ppermute | solution.py:280
  124.8 2.2 collective-permute-start.18
  127.0 1.6 collective-permute-start.19
  128.7 0.9 collective-permute-start.20
  129.6 3.1 %collective-permute-done.18 = bf16[432,128]{1,0:T(8,128)(2,1)S(1)} collective-permute-done((bf16[432,128]{1,0:T(8,128)(2,1)S(1)}, bf16[432,128]{1,0:T(8,128)(2,1)S(1)}, u32[]{:S(2)}, u32[]{:S(2)}) %collective-permute-start.18) | collective-permute-done | bytes 110624 | tf_op jit(solution)/shard_map/ppermute | solution.py:280
  132.6 3.0 %collective-permute-done.19 = bf16[432,128]{1,0:T(8,128)(2,1)S(1)} collective-permute-done((bf16[432,128]{1,0:T(8,128)(2,1)S(1)}, bf16[432,128]{1,0:T(8,128)(2,1)S(1)}, u32[]{:S(2)}, u32[]{:S(2)}) %collective-permute-start.19) | collective-permute-done | bytes 110624 | tf_op jit(solution)/shard_map/ppermute | solution.py:280
  135.7 1.1 collective-permute-start.21
  136.8 1.5 collective-permute-start.23
  138.5 4.3 %collective-permute-done.21 = bf16[864,128]{1,0:T(8,128)(2,1)S(1)} collective-permute-done((bf16[864,128]{1,0:T(8,128)(2,1)S(1)}, bf16[864,128]{1,0:T(8,128)(2,1)S(1)}, u32[]{:S(2)}, u32[]{:S(2)}) %collective-permute-start.21) | collective-permute-done | bytes 221216 | tf_op jit(solution)/shard_map/ppermute | solution.py:246
  142.8 1.8 collective-permute-start.22
  144.6 1.0 collective-permute-start.24
  145.6 0.1 broadcast.19.clone.1
  145.8 0.1 broadcast.19.clone
  146.0 8.0 %collective-permute-done.22 = bf16[1728,128]{1,0:T(8,128)(2,1)S(1)} collective-permute-done((bf16[1728,128]{1,0:T(8,128)(2,1)S(1)}, bf16[1728,128]{1,0:T(8,128)(2,1)S(1)}, u32[]{:S(2)}, u32[]{:S(2)}) %collective-permute-start.22) | collective-permute-done | bytes 442400 | tf_op jit(solution)/shard_map/ppermute | solution.py:246
  154.0 1.5 collective-permute-done.24
  155.6 1.3 pad_maximum_fusion.1
  156.9 15.5 %backward.3.refs_3_ = f32[1344,256]{1,0:T(8,128)} custom-call(f32[27,8,256]{2,1,0:T(8,128)} %get-tuple-element.11.refs_0_, bf16[768,256]{1,0:T(8,128)(2,1)} %get-tuple-element.12.refs_1_, bf16[27,256,256]{2,1,0:T(8,128)(2,1)} %refs_2_.5), custom_call_target="tpu_custom_call" | custom-call | tf_op jit(solution)/shard_map/backward/pallas_call | solution.py:188
  172.4 15.9 %backward.4.refs_3_ = f32[1344,256]{1,0:T(8,128)} custom-call(f32[27,8,256]{2,1,0:T(8,128)} %get-tuple-element.11.refs_0_, bf16[768,256]{1,0:T(8,128)(2,1)} %get-tuple-element.12.refs_1_, bf16[27,256,256]{2,1,0:T(8,128)(2,1)} %refs_2_.5, f32[1344,256]{1,0:T(8,128)} %backward.3.refs_3_), custom_call_target="tpu_custom_call" | custom-call | tf_op jit(solution)/shard_map/backward/pallas_call | solution.py:188
  188.4 16.0 %backward.5.grad_ref = f32[1344,256]{1,0:T(8,128)} custom-call(f32[27,8,256]{2,1,0:T(8,128)} %get-tuple-element.11.refs_0_, bf16[768,256]{1,0:T(8,128)(2,1)} %get-tuple-element.12.refs_1_, bf16[27,256,256]{2,1,0:T(8,128)(2,1)} %refs_2_.5, f32[1344,256]{1,0:T(8,128)} %backward.4.refs_3_), custom_call_target="tpu_custom_call" | custom-call | tf_op jit(solution)/shard_map/backward/pallas_call | solution.py:188
  204.3 1.4 convert.4
  205.7 0.7 fusion.15
  206.4 0.3 collective-permute-start.5
  206.7 5.0 %collective-permute-start.6 = (bf16[96,256]{1,0:T(8,128)(2,1)}, bf16[96,256]{1,0:T(8,128)(2,1)S(1)}, u32[]{:S(2)}, u32[]{:S(2)}) collective-permute-start(bf16[96,256]{1,0:T(8,128)(2,1)} %get-tuple-element.24), channel_id=1, source_target_pairs={{0,4},{4,8},{8,12},{1,5},{5,9},{9,13},{2,6},{6,10},{10,14},{3,7},{... | collective-permute-start | bytes 147464 | tf_op jit(solution)/shard_map/ppermute | solution.py:235
  211.7 1.3 collective-permute-start.7
  213.0 1.9 collective-permute-start.8
  214.9 1.3 collective-permute-start.9
  216.2 0.8 bitcast_dynamic-update-slice_fusion.8
  217.1 0.8 collective-permute-done.7
  217.9 1.2 collective-permute-done.9
  219.1 0.7 copy-done.1
  219.8 2.7 %finish.1 = bf16[768,256]{1,0:T(8,128)(2,1)} custom-call(s32[6,96]{1,0:T(8,128)} %bitcast.91, f32[1344,256]{1,0:T(8,128)} %backward.5.grad_ref, bf16[6,96,256]{2,1,0:T(8,128)(2,1)} %copy-done.1), custom_call_target="tpu_custom_call" | custom-call | tf_op jit(solution)/shard_map/finish/pallas_call | solution.py:212
  222.6 0.7 broadcast_select_fusion.1
  223.2 2.2 pad_maximum_fusion
  (49 shorter events, 1.2 us)
Async XLA Ops:
  5.1 22.0 %collective-permute-start = (bf16[96,256]{1,0:T(8,128)(2,1)S(1)}, bf16[96,256]{1,0:T(8,128)(2,1)S(1)}, u32[]{:S(2)}, u32[]{:S(2)}) collective-permute-start(bf16[96,256]{1,0:T(8,128)(2,1)S(1)} %get-tuple-element.35), channel_id=1, source_target_pairs={{0,16},{16,0},{1,17},{17,1},{2,18},{18,2},{3,19},{19,3},{4,20},{20... | collective-permute-start | bytes 147464 | tf_op jit(solution)/shard_map/ppermute | solution.py:230
  8.1 19.0 %collective-permute-start.1 = (bf16[96,256]{1,0:T(8,128)(2,1)S(1)}, bf16[96,256]{1,0:T(8,128)(2,1)S(1)}, u32[]{:S(2)}, u32[]{:S(2)}) collective-permute-start(bf16[96,256]{1,0:T(8,128)(2,1)S(1)} %get-tuple-element.34), channel_id=1, source_target_pairs={{0,4},{4,8},{8,12},{1,5},{5,9},{9,13},{2,6},{6,10},{10,14},{3,7},{... | collective-permute-start | bytes 147464 | tf_op jit(solution)/shard_map/ppermute | solution.py:235
  11.6 15.6 %collective-permute-start.2 = (bf16[96,256]{1,0:T(8,128)(2,1)S(1)}, bf16[96,256]{1,0:T(8,128)(2,1)S(1)}, u32[]{:S(2)}, u32[]{:S(2)}) collective-permute-start(bf16[96,256]{1,0:T(8,128)(2,1)S(1)} %get-tuple-element.33), channel_id=1, source_target_pairs={{4,0},{8,4},{12,8},{5,1},{9,5},{13,9},{6,2},{10,6},{14,10},{7,3},{... | collective-permute-start | bytes 147464 | tf_op jit(solution)/shard_map/ppermute | solution.py:236
  12.9 14.3 %collective-permute-start.3 = (bf16[96,256]{1,0:T(8,128)(2,1)S(1)}, bf16[96,256]{1,0:T(8,128)(2,1)S(1)}, u32[]{:S(2)}, u32[]{:S(2)}) collective-permute-start(bf16[96,256]{1,0:T(8,128)(2,1)S(1)} %get-tuple-element.32), channel_id=1, source_target_pairs={{0,1},{1,2},{2,3},{4,5},{5,6},{6,7},{8,9},{9,10},{10,11},{12,13},{... | collective-permute-start | bytes 147464 | tf_op jit(solution)/shard_map/ppermute | solution.py:235
  14.2 13.0 %collective-permute-start.4 = (bf16[96,256]{1,0:T(8,128)(2,1)S(1)}, bf16[96,256]{1,0:T(8,128)(2,1)S(1)}, u32[]{:S(2)}, u32[]{:S(2)}) collective-permute-start(bf16[96,256]{1,0:T(8,128)(2,1)S(1)} %get-tuple-element.31), channel_id=1, source_target_pairs={{1,0},{2,1},{3,2},{5,4},{6,5},{7,6},{9,8},{10,9},{11,10},{13,12},{... | collective-permute-start | bytes 147464 | tf_op jit(solution)/shard_map/ppermute | solution.py:236
  27.3 0.7 copy-start
  83.9 6.4 %collective-permute-start.10 = (bf16[6912,128]{1,0:T(8,128)(2,1)}, bf16[6912,128]{1,0:T(8,128)(2,1)S(1)}, u32[]{:S(2)}, u32[]{:S(2)}) collective-permute-start(bf16[6912,128]{1,0:T(8,128)(2,1)} %get-tuple-element.14), channel_id=1, source_target_pairs={{0,1},{1,0},{2,3},{3,2},{4,5},{5,4},{6,7},{7,6},{8,9},{9,8},{10,11... | collective-permute-start | bytes 5308424 | tf_op jit(solution)/shard_map/ppermute | solution.py:246
  92.4 12.5 %collective-permute-start.13 = (bf16[1728,128]{1,0:T(8,128)(2,1)S(1)}, bf16[1728,128]{1,0:T(8,128)(2,1)S(1)}, u32[]{:S(2)}, u32[]{:S(2)}) collective-permute-start(bf16[1728,128]{1,0:T(8,128)(2,1)S(1)} %constant_dynamic-slice_fusion.1), channel_id=1, source_target_pairs={{0,2},{1,3},{2,0},{3,1},{4,6},{5,7},{6,4},{7,5},{8,10},{9,11},{10,... | collective-permute-start | bytes 1327112 | tf_op jit(solution)/shard_map/ppermute | solution.py:246
  94.5 12.0 %collective-permute-start.11 = (bf16[1728,128]{1,0:T(8,128)(2,1)S(1)}, bf16[1728,128]{1,0:T(8,128)(2,1)S(1)}, u32[]{:S(2)}, u32[]{:S(2)}) collective-permute-start(bf16[1728,128]{1,0:T(8,128)(2,1)S(1)} %constant_dynamic-slice_fusion.3), channel_id=1, source_target_pairs={{0,16},{16,0},{1,17},{17,1},{2,18},{18,2},{3,19},{19,3},{4,20},{20... | collective-permute-start | bytes 1327112 | tf_op jit(solution)/shard_map/ppermute | solution.py:246
  105.1 7.0 %collective-permute-start.14 = (bf16[864,128]{1,0:T(8,128)(2,1)S(1)}, bf16[864,128]{1,0:T(8,128)(2,1)S(1)}, u32[]{:S(2)}, u32[]{:S(2)}) collective-permute-start(bf16[864,128]{1,0:T(8,128)(2,1)S(1)} %constant_dynamic-slice_fusion), channel_id=1, source_target_pairs={{0,16},{16,0},{1,17},{17,1},{2,18},{18,2},{3,19},{19,3},{4,20},{20... | collective-permute-start | bytes 663560 | tf_op jit(solution)/shard_map/ppermute | solution.py:246
  106.6 6.4 %collective-permute-start.12 = (bf16[864,128]{1,0:T(8,128)(2,1)S(1)}, bf16[864,128]{1,0:T(8,128)(2,1)S(1)}, u32[]{:S(2)}, u32[]{:S(2)}) collective-permute-start(bf16[864,128]{1,0:T(8,128)(2,1)S(1)} %constant_dynamic-slice_fusion.2), channel_id=1, source_target_pairs={{0,2},{1,3},{2,0},{3,1},{4,6},{5,7},{6,4},{7,5},{8,10},{9,11},{10,... | collective-permute-start | bytes 663560 | tf_op jit(solution)/shard_map/ppermute | solution.py:246
  113.1 8.6 %collective-permute-start.15 = (bf16[432,128]{1,0:T(8,128)(2,1)S(1)}, bf16[432,128]{1,0:T(8,128)(2,1)S(1)}, u32[]{:S(2)}, u32[]{:S(2)}) collective-permute-start(bf16[432,128]{1,0:T(8,128)(2,1)S(1)} %get-tuple-element.28), channel_id=1, source_target_pairs={{0,4},{4,8},{8,12},{12,0},{1,5},{5,9},{9,13},{13,1},{2,6},{6,10},{... | collective-permute-start | bytes 331784 | tf_op jit(solution)/shard_map/ppermute | solution.py:280
  115.8 8.9 %collective-permute-start.16 = (bf16[432,128]{1,0:T(8,128)(2,1)S(1)}, bf16[432,128]{1,0:T(8,128)(2,1)S(1)}, u32[]{:S(2)}, u32[]{:S(2)}) collective-permute-start(bf16[432,128]{1,0:T(8,128)(2,1)S(1)} %get-tuple-element.29), channel_id=1, source_target_pairs={{0,8},{4,12},{8,0},{12,4},{1,9},{5,13},{9,1},{13,5},{2,10},{6,14},... | collective-permute-start | bytes 331784 | tf_op jit(solution)/shard_map/ppermute | solution.py:280
  118.4 6.3 %collective-permute-start.17 = (bf16[432,128]{1,0:T(8,128)(2,1)S(1)}, bf16[432,128]{1,0:T(8,128)(2,1)S(1)}, u32[]{:S(2)}, u32[]{:S(2)}) collective-permute-start(bf16[432,128]{1,0:T(8,128)(2,1)S(1)} %get-tuple-element.30), channel_id=1, source_target_pairs={{0,12},{4,0},{8,4},{12,8},{1,13},{5,1},{9,5},{13,9},{2,14},{6,2},{... | collective-permute-start | bytes 331784 | tf_op jit(solution)/shard_map/ppermute | solution.py:280
  124.8 7.8 %collective-permute-start.18 = (bf16[432,128]{1,0:T(8,128)(2,1)S(1)}, bf16[432,128]{1,0:T(8,128)(2,1)S(1)}, u32[]{:S(2)}, u32[]{:S(2)}) collective-permute-start(bf16[432,128]{1,0:T(8,128)(2,1)S(1)} %get-tuple-element.16), channel_id=1, source_target_pairs={{0,4},{4,8},{8,12},{12,0},{1,5},{5,9},{9,13},{13,1},{2,6},{6,10},{... | collective-permute-start | bytes 331784 | tf_op jit(solution)/shard_map/ppermute | solution.py:280
  127.0 8.6 %collective-permute-start.19 = (bf16[432,128]{1,0:T(8,128)(2,1)S(1)}, bf16[432,128]{1,0:T(8,128)(2,1)S(1)}, u32[]{:S(2)}, u32[]{:S(2)}) collective-permute-start(bf16[432,128]{1,0:T(8,128)(2,1)S(1)} %get-tuple-element.16), channel_id=1, source_target_pairs={{0,8},{4,12},{8,0},{12,4},{1,9},{5,13},{9,1},{13,5},{2,10},{6,14},... | collective-permute-start | bytes 331784 | tf_op jit(solution)/shard_map/ppermute | solution.py:280
  128.7 6.9 %collective-permute-start.20 = (bf16[432,128]{1,0:T(8,128)(2,1)S(1)}, bf16[432,128]{1,0:T(8,128)(2,1)S(1)}, u32[]{:S(2)}, u32[]{:S(2)}) collective-permute-start(bf16[432,128]{1,0:T(8,128)(2,1)S(1)} %get-tuple-element.16), channel_id=1, source_target_pairs={{0,12},{4,0},{8,4},{12,8},{1,13},{5,1},{9,5},{13,9},{2,14},{6,2},{... | collective-permute-start | bytes 331784 | tf_op jit(solution)/shard_map/ppermute | solution.py:280
  135.7 7.1 %collective-permute-start.21 = (bf16[864,128]{1,0:T(8,128)(2,1)S(1)}, bf16[864,128]{1,0:T(8,128)(2,1)S(1)}, u32[]{:S(2)}, u32[]{:S(2)}) collective-permute-start(bf16[864,128]{1,0:T(8,128)(2,1)S(1)} %bitcast.84), channel_id=1, source_target_pairs={{0,2},{1,3},{2,0},{3,1},{4,6},{5,7},{6,4},{7,5},{8,10},{9,11},{10,... | collective-permute-start | bytes 663560 | tf_op jit(solution)/shard_map/ppermute | solution.py:246
  136.8 7.8 %collective-permute-start.23 = (bf16[864,128]{1,0:T(8,128)(2,1)S(1)}, bf16[864,128]{1,0:T(8,128)(2,1)S(1)}, u32[]{:S(2)}, u32[]{:S(2)}) collective-permute-start(bf16[864,128]{1,0:T(8,128)(2,1)S(1)} %bitcast.82), channel_id=1, source_target_pairs={{0,16},{16,0},{1,17},{17,1},{2,18},{18,2},{3,19},{19,3},{4,20},{20... | collective-permute-start | bytes 663560 | tf_op jit(solution)/shard_map/ppermute | solution.py:246
  142.8 11.2 %collective-permute-start.22 = (bf16[1728,128]{1,0:T(8,128)(2,1)S(1)}, bf16[1728,128]{1,0:T(8,128)(2,1)S(1)}, u32[]{:S(2)}, u32[]{:S(2)}) collective-permute-start(bf16[1728,128]{1,0:T(8,128)(2,1)S(1)} %constant_dynamic-update-slice_fusion.6), channel_id=1, source_target_pairs={{0,16},{16,0},{1,17},{17,1},{2,18},{18,2},{3,19},{19,3},{4,20},{20... | collective-permute-start | bytes 1327112 | tf_op jit(solution)/shard_map/ppermute | solution.py:246
  144.6 10.9 %collective-permute-start.24 = (bf16[1728,128]{1,0:T(8,128)(2,1)S(1)}, bf16[1728,128]{1,0:T(8,128)(2,1)S(1)}, u32[]{:S(2)}, u32[]{:S(2)}) collective-permute-start(bf16[1728,128]{1,0:T(8,128)(2,1)S(1)} %constant_dynamic-update-slice_fusion.2), channel_id=1, source_target_pairs={{0,2},{1,3},{2,0},{3,1},{4,6},{5,7},{6,4},{7,5},{8,10},{9,11},{10,... | collective-permute-start | bytes 1327112 | tf_op jit(solution)/shard_map/ppermute | solution.py:246
  156.9 65.6 %collective-permute-start.25 = (bf16[6912,128]{1,0:T(8,128)(2,1)}, bf16[6912,128]{1,0:T(8,128)(2,1)S(1)}, u32[]{:S(2)}, u32[]{:S(2)}) collective-permute-start(bf16[6912,128]{1,0:T(8,128)(2,1)} %pad_maximum_fusion.1), channel_id=1, source_target_pairs={{0,1},{1,0},{2,3},{3,2},{4,5},{5,4},{6,7},{7,6},{8,9},{9,8},{10,11... | collective-permute-start | bytes 5308424 | tf_op jit(solution)/shard_map/ppermute | solution.py:246
  206.4 8.5 %collective-permute-start.5 = (bf16[96,256]{1,0:T(8,128)(2,1)}, bf16[96,256]{1,0:T(8,128)(2,1)}, u32[]{:S(2)}, u32[]{:S(2)}) collective-permute-start(bf16[96,256]{1,0:T(8,128)(2,1)} %get-tuple-element.25), channel_id=1, source_target_pairs={{0,16},{16,0},{1,17},{17,1},{2,18},{18,2},{3,19},{19,3},{4,20},{20... | collective-permute-start | bytes 147464 | tf_op jit(solution)/shard_map/ppermute | solution.py:230
  206.7 10.3 %collective-permute-start.6 = (bf16[96,256]{1,0:T(8,128)(2,1)}, bf16[96,256]{1,0:T(8,128)(2,1)S(1)}, u32[]{:S(2)}, u32[]{:S(2)}) collective-permute-start(bf16[96,256]{1,0:T(8,128)(2,1)} %get-tuple-element.24), channel_id=1, source_target_pairs={{0,4},{4,8},{8,12},{1,5},{5,9},{9,13},{2,6},{6,10},{10,14},{3,7},{... | collective-permute-start | bytes 147464 | tf_op jit(solution)/shard_map/ppermute | solution.py:235
  211.7 6.2 %collective-permute-start.7 = (bf16[96,256]{1,0:T(8,128)(2,1)}, bf16[96,256]{1,0:T(8,128)(2,1)S(1)}, u32[]{:S(2)}, u32[]{:S(2)}) collective-permute-start(bf16[96,256]{1,0:T(8,128)(2,1)} %get-tuple-element.23), channel_id=1, source_target_pairs={{4,0},{8,4},{12,8},{5,1},{9,5},{13,9},{6,2},{10,6},{14,10},{7,3},{... | collective-permute-start | bytes 147464 | tf_op jit(solution)/shard_map/ppermute | solution.py:236
  213.0 4.9 %collective-permute-start.8 = (bf16[96,256]{1,0:T(8,128)(2,1)}, bf16[96,256]{1,0:T(8,128)(2,1)S(1)}, u32[]{:S(2)}, u32[]{:S(2)}) collective-permute-start(bf16[96,256]{1,0:T(8,128)(2,1)} %get-tuple-element.22), channel_id=1, source_target_pairs={{0,1},{1,2},{2,3},{4,5},{5,6},{6,7},{8,9},{9,10},{10,11},{12,13},{... | collective-permute-start | bytes 147464 | tf_op jit(solution)/shard_map/ppermute | solution.py:235
  214.9 4.2 %collective-permute-start.9 = (bf16[96,256]{1,0:T(8,128)(2,1)}, bf16[96,256]{1,0:T(8,128)(2,1)S(1)}, u32[]{:S(2)}, u32[]{:S(2)}) collective-permute-start(bf16[96,256]{1,0:T(8,128)(2,1)} %get-tuple-element.21), channel_id=1, source_target_pairs={{1,0},{2,1},{3,2},{5,4},{6,5},{7,6},{9,8},{10,9},{11,10},{13,12},{... | collective-permute-start | bytes 147464 | tf_op jit(solution)/shard_map/ppermute | solution.py:236
  219.1 0.7 copy-start.1

commit v2 on v1

v2 whole, which is shorter than its diff:
```python
import jax
import jax.numpy as jnp
from jax import lax
from jax.experimental import pallas as pl
from jax.experimental.pallas import tpu as pltpu
from jax.sharding import PartitionSpec as P

BF = jnp.bfloat16
F32 = jnp.float32
NT = (((1,), (1,)), ((), ()))
NN = (((1,), (0,)), ((), ()))
TN = (((0,), (0,)), ((), ()))
LIMIT = 24 << 20
AXES = ("gx", "gy", "gz")


def dot(a, b, dims=NN):
    return lax.dot_general(a, b, dims, preferred_element_type=F32)


def one_hot(mask):
    return jnp.where(mask, jnp.ones((), F32), jnp.zeros((), F32)).astype(BF)


def whole(shape):
    return pl.BlockSpec(shape, lambda k: (0,) * len(shape))


def send_kernel(rows_ref, own_ref, sent_ref):
    directions, face = rows_ref.shape
    own = own_ref.shape[0]
    places = lax.broadcasted_iota(jnp.int32, (own, face), 0)
    for d in range(directions):
        hot = one_hot(places == rows_ref[d : d + 1, :])
        sent_ref[d] = dot(hot, own_ref[...], TN).astype(BF)


def send(rows, own_features):
    directions, face = rows.shape
    return pl.pallas_call(
        send_kernel,
        out_shape=jax.ShapeDtypeStruct((directions, face, own_features.shape[1]), BF),
        compiler_params=pltpu.CompilerParams(vmem_limit_bytes=LIMIT),
        name="send",
    )(rows, own_features)


def invert_kernel(block, missing, in_ref, out_ref, live_ref, col_ref, row_ref):
    taps, own = in_ref.shape
    lows = lax.broadcasted_iota(jnp.int32, (block, own), 0)
    ranks = lax.broadcasted_iota(jnp.int32, (8, own), 0)
    for k in range(taps):
        target = out_ref[pl.ds(k, 1), :]
        source = jnp.where(live_ref[pl.ds(k, 1), :] > 0, in_ref[pl.ds(k, 1), :], missing)
        high = target // block
        hot = one_hot(lows == target - high * block)
        big = (source // 16) * 16
        spread = jnp.where(ranks == high, big, jnp.where(ranks - 4 == high, source - big, 0))
        spread = spread.astype(F32).astype(BF)
        col_ref[k] = dot(hot, spread, NT)
        row_ref[k] = dot(spread, hot, NT)


def invert(in_rows, out_rows, live, missing, block):
    taps, own = in_rows.shape
    return pl.pallas_call(
        lambda *refs: invert_kernel(block, missing, *refs),
        out_shape=(
            jax.ShapeDtypeStruct((taps, block, 8), F32),
            jax.ShapeDtypeStruct((taps, 8, block), F32),
        ),
        compiler_params=pltpu.CompilerParams(vmem_limit_bytes=LIMIT),
        name="invert",
    )(in_rows, out_rows, live)


def forward_kernel(
    block, parts, odd_ref, col_ref, own_ref, face_ref, w_hbm, up_ref,
    act_ref, gp_ref, keep_ref, give_ref, ext, got, turned_got, weights, turned, sem,
):
    taps = col_ref.shape[0]
    own, ch = own_ref.shape
    rows = ext.shape[0]
    half = ch // 2
    fetch = pltpu.make_async_copy(w_hbm, weights, sem)
    fetch.start()
    ext[pl.ds(0, own), :] = own_ref[...]
    ext[pl.ds(own, rows - own), :] = face_ref[...]
    lanes = lax.broadcasted_iota(jnp.int32, (block, rows), 1)

    def gather(k, carried):
        at = pl.multiple_of(k * ch, ch)
        for h in range(parts):
            place = (col_ref[k, :, h : h + 1] + col_ref[k, :, h + 4 : h + 5]).astype(jnp.int32)
            picked = dot(one_hot(lanes == place), ext[...]).astype(BF)
            got[pl.ds(h * block, block), pl.ds(at, ch)] = picked
            turned_got[pl.ds(at, ch), pl.ds(h * block, block)] = picked.T
        return carried

    lax.fori_loop(0, taps, gather, 0, unroll=9)
    fetch.wait()
    for h in range(parts):
        part = pl.ds(h * block, block)
        v = dot(got[part, :], weights[...])
        s = jax.nn.sigmoid(v)
        act_ref[part, :] = (v * s).astype(BF)
        g = up_ref[part, :].astype(F32) * (s * (1.0 + v * (1.0 - s)))
        gp_ref[part, :] = g.astype(BF)
        turned[part, :half] = jnp.where(odd_ref[0] > 0, g[:, half:], g[:, :half]).astype(BF)
        turned[part, half:] = jnp.where(odd_ref[0] > 0, g[:, :half], g[:, half:]).astype(BF)

    def one(t, carried):
        at = pl.multiple_of(t * ch, ch)
        r = dot(turned_got[pl.ds(at, ch), :], turned[...])
        keep_ref[pl.ds(at, ch), :] = r[:, :half]
        give_ref[pl.ds(at, ch), :] = r[:, half:].astype(BF)
        return carried

    lax.fori_loop(0, taps, one, 0, unroll=3)


def forward(odd, col, own_features, faces, weight, upstream):
    taps, block, _ = col.shape
    own, ch = own_features.shape
    rows = own + faces.shape[0]
    like = jax.ShapeDtypeStruct
    vmem = pl.BlockSpec(memory_space=pltpu.VMEM)
    return pl.pallas_call(
        lambda *refs: forward_kernel(block, own // block, *refs),
        in_specs=[
            pl.BlockSpec(memory_space=pltpu.SMEM),
            vmem,
            vmem,
            vmem,
            pl.BlockSpec(memory_space=pl.ANY),
            vmem,
        ],
        out_specs=[vmem, vmem, vmem, vmem],
        out_shape=[
            like((own, ch), BF),
            like((own, ch), BF),
            like((taps * ch, ch // 2), F32),
            like((taps * ch, ch // 2), BF),
        ],
        scratch_shapes=[
            pltpu.VMEM((rows, ch), BF),
            pltpu.VMEM((own, taps * ch), BF),
            pltpu.VMEM((taps * ch, own), BF),
            pltpu.VMEM((taps * ch, ch), BF),
            pltpu.VMEM((own, ch), BF),
            pltpu.SemaphoreType.DMA,
        ],
        compiler_params=pltpu.CompilerParams(vmem_limit_bytes=44 << 20),
        name="forward",
    )(odd, col, own_features, faces, weight.reshape(taps * ch, ch), upstream)


def backward_kernel(first, count, row_ref, gp_ref, w_hbm, *rest):
    before = rest[:-4]
    out_ref, got, weights, sems = rest[-4:]
    rows, ch = out_ref.shape
    block = row_ref.shape[2]
    parts = gp_ref.shape[0] // block
    step = 336
    fetches = [
        pltpu.make_async_copy(w_hbm.at[first + j], weights.at[:, pl.ds(j * ch, ch)], sems.at[j])
        for j in range(count)
    ]
    for fetch in fetches:
        fetch.start()

    def gather(j, carried):
        at = pl.multiple_of(j * ch, ch)
        for r in range(0, rows, step):
            lines = lax.broadcasted_iota(jnp.int32, (step, block), 0) + r
            hots = []
            for h in range(parts):
                k = first + j
                place = (row_ref[k, h : h + 1, :] + row_ref[k, h + 4 : h + 5, :]).astype(jnp.int32)
                hots.append(one_hot(lines == place))
            got[pl.ds(r, step), pl.ds(at, ch)] = dot(jnp.concatenate(hots, axis=1), gp_ref[...]).astype(BF)
        return carried

    lax.fori_loop(0, count, gather, 0, unroll=3)
    for fetch in fetches:
        fetch.wait()
    for r in range(0, rows, step):
        total = dot(got[pl.ds(r, step), :], weights[...], NT)
        if before:
            total = total + before[0][pl.ds(r, step), :]
        out_ref[pl.ds(r, step), :] = total


def backward(row, gp, weight, first, count, before, rows):
    own, ch = gp.shape
    vmem = pl.BlockSpec(memory_space=pltpu.VMEM)
    specs = [vmem, vmem, pl.BlockSpec(memory_space=pl.ANY)]
    args = [row, gp, weight]
    if before is not None:
        specs.append(vmem)
        args.append(before)
    return pl.pallas_call(
        lambda *refs: backward_kernel(first, count, *refs),
        in_specs=specs,
        out_specs=vmem,
        out_shape=jax.ShapeDtypeStruct((rows, ch), F32),
        scratch_shapes=[
            pltpu.VMEM((rows, count * ch), BF),
            pltpu.VMEM((ch, count * ch), BF),
            pltpu.SemaphoreType.DMA((count,)),
        ],
        compiler_params=pltpu.CompilerParams(vmem_limit_bytes=24 << 20),
        name="backward",
    )(*args)


def finish_kernel(rows_ref, grad_ref, back_ref, out_ref):
    directions, face = rows_ref.shape
    own = out_ref.shape[0]
    places = lax.broadcasted_iota(jnp.int32, (own, face), 0)
    total = grad_ref[...]
    for d in range(directions):
        hot = one_hot(places == rows_ref[d : d + 1, :])
        total = total + dot(hot, back_ref[d])
    out_ref[...] = total.astype(BF)


def finish(rows, grad_extended, returned, own):
    ch = grad_extended.shape[1]
    return pl.pallas_call(
        finish_kernel,
        grid=(1,),
        in_specs=[whole(rows.shape), whole((own, ch)), whole(returned.shape)],
        out_specs=whole((own, ch)),
        out_shape=jax.ShapeDtypeStruct((own, ch), BF),
        compiler_params=pltpu.CompilerParams(vmem_limit_bytes=LIMIT),
        name="finish",
    )(rows, grad_extended, returned)


def trade(faces):
    got = [None] * 6
    for i, axis in enumerate(AXES):
        lower, upper = 2 * i, 2 * i + 1
        n = lax.axis_size(axis)
        if n == 2:
            last = lax.axis_index(axis) == 1
            moved = lax.ppermute(jnp.where(last, faces[lower], faces[upper]), axis, [(0, 1), (1, 0)])
            blank = jnp.zeros_like(moved)
            got[lower] = jnp.where(last, moved, blank)
            got[upper] = jnp.where(last, blank, moved)
        else:
            got[lower] = lax.ppermute(faces[upper], axis, [(j, j + 1) for j in range(n - 1)])
            got[upper] = lax.ppermute(faces[lower], axis, [(j + 1, j) for j in range(n - 1)])
    return jnp.stack(got)


def swap(x, axis, bit):
    n = lax.axis_size(axis)
    return lax.ppermute(x, axis, [(j, j ^ (1 << bit)) for j in range(n)])


def side(axis, bit):
    return (lax.axis_index(axis) >> bit) & 1


def cut(pair, which, size):
    kept, came = (lax.dynamic_slice_in_dim(x, which * size, size, 0) for x in pair)
    return kept + came.astype(F32)


def join(mine, other, which):
    half = mine.shape[0]
    out = jnp.zeros((2 * half,) + mine.shape[1:], mine.dtype)
    out = lax.dynamic_update_slice_in_dim(out, mine, which * half, 0)
    return lax.dynamic_update_slice_in_dim(out, other, (1 - which) * half, 0)


def reduce_all(keep, give, scaling, beside):
    bits = lambda axis, low: [(axis, b) for b in range(low, lax.axis_size(axis).bit_length() - 1)]
    plane = [bits("gx", 0) + bits("gz", 1), bits("gz", 1) + bits("gx", 0)]
    turns = len(plane[0])
    came = swap(give, "gz", 0)
    rows, ch = keep.shape
    pairs = [(keep[: rows // 2], came[: rows // 2]), (keep[rows // 2 :], came[rows // 2 :])]
    for turn in range(turns):
        where = [(axis, bit, side(axis, bit)) for axis, bit in (plane[i][turn] for i in range(2))]
        size = pairs[0][0].shape[0] // 2
        out = [cut(pairs[i], 1 - where[i][2], size).astype(BF) for i in range(2)]
        came = [swap(out[i], *where[i][:2]) for i in range(2)]
        came = beside(out, came)
        pairs = [(cut(pairs[i], where[i][2], size), came[i]) for i in range(2)]
    n = lax.axis_size("gy")
    at = lax.axis_index("gy")
    size = pairs[0][0].shape[0] // n
    slot = lambda s: jnp.concatenate([cut(p, (at + s) % n, size) for p in pairs], axis=0)
    turn_by = lambda y, s: lax.ppermute(y, "gy", [(j, (j + s) % n) for j in range(n)])
    out = [slot(s).astype(BF) for s in range(1, n)]
    came = beside(out, [turn_by(y, s + 1) for s, y in enumerate(out)])
    total = slot(0)
    for y in came:
        total = total + y.astype(F32)
    mine = (total * scaling).astype(BF)
    came = beside([mine], [turn_by(mine, s) for s in range(1, n)])
    full = jnp.zeros((n, 2 * size, ch), BF)
    full = lax.dynamic_update_index_in_dim(full, mine, at, 0)
    for s, y in enumerate(came):
        full = lax.dynamic_update_index_in_dim(full, y, (at - s - 1) % n, 0)
    pieces = [full[:, :size].reshape(-1, ch), full[:, size:].reshape(-1, ch)]
    for turn in reversed(range(turns)):
        came = beside(pieces, [swap(pieces[i], *plane[i][turn]) for i in range(2)])
        pieces = [join(pieces[i], came[i], side(*plane[i][turn])) for i in range(2)]
    mine = jnp.concatenate(pieces, axis=0)
    other = swap(mine, "gz", 0)
    odd = side("gz", 0) == 1
    return jnp.concatenate([jnp.where(odd, other, mine), jnp.where(odd, mine, other)], axis=1)


def shards(features, weight, upstream, send_rows, in_rows, out_rows, tap_pair_exists):
    own_features = features[0, 0, 0]
    own, ch = own_features.shape
    sends = send_rows[0, 0, 0]
    taps = weight.shape[0]
    block = 256
    sent = send(sends, own_features)
    faces = trade([sent[d] for d in range(6)]).reshape(-1, ch)
    rows = own + faces.shape[0]
    col, row = invert(in_rows[0, 0, 0], out_rows[0, 0, 0], tap_pair_exists[0, 0, 0], 2000, block)
    odd = side("gz", 0).reshape(1)
    activated, gp, keep, give = forward(odd, col, own_features, faces, weight, upstream[0, 0, 0])
    devices = lax.axis_size("gx") * lax.axis_size("gy") * lax.axis_size("gz")
    steps = [(0, 9), (9, 6), (15, 6), (21, taps - 21)]
    state = {"turn": 0, "grad": None, "returned": None}

    def beside(out, came):
        turn = state["turn"]
        state["turn"] = turn + 1
        if turn < len(steps):
            held = lax.optimization_barrier((gp, *out))
            grad = backward(row, held[0], weight, *steps[turn], state["grad"], rows)
            held = lax.optimization_barrier((grad, *came))
            state["grad"] = held[0]
            return list(held[1:])
        if turn == len(steps):
            back = state["grad"][own:].astype(BF).reshape(6, -1, ch)
            held = lax.optimization_barrier((back, *out))
            state["returned"] = trade([held[0][d] for d in range(6)])
            held = lax.optimization_barrier((state["returned"], *came))
            state["returned"] = held[0]
            return list(held[1:])
        return came

    grad_weight = reduce_all(keep, give, float(devices * own) ** -0.5, beside).reshape(weight.shape)
    grad_features = finish(sends, state["grad"], state["returned"], own)
    return activated[None, None, None], grad_features[None, None, None], grad_weight


def solution(mesh):
    part = P("gx", "gy", "gz", None, None)
    return jax.shard_map(
        shards,
        mesh=mesh,
        in_specs=(part, P(), part, part, part, part, part),
        out_specs=(part, part, P()),
        check_vma=False,
    )
```

time: 229 us -> 172 us (0.75)
  Pallas kernels: 117 us -> 57.6 us
  waiting for transfers between devices: 46.3 us -> 20.2 us
  local copies, waits for them, and re-layouts: 6.99 us -> 30 us
  other arithmetic: 10.5 us -> 19.1 us
    pallas_call x4 -> x5, Pallas kernels: 103 us -> 49.9 us  [the longest x1 27.6 us: forward(): pl.pallas_call(lambda *refs: forward_kernel(block, own // block, *refs),...]
    ppermute x10, waiting for transfers between devices: 33.3 us -> 16.3 us  [swap(): return lax.ppermute(x, axis, [(j, j ^ 1 << bit) for j in range(n)])]
    unnamed x13 -> x65, local copies, waits for them, and re-layouts: 5.87 us -> 20.7 us
    ppermute x6, waiting for transfers between devices: 11 us -> 0.02 us  [reduce_all(): lax.ppermute(y, 'gy', [(j, (j + s) % n) for j in range(n)])]
    add x0 -> x4, other arithmetic: none -> 6.44 us  [cut(): return kept + came.astype(F32)]
    dynamic_update_slice x3, local copies, waits for them, and re-layouts: 0.05 us -> 4.78 us  [reduce_all(): full = lax.dynamic_update_index_in_dim(full, y, (at - s - 1) % n, 0)]
    ppermute x4, starting transfers between devices: 11.6 us -> 8.52 us  [trade(): lax.ppermute(faces[upper], axis, [(j, j + 1) for j in range(n - 1)])]
    pallas_call x1, Pallas kernels: 8.48 us -> 5.62 us  [invert(): pl.pallas_call(lambda *refs: invert_kernel(block, missing, *refs), out_sh...]
  transfers between devices with their start and end apart: 26 -> 26, of which waited for: 14 -> 8; matrix products, arithmetic and copies ran while one was open for 3% -> 4% of each run, Pallas kernels for 26% -> 17%
where the time goes in v2:
time: 172 us; the launch traced here: 171 us
  Pallas kernels  57.6 us (33%)
  starting transfers between devices  42.6 us (25%)
  local copies, waits for them, and re-layouts  30 us (17%)
  waiting for transfers between devices  20.2 us (12%)
  other arithmetic  19.1 us (11%)
    pallas_call x1, Pallas kernels, forward(): pl.pallas_call(lambda *refs: forward_kernel(block, own // block, *refs),...  27.6 us
    pallas_call x4, Pallas kernels, backward(): pl.pallas_call(lambda *refs: backward_kernel(first, count, *refs), in_spe...  22.3 us
    unnamed x65, local copies, waits for them, and re-layouts  20.7 us
    ppermute x10, waiting for transfers between devices, swap(): return lax.ppermute(x, axis, [(j, j ^ 1 << bit) for j in range(n)])  16.3 us
    ppermute x10, starting transfers between devices, swap(): return lax.ppermute(x, axis, [(j, j ^ 1 << bit) for j in range(n)])  13.5 us
    ppermute x6, starting transfers between devices, reduce_all(): lax.ppermute(y, 'gy', [(j, (j + s) % n) for j in range(n)])  10.5 us
    ppermute x4, starting transfers between devices, trade(): lax.ppermute(faces[upper], axis, [(j, j + 1) for j in range(n - 1)])  8.52 us
    add x4, other arithmetic, cut(): return kept + came.astype(F32)  6.44 us
  transfers between devices with their start and end apart: 26, of which 8 were waited for; matrix products, arithmetic and copies ran while one was open for 4% of the time, Pallas kernels for 17%

profile of v2, /device:TPU:0, one launch (start us, length us, event | category | flops | bytes accessed | tf_op | source)
XLA Modules:
  0.0 170.6 jit_solution(1039180018089491682)
XLA Ops:
  1.3 1.0 copy-done.19
  2.9 3.0 %collective-permute-start = (bf16[96,256]{1,0:T(8,128)(2,1)S(1)}, bf16[96,256]{1,0:T(8,128)(2,1)S(1)}, u32[]{:S(2)}, u32[]{:S(2)}) collective-permute-start(bf16[96,256]{1,0:T(8,128)(2,1)S(1)} %get-tuple-element.94), channel_id=1, source_target_pairs={{0,16},{16,0},{1,17},{17,1},{2,18},{18,2},{3,19},{19,3},{4,20},{20... | collective-permute-start | bytes 147464 | tf_op jit(solution)/shard_map/ppermute | solution.py:248
  5.9 3.5 %collective-permute-start.1 = (bf16[96,256]{1,0:T(8,128)(2,1)S(1)}, bf16[96,256]{1,0:T(8,128)(2,1)S(1)}, u32[]{:S(2)}, u32[]{:S(2)}) collective-permute-start(bf16[96,256]{1,0:T(8,128)(2,1)S(1)} %get-tuple-element.93), channel_id=1, source_target_pairs={{0,4},{4,8},{8,12},{1,5},{5,9},{9,13},{2,6},{6,10},{10,14},{3,7},{... | collective-permute-start | bytes 147464 | tf_op jit(solution)/shard_map/ppermute | solution.py:253
  9.4 1.3 collective-permute-start.2
  10.7 1.3 collective-permute-start.3
  12.0 1.3 collective-permute-start.4
  13.3 0.9 copy_bitcast_fusion
  15.2 5.6 %invert.1 = (f32[27,256,8]{2,1,0:T(8,128)S(1)}, f32[27,8,256]{2,1,0:T(8,128)S(1)}) custom-call(s32[27,768]{1,0:T(8,128)S(1)} %bitcast.78, s32[27,768]{1,0:T(8,128)S(1)} %get-tuple-element.96.refs_1_, s32[27,768]{1,0:T(8,128)S(1)} %get-tuple-element.95.refs_2_), custom_call_target="tpu_custom_call" | custom-call | tf_op jit(solution)/shard_map/invert/pallas_call | solution.py:66
  21.5 1.0 copy-done.20
  22.5 1.0 copy-done.21
  23.5 27.6 %forward.1 = (bf16[768,256]{1,0:T(8,128)(2,1)}, bf16[768,256]{1,0:T(8,128)(2,1)S(1)}, f32[6912,128]{1,0:T(8,128)S(1)}, bf16[6912,128]{1,0:T(8,128)(2,1)}) custom-call(s32[1]{0:T(128)} %bitcast.refs_0_, f32[27,256,8]{2,1,0:T(8,128)S(1)} %get-tuple-element.31.refs_1_, bf16[768,256]{1,0:T(8,128)(2,1)S(1)} %bitcast.75, bf16[576,256]{1,0:T(8,128)(2,1)S(1)} %bitcast.76, ...), custom_call_target="tpu_custom_call" | custom-call | tf_op jit(solution)/shard_map/forward/pallas_call | solution.py:128
  51.8 2.9 %collective-permute-start.5 = (bf16[6912,128]{1,0:T(8,128)(2,1)}, bf16[6912,128]{1,0:T(8,128)(2,1)}, u32[]{:S(2)}, u32[]{:S(2)}) collective-permute-start(bf16[6912,128]{1,0:T(8,128)(2,1)} %get-tuple-element.36), channel_id=1, source_target_pairs={{0,1},{1,0},{2,3},{3,2},{4,5},{5,4},{6,7},{7,6},{8,9},{9,8},{10,11... | collective-permute-start | bytes 5308424 | tf_op jit(solution)/shard_map/ppermute | solution.py:260
  54.9 3.4 %collective-permute-done.5 = bf16[6912,128]{1,0:T(8,128)(2,1)} collective-permute-done((bf16[6912,128]{1,0:T(8,128)(2,1)}, bf16[6912,128]{1,0:T(8,128)(2,1)}, u32[]{:S(2)}, u32[]{:S(2)}) %collective-permute-start.5) | collective-permute-done | bytes 1769504 | tf_op jit(solution)/shard_map/ppermute | solution.py:260
  58.3 1.5 fusion.7
  59.9 1.2 convert_add_fusion.1
  61.7 1.3 add_convert_fusion
  63.0 2.0 %collective-permute-start.7 = (bf16[1728,128]{1,0:T(8,128)(2,1)}, bf16[1728,128]{1,0:T(8,128)(2,1)}, u32[]{:S(2)}, u32[]{:S(2)}) collective-permute-start(bf16[1728,128]{1,0:T(8,128)(2,1)} %get-tuple-element.67), channel_id=1, source_target_pairs={{0,2},{1,3},{2,0},{3,1},{4,6},{5,7},{6,4},{7,5},{8,10},{9,11},{10,... | collective-permute-start | bytes 1327112 | tf_op jit(solution)/shard_map/ppermute | solution.py:260
  65.0 1.0 copy-done.4
  66.0 0.9 copy-done.15
  66.9 7.5 %backward.4.refs_3_ = f32[1344,256]{1,0:T(8,128)S(1)} custom-call(f32[27,8,256]{2,1,0:T(8,128)S(1)} %copy-done.15, bf16[768,256]{1,0:T(8,128)(2,1)S(1)} %copy-done.4, bf16[27,256,256]{2,1,0:T(8,128)(2,1)S(1)} %copy-done), custom_call_target="tpu_custom_call" | custom-call | tf_op jit(solution)/shard_map/backward/pallas_call | solution.py:202
  74.5 1.0 collective-permute-done.7
  75.5 2.0 %convert_add_fusion.3 = (f32[864,128]{1,0:T(8,128)}, bf16[864,128]{1,0:T(8,128)(2,1)}) fusion(f32[1728,128]{1,0:T(8,128)S(1)} %copy-done.22, s32[]{:T(128)S(6)} %select_n.171, bf16[1728,128]{1,0:T(8,128)(2,1)} %collective-permute-done.6, s32[]{:T(128)S(6)} %select_n.176), kind=kLoop, calls=%fused_computation.12 | loop fusion | flops 552960 | bytes 1990664 | tf_op jit(solution)/shard_map/add | solution.py:269
  77.5 1.7 %collective-permute-start.8 = (bf16[864,128]{1,0:T(8,128)(2,1)}, bf16[864,128]{1,0:T(8,128)(2,1)}, u32[]{:S(2)}, u32[]{:S(2)}) collective-permute-start(bf16[864,128]{1,0:T(8,128)(2,1)} %get-tuple-element.72), channel_id=1, source_target_pairs={{0,2},{1,3},{2,0},{3,1},{4,6},{5,7},{6,4},{7,5},{8,10},{9,11},{10,... | collective-permute-start | bytes 663560 | tf_op jit(solution)/shard_map/ppermute | solution.py:260
  79.2 2.0 %add_convert_fusion.2 = (bf16[864,128]{1,0:T(8,128)(2,1)}, f32[864,128]{1,0:T(8,128)}) fusion(f32[1728,128]{1,0:T(8,128)S(1)} %copy-done.23, s32[]{:T(128)S(6)} %select_n.178, bf16[1728,128]{1,0:T(8,128)(2,1)} %collective-permute-done.7, s32[]{:T(128)S(6)} %select_n.179), kind=kLoop, calls=%fused_computation.10 | loop fusion | flops 552960 | bytes 1990664 | tf_op jit(solution)/shard_map/convert_element_type | solution.py:289
  81.2 1.5 collective-permute-start.9
  82.6 1.0 copy-done.5
  83.6 1.3 copy-done.9
  85.0 0.9 copy-done.16
  85.9 4.9 %backward.5.refs_3_ = f32[1344,256]{1,0:T(8,128)S(1)} custom-call(f32[27,8,256]{2,1,0:T(8,128)S(1)} %copy-done.16, bf16[768,256]{1,0:T(8,128)(2,1)S(1)} %copy-done.5, bf16[27,256,256]{2,1,0:T(8,128)(2,1)S(1)} %copy-done, f32[1344,256]{1,0:T(8,128)S(1)} %copy-done.9), custom_call_target="tpu_custom_call" | custom-call | tf_op jit(solution)/shard_map/backward/pallas_call | solution.py:202
  90.9 1.1 copy-done.12
  92.0 1.6 convert_add_fusion.5
  93.6 1.6 convert_add_fusion.4
  95.8 4.7 %collective-permute-start.12 = (bf16[432,128]{1,0:T(8,128)(2,1)}, bf16[432,128]{1,0:T(8,128)(2,1)}, u32[]{:S(2)}, u32[]{:S(2)}) collective-permute-start(bf16[432,128]{1,0:T(8,128)(2,1)} %pad_maximum_fusion.4), channel_id=1, source_target_pairs={{0,12},{4,0},{8,4},{12,8},{1,13},{5,1},{9,5},{13,9},{2,14},{6,2},{... | collective-permute-start | bytes 331784 | tf_op jit(solution)/shard_map/ppermute | solution.py:297
  101.8 1.0 collective-permute-start.10
  102.8 1.0 copy-done.6
  103.8 1.3 copy-done.13
  106.1 4.9 %backward.6.refs_3_ = f32[1344,256]{1,0:T(8,128)S(1)} custom-call(f32[27,8,256]{2,1,0:T(8,128)S(1)} %copy-done.17, bf16[768,256]{1,0:T(8,128)(2,1)S(1)} %copy-done.6, bf16[27,256,256]{2,1,0:T(8,128)(2,1)S(1)} %copy-done, f32[1344,256]{1,0:T(8,128)S(1)} %copy-done.13), custom_call_target="tpu_custom_call" | custom-call | tf_op jit(solution)/shard_map/backward/pallas_call | solution.py:202
  111.0 1.1 copy-done.10
  113.0 1.7 %bitcast_dynamic-update-slice_fusion.3 = (bf16[4,432,128]{2,1,0:T(8,128)(2,1)}, bf16[432,128]{1,0:T(8,128)(2,1)}) fusion(bf16[4,432,128]{2,1,0:T(8,128)(2,1)} %broadcast_in_dim.23, s32[]{:T(128)S(6)} %select_n.186, bf16[432,128]{1,0:T(8,128)(2,1)} %collective-permute-done.12, bf16[432,128]{1,0:T(8,128)(2,1)} %collective-permute-done.11, ...), kind=kLoop, calls=%fused_computation.24 | loop fusion | flops 497664 | bytes 774148 | tf_op jit(solution)/shard_map/jit(dynamic_update_index_in_dim)/dynamic_update_slice | solution.py:306
  114.7 2.5 %collective-permute-start.13 = (bf16[432,128]{1,0:T(8,128)(2,1)}, bf16[432,128]{1,0:T(8,128)(2,1)}, u32[]{:S(2)}, u32[]{:S(2)}) collective-permute-start(bf16[432,128]{1,0:T(8,128)(2,1)} %get-tuple-element.60), channel_id=1, source_target_pairs={{0,4},{4,8},{8,12},{12,0},{1,5},{5,9},{9,13},{13,1},{2,6},{6,10},{... | collective-permute-start | bytes 331784 | tf_op jit(solution)/shard_map/ppermute | solution.py:297
  117.2 0.9 collective-permute-start.14
  118.1 1.5 collective-permute-start.15
  119.6 1.0 copy-done.7
  120.6 1.3 copy-done.11
  122.9 4.9 %backward.7.grad_ref = f32[1344,256]{1,0:T(8,128)S(1)} custom-call(f32[27,8,256]{2,1,0:T(8,128)S(1)} %copy-done.18, bf16[768,256]{1,0:T(8,128)(2,1)S(1)} %copy-done.7, bf16[27,256,256]{2,1,0:T(8,128)(2,1)S(1)} %copy-done, f32[1344,256]{1,0:T(8,128)S(1)} %copy-done.11), custom_call_target="tpu_custom_call" | custom-call | tf_op jit(solution)/shard_map/backward/pallas_call | solution.py:202
  127.8 1.7 bitcast_dynamic-update-slice_fusion.2
  129.5 1.5 bitcast_dynamic-update-slice_fusion.1
  131.1 1.5 bitcast_dynamic-update-slice_fusion
  132.6 1.1 fusion.8
  134.6 1.6 collective-permute-start.16
  136.2 2.5 %collective-permute-start.17 = (bf16[96,256]{1,0:T(8,128)(2,1)S(1)}, bf16[96,256]{1,0:T(8,128)(2,1)S(1)}, u32[]{:S(2)}, u32[]{:S(2)}) collective-permute-start(bf16[96,256]{1,0:T(8,128)(2,1)S(1)} %get-tuple-element.88), channel_id=1, source_target_pairs={{0,4},{4,8},{8,12},{1,5},{5,9},{9,13},{2,6},{6,10},{10,14},{3,7},{... | collective-permute-start | bytes 147464 | tf_op jit(solution)/shard_map/ppermute | solution.py:253
  138.7 1.3 collective-permute-start.18
  140.5 1.3 collective-permute-start.19
  141.9 1.6 collective-permute-start.20
  143.4 1.2 collective-permute-done.18
  144.7 2.3 %collective-permute-done.20 = bf16[96,256]{1,0:T(8,128)(2,1)S(1)} collective-permute-done((bf16[96,256]{1,0:T(8,128)(2,1)S(1)}, bf16[96,256]{1,0:T(8,128)(2,1)S(1)}, u32[]{:S(2)}, u32[]{:S(2)}) %collective-permute-start.20) | collective-permute-done | bytes 49184 | tf_op jit(solution)/shard_map/ppermute | solution.py:254
  147.7 2.7 %collective-permute-start.24 = (bf16[1728,128]{1,0:T(8,128)(2,1)S(1)}, bf16[1728,128]{1,0:T(8,128)(2,1)S(1)}, u32[]{:S(2)}, u32[]{:S(2)}) collective-permute-start(bf16[1728,128]{1,0:T(8,128)(2,1)S(1)} %constant_dynamic-update-slice_fusion.6), channel_id=1, source_target_pairs={{0,2},{1,3},{2,0},{3,1},{4,6},{5,7},{6,4},{7,5},{8,10},{9,11},{10,... | collective-permute-start | bytes 1327112 | tf_op jit(solution)/shard_map/ppermute | solution.py:260
  150.8 7.5 %collective-permute-done.23 = bf16[1728,128]{1,0:T(8,128)(2,1)S(1)} collective-permute-done((bf16[1728,128]{1,0:T(8,128)(2,1)S(1)}, bf16[1728,128]{1,0:T(8,128)(2,1)S(1)}, u32[]{:S(2)}, u32[]{:S(2)}) %collective-permute-start.23) | collective-permute-done | bytes 442400 | tf_op jit(solution)/shard_map/ppermute | solution.py:260
  158.3 2.2 %collective-permute-done.24 = bf16[1728,128]{1,0:T(8,128)(2,1)S(1)} collective-permute-done((bf16[1728,128]{1,0:T(8,128)(2,1)S(1)}, bf16[1728,128]{1,0:T(8,128)(2,1)S(1)}, u32[]{:S(2)}, u32[]{:S(2)}) %collective-permute-start.24) | collective-permute-done | bytes 442400 | tf_op jit(solution)/shard_map/ppermute | solution.py:260
  160.6 1.3 pad_maximum_fusion.1
  162.6 1.5 finish.1
  164.1 2.2 %collective-permute-done.25 = bf16[6912,128]{1,0:T(8,128)(2,1)} collective-permute-done((bf16[6912,128]{1,0:T(8,128)(2,1)}, bf16[6912,128]{1,0:T(8,128)(2,1)}, u32[]{:S(2)}, u32[]{:S(2)}) %collective-permute-start.25) | collective-permute-done | bytes 1769504 | tf_op jit(solution)/shard_map/ppermute | solution.py:260
  166.3 2.2 %broadcast_select_fusion.1 = (bf16[6912,128]{1,0:T(8,128)(2,1)S(1)}, bf16[6912,128]{1,0:T(8,128)(2,1)S(1)}) fusion(bf16[6912,128]{1,0:T(8,128)(2,1)} %collective-permute-done.25, pred[]{:T(512)S(6)} %eq.20, bf16[3456,128]{1,0:T(8,128)(2,1)S(1)} %constant_dynamic-update-slice_fusion.2, bf16[3456,128]{1,0:T(8,128)(2,1)S(1)} %constant_dynamic-update-slice_fusion), kind=kLoop, calls=%fused_computation.3 | loop fusion | flops 5308416 | bytes 7077889 | tf_op jit(solution)/shard_map/jit(_where)/select_n | solution.py:316
  168.5 2.2 %pad_maximum_fusion = bf16[6912,256]{1,0:T(8,128)(2,1)} fusion(bf16[6912,128]{1,0:T(8,128)(2,1)S(1)} %get-tuple-element.62, bf16[6912,128]{1,0:T(8,128)(2,1)S(1)} %get-tuple-element.61), kind=kLoop, calls=%fused_computation | loop fusion | flops 7077888 | bytes 7077888 | tf_op jit(solution)/shard_map/concatenate | solution.py:316
  (102 shorter events, 12.4 us)
Async XLA Ops:
  1.3 1.0 copy-start.19
  2.9 17.9 %collective-permute-start = (bf16[96,256]{1,0:T(8,128)(2,1)S(1)}, bf16[96,256]{1,0:T(8,128)(2,1)S(1)}, u32[]{:S(2)}, u32[]{:S(2)}) collective-permute-start(bf16[96,256]{1,0:T(8,128)(2,1)S(1)} %get-tuple-element.94), channel_id=1, source_target_pairs={{0,16},{16,0},{1,17},{17,1},{2,18},{18,2},{3,19},{19,3},{4,20},{20... | collective-permute-start | bytes 147464 | tf_op jit(solution)/shard_map/ppermute | solution.py:248
  5.9 14.9 %collective-permute-start.1 = (bf16[96,256]{1,0:T(8,128)(2,1)S(1)}, bf16[96,256]{1,0:T(8,128)(2,1)S(1)}, u32[]{:S(2)}, u32[]{:S(2)}) collective-permute-start(bf16[96,256]{1,0:T(8,128)(2,1)S(1)} %get-tuple-element.93), channel_id=1, source_target_pairs={{0,4},{4,8},{8,12},{1,5},{5,9},{9,13},{2,6},{6,10},{10,14},{3,7},{... | collective-permute-start | bytes 147464 | tf_op jit(solution)/shard_map/ppermute | solution.py:253
  9.4 11.5 %collective-permute-start.2 = (bf16[96,256]{1,0:T(8,128)(2,1)S(1)}, bf16[96,256]{1,0:T(8,128)(2,1)S(1)}, u32[]{:S(2)}, u32[]{:S(2)}) collective-permute-start(bf16[96,256]{1,0:T(8,128)(2,1)S(1)} %get-tuple-element.92), channel_id=1, source_target_pairs={{4,0},{8,4},{12,8},{5,1},{9,5},{13,9},{6,2},{10,6},{14,10},{7,3},{... | collective-permute-start | bytes 147464 | tf_op jit(solution)/shard_map/ppermute | solution.py:254
  10.7 10.2 %collective-permute-start.3 = (bf16[96,256]{1,0:T(8,128)(2,1)S(1)}, bf16[96,256]{1,0:T(8,128)(2,1)S(1)}, u32[]{:S(2)}, u32[]{:S(2)}) collective-permute-start(bf16[96,256]{1,0:T(8,128)(2,1)S(1)} %get-tuple-element.91), channel_id=1, source_target_pairs={{0,1},{1,2},{2,3},{4,5},{5,6},{6,7},{8,9},{9,10},{10,11},{12,13},{... | collective-permute-start | bytes 147464 | tf_op jit(solution)/shard_map/ppermute | solution.py:253
  12.0 8.9 %collective-permute-start.4 = (bf16[96,256]{1,0:T(8,128)(2,1)S(1)}, bf16[96,256]{1,0:T(8,128)(2,1)S(1)}, u32[]{:S(2)}, u32[]{:S(2)}) collective-permute-start(bf16[96,256]{1,0:T(8,128)(2,1)S(1)} %get-tuple-element.90), channel_id=1, source_target_pairs={{1,0},{2,1},{3,2},{5,4},{6,5},{7,6},{9,8},{10,9},{11,10},{13,12},{... | collective-permute-start | bytes 147464 | tf_op jit(solution)/shard_map/ppermute | solution.py:254
  20.8 0.7 copy-start.14
  21.5 1.0 copy-start.20
  22.5 1.0 copy-start.21
  51.0 0.7 copy-start.3
  51.8 6.5 %collective-permute-start.5 = (bf16[6912,128]{1,0:T(8,128)(2,1)}, bf16[6912,128]{1,0:T(8,128)(2,1)}, u32[]{:S(2)}, u32[]{:S(2)}) collective-permute-start(bf16[6912,128]{1,0:T(8,128)(2,1)} %get-tuple-element.36), channel_id=1, source_target_pairs={{0,1},{1,0},{2,3},{3,2},{4,5},{5,4},{6,7},{7,6},{8,9},{9,8},{10,11... | collective-permute-start | bytes 5308424 | tf_op jit(solution)/shard_map/ppermute | solution.py:260
  61.1 13.3 %collective-permute-start.6 = (bf16[1728,128]{1,0:T(8,128)(2,1)}, bf16[1728,128]{1,0:T(8,128)(2,1)}, u32[]{:S(2)}, u32[]{:S(2)}) collective-permute-start(bf16[1728,128]{1,0:T(8,128)(2,1)} %get-tuple-element.66), channel_id=1, source_target_pairs={{0,16},{16,0},{1,17},{17,1},{2,18},{18,2},{3,19},{19,3},{4,20},{20... | collective-permute-start | bytes 1327112 | tf_op jit(solution)/shard_map/ppermute | solution.py:260
  61.7 3.3 %copy-start = (bf16[27,256,256]{2,1,0:T(8,128)(2,1)S(1)}, bf16[27,256,256]{2,1,0:T(8,128)(2,1)}, u32[]{:S(2)}) copy-start(bf16[27,256,256]{2,1,0:T(8,128)(2,1)} %refs_2_.7) | copy-start | bytes 10616836
  63.0 12.5 %collective-permute-start.7 = (bf16[1728,128]{1,0:T(8,128)(2,1)}, bf16[1728,128]{1,0:T(8,128)(2,1)}, u32[]{:S(2)}, u32[]{:S(2)}) collective-permute-start(bf16[1728,128]{1,0:T(8,128)(2,1)} %get-tuple-element.67), channel_id=1, source_target_pairs={{0,2},{1,3},{2,0},{3,1},{4,6},{5,7},{6,4},{7,5},{8,10},{9,11},{10,... | collective-permute-start | bytes 1327112 | tf_op jit(solution)/shard_map/ppermute | solution.py:260
  65.0 1.0 copy-start.4
  66.0 0.9 copy-start.15
  66.9 8.6 %copy-start.22 = (f32[1728,128]{1,0:T(8,128)S(1)}, f32[1728,128]{1,0:T(8,128)}, u32[]{:S(2)}) copy-start(f32[1728,128]{1,0:T(8,128)} %get-tuple-element.65) | copy-start | bytes 2654212
  74.4 6.7 %copy-start.8 = (f32[1344,256]{1,0:T(8,128)}, f32[1344,256]{1,0:T(8,128)S(1)}, u32[]{:S(2)}) copy-start(f32[1344,256]{1,0:T(8,128)S(1)} %backward.4.refs_3_) | copy-start | bytes 4128772
  74.4 4.8 %copy-start.23 = (f32[1728,128]{1,0:T(8,128)S(1)}, f32[1728,128]{1,0:T(8,128)}, u32[]{:S(2)}) copy-start(f32[1728,128]{1,0:T(8,128)} %get-tuple-element.68) | copy-start | bytes 2654212
  77.5 14.5 %collective-permute-start.8 = (bf16[864,128]{1,0:T(8,128)(2,1)}, bf16[864,128]{1,0:T(8,128)(2,1)}, u32[]{:S(2)}, u32[]{:S(2)}) collective-permute-start(bf16[864,128]{1,0:T(8,128)(2,1)} %get-tuple-element.72), channel_id=1, source_target_pairs={{0,2},{1,3},{2,0},{3,1},{4,6},{5,7},{6,4},{7,5},{8,10},{9,11},{10,... | collective-permute-start | bytes 663560 | tf_op jit(solution)/shard_map/ppermute | solution.py:260
  81.2 10.8 %collective-permute-start.9 = (bf16[864,128]{1,0:T(8,128)(2,1)}, bf16[864,128]{1,0:T(8,128)(2,1)}, u32[]{:S(2)}, u32[]{:S(2)}) collective-permute-start(bf16[864,128]{1,0:T(8,128)(2,1)} %get-tuple-element.73), channel_id=1, source_target_pairs={{0,16},{16,0},{1,17},{17,1},{2,18},{18,2},{3,19},{19,3},{4,20},{20... | collective-permute-start | bytes 663560 | tf_op jit(solution)/shard_map/ppermute | solution.py:260
  82.6 1.0 copy-start.5
  83.6 1.3 copy-start.9
  85.0 0.9 copy-start.16
  85.9 6.0 %copy-start.24 = (f32[864,128]{1,0:T(8,128)S(1)}, f32[864,128]{1,0:T(8,128)}, u32[]{:S(2)}) copy-start(f32[864,128]{1,0:T(8,128)} %get-tuple-element.71) | copy-start | bytes 1327108
  85.9 7.7 %copy-start.25 = (f32[864,128]{1,0:T(8,128)S(1)}, f32[864,128]{1,0:T(8,128)}, u32[]{:S(2)}) copy-start(f32[864,128]{1,0:T(8,128)} %get-tuple-element.74) | copy-start | bytes 1327108
  90.9 1.1 copy-start.12
  95.8 16.3 %collective-permute-start.12 = (bf16[432,128]{1,0:T(8,128)(2,1)}, bf16[432,128]{1,0:T(8,128)(2,1)}, u32[]{:S(2)}, u32[]{:S(2)}) collective-permute-start(bf16[432,128]{1,0:T(8,128)(2,1)} %pad_maximum_fusion.4), channel_id=1, source_target_pairs={{0,12},{4,0},{8,4},{12,8},{1,13},{5,1},{9,5},{13,9},{2,14},{6,2},{... | collective-permute-start | bytes 331784 | tf_op jit(solution)/shard_map/ppermute | solution.py:297
  101.1 11.0 %collective-permute-start.11 = (bf16[432,128]{1,0:T(8,128)(2,1)}, bf16[432,128]{1,0:T(8,128)(2,1)}, u32[]{:S(2)}, u32[]{:S(2)}) collective-permute-start(bf16[432,128]{1,0:T(8,128)(2,1)} %pad_maximum_fusion.3), channel_id=1, source_target_pairs={{0,8},{4,12},{8,0},{12,4},{1,9},{5,13},{9,1},{13,5},{2,10},{6,14},... | collective-permute-start | bytes 331784 | tf_op jit(solution)/shard_map/ppermute | solution.py:297
  101.8 10.3 %collective-permute-start.10 = (bf16[432,128]{1,0:T(8,128)(2,1)}, bf16[432,128]{1,0:T(8,128)(2,1)}, u32[]{:S(2)}, u32[]{:S(2)}) collective-permute-start(bf16[432,128]{1,0:T(8,128)(2,1)} %pad_maximum_fusion.2), channel_id=1, source_target_pairs={{0,4},{4,8},{8,12},{12,0},{1,5},{5,9},{9,13},{13,1},{2,6},{6,10},{... | collective-permute-start | bytes 331784 | tf_op jit(solution)/shard_map/ppermute | solution.py:297
  102.8 1.0 copy-start.6
  103.8 1.3 copy-start.13
  105.1 0.9 copy-start.17
  106.1 6.9 %copy-start.26 = (f32[216,128]{1,0:T(8,128)S(1)}, f32[216,128]{1,0:T(8,128)}, u32[]{:S(2)}) copy-start(f32[216,128]{1,0:T(8,128)} %get-tuple-element.75) | copy-start | bytes 331780
  106.1 6.9 %copy-start.27 = (f32[216,128]{1,0:T(8,128)S(1)}, f32[216,128]{1,0:T(8,128)}, u32[]{:S(2)}) copy-start(f32[216,128]{1,0:T(8,128)} %get-tuple-element.79) | copy-start | bytes 331780
  111.0 1.1 copy-start.10
  114.7 13.1 %collective-permute-start.13 = (bf16[432,128]{1,0:T(8,128)(2,1)}, bf16[432,128]{1,0:T(8,128)(2,1)}, u32[]{:S(2)}, u32[]{:S(2)}) collective-permute-start(bf16[432,128]{1,0:T(8,128)(2,1)} %get-tuple-element.60), channel_id=1, source_target_pairs={{0,4},{4,8},{8,12},{12,0},{1,5},{5,9},{9,13},{13,1},{2,6},{6,10},{... | collective-permute-start | bytes 331784 | tf_op jit(solution)/shard_map/ppermute | solution.py:297
  117.2 10.6 %collective-permute-start.14 = (bf16[432,128]{1,0:T(8,128)(2,1)}, bf16[432,128]{1,0:T(8,128)(2,1)}, u32[]{:S(2)}, u32[]{:S(2)}) collective-permute-start(bf16[432,128]{1,0:T(8,128)(2,1)} %get-tuple-element.60), channel_id=1, source_target_pairs={{0,8},{4,12},{8,0},{12,4},{1,9},{5,13},{9,1},{13,5},{2,10},{6,14},... | collective-permute-start | bytes 331784 | tf_op jit(solution)/shard_map/ppermute | solution.py:297
  118.1 9.7 %collective-permute-start.15 = (bf16[432,128]{1,0:T(8,128)(2,1)}, bf16[432,128]{1,0:T(8,128)(2,1)}, u32[]{:S(2)}, u32[]{:S(2)}) collective-permute-start(bf16[432,128]{1,0:T(8,128)(2,1)} %get-tuple-element.60), channel_id=1, source_target_pairs={{0,12},{4,0},{8,4},{12,8},{1,13},{5,1},{9,5},{13,9},{2,14},{6,2},{... | collective-permute-start | bytes 331784 | tf_op jit(solution)/shard_map/ppermute | solution.py:297
  119.6 1.0 copy-start.7
  120.6 1.3 copy-start.11
  121.9 0.9 copy-start.18
  127.8 12.3 %copy-start.1 = (f32[1344,256]{1,0:T(8,128)}, f32[1344,256]{1,0:T(8,128)S(1)}, u32[]{:S(2)}) copy-start(f32[1344,256]{1,0:T(8,128)S(1)} %backward.7.grad_ref) | copy-start | bytes 4128772
  133.7 13.3 %collective-permute-start.21 = (bf16[864,128]{1,0:T(8,128)(2,1)S(1)}, bf16[864,128]{1,0:T(8,128)(2,1)S(1)}, u32[]{:S(2)}, u32[]{:S(2)}) collective-permute-start(bf16[864,128]{1,0:T(8,128)(2,1)S(1)} %bitcast.85), channel_id=1, source_target_pairs={{0,2},{1,3},{2,0},{3,1},{4,6},{5,7},{6,4},{7,5},{8,10},{9,11},{10,... | collective-permute-start | bytes 663560 | tf_op jit(solution)/shard_map/ppermute | solution.py:260
  134.1 12.9 %collective-permute-start.22 = (bf16[864,128]{1,0:T(8,128)(2,1)S(1)}, bf16[864,128]{1,0:T(8,128)(2,1)S(1)}, u32[]{:S(2)}, u32[]{:S(2)}) collective-permute-start(bf16[864,128]{1,0:T(8,128)(2,1)S(1)} %bitcast.83), channel_id=1, source_target_pairs={{0,16},{16,0},{1,17},{17,1},{2,18},{18,2},{3,19},{19,3},{4,20},{20... | collective-permute-start | bytes 663560 | tf_op jit(solution)/shard_map/ppermute | solution.py:260
  134.6 5.9 %collective-permute-start.16 = (bf16[96,256]{1,0:T(8,128)(2,1)S(1)}, bf16[96,256]{1,0:T(8,128)(2,1)S(1)}, u32[]{:S(2)}, u32[]{:S(2)}) collective-permute-start(bf16[96,256]{1,0:T(8,128)(2,1)S(1)} %get-tuple-element.89), channel_id=1, source_target_pairs={{0,16},{16,0},{1,17},{17,1},{2,18},{18,2},{3,19},{19,3},{4,20},{20... | collective-permute-start | bytes 147464 | tf_op jit(solution)/shard_map/ppermute | solution.py:248
  136.2 5.7 %collective-permute-start.17 = (bf16[96,256]{1,0:T(8,128)(2,1)S(1)}, bf16[96,256]{1,0:T(8,128)(2,1)S(1)}, u32[]{:S(2)}, u32[]{:S(2)}) collective-permute-start(bf16[96,256]{1,0:T(8,128)(2,1)S(1)} %get-tuple-element.88), channel_id=1, source_target_pairs={{0,4},{4,8},{8,12},{1,5},{5,9},{9,13},{2,6},{6,10},{10,14},{3,7},{... | collective-permute-start | bytes 147464 | tf_op jit(solution)/shard_map/ppermute | solution.py:253
  138.7 6.0 %collective-permute-start.18 = (bf16[96,256]{1,0:T(8,128)(2,1)S(1)}, bf16[96,256]{1,0:T(8,128)(2,1)S(1)}, u32[]{:S(2)}, u32[]{:S(2)}) collective-permute-start(bf16[96,256]{1,0:T(8,128)(2,1)S(1)} %get-tuple-element.87), channel_id=1, source_target_pairs={{4,0},{8,4},{12,8},{5,1},{9,5},{13,9},{6,2},{10,6},{14,10},{7,3},{... | collective-permute-start | bytes 147464 | tf_op jit(solution)/shard_map/ppermute | solution.py:254
  140.5 4.1 %collective-permute-start.19 = (bf16[96,256]{1,0:T(8,128)(2,1)S(1)}, bf16[96,256]{1,0:T(8,128)(2,1)S(1)}, u32[]{:S(2)}, u32[]{:S(2)}) collective-permute-start(bf16[96,256]{1,0:T(8,128)(2,1)S(1)} %get-tuple-element.86), channel_id=1, source_target_pairs={{0,1},{1,2},{2,3},{4,5},{5,6},{6,7},{8,9},{9,10},{10,11},{12,13},{... | collective-permute-start | bytes 147464 | tf_op jit(solution)/shard_map/ppermute | solution.py:253
  141.9 5.1 %collective-permute-start.20 = (bf16[96,256]{1,0:T(8,128)(2,1)S(1)}, bf16[96,256]{1,0:T(8,128)(2,1)S(1)}, u32[]{:S(2)}, u32[]{:S(2)}) collective-permute-start(bf16[96,256]{1,0:T(8,128)(2,1)S(1)} %get-tuple-element.85), channel_id=1, source_target_pairs={{1,0},{2,1},{3,2},{5,4},{6,5},{7,6},{9,8},{10,9},{11,10},{13,12},{... | collective-permute-start | bytes 147464 | tf_op jit(solution)/shard_map/ppermute | solution.py:254
  147.0 11.2 %collective-permute-start.23 = (bf16[1728,128]{1,0:T(8,128)(2,1)S(1)}, bf16[1728,128]{1,0:T(8,128)(2,1)S(1)}, u32[]{:S(2)}, u32[]{:S(2)}) collective-permute-start(bf16[1728,128]{1,0:T(8,128)(2,1)S(1)} %constant_dynamic-update-slice_fusion.3), channel_id=1, source_target_pairs={{0,16},{16,0},{1,17},{17,1},{2,18},{18,2},{3,19},{19,3},{4,20},{20... | collective-permute-start | bytes 1327112 | tf_op jit(solution)/shard_map/ppermute | solution.py:260
  147.7 12.8 %collective-permute-start.24 = (bf16[1728,128]{1,0:T(8,128)(2,1)S(1)}, bf16[1728,128]{1,0:T(8,128)(2,1)S(1)}, u32[]{:S(2)}, u32[]{:S(2)}) collective-permute-start(bf16[1728,128]{1,0:T(8,128)(2,1)S(1)} %constant_dynamic-update-slice_fusion.6), channel_id=1, source_target_pairs={{0,2},{1,3},{2,0},{3,1},{4,6},{5,7},{6,4},{7,5},{8,10},{9,11},{10,... | collective-permute-start | bytes 1327112 | tf_op jit(solution)/shard_map/ppermute | solution.py:260
  160.6 2.0 %copy-start.2 = (f32[1344,256]{1,0:T(8,128)S(1)}, f32[1344,256]{1,0:T(8,128)}, u32[]{:S(2)}) copy-start(f32[1344,256]{1,0:T(8,128)} %copy-done.1) | copy-start | bytes 4128772
  161.9 4.4 %collective-permute-start.25 = (bf16[6912,128]{1,0:T(8,128)(2,1)}, bf16[6912,128]{1,0:T(8,128)(2,1)}, u32[]{:S(2)}, u32[]{:S(2)}) collective-permute-start(bf16[6912,128]{1,0:T(8,128)(2,1)} %pad_maximum_fusion.1), channel_id=1, source_target_pairs={{0,1},{1,0},{2,3},{3,2},{4,5},{5,4},{6,7},{7,6},{8,9},{9,8},{10,11... | collective-permute-start | bytes 5308424 | tf_op jit(solution)/shard_map/ppermute | solution.py:260

commit v3 on v2

v3 whole, which is shorter than its diff:
```python
import jax
import jax.numpy as jnp
from jax import lax
from jax.experimental import pallas as pl
from jax.experimental.pallas import tpu as pltpu
from jax.sharding import PartitionSpec as P

BF = jnp.bfloat16
F32 = jnp.float32
NT = (((1,), (1,)), ((), ()))
NN = (((1,), (0,)), ((), ()))
TN = (((0,), (0,)), ((), ()))
AXES = ("gx", "gy", "gz")
MISSING = 2000
VMEM = pl.BlockSpec(memory_space=pltpu.VMEM)
SMEM = pl.BlockSpec(memory_space=pltpu.SMEM)
ANY = pl.BlockSpec(memory_space=pl.ANY)
HBM = pl.BlockSpec(memory_space=pltpu.HBM)


def dot(a, b, dims=NN):
    return lax.dot_general(a, b, dims, preferred_element_type=F32)


def one_hot(mask):
    return jnp.where(mask, jnp.ones((), F32), jnp.zeros((), F32)).astype(BF)


def hold(x):
    return pltpu.with_memory_space_constraint(x, pltpu.HBM)


def params(megabytes):
    return pltpu.CompilerParams(vmem_limit_bytes=megabytes << 20)


def routes():
    out = []
    for i, axis in enumerate(AXES):
        if lax.axis_size(axis) == 2:
            out.append(("pair", i))
        else:
            out.extend([("up", i), ("down", i)])
    return out


def exchange(arrays, ways):
    got = []
    for array, (kind, i) in zip(arrays, ways):
        n = lax.axis_size(AXES[i])
        if kind == "pair":
            pairs = [(0, 1), (1, 0)]
        elif kind == "up":
            pairs = [(j, j + 1) for j in range(n - 1)]
        else:
            pairs = [(j + 1, j) for j in range(n - 1)]
        got.append(lax.ppermute(array, AXES[i], pairs))
    return got


def send_kernel(ways, flags, rows_ref, own_ref, *outs):
    face = rows_ref.shape[1]
    own = own_ref.shape[0]
    places = lax.broadcasted_iota(jnp.int32, (own, face), 0)
    for out, (kind, i) in zip(outs, ways):
        lower, upper = rows_ref[2 * i : 2 * i + 1, :], rows_ref[2 * i + 1 : 2 * i + 2, :]
        if kind == "pair":
            rows = jnp.where(flags[1 + i] > 0, lower, upper)
        else:
            rows = upper if kind == "up" else lower
        out[...] = dot(one_hot(places == rows), own_ref[...], TN).astype(BF)


def send(ways, flags, rows, own_features):
    shape = jax.ShapeDtypeStruct((rows.shape[1], own_features.shape[1]), BF)
    return pl.pallas_call(
        lambda *refs: send_kernel(ways, *refs),
        in_specs=[SMEM, VMEM, VMEM],
        out_specs=[VMEM] * len(ways),
        out_shape=[shape] * len(ways),
        compiler_params=params(8),
        name="send",
    )(flags, rows, own_features)


def invert_kernel(block, in_hbm, out_hbm, live_hbm, col_ref, row_hbm, tables, row_ref, sems):
    copies = [
        pltpu.make_async_copy(hbm, tables.at[j], sems.at[j])
        for j, hbm in enumerate((in_hbm, out_hbm, live_hbm))
    ]
    for copy in copies:
        copy.start()
    taps, own = in_hbm.shape
    lows = lax.broadcasted_iota(jnp.int32, (block, own), 0)
    ranks = lax.broadcasted_iota(jnp.int32, (8, own), 0)
    for copy in copies:
        copy.wait()
    for k in range(taps):
        target = tables[1, pl.ds(k, 1), :]
        source = jnp.where(tables[2, pl.ds(k, 1), :] > 0, tables[0, pl.ds(k, 1), :], MISSING)
        high = target // block
        hot = one_hot(lows == target - high * block)
        big = (source // 16) * 16
        spread = jnp.where(ranks == high, big, jnp.where(ranks - 4 == high, source - big, 0))
        spread = spread.astype(F32).astype(BF)
        col_ref[k] = dot(hot, spread, NT)
        row_ref[k] = dot(spread, hot, NT)
    copy = pltpu.make_async_copy(row_ref, row_hbm, sems.at[3])
    copy.start()
    copy.wait()


def invert(in_rows, out_rows, live, block):
    taps, own = in_rows.shape
    return pl.pallas_call(
        lambda *refs: invert_kernel(block, *refs),
        in_specs=[HBM, HBM, HBM],
        out_specs=[VMEM, HBM],
        out_shape=(
            jax.ShapeDtypeStruct((taps, block, 8), F32),
            pltpu.HBM((taps, 8, block), F32),
        ),
        scratch_shapes=[
            pltpu.VMEM((3, taps, own), jnp.int32),
            pltpu.VMEM((taps, 8, block), F32),
            pltpu.SemaphoreType.DMA((4,)),
        ],
        compiler_params=params(12),
        name="invert",
    )(hold(in_rows), hold(out_rows), hold(live))


def forward_kernel(ways, block, flags, col_ref, own_hbm, w_hbm, up_hbm, *rest):
    faces = rest[: len(ways)]
    act_hbm, gp_hbm, keep_hbm, give_hbm = rest[len(ways) : len(ways) + 4]
    ext, got, got_t, weights, turned, up, act, gp, keep, give, sems = rest[len(ways) + 4 :]
    taps = col_ref.shape[0]
    own, ch = up.shape
    rows = ext.shape[0]
    half = ch // 2
    parts = own // block
    w_copy = pltpu.make_async_copy(w_hbm, weights, sems.at[0])
    up_copy = pltpu.make_async_copy(up_hbm, up, sems.at[1])
    own_copy = pltpu.make_async_copy(own_hbm, ext.at[pl.ds(0, own), :], sems.at[2])
    own_copy.start()
    w_copy.start()
    up_copy.start()
    face = faces[0].shape[0]
    for came, (kind, i) in zip(faces, ways):
        low, high = own + 2 * i * face, own + (2 * i + 1) * face
        if kind == "pair":
            value = came[...].astype(F32)
            blank = jnp.zeros_like(value)
            last = flags[1 + i] > 0
            ext[pl.ds(low, face), :] = jnp.where(last, value, blank).astype(BF)
            ext[pl.ds(high, face), :] = jnp.where(last, blank, value).astype(BF)
        elif kind == "up":
            ext[pl.ds(low, face), :] = came[...]
        else:
            ext[pl.ds(high, face), :] = came[...]
    own_copy.wait()
    lanes = lax.broadcasted_iota(jnp.int32, (block, rows), 1)

    def gather(k, carried):
        at = pl.multiple_of(k * ch, ch)
        for h in range(parts):
            place = (col_ref[k, :, h : h + 1] + col_ref[k, :, h + 4 : h + 5]).astype(jnp.int32)
            picked = dot(one_hot(lanes == place), ext[...]).astype(BF)
            got[pl.ds(h * block, block), pl.ds(at, ch)] = picked
            got_t[pl.ds(at, ch), pl.ds(h * block, block)] = picked.T
        return carried

    lax.fori_loop(0, taps, gather, 0, unroll=9)
    w_copy.wait()
    up_copy.wait()
    odd = flags[0] > 0
    for h in range(parts):
        part = pl.ds(h * block, block)
        v = dot(got[part, :], weights[...])
        s = jax.nn.sigmoid(v)
        act[part, :] = (v * s).astype(BF)
        g = up[part, :].astype(F32) * (s * (1.0 + v * (1.0 - s)))
        gp[part, :] = g.astype(BF)
        turned[part, :half] = jnp.where(odd, g[:, half:], g[:, :half]).astype(BF)
        turned[part, half:] = jnp.where(odd, g[:, :half], g[:, half:]).astype(BF)
    out_copies = [
        pltpu.make_async_copy(act, act_hbm, sems.at[3]),
        pltpu.make_async_copy(gp, gp_hbm, sems.at[4]),
    ]
    for copy in out_copies:
        copy.start()

    def one(t, carried):
        at = pl.multiple_of(t * ch, ch)
        r = dot(got_t[pl.ds(at, ch), :], turned[...])
        keep[pl.ds(at, ch), :] = r[:, :half]
        give[pl.ds(at, ch), :] = r[:, half:].astype(BF)
        return carried

    bounds = [0, 9, 18, taps] if taps > 18 else [0, taps]
    for j in range(len(bounds) - 1):
        lax.fori_loop(bounds[j], bounds[j + 1], one, 0, unroll=3)
        part = pl.ds(bounds[j] * ch, (bounds[j + 1] - bounds[j]) * ch)
        for source, target, sem in ((give, give_hbm, 5 + j), (keep, keep_hbm, 8 + j)):
            copy = pltpu.make_async_copy(source.at[part, :], target.at[part, :], sems.at[sem])
            copy.start()
            out_copies.append(copy)
    for copy in out_copies:
        copy.wait()


def forward(ways, flags, col, own_features, faces, weight, upstream):
    taps, block, _ = col.shape
    own, ch = own_features.shape
    rows = own + 6 * faces[0].shape[0]
    like = jax.ShapeDtypeStruct
    return pl.pallas_call(
        lambda *refs: forward_kernel(ways, block, *refs),
        in_specs=[SMEM, VMEM, HBM, HBM, HBM] + [VMEM] * len(faces),
        out_specs=[HBM, HBM, ANY, ANY],
        out_shape=[
            pltpu.HBM((own, ch), BF),
            pltpu.HBM((own, ch), BF),
            like((taps * ch, ch // 2), F32),
            like((taps * ch, ch // 2), BF),
        ],
        scratch_shapes=[
            pltpu.VMEM((rows, ch), BF),
            pltpu.VMEM((own, taps * ch), BF),
            pltpu.VMEM((taps * ch, own), BF),
            pltpu.VMEM((taps * ch, ch), BF),
            pltpu.VMEM((own, ch), BF),
            pltpu.VMEM((own, ch), BF),
            pltpu.VMEM((own, ch), BF),
            pltpu.VMEM((own, ch), BF),
            pltpu.VMEM((taps * ch, ch // 2), F32),
            pltpu.VMEM((taps * ch, ch // 2), BF),
            pltpu.SemaphoreType.DMA((11,)),
        ],
        compiler_params=params(36),
        name="forward",
    )(flags, col, hold(own_features), hold(weight.reshape(taps * ch, ch)), hold(upstream), *faces)


def backward_kernel(ways, first, count, final, more, *refs):
    refs = list(refs)
    flags = refs.pop(0) if final else None
    row_hbm, gp_hbm, w_hbm = refs[:3]
    before_hbm = refs[3] if more else None
    outs = refs[3 + more : -6]
    row, gp, got, weights, total, sems = refs[-6:]
    rows, ch = total.shape
    block = row.shape[2]
    own = gp.shape[0]
    parts = own // block
    step = 336
    row_copy = pltpu.make_async_copy(row_hbm.at[pl.ds(first, count)], row, sems.at[0])
    gp_copy = pltpu.make_async_copy(gp_hbm, gp, sems.at[1])
    row_copy.start()
    gp_copy.start()
    later = [
        pltpu.make_async_copy(w_hbm.at[first + j], weights.at[:, pl.ds(j * ch, ch)], sems.at[3 + j])
        for j in range(count)
    ]
    if more:
        later.append(pltpu.make_async_copy(before_hbm, total, sems.at[2]))
    for copy in later:
        copy.start()
    row_copy.wait()
    gp_copy.wait()

    def gather(j, carried):
        at = pl.multiple_of(j * ch, ch)
        for r in range(0, rows, step):
            lines = lax.broadcasted_iota(jnp.int32, (step, block), 0) + r
            hots = []
            for h in range(parts):
                place = (row[j, h : h + 1, :] + row[j, h + 4 : h + 5, :]).astype(jnp.int32)
                hots.append(one_hot(lines == place))
            got[pl.ds(r, step), pl.ds(at, ch)] = dot(jnp.concatenate(hots, axis=1), gp[...]).astype(BF)
        return carried

    lax.fori_loop(0, count, gather, 0, unroll=3)
    for copy in later:
        copy.wait()
    for r in range(0, rows, step):
        value = dot(got[pl.ds(r, step), :], weights[...], NT)
        total[pl.ds(r, step), :] = value + total[pl.ds(r, step), :] if more else value
    if final:
        copy = pltpu.make_async_copy(total.at[pl.ds(0, own), :], outs[0], sems.at[0])
        copy.start()
        face = outs[1].shape[0]
        for out, (kind, i) in zip(outs[1:], ways):
            lower = total[pl.ds(own + 2 * i * face, face), :]
            upper = total[pl.ds(own + (2 * i + 1) * face, face), :]
            if kind == "pair":
                out[...] = jnp.where(flags[1 + i] > 0, lower, upper).astype(BF)
            else:
                out[...] = (upper if kind == "up" else lower).astype(BF)
    else:
        copy = pltpu.make_async_copy(total, outs[0], sems.at[0])
        copy.start()
    copy.wait()


def backward(ways, flags, row, gp, weight, first, count, before, rows, final):
    block = row.shape[2]
    own, ch = gp.shape
    face = (rows - own) // 6
    args = [hold(x) for x in [row, gp, weight] + ([] if before is None else [before])]
    args = ([flags] if final else []) + args
    specs = ([SMEM] if final else []) + [HBM] * (len(args) - (1 if final else 0))
    like = jax.ShapeDtypeStruct
    if final:
        out_shape = [pltpu.HBM((own, ch), F32)] + [like((face, ch), BF)] * len(ways)
        out_specs = [HBM] + [VMEM] * len(ways)
    else:
        out_shape = [pltpu.HBM((rows, ch), F32)]
        out_specs = [HBM]
    return pl.pallas_call(
        lambda *refs: backward_kernel(ways, first, count, final, int(before is not None), *refs),
        in_specs=specs,
        out_specs=out_specs,
        out_shape=out_shape,
        scratch_shapes=[
            pltpu.VMEM((count,) + row.shape[1:], F32),
            pltpu.VMEM((own, ch), BF),
            pltpu.VMEM((rows, count * ch), BF),
            pltpu.VMEM((ch, count * ch), BF),
            pltpu.VMEM((rows, ch), F32),
            pltpu.SemaphoreType.DMA((3 + count,)),
        ],
        compiler_params=params(12),
        name="backward",
    )(*args)


def finish_kernel(ways, flags, rows_ref, grad_hbm, *rest):
    faces = rest[: len(ways)]
    out_ref, grad, sem = rest[len(ways) :]
    copy = pltpu.make_async_copy(grad_hbm, grad, sem)
    copy.start()
    face = rows_ref.shape[1]
    own = out_ref.shape[0]
    places = lax.broadcasted_iota(jnp.int32, (own, face), 0)
    total = None
    for came, (kind, i) in zip(faces, ways):
        lower, upper = rows_ref[2 * i : 2 * i + 1, :], rows_ref[2 * i + 1 : 2 * i + 2, :]
        if kind == "pair":
            rows = jnp.where(flags[1 + i] > 0, lower, upper)
        else:
            rows = lower if kind == "up" else upper
        term = dot(one_hot(places == rows), came[...])
        total = term if total is None else total + term
    copy.wait()
    out_ref[...] = (grad[...] + total).astype(BF)


def finish(ways, flags, rows, grad, returned):
    return pl.pallas_call(
        lambda *refs: finish_kernel(ways, *refs),
        in_specs=[SMEM, VMEM, HBM] + [VMEM] * len(returned),
        out_specs=VMEM,
        out_shape=jax.ShapeDtypeStruct(grad.shape, BF),
        scratch_shapes=[pltpu.VMEM(grad.shape, F32), pltpu.SemaphoreType.DMA],
        compiler_params=params(8),
        name="finish",
    )(flags, rows, hold(grad), *returned)


def swap(x, axis, bit):
    n = lax.axis_size(axis)
    return lax.ppermute(x, axis, [(j, j ^ (1 << bit)) for j in range(n)])


def side(axis, bit):
    return (lax.axis_index(axis) >> bit) & 1


def place_kernel(size, spots_ref, *refs):
    count = len(refs) - 2
    arrays, out, sem = refs[: count - (count % 2)], refs[-2], refs[-1]
    copies = []
    for a, array in enumerate(arrays):
        blocks = array.shape[0] // size
        for b in range(blocks):
            at = pl.multiple_of(spots_ref[a * blocks + b], 8)
            lane = pl.multiple_of(spots_ref[len(arrays) * blocks + a], 128)
            target = out.at[pl.ds(at, size), pl.ds(lane, array.shape[1])]
            copies.append(pltpu.make_async_copy(array.at[pl.ds(b * size, size), :], target, sem.at[a * blocks + b]))
    for copy in copies:
        copy.start()
    for copy in copies:
        copy.wait()


def place(spots, arrays, size, rows, before):
    blocks = len(arrays) * (arrays[0].shape[0] // size)
    args = list(arrays) + ([] if before is None else [before])
    return pl.pallas_call(
        lambda *refs: place_kernel(size, *refs),
        in_specs=[SMEM] + [ANY] * len(arrays) + [HBM] * (len(args) - len(arrays)),
        out_specs=HBM,
        out_shape=jax.ShapeDtypeStruct((rows, 2 * arrays[0].shape[1]), BF),
        scratch_shapes=[pltpu.SemaphoreType.DMA((blocks,))],
        input_output_aliases={} if before is None else {len(args): 0},
        compiler_params=params(4),
        name="place",
    )(spots, *args)


def reduce_all(keep, give, scaling, beside):
    bits = lambda axis, low: [(axis, b) for b in range(low, lax.axis_size(axis).bit_length() - 1)]
    plane = [bits("gx", 0) + bits("gz", 1), bits("gz", 1) + bits("gx", 0)]
    turns = len(plane[0])
    rows, ch = keep.shape
    came = swap(give, "gz", 0)
    terms = [[(keep, i * (rows // 2)), (came, i * (rows // 2))] for i in range(2)]

    def total(i, extra, size):
        out = None
        for array, start in terms[i]:
            value = lax.dynamic_slice_in_dim(array, start + extra, size, 0).astype(F32)
            out = value if out is None else out + value
        return out

    size = rows // 2
    for turn in range(turns):
        size = size // 2
        mine = [side(*plane[i][turn]) for i in range(2)]
        out = [total(i, (1 - mine[i]) * size, size).astype(BF) for i in range(2)]
        came = beside(out, [swap(out[i], *plane[i][turn]) for i in range(2)])
        for i in range(2):
            terms[i] = [(a, start + mine[i] * size) for a, start in terms[i]] + [(came[i], 0)]
    n = lax.axis_size("gy")
    at = lax.axis_index("gy")
    size = size // n
    slot = lambda s: jnp.concatenate([total(i, ((at + s) % n) * size, size) for i in range(2)], axis=0)
    turn_by = lambda y, s: lax.ppermute(y, "gy", [(j, (j + s) % n) for j in range(n)])
    out = [slot(s).astype(BF) for s in range(1, n)]
    came = beside(out, [turn_by(y, s + 1) for s, y in enumerate(out)])
    final = slot(0)
    for y in came:
        final = final + y.astype(F32)
    mine = (final * scaling).astype(BF)
    came = beside([mine], [turn_by(mine, s) for s in range(1, n)])
    pieces = [jnp.concatenate([y[i * size : (i + 1) * size] for y in [mine] + came], axis=0) for i in range(2)]
    for turn in range(turns - 1, 0, -1):
        came = beside(pieces, [swap(pieces[i], *plane[i][turn]) for i in range(2)])
        pieces = [jnp.concatenate([pieces[i], came[i]], axis=0) for i in range(2)]
    odd = side("gz", 0)
    cross = lambda arrays: [swap(y, "gz", 0) for y in arrays]
    came = [swap(pieces[i], *plane[i][0]) for i in range(2)]
    twins = cross(pieces)
    sides = [[side(*plane[i][t]) for t in range(turns)] for i in range(2)]
    if size % 8 == 0:
        lanes = jnp.stack([odd, odd, 1 - odd, 1 - odd]) * ch

        def spots(flip):
            out = []
            for i in range(2):
                base = jnp.asarray(i * (rows // 2) + (sides[i][0] ^ flip) * (rows // 4))[None]
                for t in range(1, turns):
                    order = jnp.stack([sides[i][t], 1 - sides[i][t]]) * (rows // (4 << t))
                    base = (base[:, None] + order[None, :]).reshape(-1)
                order = ((at - jnp.arange(n)) % n) * size
                out.append((base[:, None] + order[None, :]).reshape(-1))
            return jnp.concatenate(out + out + [lanes]).astype(jnp.int32)

        half = place(spots(0), pieces + twins, size, rows, None)
        came = beside(pieces, came + [half])
        half = came.pop()
        last = beside(came, cross(came))
        return place(spots(1), came + last, size, rows, half)
    came = beside(pieces, came)
    last = beside(came, cross(came))

    def ordered(i, first, second):
        x = jnp.concatenate([first, second], axis=0).reshape((2,) * turns + (n, size, ch))
        for t in range(turns):
            x = jnp.where(sides[i][t] == 1, jnp.flip(x, t), x)
        x = jnp.take(x, (at - jnp.arange(n)) % n, axis=turns)
        return x.reshape(rows // 2, ch)

    mine = jnp.concatenate([ordered(i, pieces[i], came[i]) for i in range(2)], axis=0)
    other = jnp.concatenate([ordered(i, twins[i], last[i]) for i in range(2)], axis=0)
    low, high = jnp.where(odd == 1, other, mine), jnp.where(odd == 1, mine, other)
    return jnp.concatenate([low, high], axis=1)


def shards(features, weight, upstream, send_rows, in_rows, out_rows, tap_pair_exists):
    own_features = features[0, 0, 0]
    own, ch = own_features.shape
    sends = send_rows[0, 0, 0]
    taps = weight.shape[0]
    block = 256
    ways = routes()
    last = [lax.axis_index(a) == lax.axis_size(a) - 1 for a in AXES]
    flags = jnp.stack([side("gz", 0)] + last).astype(jnp.int32)
    faces = exchange(send(ways, flags, sends, own_features), ways)
    rows = own + 6 * sends.shape[1]
    col, row = invert(in_rows[0, 0, 0], out_rows[0, 0, 0], tap_pair_exists[0, 0, 0], block)
    activated, gp, keep, give = forward(ways, flags, col, own_features, faces, weight, upstream[0, 0, 0])
    devices = lax.axis_size("gx") * lax.axis_size("gy") * lax.axis_size("gz")
    counts = [9, 6, 6, 3, 3]
    steps = [(sum(counts[:j]), c) for j, c in enumerate(counts)]
    steps[-1] = (steps[-1][0], taps - steps[-1][0])
    state = {"turn": 0, "grad": None}

    def beside(out, came):
        turn = state["turn"]
        state["turn"] = turn + 1
        if turn < len(steps):
            final = turn == len(steps) - 1
            held = lax.optimization_barrier((gp, *out))
            grad = backward(ways, flags, row, held[0], weight, *steps[turn], state["grad"], rows, final)
            held = lax.optimization_barrier((*grad, *came))
            state["grad"] = held[0]
            state["back"] = held[1 : len(grad)]
            return list(held[len(grad) :])
        if turn == len(steps):
            held = lax.optimization_barrier((*state["back"], *out))
            returned = exchange(held[: len(ways)], ways)
            held = lax.optimization_barrier((*returned, *came))
            state["returned"] = list(held[: len(ways)])
            return list(held[len(ways) :])
        if turn == len(steps) + 1:
            held = lax.optimization_barrier((state["grad"], *out))
            state["done"] = finish(ways, flags, sends, held[0], state["returned"])
        return came

    grad_weight = reduce_all(keep, give, float(devices * own) ** -0.5, beside).reshape(weight.shape)
    return activated[None, None, None], state["done"][None, None, None], grad_weight


def solution(mesh):
    part = P("gx", "gy", "gz", None, None)
    return jax.shard_map(
        shards,
        mesh=mesh,
        in_specs=(part, P(), part, part, part, part, part),
        out_specs=(part, part, P()),
        check_vma=False,
    )
```

time: 172 us -> 159 us (0.924)
  local copies, waits for them, and re-layouts: 30 us -> 5.53 us
  Pallas kernels: 57.6 us -> 77.7 us
  other arithmetic: 19.1 us -> 7.47 us
  starting transfers between devices: 42.6 us -> 45.4 us
    pallas_call x8 -> x11, Pallas kernels: 57.6 us -> 77.7 us  [the longest x5 33.3 us: backward(): pl.pallas_call(lambda *refs: backward_kernel(ways, first, count, final, i...]
    unnamed x65 -> x9, local copies, waits for them, and re-layouts: 20.7 us -> 4.98 us
    ppermute x10 -> x13, waiting for transfers between devices: 16.3 us -> 4.91 us  [swap(): return lax.ppermute(x, axis, [(j, j ^ 1 << bit) for j in range(n)])]
    ppermute x10, waiting for transfers between devices: 3.87 us -> 13.3 us  [exchange(): got.append(lax.ppermute(array, AXES[i], pairs))]
    add x4 -> x3, other arithmetic: 6.44 us -> 0.23 us  [the longest x2 0.15 us: spots(): base = (base[:, None] + order[None, :]).reshape(-1)]
    concatenate x5, other arithmetic: 5.45 us -> 0.06 us  [the longest x2 0.03 us: reduce_all(): jnp.concatenate([y[i * size:(i + 1) * size] for y in [mine] + came], axis=0)]
    dynamic_update_slice x11 -> x0, local copies, waits for them, and re-layouts: 5.16 us -> none  [the longest x3 4.78 us: reduce_all(): full = lax.dynamic_update_index_in_dim(full, y, (at - s - 1) % n, 0)]
    slice x4 -> x0, local copies, waits for them, and re-layouts: 2.88 us -> none  [the longest x1 1.55 us: reduce_all(): came[:rows // 2]]
  transfers between devices with their start and end apart: 26 -> 29, of which waited for: 8 -> 9; matrix products, arithmetic and copies ran while one was open for 4% -> 3% of each run, Pallas kernels for 17% -> 29%
where the time goes in v3:
time: 159 us; the launch traced here: 157 us
  Pallas kernels  77.7 us (49%)
  starting transfers between devices  45.4 us (29%)
  waiting for transfers between devices  20.1 us (13%)
  other arithmetic  7.47 us (5%)
  local copies, waits for them, and re-layouts  5.53 us (3%)
    pallas_call x5, Pallas kernels, backward(): pl.pallas_call(lambda *refs: backward_kernel(ways, first, count, final, i...  33.3 us
    pallas_call x1, Pallas kernels, forward(): pl.pallas_call(lambda *refs: forward_kernel(ways, block, *refs), in_specs...  29 us
    ppermute x10, starting transfers between devices, exchange(): got.append(lax.ppermute(array, AXES[i], pairs))  18.7 us
    ppermute x13, starting transfers between devices, swap(): return lax.ppermute(x, axis, [(j, j ^ 1 << bit) for j in range(n)])  16.1 us
    ppermute x10, waiting for transfers between devices, exchange(): got.append(lax.ppermute(array, AXES[i], pairs))  13.3 us
    ppermute x6, starting transfers between devices, reduce_all(): lax.ppermute(y, 'gy', [(j, (j + s) % n) for j in range(n)])  10.6 us
    pallas_call x1, Pallas kernels, invert(): pl.pallas_call(lambda *refs: invert_kernel(block, *refs), in_specs=[HBM,...  7.33 us
    unnamed x9, local copies, waits for them, and re-layouts  4.98 us
  transfers between devices with their start and end apart: 29, of which 9 were waited for; matrix products, arithmetic and copies ran while one was open for 3% of the time, Pallas kernels for 29%

profile of v3, /device:TPU:0, one launch (start us, length us, event | category | flops | bytes accessed | tf_op | source)
XLA Modules:
  0.0 157.3 jit_solution(14830925489488588661)
XLA Ops:
  0.6 0.7 copy.20
  1.3 0.1 fusion.4
  1.4 1.0 copy-done
  2.4 1.0 send.1
  3.4 3.0 %collective-permute-start = (bf16[96,256]{1,0:T(8,128)(2,1)S(1)}, bf16[96,256]{1,0:T(8,128)(2,1)S(1)}, u32[]{:S(2)}, u32[]{:S(2)}) collective-permute-start(bf16[96,256]{1,0:T(8,128)(2,1)S(1)} %get-tuple-element.62), channel_id=1, source_target_pairs={{0,16},{16,0},{1,17},{17,1},{2,18},{18,2},{3,19},{19,3},{4,20},{20... | collective-permute-start | bytes 147464 | tf_op jit(solution)/shard_map/ppermute | solution.py:57
  6.4 3.5 %collective-permute-start.1 = (bf16[96,256]{1,0:T(8,128)(2,1)S(1)}, bf16[96,256]{1,0:T(8,128)(2,1)S(1)}, u32[]{:S(2)}, u32[]{:S(2)}) collective-permute-start(bf16[96,256]{1,0:T(8,128)(2,1)S(1)} %get-tuple-element.63), channel_id=1, source_target_pairs={{0,4},{4,8},{8,12},{1,5},{5,9},{9,13},{2,6},{6,10},{10,14},{3,7},{... | collective-permute-start | bytes 147464 | tf_op jit(solution)/shard_map/ppermute | solution.py:57
  9.9 1.3 collective-permute-start.2
  11.2 1.3 collective-permute-start.3
  12.5 1.3 collective-permute-start.4
  13.8 1.6 %copy_bitcast_fusion = (s32[27,768]{1,0:T(8,128)}, s32[27,768]{1,0:T(8,128)}) fusion(s32[1,1,1,27,768]{4,2,3,1,0:T(1,128)} %param.13, s32[1,1,1,27,768]{4,2,3,1,0:T(1,128)} %param.12), kind=kLoop, calls=%fused_computation.22 | loop fusion | bytes 331776
  15.4 1.5 copy.19
  16.9 7.3 %invert.1 = (f32[27,256,8]{2,1,0:T(8,128)S(1)}, f32[27,8,256]{2,1,0:T(8,128)}) custom-call(s32[27,768]{1,0:T(8,128)} %bitcast.32, s32[27,768]{1,0:T(8,128)} %get-tuple-element.158.refs_1_, s32[27,768]{1,0:T(8,128)} %get-tuple-element.157.refs_2_), custom_call_target="tpu_custom_call" | custom-call | tf_op jit(solution)/shard_map/invert/pallas_call | solution.py:115
  24.3 29.0 %forward.1 = (bf16[768,256]{1,0:T(8,128)(2,1)}, bf16[768,256]{1,0:T(8,128)(2,1)}, f32[6912,128]{1,0:T(8,128)S(1)}, bf16[6912,128]{1,0:T(8,128)(2,1)}) custom-call(s32[4]{0:T(128)S(1)} %get-tuple-element.152.refs_0_, f32[27,256,8]{2,1,0:T(8,128)S(1)} %get-tuple-element.61.refs_1_, bf16[768,256]{1,0:T(8,128)(2,1)} %bitcast.25, bf16[6912,256]{1,0:T(8,128)(2,1)} %bitcast.29, ...), custom_call_target="tpu_custom_call" | custom-call | tf_op jit(solution)/shard_map/forward/pallas_call | solution.py:217
  53.4 2.9 %collective-permute-start.5 = (bf16[6912,128]{1,0:T(8,128)(2,1)}, bf16[6912,128]{1,0:T(8,128)(2,1)}, u32[]{:S(2)}, u32[]{:S(2)}) collective-permute-start(bf16[6912,128]{1,0:T(8,128)(2,1)} %get-tuple-element.71), channel_id=1, source_target_pairs={{0,1},{1,0},{2,3},{3,2},{4,5},{5,4},{6,7},{7,6},{8,9},{9,8},{10,11... | collective-permute-start | bytes 5308424 | tf_op jit(solution)/shard_map/ppermute | solution.py:373
  56.3 3.7 %collective-permute-done.5 = bf16[6912,128]{1,0:T(8,128)(2,1)} collective-permute-done((bf16[6912,128]{1,0:T(8,128)(2,1)}, bf16[6912,128]{1,0:T(8,128)(2,1)}, u32[]{:S(2)}, u32[]{:S(2)}) %collective-permute-start.5) | collective-permute-done | bytes 1769504 | tf_op jit(solution)/shard_map/ppermute | solution.py:373
  60.0 2.2 %add_convert_fusion = (bf16[1728,128]{1,0:T(8,128)(2,1)}, bf16[1728,128]{1,0:T(8,128)(2,1)}) fusion(f32[6912,128]{1,0:T(8,128)S(1)} %get-tuple-element.70, s32[]{:T(128)S(6)} %select_n.140, bf16[6912,128]{1,0:T(8,128)(2,1)} %collective-permute-done.5, s32[]{:T(128)S(6)} %select_n.139), kind=kLoop, calls=%fused_computation | loop fusion | flops 1327104 | bytes 3538952 | tf_op jit(solution)/shard_map/convert_element_type | solution.py:431
  62.2 0.6 collective-permute-start.6
  62.8 2.0 %collective-permute-start.7 = (bf16[1728,128]{1,0:T(8,128)(2,1)}, bf16[1728,128]{1,0:T(8,128)(2,1)}, u32[]{:S(2)}, u32[]{:S(2)}) collective-permute-start(bf16[1728,128]{1,0:T(8,128)(2,1)} %get-tuple-element.129), channel_id=1, source_target_pairs={{0,2},{1,3},{2,0},{3,1},{4,6},{5,7},{6,4},{7,5},{8,10},{9,11},{10,... | collective-permute-start | bytes 1327112 | tf_op jit(solution)/shard_map/ppermute | solution.py:373
  64.7 9.6 %backward.5.refs_3_ = f32[1344,256]{1,0:T(8,128)} custom-call(f32[27,8,256]{2,1,0:T(8,128)} %get-tuple-element.68.refs_0_.refs_1_, bf16[768,256]{1,0:T(8,128)(2,1)} %get-tuple-element.89.refs_1_.refs_2_, bf16[27,256,256]{2,1,0:T(8,128)(2,1)} %refs_3_.1), custom_call_target="tpu_custom_call" | custom-call | tf_op jit(solution)/shard_map/backward/pallas_call | solution.py:320
  74.3 0.7 collective-permute-done.6
  75.0 0.3 collective-permute-done.7
  75.2 2.2 %add_convert_fusion.2 = (bf16[864,128]{1,0:T(8,128)(2,1)}, bf16[864,128]{1,0:T(8,128)(2,1)}) fusion(f32[6912,128]{1,0:T(8,128)S(1)} %get-tuple-element.70, s32[]{:T(128)S(6)} %select_n.144, bf16[1728,128]{1,0:T(8,128)(2,1)} %collective-permute-done.7, s32[]{:T(128)S(6)} %select_n.145, bf16[6912,128]{1,0:T(8,128)(2,1)} %collective-permute-done.5, ...), kind=kLoop, calls=%fused_computation.2 | loop fusion | flops 1105920 | bytes 2211856 | tf_op jit(solution)/shard_map/convert_element_type | solution.py:431
  77.5 1.7 %collective-permute-start.8 = (bf16[864,128]{1,0:T(8,128)(2,1)}, bf16[864,128]{1,0:T(8,128)(2,1)}, u32[]{:S(2)}, u32[]{:S(2)}) collective-permute-start(bf16[864,128]{1,0:T(8,128)(2,1)} %get-tuple-element.128), channel_id=1, source_target_pairs={{0,2},{1,3},{2,0},{3,1},{4,6},{5,7},{6,4},{7,5},{8,10},{9,11},{10,... | collective-permute-start | bytes 663560 | tf_op jit(solution)/shard_map/ppermute | solution.py:373
  79.2 1.5 collective-permute-start.9
  80.7 7.0 %backward.6.refs_3_ = f32[1344,256]{1,0:T(8,128)} custom-call(f32[27,8,256]{2,1,0:T(8,128)} %get-tuple-element.68.refs_0_.refs_1_, bf16[768,256]{1,0:T(8,128)(2,1)} %get-tuple-element.89.refs_1_.refs_2_, bf16[27,256,256]{2,1,0:T(8,128)(2,1)} %refs_3_.1, f32[1344,256]{1,0:T(8,128)} %backward.5.refs_3_), custom_call_target="tpu_custom_call" | custom-call | tf_op jit(solution)/shard_map/backward/pallas_call | solution.py:320
  87.8 1.2 add_convert_fusion.5
  89.0 1.2 add_convert_fusion.4
  90.3 4.7 %collective-permute-start.12 = (bf16[432,128]{1,0:T(8,128)(2,1)S(1)}, bf16[432,128]{1,0:T(8,128)(2,1)S(1)}, u32[]{:S(2)}, u32[]{:S(2)}) collective-permute-start(bf16[432,128]{1,0:T(8,128)(2,1)S(1)} %pad_maximum_fusion.4), channel_id=1, source_target_pairs={{0,12},{4,0},{8,4},{12,8},{1,13},{5,1},{9,5},{13,9},{2,14},{6,2},{... | collective-permute-start | bytes 331784 | tf_op jit(solution)/shard_map/ppermute | solution.py:439
  95.1 1.0 collective-permute-start.10
  96.1 7.0 %backward.7.refs_3_ = f32[1344,256]{1,0:T(8,128)} custom-call(f32[27,8,256]{2,1,0:T(8,128)} %get-tuple-element.68.refs_0_.refs_1_, bf16[768,256]{1,0:T(8,128)(2,1)} %get-tuple-element.89.refs_1_.refs_2_, bf16[27,256,256]{2,1,0:T(8,128)(2,1)} %refs_3_.1, f32[1344,256]{1,0:T(8,128)} %backward.6.refs_3_), custom_call_target="tpu_custom_call" | custom-call | tf_op jit(solution)/shard_map/backward/pallas_call | solution.py:320
  103.2 0.8 collective-permute-done.11
  104.0 1.8 %collective-permute-start.13 = (bf16[432,128]{1,0:T(8,128)(2,1)S(1)}, bf16[432,128]{1,0:T(8,128)(2,1)S(1)}, u32[]{:S(2)}, u32[]{:S(2)}) collective-permute-start(bf16[432,128]{1,0:T(8,128)(2,1)S(1)} %fusion.3), channel_id=1, source_target_pairs={{0,4},{4,8},{8,12},{12,0},{1,5},{5,9},{9,13},{13,1},{2,6},{6,10},{... | collective-permute-start | bytes 331784 | tf_op jit(solution)/shard_map/ppermute | solution.py:439
  105.8 0.9 collective-permute-start.14
  106.7 2.1 %collective-permute-start.15 = (bf16[432,128]{1,0:T(8,128)(2,1)S(1)}, bf16[432,128]{1,0:T(8,128)(2,1)S(1)}, u32[]{:S(2)}, u32[]{:S(2)}) collective-permute-start(bf16[432,128]{1,0:T(8,128)(2,1)S(1)} %fusion.3), channel_id=1, source_target_pairs={{0,12},{4,0},{8,4},{12,8},{1,13},{5,1},{9,5},{13,9},{2,14},{6,2},{... | collective-permute-start | bytes 331784 | tf_op jit(solution)/shard_map/ppermute | solution.py:439
  108.8 4.7 %backward.8.refs_4_ = f32[1344,256]{1,0:T(8,128)} custom-call(f32[27,8,256]{2,1,0:T(8,128)} %get-tuple-element.68.refs_0_.refs_1_, bf16[768,256]{1,0:T(8,128)(2,1)} %get-tuple-element.89.refs_1_.refs_2_, bf16[27,256,256]{2,1,0:T(8,128)(2,1)} %refs_3_.1, f32[1344,256]{1,0:T(8,128)} %backward.7.refs_3_), custom_call_target="tpu_custom_call" | custom-call | tf_op jit(solution)/shard_map/backward/pallas_call | solution.py:320
  113.6 1.2 collective-permute-done.14
  114.9 0.7 collective-permute-start.17
  115.6 0.7 collective-permute-start.16
  116.2 5.0 %backward.9 = (f32[768,256]{1,0:T(8,128)}, bf16[96,256]{1,0:T(8,128)(2,1)S(1)}, bf16[96,256]{1,0:T(8,128)(2,1)S(1)}, bf16[96,256]{1,0:T(8,128)(2,1)S(1)}, bf16[9...) custom-call(s32[4]{0:T(128)S(1)} %get-tuple-element.152.refs_0_, f32[27,8,256]{2,1,0:T(8,128)} %get-tuple-element.68.refs_0_.refs_1_, ...), custom_call_target="tpu_custom_call" | custom-call | tf_op jit(solution)/shard_map/backward/pallas_call | solution.py:320
  121.3 0.3 collective-permute-done.16
  121.7 0.6 collective-permute-start.25
  122.3 0.1 broadcast_add_fusion.6
  122.4 1.2 collective-permute-start.24
  123.5 1.4 collective-permute-start.23
  124.9 0.6 collective-permute-start.18
  125.5 0.1 broadcast_add_fusion.4
  125.6 10.8 %collective-permute-done.18.refs_3_ = bf16[96,256]{1,0:T(8,128)(2,1)S(1)} collective-permute-done((bf16[96,256]{1,0:T(8,128)(2,1)S(1)}, bf16[96,256]{1,0:T(8,128)(2,1)S(1)}, u32[]{:S(2)}, u32[]{:S(2)}) %collective-permute-start.18) | collective-permute-done | bytes 49184 | tf_op jit(solution)/shard_map/ppermute | solution.py:57
  136.4 3.8 %collective-permute-start.19 = (bf16[96,256]{1,0:T(8,128)(2,1)S(1)}, bf16[96,256]{1,0:T(8,128)(2,1)S(1)}, u32[]{:S(2)}, u32[]{:S(2)}) collective-permute-start(bf16[96,256]{1,0:T(8,128)(2,1)S(1)} %get-tuple-element.106), channel_id=1, source_target_pairs={{0,4},{4,8},{8,12},{1,5},{5,9},{9,13},{2,6},{6,10},{10,14},{3,7},{... | collective-permute-start | bytes 147464 | tf_op jit(solution)/shard_map/ppermute | solution.py:57
  140.3 1.7 %collective-permute-done.19.refs_4_ = bf16[96,256]{1,0:T(8,128)(2,1)S(1)} collective-permute-done((bf16[96,256]{1,0:T(8,128)(2,1)S(1)}, bf16[96,256]{1,0:T(8,128)(2,1)S(1)}, u32[]{:S(2)}, u32[]{:S(2)}) %collective-permute-start.19) | collective-permute-done | bytes 49184 | tf_op jit(solution)/shard_map/ppermute | solution.py:57
  142.0 1.3 collective-permute-start.20
  143.3 1.3 collective-permute-start.21
  144.6 1.3 collective-permute-start.22
  145.9 0.1 add_multiply_fusion.2
  145.9 0.1 add.536
  146.0 0.1 add.541
  146.1 0.1 concatenate.61.refs_0_
  146.2 2.0 %place.2.refs_5_ = bf16[6912,256]{1,0:T(8,128)(2,1)} custom-call(s32[36]{0:T(128)S(1)} %concatenate.61.refs_0_, bf16[1728,128]{1,0:T(8,128)(2,1)S(1)} %constant_dynamic-update-slice_fusion.refs_1_, bf16[1728,128]{1,0:T(8,128)(2,1)S(1)} %constant_dynamic-update-slice_fusion.5.refs_2_, bf16[1728,128]{1,0:T(8,128)(2,1)S(1)} %collective-permute-done.25.refs_3_, ...), custom_call_target="tpu_custom_call" | custom-call | tf_op jit(solution)/shard_map/place/pallas_call | solution.py:400
  148.3 0.8 collective-permute-done.22.refs_7_
  149.1 2.8 %collective-permute-start.27 = (bf16[1728,128]{1,0:T(8,128)(2,1)S(1)}, bf16[1728,128]{1,0:T(8,128)(2,1)S(1)}, u32[]{:S(2)}, u32[]{:S(2)}) collective-permute-start(bf16[1728,128]{1,0:T(8,128)(2,1)S(1)} %collective-permute-done.23.refs_1_), channel_id=1, source_target_pairs={{0,1},{1,0},{2,3},{3,2},{4,5},{5,4},{6,7},{7,6},{8,9},{9,8},{10,11... | collective-permute-start | bytes 1327112 | tf_op jit(solution)/shard_map/ppermute | solution.py:373
  151.9 0.1 add.546
  152.0 0.1 add.552
  152.1 0.1 concatenate.62.refs_0_
  152.2 2.9 %finish.1 = bf16[768,256]{1,0:T(8,128)(2,1)} custom-call(s32[4]{0:T(128)S(1)} %get-tuple-element.152.refs_0_, s32[6,96]{1,0:T(8,128)S(1)} %bitcast.28, f32[768,256]{1,0:T(8,128)} %get-tuple-element.112.refs_2_, bf16[96,256]{1,0:T(8,128)(2,1)S(1)} %collective-permute-done.18.refs_3_, bf16[96,256]{1,0:T(8,128)(2,1)S(1)} %collective-permute-done.19.refs_4_, ...), custom_call_target="tpu_custom_call" | custom-call | tf_op jit(solution)/shard_map/finish/pallas_call | solution.py:360
  155.1 2.0 %place.3 = bf16[6912,256]{1,0:T(8,128)(2,1)} custom-call(s32[36]{0:T(128)S(1)} %concatenate.62.refs_0_, bf16[1728,128]{1,0:T(8,128)(2,1)S(1)} %collective-permute-done.23.refs_1_, bf16[1728,128]{1,0:T(8,128)(2,1)S(1)} %collective-permute-done.24.refs_2_, bf16[1728,128]{1,0:T(8,128)(2,1)S(1)} %collective-permute-done.27.refs_3_, ...), custom_call_target="tpu_custom_call", output_to_operand_aliasing={{}: (5, {})} | custom-call | tf_op jit(solution)/shard_map/place/pallas_call | solution.py:400
  (37 shorter events, 0.7 us)
Async XLA Ops:
  1.4 1.0 copy-start
  3.4 20.9 %collective-permute-start = (bf16[96,256]{1,0:T(8,128)(2,1)S(1)}, bf16[96,256]{1,0:T(8,128)(2,1)S(1)}, u32[]{:S(2)}, u32[]{:S(2)}) collective-permute-start(bf16[96,256]{1,0:T(8,128)(2,1)S(1)} %get-tuple-element.62), channel_id=1, source_target_pairs={{0,16},{16,0},{1,17},{17,1},{2,18},{18,2},{3,19},{19,3},{4,20},{20... | collective-permute-start | bytes 147464 | tf_op jit(solution)/shard_map/ppermute | solution.py:57
  6.4 17.9 %collective-permute-start.1 = (bf16[96,256]{1,0:T(8,128)(2,1)S(1)}, bf16[96,256]{1,0:T(8,128)(2,1)S(1)}, u32[]{:S(2)}, u32[]{:S(2)}) collective-permute-start(bf16[96,256]{1,0:T(8,128)(2,1)S(1)} %get-tuple-element.63), channel_id=1, source_target_pairs={{0,4},{4,8},{8,12},{1,5},{5,9},{9,13},{2,6},{6,10},{10,14},{3,7},{... | collective-permute-start | bytes 147464 | tf_op jit(solution)/shard_map/ppermute | solution.py:57
  9.9 14.4 %collective-permute-start.2 = (bf16[96,256]{1,0:T(8,128)(2,1)S(1)}, bf16[96,256]{1,0:T(8,128)(2,1)S(1)}, u32[]{:S(2)}, u32[]{:S(2)}) collective-permute-start(bf16[96,256]{1,0:T(8,128)(2,1)S(1)} %get-tuple-element.64), channel_id=1, source_target_pairs={{4,0},{8,4},{12,8},{5,1},{9,5},{13,9},{6,2},{10,6},{14,10},{7,3},{... | collective-permute-start | bytes 147464 | tf_op jit(solution)/shard_map/ppermute | solution.py:57
  11.2 13.1 %collective-permute-start.3 = (bf16[96,256]{1,0:T(8,128)(2,1)S(1)}, bf16[96,256]{1,0:T(8,128)(2,1)S(1)}, u32[]{:S(2)}, u32[]{:S(2)}) collective-permute-start(bf16[96,256]{1,0:T(8,128)(2,1)S(1)} %get-tuple-element.65), channel_id=1, source_target_pairs={{0,1},{1,2},{2,3},{4,5},{5,6},{6,7},{8,9},{9,10},{10,11},{12,13},{... | collective-permute-start | bytes 147464 | tf_op jit(solution)/shard_map/ppermute | solution.py:57
  12.5 11.8 %collective-permute-start.4 = (bf16[96,256]{1,0:T(8,128)(2,1)S(1)}, bf16[96,256]{1,0:T(8,128)(2,1)S(1)}, u32[]{:S(2)}, u32[]{:S(2)}) collective-permute-start(bf16[96,256]{1,0:T(8,128)(2,1)S(1)} %get-tuple-element.66), channel_id=1, source_target_pairs={{1,0},{2,1},{3,2},{5,4},{6,5},{7,6},{9,8},{10,9},{11,10},{13,12},{... | collective-permute-start | bytes 147464 | tf_op jit(solution)/shard_map/ppermute | solution.py:57
  53.4 6.6 %collective-permute-start.5 = (bf16[6912,128]{1,0:T(8,128)(2,1)}, bf16[6912,128]{1,0:T(8,128)(2,1)}, u32[]{:S(2)}, u32[]{:S(2)}) collective-permute-start(bf16[6912,128]{1,0:T(8,128)(2,1)} %get-tuple-element.71), channel_id=1, source_target_pairs={{0,1},{1,0},{2,3},{3,2},{4,5},{5,4},{6,7},{7,6},{8,9},{9,8},{10,11... | collective-permute-start | bytes 5308424 | tf_op jit(solution)/shard_map/ppermute | solution.py:373
  62.2 12.8 %collective-permute-start.6 = (bf16[1728,128]{1,0:T(8,128)(2,1)}, bf16[1728,128]{1,0:T(8,128)(2,1)}, u32[]{:S(2)}, u32[]{:S(2)}) collective-permute-start(bf16[1728,128]{1,0:T(8,128)(2,1)} %get-tuple-element.130), channel_id=1, source_target_pairs={{0,16},{16,0},{1,17},{17,1},{2,18},{18,2},{3,19},{19,3},{4,20},{20... | collective-permute-start | bytes 1327112 | tf_op jit(solution)/shard_map/ppermute | solution.py:373
  62.8 12.5 %collective-permute-start.7 = (bf16[1728,128]{1,0:T(8,128)(2,1)}, bf16[1728,128]{1,0:T(8,128)(2,1)}, u32[]{:S(2)}, u32[]{:S(2)}) collective-permute-start(bf16[1728,128]{1,0:T(8,128)(2,1)} %get-tuple-element.129), channel_id=1, source_target_pairs={{0,2},{1,3},{2,0},{3,1},{4,6},{5,7},{6,4},{7,5},{8,10},{9,11},{10,... | collective-permute-start | bytes 1327112 | tf_op jit(solution)/shard_map/ppermute | solution.py:373
  77.5 10.3 %collective-permute-start.8 = (bf16[864,128]{1,0:T(8,128)(2,1)}, bf16[864,128]{1,0:T(8,128)(2,1)}, u32[]{:S(2)}, u32[]{:S(2)}) collective-permute-start(bf16[864,128]{1,0:T(8,128)(2,1)} %get-tuple-element.128), channel_id=1, source_target_pairs={{0,2},{1,3},{2,0},{3,1},{4,6},{5,7},{6,4},{7,5},{8,10},{9,11},{10,... | collective-permute-start | bytes 663560 | tf_op jit(solution)/shard_map/ppermute | solution.py:373
  79.2 8.5 %collective-permute-start.9 = (bf16[864,128]{1,0:T(8,128)(2,1)}, bf16[864,128]{1,0:T(8,128)(2,1)}, u32[]{:S(2)}, u32[]{:S(2)}) collective-permute-start(bf16[864,128]{1,0:T(8,128)(2,1)} %get-tuple-element.127), channel_id=1, source_target_pairs={{0,16},{16,0},{1,17},{17,1},{2,18},{18,2},{3,19},{19,3},{4,20},{20... | collective-permute-start | bytes 663560 | tf_op jit(solution)/shard_map/ppermute | solution.py:373
  90.3 12.9 %collective-permute-start.12 = (bf16[432,128]{1,0:T(8,128)(2,1)S(1)}, bf16[432,128]{1,0:T(8,128)(2,1)S(1)}, u32[]{:S(2)}, u32[]{:S(2)}) collective-permute-start(bf16[432,128]{1,0:T(8,128)(2,1)S(1)} %pad_maximum_fusion.4), channel_id=1, source_target_pairs={{0,12},{4,0},{8,4},{12,8},{1,13},{5,1},{9,5},{13,9},{2,14},{6,2},{... | collective-permute-start | bytes 331784 | tf_op jit(solution)/shard_map/ppermute | solution.py:439
  95.0 8.9 %collective-permute-start.11 = (bf16[432,128]{1,0:T(8,128)(2,1)S(1)}, bf16[432,128]{1,0:T(8,128)(2,1)S(1)}, u32[]{:S(2)}, u32[]{:S(2)}) collective-permute-start(bf16[432,128]{1,0:T(8,128)(2,1)S(1)} %pad_maximum_fusion.3), channel_id=1, source_target_pairs={{0,8},{4,12},{8,0},{12,4},{1,9},{5,13},{9,1},{13,5},{2,10},{6,14},... | collective-permute-start | bytes 331784 | tf_op jit(solution)/shard_map/ppermute | solution.py:439
  95.1 8.8 %collective-permute-start.10 = (bf16[432,128]{1,0:T(8,128)(2,1)S(1)}, bf16[432,128]{1,0:T(8,128)(2,1)S(1)}, u32[]{:S(2)}, u32[]{:S(2)}) collective-permute-start(bf16[432,128]{1,0:T(8,128)(2,1)S(1)} %pad_maximum_fusion.2), channel_id=1, source_target_pairs={{0,4},{4,8},{8,12},{12,0},{1,5},{5,9},{9,13},{13,1},{2,6},{6,10},{... | collective-permute-start | bytes 331784 | tf_op jit(solution)/shard_map/ppermute | solution.py:439
  104.0 9.6 %collective-permute-start.13 = (bf16[432,128]{1,0:T(8,128)(2,1)S(1)}, bf16[432,128]{1,0:T(8,128)(2,1)S(1)}, u32[]{:S(2)}, u32[]{:S(2)}) collective-permute-start(bf16[432,128]{1,0:T(8,128)(2,1)S(1)} %fusion.3), channel_id=1, source_target_pairs={{0,4},{4,8},{8,12},{12,0},{1,5},{5,9},{9,13},{13,1},{2,6},{6,10},{... | collective-permute-start | bytes 331784 | tf_op jit(solution)/shard_map/ppermute | solution.py:439
  105.8 8.9 %collective-permute-start.14 = (bf16[432,128]{1,0:T(8,128)(2,1)S(1)}, bf16[432,128]{1,0:T(8,128)(2,1)S(1)}, u32[]{:S(2)}, u32[]{:S(2)}) collective-permute-start(bf16[432,128]{1,0:T(8,128)(2,1)S(1)} %fusion.3), channel_id=1, source_target_pairs={{0,8},{4,12},{8,0},{12,4},{1,9},{5,13},{9,1},{13,5},{2,10},{6,14},... | collective-permute-start | bytes 331784 | tf_op jit(solution)/shard_map/ppermute | solution.py:439
  106.7 8.0 %collective-permute-start.15 = (bf16[432,128]{1,0:T(8,128)(2,1)S(1)}, bf16[432,128]{1,0:T(8,128)(2,1)S(1)}, u32[]{:S(2)}, u32[]{:S(2)}) collective-permute-start(bf16[432,128]{1,0:T(8,128)(2,1)S(1)} %fusion.3), channel_id=1, source_target_pairs={{0,12},{4,0},{8,4},{12,8},{1,13},{5,1},{9,5},{13,9},{2,14},{6,2},{... | collective-permute-start | bytes 331784 | tf_op jit(solution)/shard_map/ppermute | solution.py:439
  114.9 6.4 %collective-permute-start.17 = (bf16[864,128]{1,0:T(8,128)(2,1)S(1)}, bf16[864,128]{1,0:T(8,128)(2,1)S(1)}, u32[]{:S(2)}, u32[]{:S(2)}) collective-permute-start(bf16[864,128]{1,0:T(8,128)(2,1)S(1)} %pad_maximum_fusion.1), channel_id=1, source_target_pairs={{0,16},{16,0},{1,17},{17,1},{2,18},{18,2},{3,19},{19,3},{4,20},{20... | collective-permute-start | bytes 663560 | tf_op jit(solution)/shard_map/ppermute | solution.py:373
  115.6 6.0 %collective-permute-start.16 = (bf16[864,128]{1,0:T(8,128)(2,1)S(1)}, bf16[864,128]{1,0:T(8,128)(2,1)S(1)}, u32[]{:S(2)}, u32[]{:S(2)}) collective-permute-start(bf16[864,128]{1,0:T(8,128)(2,1)S(1)} %pad_maximum_fusion), channel_id=1, source_target_pairs={{0,2},{1,3},{2,0},{3,1},{4,6},{5,7},{6,4},{7,5},{8,10},{9,11},{10,... | collective-permute-start | bytes 663560 | tf_op jit(solution)/shard_map/ppermute | solution.py:373
  121.6 21.6 %collective-permute-start.26 = (bf16[1728,128]{1,0:T(8,128)(2,1)S(1)}, bf16[1728,128]{1,0:T(8,128)(2,1)S(1)}, u32[]{:S(2)}, u32[]{:S(2)}) collective-permute-start(bf16[1728,128]{1,0:T(8,128)(2,1)S(1)} %constant_dynamic-update-slice_fusion.5.refs_2_), channel_id=1, source_target_pairs={{0,1},{1,0},{2,3},{3,2},{4,5},{5,4},{6,7},{7,6},{8,9},{9,8},{10,11... | collective-permute-start | bytes 1327112 | tf_op jit(solution)/shard_map/ppermute | solution.py:373
  121.7 22.8 %collective-permute-start.25 = (bf16[1728,128]{1,0:T(8,128)(2,1)S(1)}, bf16[1728,128]{1,0:T(8,128)(2,1)S(1)}, u32[]{:S(2)}, u32[]{:S(2)}) collective-permute-start(bf16[1728,128]{1,0:T(8,128)(2,1)S(1)} %constant_dynamic-update-slice_fusion.refs_1_), channel_id=1, source_target_pairs={{0,1},{1,0},{2,3},{3,2},{4,5},{5,4},{6,7},{7,6},{8,9},{9,8},{10,11... | collective-permute-start | bytes 1327112 | tf_op jit(solution)/shard_map/ppermute | solution.py:373
  122.4 26.7 %collective-permute-start.24 = (bf16[1728,128]{1,0:T(8,128)(2,1)S(1)}, bf16[1728,128]{1,0:T(8,128)(2,1)S(1)}, u32[]{:S(2)}, u32[]{:S(2)}) collective-permute-start(bf16[1728,128]{1,0:T(8,128)(2,1)S(1)} %constant_dynamic-update-slice_fusion.5.refs_2_), channel_id=1, source_target_pairs={{0,2},{1,3},{2,0},{3,1},{4,6},{5,7},{6,4},{7,5},{8,10},{9,11},{10,... | collective-permute-start | bytes 1327112 | tf_op jit(solution)/shard_map/ppermute | solution.py:373
  123.5 25.5 %collective-permute-start.23 = (bf16[1728,128]{1,0:T(8,128)(2,1)S(1)}, bf16[1728,128]{1,0:T(8,128)(2,1)S(1)}, u32[]{:S(2)}, u32[]{:S(2)}) collective-permute-start(bf16[1728,128]{1,0:T(8,128)(2,1)S(1)} %constant_dynamic-update-slice_fusion.refs_1_), channel_id=1, source_target_pairs={{0,16},{16,0},{1,17},{17,1},{2,18},{18,2},{3,19},{19,3},{4,20},{20... | collective-permute-start | bytes 1327112 | tf_op jit(solution)/shard_map/ppermute | solution.py:373
  124.9 11.4 %collective-permute-start.18 = (bf16[96,256]{1,0:T(8,128)(2,1)S(1)}, bf16[96,256]{1,0:T(8,128)(2,1)S(1)}, u32[]{:S(2)}, u32[]{:S(2)}) collective-permute-start(bf16[96,256]{1,0:T(8,128)(2,1)S(1)} %get-tuple-element.105), channel_id=1, source_target_pairs={{0,16},{16,0},{1,17},{17,1},{2,18},{18,2},{3,19},{19,3},{4,20},{20... | collective-permute-start | bytes 147464 | tf_op jit(solution)/shard_map/ppermute | solution.py:57
  136.4 5.6 %collective-permute-start.19 = (bf16[96,256]{1,0:T(8,128)(2,1)S(1)}, bf16[96,256]{1,0:T(8,128)(2,1)S(1)}, u32[]{:S(2)}, u32[]{:S(2)}) collective-permute-start(bf16[96,256]{1,0:T(8,128)(2,1)S(1)} %get-tuple-element.106), channel_id=1, source_target_pairs={{0,4},{4,8},{8,12},{1,5},{5,9},{9,13},{2,6},{6,10},{10,14},{3,7},{... | collective-permute-start | bytes 147464 | tf_op jit(solution)/shard_map/ppermute | solution.py:57
  142.0 6.3 %collective-permute-start.20 = (bf16[96,256]{1,0:T(8,128)(2,1)S(1)}, bf16[96,256]{1,0:T(8,128)(2,1)S(1)}, u32[]{:S(2)}, u32[]{:S(2)}) collective-permute-start(bf16[96,256]{1,0:T(8,128)(2,1)S(1)} %get-tuple-element.107), channel_id=1, source_target_pairs={{4,0},{8,4},{12,8},{5,1},{9,5},{13,9},{6,2},{10,6},{14,10},{7,3},{... | collective-permute-start | bytes 147464 | tf_op jit(solution)/shard_map/ppermute | solution.py:57
  143.3 5.0 %collective-permute-start.21 = (bf16[96,256]{1,0:T(8,128)(2,1)S(1)}, bf16[96,256]{1,0:T(8,128)(2,1)S(1)}, u32[]{:S(2)}, u32[]{:S(2)}) collective-permute-start(bf16[96,256]{1,0:T(8,128)(2,1)S(1)} %get-tuple-element.108), channel_id=1, source_target_pairs={{0,1},{1,2},{2,3},{4,5},{5,6},{6,7},{8,9},{9,10},{10,11},{12,13},{... | collective-permute-start | bytes 147464 | tf_op jit(solution)/shard_map/ppermute | solution.py:57
  144.6 4.5 %collective-permute-start.22 = (bf16[96,256]{1,0:T(8,128)(2,1)S(1)}, bf16[96,256]{1,0:T(8,128)(2,1)S(1)}, u32[]{:S(2)}, u32[]{:S(2)}) collective-permute-start(bf16[96,256]{1,0:T(8,128)(2,1)S(1)} %get-tuple-element.109), channel_id=1, source_target_pairs={{1,0},{2,1},{3,2},{5,4},{6,5},{7,6},{9,8},{10,9},{11,10},{13,12},{... | collective-permute-start | bytes 147464 | tf_op jit(solution)/shard_map/ppermute | solution.py:57
  149.1 6.1 %collective-permute-start.27 = (bf16[1728,128]{1,0:T(8,128)(2,1)S(1)}, bf16[1728,128]{1,0:T(8,128)(2,1)S(1)}, u32[]{:S(2)}, u32[]{:S(2)}) collective-permute-start(bf16[1728,128]{1,0:T(8,128)(2,1)S(1)} %collective-permute-done.23.refs_1_), channel_id=1, source_target_pairs={{0,1},{1,0},{2,3},{3,2},{4,5},{5,4},{6,7},{7,6},{8,9},{9,8},{10,11... | collective-permute-start | bytes 1327112 | tf_op jit(solution)/shard_map/ppermute | solution.py:373
  151.8 3.3 %collective-permute-start.28 = (bf16[1728,128]{1,0:T(8,128)(2,1)S(1)}, bf16[1728,128]{1,0:T(8,128)(2,1)S(1)}, u32[]{:S(2)}, u32[]{:S(2)}) collective-permute-start(bf16[1728,128]{1,0:T(8,128)(2,1)S(1)} %collective-permute-done.24.refs_2_), channel_id=1, source_target_pairs={{0,1},{1,0},{2,3},{3,2},{4,5},{5,4},{6,7},{7,6},{8,9},{9,8},{10,11... | collective-permute-start | bytes 1327112 | tf_op jit(solution)/shard_map/ppermute | solution.py:373

commit v4 on v3

--- a/solution.py
+++ b/solution.py
@@ -59,11 +59,11 @@
 
 
 def send_kernel(ways, flags, rows_ref, own_ref, *outs):
-    face = rows_ref.shape[1]
+    face = rows_ref.shape[2]
     own = own_ref.shape[0]
     places = lax.broadcasted_iota(jnp.int32, (own, face), 0)
     for out, (kind, i) in zip(outs, ways):
-        lower, upper = rows_ref[2 * i : 2 * i + 1, :], rows_ref[2 * i + 1 : 2 * i + 2, :]
+        lower, upper = rows_ref[2 * i], rows_ref[2 * i + 1]
         if kind == "pair":
             rows = jnp.where(flags[1 + i] > 0, lower, upper)
         else:
@@ -72,7 +72,7 @@
 
 
 def send(ways, flags, rows, own_features):
-    shape = jax.ShapeDtypeStruct((rows.shape[1], own_features.shape[1]), BF)
+    shape = jax.ShapeDtypeStruct((rows.shape[2], own_features.shape[1]), BF)
     return pl.pallas_call(
         lambda *refs: send_kernel(ways, *refs),
         in_specs=[SMEM, VMEM, VMEM],
@@ -90,14 +90,14 @@
     ]
     for copy in copies:
         copy.start()
-    taps, own = in_hbm.shape
+    taps, _, own = in_hbm.shape
     lows = lax.broadcasted_iota(jnp.int32, (block, own), 0)
     ranks = lax.broadcasted_iota(jnp.int32, (8, own), 0)
     for copy in copies:
         copy.wait()
     for k in range(taps):
-        target = tables[1, pl.ds(k, 1), :]
-        source = jnp.where(tables[2, pl.ds(k, 1), :] > 0, tables[0, pl.ds(k, 1), :], MISSING)
+        target = tables[1, k]
+        source = jnp.where(tables[2, k] > 0, tables[0, k], MISSING)
         high = target // block
         hot = one_hot(lows == target - high * block)
         big = (source // 16) * 16
@@ -111,7 +111,7 @@
 
 
 def invert(in_rows, out_rows, live, block):
-    taps, own = in_rows.shape
+    taps, _, own = in_rows.shape
     return pl.pallas_call(
         lambda *refs: invert_kernel(block, *refs),
         in_specs=[HBM, HBM, HBM],
@@ -121,7 +121,7 @@
             pltpu.HBM((taps, 8, block), F32),
         ),
         scratch_shapes=[
-            pltpu.VMEM((3, taps, own), jnp.int32),
+            pltpu.VMEM((3, taps, 1, own), jnp.int32),
             pltpu.VMEM((taps, 8, block), F32),
             pltpu.SemaphoreType.DMA((4,)),
         ],
@@ -330,7 +330,7 @@
             pltpu.VMEM((rows, ch), F32),
             pltpu.SemaphoreType.DMA((3 + count,)),
         ],
-        compiler_params=params(12),
+        compiler_params=params(16),
         name="backward",
     )(*args)
 
@@ -340,12 +340,12 @@
     out_ref, grad, sem = rest[len(ways) :]
     copy = pltpu.make_async_copy(grad_hbm, grad, sem)
     copy.start()
-    face = rows_ref.shape[1]
+    face = rows_ref.shape[2]
     own = out_ref.shape[0]
     places = lax.broadcasted_iota(jnp.int32, (own, face), 0)
     total = None
     for came, (kind, i) in zip(faces, ways):
-        lower, upper = rows_ref[2 * i : 2 * i + 1, :], rows_ref[2 * i + 1 : 2 * i + 2, :]
+        lower, upper = rows_ref[2 * i], rows_ref[2 * i + 1]
         if kind == "pair":
             rows = jnp.where(flags[1 + i] > 0, lower, upper)
         else:
@@ -409,7 +409,7 @@
     )(spots, *args)
 
 
-def reduce_all(keep, give, scaling, beside):
+def reduce_all(keep, give, scaling, beside, after):
     bits = lambda axis, low: [(axis, b) for b in range(low, lax.axis_size(axis).bit_length() - 1)]
     plane = [bits("gx", 0) + bits("gz", 1), bits("gz", 1) + bits("gx", 0)]
     turns = len(plane[0])
@@ -450,8 +450,8 @@
         pieces = [jnp.concatenate([pieces[i], came[i]], axis=0) for i in range(2)]
     odd = side("gz", 0)
     cross = lambda arrays: [swap(y, "gz", 0) for y in arrays]
-    came = [swap(pieces[i], *plane[i][0]) for i in range(2)]
-    twins = cross(pieces)
+    came = beside(pieces, [swap(pieces[i], *plane[i][0]) for i in range(2)])
+    twins = cross(after(pieces))
     sides = [[side(*plane[i][t]) for t in range(turns)] for i in range(2)]
     if size % 8 == 0:
         lanes = jnp.stack([odd, odd, 1 - odd, 1 - odd]) * ch
@@ -468,12 +468,11 @@
             return jnp.concatenate(out + out + [lanes]).astype(jnp.int32)
 
         half = place(spots(0), pieces + twins, size, rows, None)
-        came = beside(pieces, came + [half])
-        half = came.pop()
-        last = beside(came, cross(came))
+        came = lax.optimization_barrier((half, *came))
+        half, came = came[0], list(came[1:])
+        last = cross(came)
         return place(spots(1), came + last, size, rows, half)
-    came = beside(pieces, came)
-    last = beside(came, cross(came))
+    last = cross(came)
 
     def ordered(i, first, second):
         x = jnp.concatenate([first, second], axis=0).reshape((2,) * turns + (n, size, ch))
@@ -491,21 +490,24 @@
 def shards(features, weight, upstream, send_rows, in_rows, out_rows, tap_pair_exists):
     own_features = features[0, 0, 0]
     own, ch = own_features.shape
-    sends = send_rows[0, 0, 0]
+    single = lambda x: x[0, 0, 0][:, None, :]
+    sends = single(send_rows)
     taps = weight.shape[0]
     block = 256
     ways = routes()
     last = [lax.axis_index(a) == lax.axis_size(a) - 1 for a in AXES]
     flags = jnp.stack([side("gz", 0)] + last).astype(jnp.int32)
     faces = exchange(send(ways, flags, sends, own_features), ways)
-    rows = own + 6 * sends.shape[1]
-    col, row = invert(in_rows[0, 0, 0], out_rows[0, 0, 0], tap_pair_exists[0, 0, 0], block)
+    rows = own + 6 * sends.shape[2]
+    col, row = invert(single(in_rows), single(out_rows), single(tap_pair_exists), block)
     activated, gp, keep, give = forward(ways, flags, col, own_features, faces, weight, upstream[0, 0, 0])
     devices = lax.axis_size("gx") * lax.axis_size("gy") * lax.axis_size("gz")
-    counts = [9, 6, 6, 3, 3]
+    counts = [12, 6, 9]
     steps = [(sum(counts[:j]), c) for j, c in enumerate(counts)]
     steps[-1] = (steps[-1][0], taps - steps[-1][0])
-    state = {"turn": 0, "grad": None}
+    state = {"turn": 0, "grad": None, "returned": {}}
+    early = [j for j, (_, i) in enumerate(ways) if i != 1][:2]
+    late = [j for j in range(len(ways)) if j not in early]
 
     def beside(out, came):
         turn = state["turn"]
@@ -518,18 +520,25 @@
             state["grad"] = held[0]
             state["back"] = held[1 : len(grad)]
             return list(held[len(grad) :])
-        if turn == len(steps):
-            held = lax.optimization_barrier((*state["back"], *out))
-            returned = exchange(held[: len(ways)], ways)
-            held = lax.optimization_barrier((*returned, *came))
-            state["returned"] = list(held[: len(ways)])
-            return list(held[len(ways) :])
-        if turn == len(steps) + 1:
+        if turn < len(steps) + 2:
+            picks = early if turn == len(steps) else late
+            held = lax.optimization_barrier((*[state["back"][j] for j in picks], *out))
+            got = exchange(held[: len(picks)], [ways[j] for j in picks])
+            held = lax.optimization_barrier((*got, *came))
+            for j, face in zip(picks, held):
+                state["returned"][j] = face
+            return list(held[len(picks) :])
+        if turn == len(steps) + 2:
             held = lax.optimization_barrier((state["grad"], *out))
-            state["done"] = finish(ways, flags, sends, held[0], state["returned"])
+            state["done"] = finish(ways, flags, sends, held[0], [state["returned"][j] for j in range(len(ways))])
         return came
 
-    grad_weight = reduce_all(keep, give, float(devices * own) ** -0.5, beside).reshape(weight.shape)
+    def after(out):
+        held = lax.optimization_barrier((state["done"], *out))
+        state["done"] = held[0]
+        return list(held[1:])
+
+    grad_weight = reduce_all(keep, give, float(devices * own) ** -0.5, beside, after).reshape(weight.shape)
     return activated[None, None, None], state["done"][None, None, None], grad_weight
 
 

time: 159 us -> 143 us (0.90)
  Pallas kernels: 77.7 us -> 73 us
  starting transfers between devices: 45.4 us -> 41.8 us
  waiting for transfers between devices: 20.1 us -> 16.8 us
  local copies, waits for them, and re-layouts: 5.53 us -> 2.38 us
    ppermute x10, waiting for transfers between devices: 13.3 us -> 5.55 us  [exchange(): got.append(lax.ppermute(array, AXES[i], pairs))]
    pallas_call x5 -> x3, Pallas kernels: 33.3 us -> 28.7 us  [backward(): pl.pallas_call(lambda *refs: backward_kernel(ways, first, count, final, i...]
    ppermute x13, waiting for transfers between devices: 4.91 us -> 9.31 us  [swap(): return lax.ppermute(x, axis, [(j, j ^ 1 << bit) for j in range(n)])]
    unnamed x9 -> x10, local copies, waits for them, and re-layouts: 4.98 us -> 1.84 us
    ppermute x13, starting transfers between devices: 16.1 us -> 13.5 us  [swap(): return lax.ppermute(x, axis, [(j, j ^ 1 << bit) for j in range(n)])]
    add x0 -> x2, other arithmetic: none -> 2.49 us  [total(): out = value if out is None else out + value]
    another operation x2 -> x0, other arithmetic: 2.48 us -> none
  transfers between devices with their start and end apart: 29 -> 29, of which waited for: 9 -> 10; matrix products, arithmetic and copies ran while one was open for 3% -> 1% of each run, Pallas kernels for 29% -> 29%
where the time goes in v4:
time: 143 us
  Pallas kernels  73 us (51%)
  starting transfers between devices  41.8 us (29%)
  waiting for transfers between devices  16.8 us (12%)
  other arithmetic  7.46 us (5%)
  local copies, waits for them, and re-layouts  2.38 us (2%)
    pallas_call x1, Pallas kernels, forward(): pl.pallas_call(lambda *refs: forward_kernel(ways, block, *refs), in_specs...  29 us
    pallas_call x3, Pallas kernels, backward(): pl.pallas_call(lambda *refs: backward_kernel(ways, first, count, final, i...  28.7 us
    ppermute x10, starting transfers between devices, exchange(): got.append(lax.ppermute(array, AXES[i], pairs))  17.5 us
    ppermute x13, starting transfers between devices, swap(): return lax.ppermute(x, axis, [(j, j ^ 1 << bit) for j in range(n)])  13.5 us
    ppermute x6, starting transfers between devices, reduce_all(): lax.ppermute(y, 'gy', [(j, (j + s) % n) for j in range(n)])  10.8 us
    ppermute x13, waiting for transfers between devices, swap(): return lax.ppermute(x, axis, [(j, j ^ 1 << bit) for j in range(n)])  9.31 us
    pallas_call x1, Pallas kernels, invert(): pl.pallas_call(lambda *refs: invert_kernel(block, *refs), in_specs=[HBM,...  7.33 us
    ppermute x10, waiting for transfers between devices, exchange(): got.append(lax.ppermute(array, AXES[i], pairs))  5.55 us
  transfers between devices with their start and end apart: 29, of which 10 were waited for; matrix products, arithmetic and copies ran while one was open for 1% of the time, Pallas kernels for 29%

profile of v4, /device:TPU:0, one launch (start us, length us, event | category | flops | bytes accessed | tf_op | source)
XLA Modules:
  0.0 142.6 jit_solution(18179803192012113494)
XLA Ops:
  0.6 0.1 fusion.4
  0.7 1.0 copy-done
  1.7 0.7 copy-done.1
  2.4 1.0 send.1
  3.4 3.0 %collective-permute-start = (bf16[96,256]{1,0:T(8,128)(2,1)S(1)}, bf16[96,256]{1,0:T(8,128)(2,1)S(1)}, u32[]{:S(2)}, u32[]{:S(2)}) collective-permute-start(bf16[96,256]{1,0:T(8,128)(2,1)S(1)} %get-tuple-element.61), channel_id=1, source_target_pairs={{0,16},{16,0},{1,17},{17,1},{2,18},{18,2},{3,19},{19,3},{4,20},{20... | collective-permute-start | bytes 147464 | tf_op jit(solution)/shard_map/ppermute | solution.py:57
  6.4 3.5 %collective-permute-start.1 = (bf16[96,256]{1,0:T(8,128)(2,1)S(1)}, bf16[96,256]{1,0:T(8,128)(2,1)S(1)}, u32[]{:S(2)}, u32[]{:S(2)}) collective-permute-start(bf16[96,256]{1,0:T(8,128)(2,1)S(1)} %get-tuple-element.62), channel_id=1, source_target_pairs={{0,4},{4,8},{8,12},{1,5},{5,9},{9,13},{2,6},{6,10},{10,14},{3,7},{... | collective-permute-start | bytes 147464 | tf_op jit(solution)/shard_map/ppermute | solution.py:57
  9.9 1.3 collective-permute-start.2
  11.2 1.3 collective-permute-start.3
  12.5 1.3 collective-permute-start.4
  13.8 7.3 %invert.1 = (f32[27,256,8]{2,1,0:T(8,128)S(1)}, f32[27,8,256]{2,1,0:T(8,128)}) custom-call(s32[27,1,768]{2,1,0:T(1,128)} %bitcast.27, s32[27,1,768]{2,1,0:T(1,128)} %bitcast.28, s32[27,1,768]{2,1,0:T(1,128)} %bitcast.29), custom_call_target="tpu_custom_call" | custom-call | tf_op jit(solution)/shard_map/invert/pallas_call | solution.py:115
  21.2 29.0 %forward.1 = (bf16[768,256]{1,0:T(8,128)(2,1)}, bf16[768,256]{1,0:T(8,128)(2,1)}, f32[6912,128]{1,0:T(8,128)S(1)}, bf16[6912,128]{1,0:T(8,128)(2,1)}) custom-call(s32[4]{0:T(128)S(1)} %get-tuple-element.150.refs_0_, f32[27,256,8]{2,1,0:T(8,128)S(1)} %get-tuple-element.60.refs_1_, bf16[768,256]{1,0:T(8,128)(2,1)} %bitcast.19, bf16[6912,256]{1,0:T(8,128)(2,1)} %bitcast.23, ...), custom_call_target="tpu_custom_call" | custom-call | tf_op jit(solution)/shard_map/forward/pallas_call | solution.py:217
  50.2 2.9 %collective-permute-start.5 = (bf16[6912,128]{1,0:T(8,128)(2,1)}, bf16[6912,128]{1,0:T(8,128)(2,1)}, u32[]{:S(2)}, u32[]{:S(2)}) collective-permute-start(bf16[6912,128]{1,0:T(8,128)(2,1)} %get-tuple-element.70), channel_id=1, source_target_pairs={{0,1},{1,0},{2,3},{3,2},{4,5},{5,4},{6,7},{7,6},{8,9},{9,8},{10,11... | collective-permute-start | bytes 5308424 | tf_op jit(solution)/shard_map/ppermute | solution.py:373
  53.1 3.7 %collective-permute-done.5 = bf16[6912,128]{1,0:T(8,128)(2,1)} collective-permute-done((bf16[6912,128]{1,0:T(8,128)(2,1)}, bf16[6912,128]{1,0:T(8,128)(2,1)}, u32[]{:S(2)}, u32[]{:S(2)}) %collective-permute-start.5) | collective-permute-done | bytes 1769504 | tf_op jit(solution)/shard_map/ppermute | solution.py:373
  56.8 2.2 %add_convert_fusion = (bf16[1728,128]{1,0:T(8,128)(2,1)}, bf16[1728,128]{1,0:T(8,128)(2,1)}) fusion(f32[6912,128]{1,0:T(8,128)S(1)} %get-tuple-element.69, s32[]{:T(128)S(6)} %select_n.140, bf16[6912,128]{1,0:T(8,128)(2,1)} %collective-permute-done.5, s32[]{:T(128)S(6)} %select_n.139), kind=kLoop, calls=%fused_computation | loop fusion | flops 1327104 | bytes 3538952 | tf_op jit(solution)/shard_map/convert_element_type | solution.py:431
  59.0 0.6 collective-permute-start.6
  59.6 2.0 %collective-permute-start.7 = (bf16[1728,128]{1,0:T(8,128)(2,1)}, bf16[1728,128]{1,0:T(8,128)(2,1)}, u32[]{:S(2)}, u32[]{:S(2)}) collective-permute-start(bf16[1728,128]{1,0:T(8,128)(2,1)} %get-tuple-element.127), channel_id=1, source_target_pairs={{0,2},{1,3},{2,0},{3,1},{4,6},{5,7},{6,4},{7,5},{8,10},{9,11},{10,... | collective-permute-start | bytes 1327112 | tf_op jit(solution)/shard_map/ppermute | solution.py:373
  61.6 11.9 %backward.3.refs_3_ = f32[1344,256]{1,0:T(8,128)} custom-call(f32[27,8,256]{2,1,0:T(8,128)} %get-tuple-element.67.refs_0_.refs_1_, bf16[768,256]{1,0:T(8,128)(2,1)} %get-tuple-element.78.refs_1_.refs_2_, bf16[27,256,256]{2,1,0:T(8,128)(2,1)} %refs_3_.1), custom_call_target="tpu_custom_call" | custom-call | tf_op jit(solution)/shard_map/backward/pallas_call | solution.py:320
  73.5 2.2 %add_convert_fusion.2 = (bf16[864,128]{1,0:T(8,128)(2,1)}, bf16[864,128]{1,0:T(8,128)(2,1)}) fusion(f32[6912,128]{1,0:T(8,128)S(1)} %get-tuple-element.69, s32[]{:T(128)S(6)} %select_n.144, bf16[1728,128]{1,0:T(8,128)(2,1)} %collective-permute-done.7, s32[]{:T(128)S(6)} %select_n.145, bf16[6912,128]{1,0:T(8,128)(2,1)} %collective-permute-done.5, ...), kind=kLoop, calls=%fused_computation.2 | loop fusion | flops 1105920 | bytes 2211856 | tf_op jit(solution)/shard_map/convert_element_type | solution.py:431
  75.7 0.3 collective-permute-start.8
  76.0 1.5 %collective-permute-start.9 = (bf16[864,128]{1,0:T(8,128)(2,1)}, bf16[864,128]{1,0:T(8,128)(2,1)}, u32[]{:S(2)}, u32[]{:S(2)}) collective-permute-start(bf16[864,128]{1,0:T(8,128)(2,1)} %get-tuple-element.125), channel_id=1, source_target_pairs={{0,16},{16,0},{1,17},{17,1},{2,18},{18,2},{3,19},{19,3},{4,20},{20... | collective-permute-start | bytes 663560 | tf_op jit(solution)/shard_map/ppermute | solution.py:373
  77.5 7.0 %backward.4.refs_4_ = f32[1344,256]{1,0:T(8,128)} custom-call(f32[27,8,256]{2,1,0:T(8,128)} %get-tuple-element.67.refs_0_.refs_1_, bf16[768,256]{1,0:T(8,128)(2,1)} %get-tuple-element.78.refs_1_.refs_2_, bf16[27,256,256]{2,1,0:T(8,128)(2,1)} %refs_3_.1, f32[1344,256]{1,0:T(8,128)} %backward.3.refs_3_), custom_call_target="tpu_custom_call" | custom-call | tf_op jit(solution)/shard_map/backward/pallas_call | solution.py:320
  84.6 1.2 convert_add_fusion.1
  85.8 1.2 convert_add_fusion
  87.1 4.7 %collective-permute-start.12 = (bf16[432,128]{1,0:T(8,128)(2,1)S(1)}, bf16[432,128]{1,0:T(8,128)(2,1)S(1)}, u32[]{:S(2)}, u32[]{:S(2)}) collective-permute-start(bf16[432,128]{1,0:T(8,128)(2,1)S(1)} %pad_maximum_fusion.4), channel_id=1, source_target_pairs={{0,12},{4,0},{8,4},{12,8},{1,13},{5,1},{9,5},{13,9},{2,14},{6,2},{... | collective-permute-start | bytes 331784 | tf_op jit(solution)/shard_map/ppermute | solution.py:439
  91.8 0.1 collective-permute-start.11
  91.9 1.0 collective-permute-start.10
  93.0 9.7 %backward.5 = (f32[768,256]{1,0:T(8,128)}, bf16[96,256]{1,0:T(8,128)(2,1)S(1)}, bf16[96,256]{1,0:T(8,128)(2,1)S(1)}, bf16[96,256]{1,0:T(8,128)(2,1)S(1)}, bf16[9...) custom-call(s32[4]{0:T(128)S(1)} %get-tuple-element.150.refs_0_, f32[27,8,256]{2,1,0:T(8,128)} %get-tuple-element.67.refs_0_.refs_1_, ...), custom_call_target="tpu_custom_call" | custom-call | tf_op jit(solution)/shard_map/backward/pallas_call | solution.py:320
  102.7 0.1 fusion.3
  102.8 2.5 %collective-permute-start.15 = (bf16[432,128]{1,0:T(8,128)(2,1)S(1)}, bf16[432,128]{1,0:T(8,128)(2,1)S(1)}, u32[]{:S(2)}, u32[]{:S(2)}) collective-permute-start(bf16[432,128]{1,0:T(8,128)(2,1)S(1)} %fusion.3), channel_id=1, source_target_pairs={{0,4},{4,8},{8,12},{12,0},{1,5},{5,9},{9,13},{13,1},{2,6},{6,10},{... | collective-permute-start | bytes 331784 | tf_op jit(solution)/shard_map/ppermute | solution.py:439
  105.3 0.9 collective-permute-start.16
  106.2 1.5 %collective-permute-start.17 = (bf16[432,128]{1,0:T(8,128)(2,1)S(1)}, bf16[432,128]{1,0:T(8,128)(2,1)S(1)}, u32[]{:S(2)}, u32[]{:S(2)}) collective-permute-start(bf16[432,128]{1,0:T(8,128)(2,1)S(1)} %fusion.3), channel_id=1, source_target_pairs={{0,12},{4,0},{8,4},{12,8},{1,13},{5,1},{9,5},{13,9},{2,14},{6,2},{... | collective-permute-start | bytes 331784 | tf_op jit(solution)/shard_map/ppermute | solution.py:439
  107.8 0.5 collective-permute-start.13
  108.3 1.3 collective-permute-start.14
  109.6 2.2 %collective-permute-done.13.refs_3_ = bf16[96,256]{1,0:T(8,128)(2,1)S(1)} collective-permute-done((bf16[96,256]{1,0:T(8,128)(2,1)S(1)}, bf16[96,256]{1,0:T(8,128)(2,1)S(1)}, u32[]{:S(2)}, u32[]{:S(2)}) %collective-permute-start.13) | collective-permute-done | bytes 49184 | tf_op jit(solution)/shard_map/ppermute | solution.py:57
  111.8 1.9 %collective-permute-done.16 = bf16[432,128]{1,0:T(8,128)(2,1)S(1)} collective-permute-done((bf16[432,128]{1,0:T(8,128)(2,1)S(1)}, bf16[432,128]{1,0:T(8,128)(2,1)S(1)}, u32[]{:S(2)}, u32[]{:S(2)}) %collective-permute-start.16) | collective-permute-done | bytes 110624 | tf_op jit(solution)/shard_map/ppermute | solution.py:439
  113.9 0.6 collective-permute-start.22
  114.5 2.7 %collective-permute-start.21 = (bf16[864,128]{1,0:T(8,128)(2,1)S(1)}, bf16[864,128]{1,0:T(8,128)(2,1)S(1)}, u32[]{:S(2)}, u32[]{:S(2)}) collective-permute-start(bf16[864,128]{1,0:T(8,128)(2,1)S(1)} %pad_maximum_fusion), channel_id=1, source_target_pairs={{0,2},{1,3},{2,0},{3,1},{4,6},{5,7},{6,4},{7,5},{8,10},{9,11},{10,... | collective-permute-start | bytes 663560 | tf_op jit(solution)/shard_map/ppermute | solution.py:373
  117.3 2.7 %collective-permute-start.18 = (bf16[96,256]{1,0:T(8,128)(2,1)S(1)}, bf16[96,256]{1,0:T(8,128)(2,1)S(1)}, u32[]{:S(2)}, u32[]{:S(2)}) collective-permute-start(bf16[96,256]{1,0:T(8,128)(2,1)S(1)} %get-tuple-element.100), channel_id=1, source_target_pairs={{0,4},{4,8},{8,12},{1,5},{5,9},{9,13},{2,6},{6,10},{10,14},{3,7},{... | collective-permute-start | bytes 147464 | tf_op jit(solution)/shard_map/ppermute | solution.py:57
  120.0 1.3 collective-permute-start.19
  121.3 1.3 collective-permute-start.20
  122.6 0.1 broadcast_add_fusion.4
  122.7 3.3 %collective-permute-done.19.refs_5_ = bf16[96,256]{1,0:T(8,128)(2,1)S(1)} collective-permute-done((bf16[96,256]{1,0:T(8,128)(2,1)S(1)}, bf16[96,256]{1,0:T(8,128)(2,1)S(1)}, u32[]{:S(2)}, u32[]{:S(2)}) %collective-permute-start.19) | collective-permute-done | bytes 49184 | tf_op jit(solution)/shard_map/ppermute | solution.py:57
  126.0 0.4 collective-permute-start.26
  126.4 1.6 %collective-permute-start.25 = (bf16[1728,128]{1,0:T(8,128)(2,1)S(1)}, bf16[1728,128]{1,0:T(8,128)(2,1)S(1)}, u32[]{:S(2)}, u32[]{:S(2)}) collective-permute-start(bf16[1728,128]{1,0:T(8,128)(2,1)S(1)} %constant_dynamic-update-slice_fusion.refs_1_), channel_id=1, source_target_pairs={{0,16},{16,0},{1,17},{17,1},{2,18},{18,2},{3,19},{19,3},{4,20},{20... | collective-permute-start | bytes 1327112 | tf_op jit(solution)/shard_map/ppermute | solution.py:373
  128.0 2.9 %finish.1 = bf16[768,256]{1,0:T(8,128)(2,1)} custom-call(s32[4]{0:T(128)S(1)} %get-tuple-element.150.refs_0_, s32[6,1,96]{2,1,0:T(1,128)S(1)} %bitcast.22, f32[768,256]{1,0:T(8,128)} %get-tuple-element.105.refs_2_, bf16[96,256]{1,0:T(8,128)(2,1)S(1)} %collective-permute-done.13.refs_3_, bf16[96,256]{1,0:T(8,128)(2,1)S(1)} %collective-permute-done.18.refs_4_, ...), custom_call_target="tpu_custom_call" | custom-call | tf_op jit(solution)/shard_map/finish/pallas_call | solution.py:360
  131.0 0.5 collective-permute-start.24
  131.5 0.1 broadcast_add_fusion.6
  131.6 0.1 broadcast_add_fusion
  131.7 0.1 add.547
  131.7 0.1 add.552
  131.8 0.1 add_multiply_fusion.2
  131.9 0.1 concatenate.62.refs_0_
  132.0 0.8 collective-permute-done.23.refs_3_
  132.8 0.6 collective-permute-done.24.refs_4_
  133.4 2.0 %place.2.refs_5_ = bf16[6912,256]{1,0:T(8,128)(2,1)} custom-call(s32[36]{0:T(128)S(1)} %concatenate.62.refs_0_, bf16[1728,128]{1,0:T(8,128)(2,1)S(1)} %constant_dynamic-update-slice_fusion.refs_1_, bf16[1728,128]{1,0:T(8,128)(2,1)S(1)} %constant_dynamic-update-slice_fusion.5.refs_2_, bf16[1728,128]{1,0:T(8,128)(2,1)S(1)} %collective-permute-done.23.refs_3_, ...), custom_call_target="tpu_custom_call" | custom-call | tf_op jit(solution)/shard_map/place/pallas_call | solution.py:400
  135.4 2.4 %collective-permute-done.26.refs_2_ = bf16[1728,128]{1,0:T(8,128)(2,1)S(1)} collective-permute-done((bf16[1728,128]{1,0:T(8,128)(2,1)S(1)}, bf16[1728,128]{1,0:T(8,128)(2,1)S(1)}, u32[]{:S(2)}, u32[]{:S(2)}) %collective-permute-start.26) | collective-permute-done | bytes 442400 | tf_op jit(solution)/shard_map/ppermute | solution.py:373
  137.8 0.1 collective-permute-done.25.refs_1_
  138.0 0.5 collective-permute-start.28
  138.5 0.1 add.536
  138.6 0.1 add.542
  138.6 0.1 concatenate.61.refs_0_
  138.7 1.0 collective-permute-done.27.refs_3_
  139.8 0.6 collective-permute-done.28.refs_4_
  140.4 2.0 %place.3 = bf16[6912,256]{1,0:T(8,128)(2,1)} custom-call(s32[36]{0:T(128)S(1)} %concatenate.61.refs_0_, bf16[1728,128]{1,0:T(8,128)(2,1)S(1)} %collective-permute-done.25.refs_1_, bf16[1728,128]{1,0:T(8,128)(2,1)S(1)} %collective-permute-done.26.refs_2_, bf16[1728,128]{1,0:T(8,128)(2,1)S(1)} %collective-permute-done.27.refs_3_, ...), custom_call_target="tpu_custom_call", output_to_operand_aliasing={{}: (5, {})} | custom-call | tf_op jit(solution)/shard_map/place/pallas_call | solution.py:400
  (36 shorter events, 0.4 us)
Async XLA Ops:
  0.7 1.0 copy-start
  1.7 0.7 copy-start.1
  3.4 17.7 %collective-permute-start = (bf16[96,256]{1,0:T(8,128)(2,1)S(1)}, bf16[96,256]{1,0:T(8,128)(2,1)S(1)}, u32[]{:S(2)}, u32[]{:S(2)}) collective-permute-start(bf16[96,256]{1,0:T(8,128)(2,1)S(1)} %get-tuple-element.61), channel_id=1, source_target_pairs={{0,16},{16,0},{1,17},{17,1},{2,18},{18,2},{3,19},{19,3},{4,20},{20... | collective-permute-start | bytes 147464 | tf_op jit(solution)/shard_map/ppermute | solution.py:57
  6.4 14.7 %collective-permute-start.1 = (bf16[96,256]{1,0:T(8,128)(2,1)S(1)}, bf16[96,256]{1,0:T(8,128)(2,1)S(1)}, u32[]{:S(2)}, u32[]{:S(2)}) collective-permute-start(bf16[96,256]{1,0:T(8,128)(2,1)S(1)} %get-tuple-element.62), channel_id=1, source_target_pairs={{0,4},{4,8},{8,12},{1,5},{5,9},{9,13},{2,6},{6,10},{10,14},{3,7},{... | collective-permute-start | bytes 147464 | tf_op jit(solution)/shard_map/ppermute | solution.py:57
  9.9 11.3 %collective-permute-start.2 = (bf16[96,256]{1,0:T(8,128)(2,1)S(1)}, bf16[96,256]{1,0:T(8,128)(2,1)S(1)}, u32[]{:S(2)}, u32[]{:S(2)}) collective-permute-start(bf16[96,256]{1,0:T(8,128)(2,1)S(1)} %get-tuple-element.63), channel_id=1, source_target_pairs={{4,0},{8,4},{12,8},{5,1},{9,5},{13,9},{6,2},{10,6},{14,10},{7,3},{... | collective-permute-start | bytes 147464 | tf_op jit(solution)/shard_map/ppermute | solution.py:57
  11.2 10.0 %collective-permute-start.3 = (bf16[96,256]{1,0:T(8,128)(2,1)S(1)}, bf16[96,256]{1,0:T(8,128)(2,1)S(1)}, u32[]{:S(2)}, u32[]{:S(2)}) collective-permute-start(bf16[96,256]{1,0:T(8,128)(2,1)S(1)} %get-tuple-element.64), channel_id=1, source_target_pairs={{0,1},{1,2},{2,3},{4,5},{5,6},{6,7},{8,9},{9,10},{10,11},{12,13},{... | collective-permute-start | bytes 147464 | tf_op jit(solution)/shard_map/ppermute | solution.py:57
  12.5 8.7 %collective-permute-start.4 = (bf16[96,256]{1,0:T(8,128)(2,1)S(1)}, bf16[96,256]{1,0:T(8,128)(2,1)S(1)}, u32[]{:S(2)}, u32[]{:S(2)}) collective-permute-start(bf16[96,256]{1,0:T(8,128)(2,1)S(1)} %get-tuple-element.65), channel_id=1, source_target_pairs={{1,0},{2,1},{3,2},{5,4},{6,5},{7,6},{9,8},{10,9},{11,10},{13,12},{... | collective-permute-start | bytes 147464 | tf_op jit(solution)/shard_map/ppermute | solution.py:57
  50.2 6.6 %collective-permute-start.5 = (bf16[6912,128]{1,0:T(8,128)(2,1)}, bf16[6912,128]{1,0:T(8,128)(2,1)}, u32[]{:S(2)}, u32[]{:S(2)}) collective-permute-start(bf16[6912,128]{1,0:T(8,128)(2,1)} %get-tuple-element.70), channel_id=1, source_target_pairs={{0,1},{1,0},{2,3},{3,2},{4,5},{5,4},{6,7},{7,6},{8,9},{9,8},{10,11... | collective-permute-start | bytes 5308424 | tf_op jit(solution)/shard_map/ppermute | solution.py:373
  59.0 14.5 %collective-permute-start.6 = (bf16[1728,128]{1,0:T(8,128)(2,1)}, bf16[1728,128]{1,0:T(8,128)(2,1)}, u32[]{:S(2)}, u32[]{:S(2)}) collective-permute-start(bf16[1728,128]{1,0:T(8,128)(2,1)} %get-tuple-element.128), channel_id=1, source_target_pairs={{0,16},{16,0},{1,17},{17,1},{2,18},{18,2},{3,19},{19,3},{4,20},{20... | collective-permute-start | bytes 1327112 | tf_op jit(solution)/shard_map/ppermute | solution.py:373
  59.6 13.9 %collective-permute-start.7 = (bf16[1728,128]{1,0:T(8,128)(2,1)}, bf16[1728,128]{1,0:T(8,128)(2,1)}, u32[]{:S(2)}, u32[]{:S(2)}) collective-permute-start(bf16[1728,128]{1,0:T(8,128)(2,1)} %get-tuple-element.127), channel_id=1, source_target_pairs={{0,2},{1,3},{2,0},{3,1},{4,6},{5,7},{6,4},{7,5},{8,10},{9,11},{10,... | collective-permute-start | bytes 1327112 | tf_op jit(solution)/shard_map/ppermute | solution.py:373
  75.7 8.8 %collective-permute-start.8 = (bf16[864,128]{1,0:T(8,128)(2,1)}, bf16[864,128]{1,0:T(8,128)(2,1)}, u32[]{:S(2)}, u32[]{:S(2)}) collective-permute-start(bf16[864,128]{1,0:T(8,128)(2,1)} %get-tuple-element.126), channel_id=1, source_target_pairs={{0,2},{1,3},{2,0},{3,1},{4,6},{5,7},{6,4},{7,5},{8,10},{9,11},{10,... | collective-permute-start | bytes 663560 | tf_op jit(solution)/shard_map/ppermute | solution.py:373
  76.0 8.5 %collective-permute-start.9 = (bf16[864,128]{1,0:T(8,128)(2,1)}, bf16[864,128]{1,0:T(8,128)(2,1)}, u32[]{:S(2)}, u32[]{:S(2)}) collective-permute-start(bf16[864,128]{1,0:T(8,128)(2,1)} %get-tuple-element.125), channel_id=1, source_target_pairs={{0,16},{16,0},{1,17},{17,1},{2,18},{18,2},{3,19},{19,3},{4,20},{20... | collective-permute-start | bytes 663560 | tf_op jit(solution)/shard_map/ppermute | solution.py:373
  87.1 15.6 %collective-permute-start.12 = (bf16[432,128]{1,0:T(8,128)(2,1)S(1)}, bf16[432,128]{1,0:T(8,128)(2,1)S(1)}, u32[]{:S(2)}, u32[]{:S(2)}) collective-permute-start(bf16[432,128]{1,0:T(8,128)(2,1)S(1)} %pad_maximum_fusion.4), channel_id=1, source_target_pairs={{0,12},{4,0},{8,4},{12,8},{1,13},{5,1},{9,5},{13,9},{2,14},{6,2},{... | collective-permute-start | bytes 331784 | tf_op jit(solution)/shard_map/ppermute | solution.py:439
  91.8 10.9 %collective-permute-start.11 = (bf16[432,128]{1,0:T(8,128)(2,1)S(1)}, bf16[432,128]{1,0:T(8,128)(2,1)S(1)}, u32[]{:S(2)}, u32[]{:S(2)}) collective-permute-start(bf16[432,128]{1,0:T(8,128)(2,1)S(1)} %pad_maximum_fusion.3), channel_id=1, source_target_pairs={{0,8},{4,12},{8,0},{12,4},{1,9},{5,13},{9,1},{13,5},{2,10},{6,14},... | collective-permute-start | bytes 331784 | tf_op jit(solution)/shard_map/ppermute | solution.py:439
  91.9 36.1 %copy-start.2 = (s32[1,1,1,6,96]{4,2,3,1,0:T(1,128)S(1)}, s32[1,1,1,6,96]{4,2,3,1,0:T(1,128)}, u32[]{:S(2)}) copy-start(s32[1,1,1,6,96]{4,2,3,1,0:T(1,128)} %param.10) | copy-start | bytes 6916
  91.9 10.8 %collective-permute-start.10 = (bf16[432,128]{1,0:T(8,128)(2,1)S(1)}, bf16[432,128]{1,0:T(8,128)(2,1)S(1)}, u32[]{:S(2)}, u32[]{:S(2)}) collective-permute-start(bf16[432,128]{1,0:T(8,128)(2,1)S(1)} %pad_maximum_fusion.2), channel_id=1, source_target_pairs={{0,4},{4,8},{8,12},{12,0},{1,5},{5,9},{9,13},{13,1},{2,6},{6,10},{... | collective-permute-start | bytes 331784 | tf_op jit(solution)/shard_map/ppermute | solution.py:439
  102.8 9.1 %collective-permute-start.15 = (bf16[432,128]{1,0:T(8,128)(2,1)S(1)}, bf16[432,128]{1,0:T(8,128)(2,1)S(1)}, u32[]{:S(2)}, u32[]{:S(2)}) collective-permute-start(bf16[432,128]{1,0:T(8,128)(2,1)S(1)} %fusion.3), channel_id=1, source_target_pairs={{0,4},{4,8},{8,12},{12,0},{1,5},{5,9},{9,13},{13,1},{2,6},{6,10},{... | collective-permute-start | bytes 331784 | tf_op jit(solution)/shard_map/ppermute | solution.py:439
  105.3 8.5 %collective-permute-start.16 = (bf16[432,128]{1,0:T(8,128)(2,1)S(1)}, bf16[432,128]{1,0:T(8,128)(2,1)S(1)}, u32[]{:S(2)}, u32[]{:S(2)}) collective-permute-start(bf16[432,128]{1,0:T(8,128)(2,1)S(1)} %fusion.3), channel_id=1, source_target_pairs={{0,8},{4,12},{8,0},{12,4},{1,9},{5,13},{9,1},{13,5},{2,10},{6,14},... | collective-permute-start | bytes 331784 | tf_op jit(solution)/shard_map/ppermute | solution.py:439
  106.2 7.5 %collective-permute-start.17 = (bf16[432,128]{1,0:T(8,128)(2,1)S(1)}, bf16[432,128]{1,0:T(8,128)(2,1)S(1)}, u32[]{:S(2)}, u32[]{:S(2)}) collective-permute-start(bf16[432,128]{1,0:T(8,128)(2,1)S(1)} %fusion.3), channel_id=1, source_target_pairs={{0,12},{4,0},{8,4},{12,8},{1,13},{5,1},{9,5},{13,9},{2,14},{6,2},{... | collective-permute-start | bytes 331784 | tf_op jit(solution)/shard_map/ppermute | solution.py:439
  107.8 4.1 %collective-permute-start.13 = (bf16[96,256]{1,0:T(8,128)(2,1)S(1)}, bf16[96,256]{1,0:T(8,128)(2,1)S(1)}, u32[]{:S(2)}, u32[]{:S(2)}) collective-permute-start(bf16[96,256]{1,0:T(8,128)(2,1)S(1)} %get-tuple-element.92), channel_id=1, source_target_pairs={{0,16},{16,0},{1,17},{17,1},{2,18},{18,2},{3,19},{19,3},{4,20},{20... | collective-permute-start | bytes 147464 | tf_op jit(solution)/shard_map/ppermute | solution.py:57
  108.3 3.6 %collective-permute-start.14 = (bf16[96,256]{1,0:T(8,128)(2,1)S(1)}, bf16[96,256]{1,0:T(8,128)(2,1)S(1)}, u32[]{:S(2)}, u32[]{:S(2)}) collective-permute-start(bf16[96,256]{1,0:T(8,128)(2,1)S(1)} %get-tuple-element.93), channel_id=1, source_target_pairs={{0,1},{1,2},{2,3},{4,5},{5,6},{6,7},{8,9},{9,10},{10,11},{12,13},{... | collective-permute-start | bytes 147464 | tf_op jit(solution)/shard_map/ppermute | solution.py:57
  113.9 12.0 %collective-permute-start.22 = (bf16[864,128]{1,0:T(8,128)(2,1)S(1)}, bf16[864,128]{1,0:T(8,128)(2,1)S(1)}, u32[]{:S(2)}, u32[]{:S(2)}) collective-permute-start(bf16[864,128]{1,0:T(8,128)(2,1)S(1)} %pad_maximum_fusion.1), channel_id=1, source_target_pairs={{0,16},{16,0},{1,17},{17,1},{2,18},{18,2},{3,19},{19,3},{4,20},{20... | collective-permute-start | bytes 663560 | tf_op jit(solution)/shard_map/ppermute | solution.py:373
  114.5 11.4 %collective-permute-start.21 = (bf16[864,128]{1,0:T(8,128)(2,1)S(1)}, bf16[864,128]{1,0:T(8,128)(2,1)S(1)}, u32[]{:S(2)}, u32[]{:S(2)}) collective-permute-start(bf16[864,128]{1,0:T(8,128)(2,1)S(1)} %pad_maximum_fusion), channel_id=1, source_target_pairs={{0,2},{1,3},{2,0},{3,1},{4,6},{5,7},{6,4},{7,5},{8,10},{9,11},{10,... | collective-permute-start | bytes 663560 | tf_op jit(solution)/shard_map/ppermute | solution.py:373
  117.3 5.4 %collective-permute-start.18 = (bf16[96,256]{1,0:T(8,128)(2,1)S(1)}, bf16[96,256]{1,0:T(8,128)(2,1)S(1)}, u32[]{:S(2)}, u32[]{:S(2)}) collective-permute-start(bf16[96,256]{1,0:T(8,128)(2,1)S(1)} %get-tuple-element.100), channel_id=1, source_target_pairs={{0,4},{4,8},{8,12},{1,5},{5,9},{9,13},{2,6},{6,10},{10,14},{3,7},{... | collective-permute-start | bytes 147464 | tf_op jit(solution)/shard_map/ppermute | solution.py:57
  120.0 6.0 %collective-permute-start.19 = (bf16[96,256]{1,0:T(8,128)(2,1)S(1)}, bf16[96,256]{1,0:T(8,128)(2,1)S(1)}, u32[]{:S(2)}, u32[]{:S(2)}) collective-permute-start(bf16[96,256]{1,0:T(8,128)(2,1)S(1)} %get-tuple-element.101), channel_id=1, source_target_pairs={{4,0},{8,4},{12,8},{5,1},{9,5},{13,9},{6,2},{10,6},{14,10},{7,3},{... | collective-permute-start | bytes 147464 | tf_op jit(solution)/shard_map/ppermute | solution.py:57
  121.3 4.7 %collective-permute-start.20 = (bf16[96,256]{1,0:T(8,128)(2,1)S(1)}, bf16[96,256]{1,0:T(8,128)(2,1)S(1)}, u32[]{:S(2)}, u32[]{:S(2)}) collective-permute-start(bf16[96,256]{1,0:T(8,128)(2,1)S(1)} %get-tuple-element.102), channel_id=1, source_target_pairs={{1,0},{2,1},{3,2},{5,4},{6,5},{7,6},{9,8},{10,9},{11,10},{13,12},{... | collective-permute-start | bytes 147464 | tf_op jit(solution)/shard_map/ppermute | solution.py:57
  126.0 11.8 %collective-permute-start.26 = (bf16[1728,128]{1,0:T(8,128)(2,1)S(1)}, bf16[1728,128]{1,0:T(8,128)(2,1)S(1)}, u32[]{:S(2)}, u32[]{:S(2)}) collective-permute-start(bf16[1728,128]{1,0:T(8,128)(2,1)S(1)} %constant_dynamic-update-slice_fusion.5.refs_2_), channel_id=1, source_target_pairs={{0,2},{1,3},{2,0},{3,1},{4,6},{5,7},{6,4},{7,5},{8,10},{9,11},{10,... | collective-permute-start | bytes 1327112 | tf_op jit(solution)/shard_map/ppermute | solution.py:373
  126.4 11.5 %collective-permute-start.25 = (bf16[1728,128]{1,0:T(8,128)(2,1)S(1)}, bf16[1728,128]{1,0:T(8,128)(2,1)S(1)}, u32[]{:S(2)}, u32[]{:S(2)}) collective-permute-start(bf16[1728,128]{1,0:T(8,128)(2,1)S(1)} %constant_dynamic-update-slice_fusion.refs_1_), channel_id=1, source_target_pairs={{0,16},{16,0},{1,17},{17,1},{2,18},{18,2},{3,19},{19,3},{4,20},{20... | collective-permute-start | bytes 1327112 | tf_op jit(solution)/shard_map/ppermute | solution.py:373
  130.9 1.9 %collective-permute-start.23 = (bf16[1728,128]{1,0:T(8,128)(2,1)S(1)}, bf16[1728,128]{1,0:T(8,128)(2,1)S(1)}, u32[]{:S(2)}, u32[]{:S(2)}) collective-permute-start(bf16[1728,128]{1,0:T(8,128)(2,1)S(1)} %constant_dynamic-update-slice_fusion.refs_1_), channel_id=1, source_target_pairs={{0,1},{1,0},{2,3},{3,2},{4,5},{5,4},{6,7},{7,6},{8,9},{9,8},{10,11... | collective-permute-start | bytes 1327112 | tf_op jit(solution)/shard_map/ppermute | solution.py:373
  131.0 2.4 %collective-permute-start.24 = (bf16[1728,128]{1,0:T(8,128)(2,1)S(1)}, bf16[1728,128]{1,0:T(8,128)(2,1)S(1)}, u32[]{:S(2)}, u32[]{:S(2)}) collective-permute-start(bf16[1728,128]{1,0:T(8,128)(2,1)S(1)} %constant_dynamic-update-slice_fusion.5.refs_2_), channel_id=1, source_target_pairs={{0,1},{1,0},{2,3},{3,2},{4,5},{5,4},{6,7},{7,6},{8,9},{9,8},{10,11... | collective-permute-start | bytes 1327112 | tf_op jit(solution)/shard_map/ppermute | solution.py:373
  138.0 1.8 %collective-permute-start.27 = (bf16[1728,128]{1,0:T(8,128)(2,1)S(1)}, bf16[1728,128]{1,0:T(8,128)(2,1)S(1)}, u32[]{:S(2)}, u32[]{:S(2)}) collective-permute-start(bf16[1728,128]{1,0:T(8,128)(2,1)S(1)} %collective-permute-done.25.refs_1_), channel_id=1, source_target_pairs={{0,1},{1,0},{2,3},{3,2},{4,5},{5,4},{6,7},{7,6},{8,9},{9,8},{10,11... | collective-permute-start | bytes 1327112 | tf_op jit(solution)/shard_map/ppermute | solution.py:373
  138.0 2.4 %collective-permute-start.28 = (bf16[1728,128]{1,0:T(8,128)(2,1)S(1)}, bf16[1728,128]{1,0:T(8,128)(2,1)S(1)}, u32[]{:S(2)}, u32[]{:S(2)}) collective-permute-start(bf16[1728,128]{1,0:T(8,128)(2,1)S(1)} %collective-permute-done.26.refs_2_), channel_id=1, source_target_pairs={{0,1},{1,0},{2,3},{3,2},{4,5},{5,4},{6,7},{7,6},{8,9},{9,8},{10,11... | collective-permute-start | bytes 1327112 | tf_op jit(solution)/shard_map/ppermute | solution.py:373

commit v5 on v4

--- a/solution.py
+++ b/solution.py
@@ -92,7 +92,7 @@
         copy.start()
     taps, _, own = in_hbm.shape
     lows = lax.broadcasted_iota(jnp.int32, (block, own), 0)
-    ranks = lax.broadcasted_iota(jnp.int32, (8, own), 0)
+    ranks = lax.broadcasted_iota(jnp.int32, (16, own), 0)
     for copy in copies:
         copy.wait()
     for k in range(taps):
@@ -101,10 +101,11 @@
         high = target // block
         hot = one_hot(lows == target - high * block)
         big = (source // 16) * 16
-        spread = jnp.where(ranks == high, big, jnp.where(ranks - 4 == high, source - big, 0))
+        spread = jnp.where(ranks == high, big, jnp.where(ranks - 8 == high, source - big, 0))
         spread = spread.astype(F32).astype(BF)
-        col_ref[k] = dot(hot, spread, NT)
-        row_ref[k] = dot(spread, hot, NT)
+        col = dot(hot, spread, NT)
+        col_ref[k] = col
+        row_ref[k] = col.T
     copy = pltpu.make_async_copy(row_ref, row_hbm, sems.at[3])
     copy.start()
     copy.wait()
@@ -117,12 +118,12 @@
         in_specs=[HBM, HBM, HBM],
         out_specs=[VMEM, HBM],
         out_shape=(
-            jax.ShapeDtypeStruct((taps, block, 8), F32),
-            pltpu.HBM((taps, 8, block), F32),
+            jax.ShapeDtypeStruct((taps, block, 16), F32),
+            pltpu.HBM((taps, 16, block), F32),
         ),
         scratch_shapes=[
             pltpu.VMEM((3, taps, 1, own), jnp.int32),
-            pltpu.VMEM((taps, 8, block), F32),
+            pltpu.VMEM((taps, 16, block), F32),
             pltpu.SemaphoreType.DMA((4,)),
         ],
         compiler_params=params(12),
@@ -130,7 +131,7 @@
     )(hold(in_rows), hold(out_rows), hold(live))
 
 
-def forward_kernel(ways, block, flags, col_ref, own_hbm, w_hbm, up_hbm, *rest):
+def forward_kernel(ways, step, flags, col_ref, own_hbm, w_hbm, up_hbm, *rest):
     faces = rest[: len(ways)]
     act_hbm, gp_hbm, keep_hbm, give_hbm = rest[len(ways) : len(ways) + 4]
     ext, got, got_t, weights, turned, up, act, gp, keep, give, sems = rest[len(ways) + 4 :]
@@ -138,7 +139,8 @@
     own, ch = up.shape
     rows = ext.shape[0]
     half = ch // 2
-    parts = own // block
+    parts = own // step
+    block = col_ref.shape[1]
     w_copy = pltpu.make_async_copy(w_hbm, weights, sems.at[0])
     up_copy = pltpu.make_async_copy(up_hbm, up, sems.at[1])
     own_copy = pltpu.make_async_copy(own_hbm, ext.at[pl.ds(0, own), :], sems.at[2])
@@ -159,15 +161,19 @@
         else:
             ext[pl.ds(high, face), :] = came[...]
     own_copy.wait()
-    lanes = lax.broadcasted_iota(jnp.int32, (block, rows), 1)
+    lanes = lax.broadcasted_iota(jnp.int32, (step, rows), 1)
 
     def gather(k, carried):
         at = pl.multiple_of(k * ch, ch)
         for h in range(parts):
-            place = (col_ref[k, :, h : h + 1] + col_ref[k, :, h + 4 : h + 5]).astype(jnp.int32)
+            places = [
+                col_ref[k, :, b : b + 1] + col_ref[k, :, b + 8 : b + 9]
+                for b in range(h * step // block, (h + 1) * step // block)
+            ]
+            place = jnp.concatenate(places, axis=0).astype(jnp.int32)
             picked = dot(one_hot(lanes == place), ext[...]).astype(BF)
-            got[pl.ds(h * block, block), pl.ds(at, ch)] = picked
-            got_t[pl.ds(at, ch), pl.ds(h * block, block)] = picked.T
+            got[pl.ds(h * step, step), pl.ds(at, ch)] = picked
+            got_t[pl.ds(at, ch), pl.ds(h * step, step)] = picked.T
         return carried
 
     lax.fori_loop(0, taps, gather, 0, unroll=9)
@@ -175,7 +181,7 @@
     up_copy.wait()
     odd = flags[0] > 0
     for h in range(parts):
-        part = pl.ds(h * block, block)
+        part = pl.ds(h * step, step)
         v = dot(got[part, :], weights[...])
         s = jax.nn.sigmoid(v)
         act[part, :] = (v * s).astype(BF)
@@ -215,7 +221,7 @@
     rows = own + 6 * faces[0].shape[0]
     like = jax.ShapeDtypeStruct
     return pl.pallas_call(
-        lambda *refs: forward_kernel(ways, block, *refs),
+        lambda *refs: forward_kernel(ways, 256, *refs),
         in_specs=[SMEM, VMEM, HBM, HBM, HBM] + [VMEM] * len(faces),
         out_specs=[HBM, HBM, ANY, ANY],
         out_shape=[
@@ -242,18 +248,10 @@
     )(flags, col, hold(own_features), hold(weight.reshape(taps * ch, ch)), hold(upstream), *faces)
 
 
-def backward_kernel(ways, first, count, final, more, *refs):
-    refs = list(refs)
-    flags = refs.pop(0) if final else None
-    row_hbm, gp_hbm, w_hbm = refs[:3]
-    before_hbm = refs[3] if more else None
-    outs = refs[3 + more : -6]
-    row, gp, got, weights, total, sems = refs[-6:]
-    rows, ch = total.shape
+def backward_body(start, first, count, step, row_hbm, gp_hbm, w_hbm, before_hbm, row, gp, got, weights, total, sems):
+    size, ch = total.shape
     block = row.shape[2]
-    own = gp.shape[0]
-    parts = own // block
-    step = 336
+    parts = gp.shape[0] // block
     row_copy = pltpu.make_async_copy(row_hbm.at[pl.ds(first, count)], row, sems.at[0])
     gp_copy = pltpu.make_async_copy(gp_hbm, gp, sems.at[1])
     row_copy.start()
@@ -262,7 +260,7 @@
         pltpu.make_async_copy(w_hbm.at[first + j], weights.at[:, pl.ds(j * ch, ch)], sems.at[3 + j])
         for j in range(count)
     ]
-    if more:
+    if before_hbm is not None:
         later.append(pltpu.make_async_copy(before_hbm, total, sems.at[2]))
     for copy in later:
         copy.start()
@@ -271,11 +269,11 @@
 
     def gather(j, carried):
         at = pl.multiple_of(j * ch, ch)
-        for r in range(0, rows, step):
-            lines = lax.broadcasted_iota(jnp.int32, (step, block), 0) + r
+        for r in range(0, size, step):
+            lines = lax.broadcasted_iota(jnp.int32, (step, block), 0) + (start + r)
             hots = []
             for h in range(parts):
-                place = (row[j, h : h + 1, :] + row[j, h + 4 : h + 5, :]).astype(jnp.int32)
+                place = (row[j, h : h + 1, :] + row[j, h + 8 : h + 9, :]).astype(jnp.int32)
                 hots.append(one_hot(lines == place))
             got[pl.ds(r, step), pl.ds(at, ch)] = dot(jnp.concatenate(hots, axis=1), gp[...]).astype(BF)
         return carried
@@ -283,89 +281,97 @@
     lax.fori_loop(0, count, gather, 0, unroll=3)
     for copy in later:
         copy.wait()
-    for r in range(0, rows, step):
+    for r in range(0, size, step):
         value = dot(got[pl.ds(r, step), :], weights[...], NT)
-        total[pl.ds(r, step), :] = value + total[pl.ds(r, step), :] if more else value
-    if final:
-        copy = pltpu.make_async_copy(total.at[pl.ds(0, own), :], outs[0], sems.at[0])
-        copy.start()
-        face = outs[1].shape[0]
-        for out, (kind, i) in zip(outs[1:], ways):
-            lower = total[pl.ds(own + 2 * i * face, face), :]
-            upper = total[pl.ds(own + (2 * i + 1) * face, face), :]
-            if kind == "pair":
-                out[...] = jnp.where(flags[1 + i] > 0, lower, upper).astype(BF)
-            else:
-                out[...] = (upper if kind == "up" else lower).astype(BF)
-    else:
-        copy = pltpu.make_async_copy(total, outs[0], sems.at[0])
-        copy.start()
+        total[pl.ds(r, step), :] = value if before_hbm is None else value + total[pl.ds(r, step), :]
+
+
+def backward_scratch(row, gp, size, count):
+    own, ch = gp.shape
+    return [
+        pltpu.VMEM((count,) + row.shape[1:], F32),
+        pltpu.VMEM((own, ch), BF),
+        pltpu.VMEM((size, count * ch), BF),
+        pltpu.VMEM((ch, count * ch), BF),
+        pltpu.VMEM((size, ch), F32),
+        pltpu.SemaphoreType.DMA((3 + count,)),
+    ]
+
+
+def faces_kernel(ways, start, count, flags, row_hbm, gp_hbm, w_hbm, *rest):
+    outs, scratch = rest[: len(ways)], rest[len(ways) :]
+    total = scratch[4]
+    face = outs[0].shape[0]
+    backward_body(start, 0, count, 3 * face, row_hbm, gp_hbm, w_hbm, None, *scratch)
+    for out, (kind, i) in zip(outs, ways):
+        lower = total[pl.ds(2 * i * face, face), :]
+        upper = total[pl.ds((2 * i + 1) * face, face), :]
+        if kind == "pair":
+            out[...] = jnp.where(flags[1 + i] > 0, lower, upper).astype(BF)
+        else:
+            out[...] = (upper if kind == "up" else lower).astype(BF)
+
+
+def backward_faces(ways, flags, row, gp, weight, face):
+    taps = row.shape[0]
+    own, ch = gp.shape
+    return pl.pallas_call(
+        lambda *refs: faces_kernel(ways, own, taps, *refs),
+        in_specs=[SMEM, HBM, HBM, HBM],
+        out_specs=[VMEM] * len(ways),
+        out_shape=[jax.ShapeDtypeStruct((face, ch), BF)] * len(ways),
+        scratch_shapes=backward_scratch(row, gp, 6 * face, taps),
+        compiler_params=params(18),
+        name="backward_faces",
+    )(flags, hold(row), hold(gp), hold(weight))
+
+
+def own_kernel(first, count, row_hbm, gp_hbm, w_hbm, out_hbm, *scratch):
+    backward_body(0, first, count, 384, row_hbm, gp_hbm, w_hbm, None, *scratch)
+    copy = pltpu.make_async_copy(scratch[4], out_hbm, scratch[5].at[2])
+    copy.start()
     copy.wait()
 
 
-def backward(ways, flags, row, gp, weight, first, count, before, rows, final):
-    block = row.shape[2]
-    own, ch = gp.shape
-    face = (rows - own) // 6
-    args = [hold(x) for x in [row, gp, weight] + ([] if before is None else [before])]
-    args = ([flags] if final else []) + args
-    specs = ([SMEM] if final else []) + [HBM] * (len(args) - (1 if final else 0))
-    like = jax.ShapeDtypeStruct
-    if final:
-        out_shape = [pltpu.HBM((own, ch), F32)] + [like((face, ch), BF)] * len(ways)
-        out_specs = [HBM] + [VMEM] * len(ways)
-    else:
-        out_shape = [pltpu.HBM((rows, ch), F32)]
-        out_specs = [HBM]
-    return pl.pallas_call(
-        lambda *refs: backward_kernel(ways, first, count, final, int(before is not None), *refs),
-        in_specs=specs,
-        out_specs=out_specs,
-        out_shape=out_shape,
-        scratch_shapes=[
-            pltpu.VMEM((count,) + row.shape[1:], F32),
-            pltpu.VMEM((own, ch), BF),
-            pltpu.VMEM((rows, count * ch), BF),
-            pltpu.VMEM((ch, count * ch), BF),
-            pltpu.VMEM((rows, ch), F32),
-            pltpu.SemaphoreType.DMA((3 + count,)),
-        ],
-        compiler_params=params(16),
-        name="backward",
-    )(*args)
-
-
-def finish_kernel(ways, flags, rows_ref, grad_hbm, *rest):
-    faces = rest[: len(ways)]
-    out_ref, grad, sem = rest[len(ways) :]
-    copy = pltpu.make_async_copy(grad_hbm, grad, sem)
-    copy.start()
+def backward_own(row, gp, weight, first, count):
+    return pl.pallas_call(
+        lambda *refs: own_kernel(first, count, *refs),
+        in_specs=[HBM, HBM, HBM],
+        out_specs=HBM,
+        out_shape=pltpu.HBM(gp.shape, F32),
+        scratch_shapes=backward_scratch(row, gp, gp.shape[0], count),
+        compiler_params=params(14),
+        name="backward_own",
+    )(hold(row), hold(gp), hold(weight))
+
+
+def finish_kernel(ways, first, count, flags, rows_ref, row_hbm, gp_hbm, w_hbm, before_hbm, *rest):
+    faces, out_ref, scratch = rest[: len(ways)], rest[len(ways)], rest[len(ways) + 1 :]
+    backward_body(0, first, count, 384, row_hbm, gp_hbm, w_hbm, before_hbm, *scratch)
     face = rows_ref.shape[2]
     own = out_ref.shape[0]
     places = lax.broadcasted_iota(jnp.int32, (own, face), 0)
-    total = None
+    total = scratch[4][...]
     for came, (kind, i) in zip(faces, ways):
         lower, upper = rows_ref[2 * i], rows_ref[2 * i + 1]
         if kind == "pair":
             rows = jnp.where(flags[1 + i] > 0, lower, upper)
         else:
             rows = lower if kind == "up" else upper
-        term = dot(one_hot(places == rows), came[...])
-        total = term if total is None else total + term
-    copy.wait()
-    out_ref[...] = (grad[...] + total).astype(BF)
-
-
-def finish(ways, flags, rows, grad, returned):
-    return pl.pallas_call(
-        lambda *refs: finish_kernel(ways, *refs),
-        in_specs=[SMEM, VMEM, HBM] + [VMEM] * len(returned),
+        total = total + dot(one_hot(places == rows), came[...])
+    out_ref[...] = total.astype(BF)
+
+
+def finish(ways, flags, rows, row, gp, weight, first, count, before, returned):
+    return pl.pallas_call(
+        lambda *refs: finish_kernel(ways, first, count, *refs),
+        in_specs=[SMEM, VMEM, HBM, HBM, HBM, HBM] + [VMEM] * len(returned),
         out_specs=VMEM,
-        out_shape=jax.ShapeDtypeStruct(grad.shape, BF),
-        scratch_shapes=[pltpu.VMEM(grad.shape, F32), pltpu.SemaphoreType.DMA],
-        compiler_params=params(8),
+        out_shape=jax.ShapeDtypeStruct(gp.shape, BF),
+        scratch_shapes=backward_scratch(row, gp, gp.shape[0], count),
+        compiler_params=params(16),
         name="finish",
-    )(flags, rows, hold(grad), *returned)
+    )(flags, rows, hold(row), hold(gp), hold(weight), hold(before), *returned)
 
 
 def swap(x, axis, bit):
@@ -409,7 +415,7 @@
     )(spots, *args)
 
 
-def reduce_all(keep, give, scaling, beside, after):
+def reduce_all(keep, give, scaling, beside):
     bits = lambda axis, low: [(axis, b) for b in range(low, lax.axis_size(axis).bit_length() - 1)]
     plane = [bits("gx", 0) + bits("gz", 1), bits("gz", 1) + bits("gx", 0)]
     turns = len(plane[0])
@@ -451,7 +457,7 @@
     odd = side("gz", 0)
     cross = lambda arrays: [swap(y, "gz", 0) for y in arrays]
     came = beside(pieces, [swap(pieces[i], *plane[i][0]) for i in range(2)])
-    twins = cross(after(pieces))
+    twins = cross(pieces)
     sides = [[side(*plane[i][t]) for t in range(turns)] for i in range(2)]
     if size % 8 == 0:
         lanes = jnp.stack([odd, odd, 1 - odd, 1 - odd]) * ch
@@ -493,52 +499,49 @@
     single = lambda x: x[0, 0, 0][:, None, :]
     sends = single(send_rows)
     taps = weight.shape[0]
-    block = 256
+    block = 128
     ways = routes()
     last = [lax.axis_index(a) == lax.axis_size(a) - 1 for a in AXES]
     flags = jnp.stack([side("gz", 0)] + last).astype(jnp.int32)
     faces = exchange(send(ways, flags, sends, own_features), ways)
-    rows = own + 6 * sends.shape[2]
     col, row = invert(single(in_rows), single(out_rows), single(tap_pair_exists), block)
     activated, gp, keep, give = forward(ways, flags, col, own_features, faces, weight, upstream[0, 0, 0])
     devices = lax.axis_size("gx") * lax.axis_size("gy") * lax.axis_size("gz")
-    counts = [12, 6, 9]
-    steps = [(sum(counts[:j]), c) for j, c in enumerate(counts)]
-    steps[-1] = (steps[-1][0], taps - steps[-1][0])
-    state = {"turn": 0, "grad": None, "returned": {}}
-    early = [j for j, (_, i) in enumerate(ways) if i != 1][:2]
-    late = [j for j in range(len(ways)) if j not in early]
+    split = 12
+    state = {"turn": 0, "returned": {}}
+    early = [j for j, (_, i) in enumerate(ways) if i != 2]
+    late = [j for j, (_, i) in enumerate(ways) if i == 2]
+
+    def tied(out, work, came):
+        held = lax.optimization_barrier((gp, *out))
+        made = work(held[0])
+        held = lax.optimization_barrier((*made, *came))
+        return held[: len(made)], list(held[len(made) :])
 
     def beside(out, came):
         turn = state["turn"]
         state["turn"] = turn + 1
-        if turn < len(steps):
-            final = turn == len(steps) - 1
-            held = lax.optimization_barrier((gp, *out))
-            grad = backward(ways, flags, row, held[0], weight, *steps[turn], state["grad"], rows, final)
-            held = lax.optimization_barrier((*grad, *came))
-            state["grad"] = held[0]
-            state["back"] = held[1 : len(grad)]
-            return list(held[len(grad) :])
-        if turn < len(steps) + 2:
-            picks = early if turn == len(steps) else late
+        if turn == 0:
+            work = lambda g: backward_faces(ways, flags, row, g, weight, sends.shape[2])
+            state["back"], came = tied(out, work, came)
+        elif turn in (1, 2):
+            picks = early if turn == 1 else late
             held = lax.optimization_barrier((*[state["back"][j] for j in picks], *out))
             got = exchange(held[: len(picks)], [ways[j] for j in picks])
             held = lax.optimization_barrier((*got, *came))
             for j, face in zip(picks, held):
                 state["returned"][j] = face
-            return list(held[len(picks) :])
-        if turn == len(steps) + 2:
-            held = lax.optimization_barrier((state["grad"], *out))
-            state["done"] = finish(ways, flags, sends, held[0], [state["returned"][j] for j in range(len(ways))])
+            came = list(held[len(picks) :])
+        elif turn == 3:
+            work = lambda g: [backward_own(row, g, weight, 0, split)]
+            (state["grad"],), came = tied(out, work, came)
+        elif turn == 5:
+            faces = [state["returned"][j] for j in range(len(ways))]
+            work = lambda g: [finish(ways, flags, sends, row, g, weight, split, taps - split, state["grad"], faces)]
+            (state["done"],), came = tied(out, work, came)
         return came
 
-    def after(out):
-        held = lax.optimization_barrier((state["done"], *out))
-        state["done"] = held[0]
-        return list(held[1:])
-
-    grad_weight = reduce_all(keep, give, float(devices * own) ** -0.5, beside, after).reshape(weight.shape)
+    grad_weight = reduce_all(keep, give, float(devices * own) ** -0.5, beside).reshape(weight.shape)
     return activated[None, None, None], state["done"][None, None, None], grad_weight
 
 

time: 143 us -> 146 us (1.021)
  waiting for transfers between devices: 16.8 us -> 22.8 us
  Pallas kernels: 73 us -> 68.5 us
  starting transfers between devices: 41.8 us -> 39.4 us
  other arithmetic: 7.46 us -> 9.65 us
    pallas_call x1, Pallas kernels: 7.33 us -> 3.27 us  [invert(): pl.pallas_call(lambda *refs: invert_kernel(block, *refs), in_specs=[HBM,...]
    another operation x0 -> x2, other arithmetic: none -> 3.71 us
    ppermute x10, waiting for transfers between devices: 5.55 us -> 9.2 us  [exchange(): got.append(lax.ppermute(array, AXES[i], pairs))]
    ppermute x13, waiting for transfers between devices: 9.31 us -> 12.1 us  [swap(): return lax.ppermute(x, axis, [(j, j ^ 1 << bit) for j in range(n)])]
    ppermute x6, starting transfers between devices: 10.8 us -> 8.11 us  [reduce_all(): lax.ppermute(y, 'gy', [(j, (j + s) % n) for j in range(n)])]
    add x2 -> x0, other arithmetic: 2.49 us -> none  [total(): out = value if out is None else out + value]
    ppermute x10, starting transfers between devices: 17.5 us -> 19.9 us  [exchange(): got.append(lax.ppermute(array, AXES[i], pairs))]
    ppermute x13, starting transfers between devices: 13.5 us -> 11.4 us  [swap(): return lax.ppermute(x, axis, [(j, j ^ 1 << bit) for j in range(n)])]
  transfers between devices with their start and end apart: 29 -> 29, of which waited for: 10 -> 10; matrix products, arithmetic and copies ran while one was open for 1% -> 1% of each run, Pallas kernels for 29% -> 24%
where the time goes in v5:
time: 146 us; the launch traced here: 145 us
  Pallas kernels  68.5 us (47%)
  starting transfers between devices  39.4 us (27%)
  waiting for transfers between devices  22.8 us (16%)
  other arithmetic  9.65 us (7%)
  local copies, waits for them, and re-layouts  3.6 us (2%)
    pallas_call x1, Pallas kernels, forward(): pl.pallas_call(lambda *refs: forward_kernel(ways, 256, *refs), in_specs=[...  29.1 us
    ppermute x10, starting transfers between devices, exchange(): got.append(lax.ppermute(array, AXES[i], pairs))  19.9 us
    pallas_call x1, Pallas kernels, backward_faces(): pl.pallas_call(lambda *refs: faces_kernel(ways, own, taps, *refs), in_spe...  12.8 us
    ppermute x13, waiting for transfers between devices, swap(): return lax.ppermute(x, axis, [(j, j ^ 1 << bit) for j in range(n)])  12.1 us
    ppermute x13, starting transfers between devices, swap(): return lax.ppermute(x, axis, [(j, j ^ 1 << bit) for j in range(n)])  11.4 us
    pallas_call x1, Pallas kernels, finish(): pl.pallas_call(lambda *refs: finish_kernel(ways, first, count, *refs), in...  10.5 us
    ppermute x10, waiting for transfers between devices, exchange(): got.append(lax.ppermute(array, AXES[i], pairs))  9.2 us
    ppermute x6, starting transfers between devices, reduce_all(): lax.ppermute(y, 'gy', [(j, (j + s) % n) for j in range(n)])  8.11 us
  transfers between devices with their start and end apart: 29, of which 10 were waited for; matrix products, arithmetic and copies ran while one was open for 1% of the time, Pallas kernels for 24%

profile of v5, /device:TPU:0, one launch (start us, length us, event | category | flops | bytes accessed | tf_op | source)
XLA Modules:
  0.0 145.3 jit_solution(3043370141082523042)
XLA Ops:
  0.6 0.1 fusion.4
  0.7 1.0 copy-done
  1.7 0.7 copy-done.1
  2.4 1.0 send.1
  3.4 3.0 %collective-permute-start = (bf16[96,256]{1,0:T(8,128)(2,1)S(1)}, bf16[96,256]{1,0:T(8,128)(2,1)S(1)}, u32[]{:S(2)}, u32[]{:S(2)}) collective-permute-start(bf16[96,256]{1,0:T(8,128)(2,1)S(1)} %get-tuple-element.55), channel_id=1, source_target_pairs={{0,16},{16,0},{1,17},{17,1},{2,18},{18,2},{3,19},{19,3},{4,20},{20... | collective-permute-start | bytes 147464 | tf_op jit(solution)/shard_map/ppermute | solution.py:57
  6.4 3.5 %collective-permute-start.1 = (bf16[96,256]{1,0:T(8,128)(2,1)S(1)}, bf16[96,256]{1,0:T(8,128)(2,1)S(1)}, u32[]{:S(2)}, u32[]{:S(2)}) collective-permute-start(bf16[96,256]{1,0:T(8,128)(2,1)S(1)} %get-tuple-element.56), channel_id=1, source_target_pairs={{0,4},{4,8},{8,12},{1,5},{5,9},{9,13},{2,6},{6,10},{10,14},{3,7},{... | collective-permute-start | bytes 147464 | tf_op jit(solution)/shard_map/ppermute | solution.py:57
  9.9 1.3 collective-permute-start.2
  11.2 1.3 collective-permute-start.3
  12.5 1.3 collective-permute-start.4
  13.8 3.3 %invert.1 = (f32[27,128,16]{2,1,0:T(8,128)S(1)}, f32[27,16,128]{2,1,0:T(8,128)}) custom-call(s32[27,1,768]{2,1,0:T(1,128)} %bitcast.27, s32[27,1,768]{2,1,0:T(1,128)} %bitcast.28, s32[27,1,768]{2,1,0:T(1,128)} %bitcast.29), custom_call_target="tpu_custom_call" | custom-call | tf_op jit(solution)/shard_map/invert/pallas_call | solution.py:116
  17.1 0.3 collective-permute-done.4.refs_9_
  17.4 29.1 %forward.1 = (bf16[768,256]{1,0:T(8,128)(2,1)}, bf16[768,256]{1,0:T(8,128)(2,1)}, f32[6912,128]{1,0:T(8,128)S(1)}, bf16[6912,128]{1,0:T(8,128)(2,1)}) custom-call(s32[4]{0:T(128)S(1)} %get-tuple-element.138.refs_0_, f32[27,128,16]{2,1,0:T(8,128)S(1)} %get-tuple-element.54.refs_1_, bf16[768,256]{1,0:T(8,128)(2,1)} %bitcast.19, bf16[6912,256]{1,0:T(8,128)(2,1)} %bitcast.23, ...), custom_call_target="tpu_custom_call" | custom-call | tf_op jit(solution)/shard_map/forward/pallas_call | solution.py:223
  46.5 2.8 %collective-permute-start.5 = (bf16[6912,128]{1,0:T(8,128)(2,1)}, bf16[6912,128]{1,0:T(8,128)(2,1)}, u32[]{:S(2)}, u32[]{:S(2)}) collective-permute-start(bf16[6912,128]{1,0:T(8,128)(2,1)} %get-tuple-element.64), channel_id=1, source_target_pairs={{0,1},{1,0},{2,3},{3,2},{4,5},{5,4},{6,7},{7,6},{8,9},{9,8},{10,11... | collective-permute-start | bytes 5308424 | tf_op jit(solution)/shard_map/ppermute | solution.py:379
  49.4 3.7 %collective-permute-done.5 = bf16[6912,128]{1,0:T(8,128)(2,1)} collective-permute-done((bf16[6912,128]{1,0:T(8,128)(2,1)}, bf16[6912,128]{1,0:T(8,128)(2,1)}, u32[]{:S(2)}, u32[]{:S(2)}) %collective-permute-start.5) | collective-permute-done | bytes 1769504 | tf_op jit(solution)/shard_map/ppermute | solution.py:379
  53.0 2.3 %add_convert_fusion = (bf16[1728,128]{1,0:T(8,128)(2,1)}, bf16[1728,128]{1,0:T(8,128)(2,1)}) fusion(f32[6912,128]{1,0:T(8,128)S(1)} %get-tuple-element.63, s32[]{:T(128)S(6)} %select_n.140, bf16[6912,128]{1,0:T(8,128)(2,1)} %collective-permute-done.5, s32[]{:T(128)S(6)} %select_n.139), kind=kLoop, calls=%fused_computation | loop fusion | flops 1327104 | bytes 3538952 | tf_op jit(solution)/shard_map/convert_element_type | solution.py:437
  55.3 1.8 %collective-permute-start.7 = (bf16[1728,128]{1,0:T(8,128)(2,1)}, bf16[1728,128]{1,0:T(8,128)(2,1)}, u32[]{:S(2)}, u32[]{:S(2)}) collective-permute-start(bf16[1728,128]{1,0:T(8,128)(2,1)} %get-tuple-element.115), channel_id=1, source_target_pairs={{0,2},{1,3},{2,0},{3,1},{4,6},{5,7},{6,4},{7,5},{8,10},{9,11},{10,... | collective-permute-start | bytes 1327112 | tf_op jit(solution)/shard_map/ppermute | solution.py:379
  57.1 0.5 collective-permute-start.6
  57.7 12.8 %backward_faces.1 = (bf16[96,256]{1,0:T(8,128)(2,1)}, bf16[96,256]{1,0:T(8,128)(2,1)}, bf16[96,256]{1,0:T(8,128)(2,1)}, bf16[96,256]{1,0:T(8,128)(2,1)S(1)}, bf16[96,256]{1,0:T(8,128)(2,1)S(1)}) custom-call(s32[4]{0:T(128)S(1)} %get-tuple-element.138.refs_0_, f32[27,16,128]{2,1,0:T(8,128)} %get-tuple-element.61.refs_1_.refs_0_.refs_2_, ...), custom_call_target="tpu_custom_call" | custom-call | tf_op jit(solution)/shard_map/backward_faces/pallas_call | solution.py:318
  70.5 0.6 copy-done.3
  71.1 0.6 copy-done.4
  71.7 2.2 %add_convert_fusion.2 = (bf16[864,128]{1,0:T(8,128)(2,1)}, bf16[864,128]{1,0:T(8,128)(2,1)}) fusion(f32[6912,128]{1,0:T(8,128)S(1)} %get-tuple-element.63, s32[]{:T(128)S(6)} %select_n.144, bf16[1728,128]{1,0:T(8,128)(2,1)} %collective-permute-done.7, s32[]{:T(128)S(6)} %select_n.145, bf16[6912,128]{1,0:T(8,128)(2,1)} %collective-permute-done.5, ...), kind=kLoop, calls=%fused_computation.2 | loop fusion | flops 1105920 | bytes 2211856 | tf_op jit(solution)/shard_map/convert_element_type | solution.py:437
  73.9 1.5 %collective-permute-start.12 = (bf16[864,128]{1,0:T(8,128)(2,1)}, bf16[864,128]{1,0:T(8,128)(2,1)}, u32[]{:S(2)}, u32[]{:S(2)}) collective-permute-start(bf16[864,128]{1,0:T(8,128)(2,1)} %get-tuple-element.113), channel_id=1, source_target_pairs={{0,16},{16,0},{1,17},{17,1},{2,18},{18,2},{3,19},{19,3},{4,20},{20... | collective-permute-start | bytes 663560 | tf_op jit(solution)/shard_map/ppermute | solution.py:379
  75.4 0.2 collective-permute-start.11
  75.6 0.5 collective-permute-start.8
  76.1 5.1 %collective-permute-start.9 = (bf16[96,256]{1,0:T(8,128)(2,1)}, bf16[96,256]{1,0:T(8,128)(2,1)}, u32[]{:S(2)}, u32[]{:S(2)}) collective-permute-start(bf16[96,256]{1,0:T(8,128)(2,1)} %get-tuple-element.77), channel_id=1, source_target_pairs={{0,4},{4,8},{8,12},{1,5},{5,9},{9,13},{2,6},{6,10},{10,14},{3,7},{... | collective-permute-start | bytes 147464 | tf_op jit(solution)/shard_map/ppermute | solution.py:57
  81.3 1.3 collective-permute-start.10
  82.7 4.8 %collective-permute-done.10.refs_8_ = bf16[96,256]{1,0:T(8,128)(2,1)} collective-permute-done((bf16[96,256]{1,0:T(8,128)(2,1)}, bf16[96,256]{1,0:T(8,128)(2,1)}, u32[]{:S(2)}, u32[]{:S(2)}) %collective-permute-start.10) | collective-permute-done | bytes 49184 | tf_op jit(solution)/shard_map/ppermute | solution.py:57
  87.6 1.9 %add_convert_fusion.4 = (bf16[216,128]{1,0:T(8,128)(2,1)S(1)}, bf16[216,128]{1,0:T(8,128)(2,1)S(1)}, bf16[216,128]{1,0:T(8,128)(2,1)S(1)}, f32[216,128]{1,0:T(8,128)}) fusion(f32[6912,128]{1,0:T(8,128)S(1)} %get-tuple-element.63, s32[]{:T(128)S(6)} %select_n.165, bf16[864,128]{1,0:T(8,128)(2,1)} %collective-permute-done.12, s32[]{:T(128)S(6)} %select_n.164, ...), kind=kLoop, calls=%fused_computation.14 | loop fusion | flops 746496 | bytes 1382448 | tf_op jit(solution)/shard_map/convert.4
  89.4 1.9 %add_convert_fusion.5 = (bf16[216,128]{1,0:T(8,128)(2,1)S(1)}, bf16[216,128]{1,0:T(8,128)(2,1)S(1)}, bf16[216,128]{1,0:T(8,128)(2,1)S(1)}, f32[216,128]{1,0:T(8,128)}) fusion(f32[6912,128]{1,0:T(8,128)S(1)} %get-tuple-element.63, s32[]{:T(128)S(6)} %select_n.162, bf16[864,128]{1,0:T(8,128)(2,1)} %collective-permute-done.11, s32[]{:T(128)S(6)} %select_n.164, ...), kind=kLoop, calls=%fused_computation.15 | loop fusion | flops 746496 | bytes 1382448 | tf_op jit(solution)/shard_map/convert.3
  91.3 1.1 collective-permute-start.15
  92.3 1.1 collective-permute-start.16
  93.5 3.0 %collective-permute-start.17 = (bf16[432,128]{1,0:T(8,128)(2,1)S(1)}, bf16[432,128]{1,0:T(8,128)(2,1)S(1)}, u32[]{:S(2)}, u32[]{:S(2)}) collective-permute-start(bf16[432,128]{1,0:T(8,128)(2,1)S(1)} %pad_maximum_fusion.4), channel_id=1, source_target_pairs={{0,12},{4,0},{8,4},{12,8},{1,13},{5,1},{9,5},{13,9},{2,14},{6,2},{... | collective-permute-start | bytes 331784 | tf_op jit(solution)/shard_map/ppermute | solution.py:445
  96.4 1.3 collective-permute-start.13
  97.7 1.3 collective-permute-start.14
  99.0 4.1 %collective-permute-done.14.refs_10_ = bf16[96,256]{1,0:T(8,128)(2,1)S(1)} collective-permute-done((bf16[96,256]{1,0:T(8,128)(2,1)}, bf16[96,256]{1,0:T(8,128)(2,1)S(1)}, u32[]{:S(2)}, u32[]{:S(2)}) %collective-permute-start.14) | collective-permute-done | bytes 49184 | tf_op jit(solution)/shard_map/ppermute | solution.py:57
  103.1 1.0 fusion.3
  104.1 0.8 collective-permute-start.20
  105.0 0.8 collective-permute-start.19
  105.7 1.4 collective-permute-start.18
  107.2 7.8 %backward_own.1.refs_5_ = f32[768,256]{1,0:T(8,128)} custom-call(f32[27,16,128]{2,1,0:T(8,128)} %get-tuple-element.61.refs_1_.refs_0_.refs_2_, bf16[768,256]{1,0:T(8,128)(2,1)} %get-tuple-element.92.refs_2_.refs_1_.refs_3_, bf16[27,256,256]{2,1,0:T(8,128)(2,1)} %refs_4_.1), custom_call_target="tpu_custom_call" | custom-call | tf_op jit(solution)/shard_map/backward_own/pallas_call | solution.py:337
  115.0 1.5 %collective-permute-done.19 = bf16[432,128]{1,0:T(8,128)(2,1)S(1)} collective-permute-done((bf16[432,128]{1,0:T(8,128)(2,1)S(1)}, bf16[432,128]{1,0:T(8,128)(2,1)S(1)}, u32[]{:S(2)}, u32[]{:S(2)}) %collective-permute-start.19) | collective-permute-done | bytes 110624 | tf_op jit(solution)/shard_map/ppermute | solution.py:445
  116.7 1.6 %collective-permute-start.22 = (bf16[864,128]{1,0:T(8,128)(2,1)S(1)}, bf16[864,128]{1,0:T(8,128)(2,1)S(1)}, u32[]{:S(2)}, u32[]{:S(2)}) collective-permute-start(bf16[864,128]{1,0:T(8,128)(2,1)S(1)} %pad_maximum_fusion.1), channel_id=1, source_target_pairs={{0,16},{16,0},{1,17},{17,1},{2,18},{18,2},{3,19},{19,3},{4,20},{20... | collective-permute-start | bytes 663560 | tf_op jit(solution)/shard_map/ppermute | solution.py:379
  118.2 1.4 collective-permute-start.21
  119.6 0.1 broadcast_add_fusion.4
  119.7 4.9 %collective-permute-done.22 = bf16[864,128]{1,0:T(8,128)(2,1)S(1)} collective-permute-done((bf16[864,128]{1,0:T(8,128)(2,1)S(1)}, bf16[864,128]{1,0:T(8,128)(2,1)S(1)}, u32[]{:S(2)}, u32[]{:S(2)}) %collective-permute-start.22) | collective-permute-done | bytes 221216 | tf_op jit(solution)/shard_map/ppermute | solution.py:379
  124.7 0.1 collective-permute-start.24
  124.8 1.1 collective-permute-done.21
  126.0 0.8 collective-permute-start.23
  126.8 0.1 broadcast_add_fusion.6
  126.8 0.1 broadcast_add_fusion
  126.9 0.1 add.552
  127.0 0.1 add.547
  127.1 0.1 add_multiply_fusion.2
  127.2 0.1 concatenate.62.refs_0_
  127.2 10.5 %finish.1 = bf16[768,256]{1,0:T(8,128)(2,1)} custom-call(s32[4]{0:T(128)S(1)} %get-tuple-element.138.refs_0_, s32[6,1,96]{2,1,0:T(1,128)S(1)} %bitcast.22, f32[27,16,128]{2,1,0:T(8,128)} %get-tuple-element.61.refs_1_.refs_0_.refs_2_, bf16[768,256]{1,0:T(8,128)(2,1)} %get-tuple-element.92.refs_2_.refs_1_.refs_3_, bf16[27,256,256]{2,1,0:T(8,128)(2,1)} %refs_4_.1, ...), custom_call_target="tpu_custom_call" | custom-call | tf_op jit(solution)/shard_map/finish/pallas_call | solution.py:366
  137.8 0.8 collective-permute-done.23.refs_1_
  138.6 2.0 %place.2.refs_5_ = bf16[6912,256]{1,0:T(8,128)(2,1)} custom-call(s32[36]{0:T(128)S(1)} %concatenate.62.refs_0_, bf16[1728,128]{1,0:T(8,128)(2,1)S(1)} %constant_dynamic-update-slice_fusion.refs_1_, bf16[1728,128]{1,0:T(8,128)(2,1)S(1)} %constant_dynamic-update-slice_fusion.5.refs_2_, bf16[1728,128]{1,0:T(8,128)(2,1)S(1)} %collective-permute-done.25.refs_3_, ...), custom_call_target="tpu_custom_call" | custom-call | tf_op jit(solution)/shard_map/place/pallas_call | solution.py:406
  140.7 0.5 collective-permute-start.28
  141.1 0.1 add.542
  141.2 0.1 add.536
  141.3 0.1 concatenate.61.refs_0_
  141.4 1.0 collective-permute-done.27.refs_3_
  142.4 0.6 collective-permute-done.28.refs_4_
  143.1 2.0 %place.3 = bf16[6912,256]{1,0:T(8,128)(2,1)} custom-call(s32[36]{0:T(128)S(1)} %concatenate.61.refs_0_, bf16[1728,128]{1,0:T(8,128)(2,1)S(1)} %collective-permute-done.23.refs_1_, bf16[1728,128]{1,0:T(8,128)(2,1)S(1)} %collective-permute-done.24.refs_2_, bf16[1728,128]{1,0:T(8,128)(2,1)S(1)} %collective-permute-done.27.refs_3_, ...), custom_call_target="tpu_custom_call", output_to_operand_aliasing={{}: (5, {})} | custom-call | tf_op jit(solution)/shard_map/place/pallas_call | solution.py:406
  (39 shorter events, 0.5 us)
Async XLA Ops:
  0.7 1.0 copy-start
  1.7 0.7 copy-start.1
  3.4 13.7 %collective-permute-start = (bf16[96,256]{1,0:T(8,128)(2,1)S(1)}, bf16[96,256]{1,0:T(8,128)(2,1)S(1)}, u32[]{:S(2)}, u32[]{:S(2)}) collective-permute-start(bf16[96,256]{1,0:T(8,128)(2,1)S(1)} %get-tuple-element.55), channel_id=1, source_target_pairs={{0,16},{16,0},{1,17},{17,1},{2,18},{18,2},{3,19},{19,3},{4,20},{20... | collective-permute-start | bytes 147464 | tf_op jit(solution)/shard_map/ppermute | solution.py:57
  6.4 10.7 %collective-permute-start.1 = (bf16[96,256]{1,0:T(8,128)(2,1)S(1)}, bf16[96,256]{1,0:T(8,128)(2,1)S(1)}, u32[]{:S(2)}, u32[]{:S(2)}) collective-permute-start(bf16[96,256]{1,0:T(8,128)(2,1)S(1)} %get-tuple-element.56), channel_id=1, source_target_pairs={{0,4},{4,8},{8,12},{1,5},{5,9},{9,13},{2,6},{6,10},{10,14},{3,7},{... | collective-permute-start | bytes 147464 | tf_op jit(solution)/shard_map/ppermute | solution.py:57
  9.9 7.2 %collective-permute-start.2 = (bf16[96,256]{1,0:T(8,128)(2,1)S(1)}, bf16[96,256]{1,0:T(8,128)(2,1)S(1)}, u32[]{:S(2)}, u32[]{:S(2)}) collective-permute-start(bf16[96,256]{1,0:T(8,128)(2,1)S(1)} %get-tuple-element.57), channel_id=1, source_target_pairs={{4,0},{8,4},{12,8},{5,1},{9,5},{13,9},{6,2},{10,6},{14,10},{7,3},{... | collective-permute-start | bytes 147464 | tf_op jit(solution)/shard_map/ppermute | solution.py:57
  11.2 5.9 %collective-permute-start.3 = (bf16[96,256]{1,0:T(8,128)(2,1)S(1)}, bf16[96,256]{1,0:T(8,128)(2,1)S(1)}, u32[]{:S(2)}, u32[]{:S(2)}) collective-permute-start(bf16[96,256]{1,0:T(8,128)(2,1)S(1)} %get-tuple-element.58), channel_id=1, source_target_pairs={{0,1},{1,2},{2,3},{4,5},{5,6},{6,7},{8,9},{9,10},{10,11},{12,13},{... | collective-permute-start | bytes 147464 | tf_op jit(solution)/shard_map/ppermute | solution.py:57
  12.5 4.9 %collective-permute-start.4 = (bf16[96,256]{1,0:T(8,128)(2,1)S(1)}, bf16[96,256]{1,0:T(8,128)(2,1)S(1)}, u32[]{:S(2)}, u32[]{:S(2)}) collective-permute-start(bf16[96,256]{1,0:T(8,128)(2,1)S(1)} %get-tuple-element.59), channel_id=1, source_target_pairs={{1,0},{2,1},{3,2},{5,4},{6,5},{7,6},{9,8},{10,9},{11,10},{13,12},{... | collective-permute-start | bytes 147464 | tf_op jit(solution)/shard_map/ppermute | solution.py:57
  46.5 6.5 %collective-permute-start.5 = (bf16[6912,128]{1,0:T(8,128)(2,1)}, bf16[6912,128]{1,0:T(8,128)(2,1)}, u32[]{:S(2)}, u32[]{:S(2)}) collective-permute-start(bf16[6912,128]{1,0:T(8,128)(2,1)} %get-tuple-element.64), channel_id=1, source_target_pairs={{0,1},{1,0},{2,3},{3,2},{4,5},{5,4},{6,7},{7,6},{8,9},{9,8},{10,11... | collective-permute-start | bytes 5308424 | tf_op jit(solution)/shard_map/ppermute | solution.py:379
  55.3 16.4 %collective-permute-start.7 = (bf16[1728,128]{1,0:T(8,128)(2,1)}, bf16[1728,128]{1,0:T(8,128)(2,1)}, u32[]{:S(2)}, u32[]{:S(2)}) collective-permute-start(bf16[1728,128]{1,0:T(8,128)(2,1)} %get-tuple-element.115), channel_id=1, source_target_pairs={{0,2},{1,3},{2,0},{3,1},{4,6},{5,7},{6,4},{7,5},{8,10},{9,11},{10,... | collective-permute-start | bytes 1327112 | tf_op jit(solution)/shard_map/ppermute | solution.py:379
  57.1 14.6 %collective-permute-start.6 = (bf16[1728,128]{1,0:T(8,128)(2,1)}, bf16[1728,128]{1,0:T(8,128)(2,1)}, u32[]{:S(2)}, u32[]{:S(2)}) collective-permute-start(bf16[1728,128]{1,0:T(8,128)(2,1)} %get-tuple-element.116), channel_id=1, source_target_pairs={{0,16},{16,0},{1,17},{17,1},{2,18},{18,2},{3,19},{19,3},{4,20},{20... | collective-permute-start | bytes 1327112 | tf_op jit(solution)/shard_map/ppermute | solution.py:379
  70.5 0.6 copy-start.3
  71.1 0.6 copy-start.4
  73.9 13.7 %collective-permute-start.12 = (bf16[864,128]{1,0:T(8,128)(2,1)}, bf16[864,128]{1,0:T(8,128)(2,1)}, u32[]{:S(2)}, u32[]{:S(2)}) collective-permute-start(bf16[864,128]{1,0:T(8,128)(2,1)} %get-tuple-element.113), channel_id=1, source_target_pairs={{0,16},{16,0},{1,17},{17,1},{2,18},{18,2},{3,19},{19,3},{4,20},{20... | collective-permute-start | bytes 663560 | tf_op jit(solution)/shard_map/ppermute | solution.py:379
  75.4 12.2 %collective-permute-start.11 = (bf16[864,128]{1,0:T(8,128)(2,1)}, bf16[864,128]{1,0:T(8,128)(2,1)}, u32[]{:S(2)}, u32[]{:S(2)}) collective-permute-start(bf16[864,128]{1,0:T(8,128)(2,1)} %get-tuple-element.114), channel_id=1, source_target_pairs={{0,2},{1,3},{2,0},{3,1},{4,6},{5,7},{6,4},{7,5},{8,10},{9,11},{10,... | collective-permute-start | bytes 663560 | tf_op jit(solution)/shard_map/ppermute | solution.py:379
  75.6 7.1 %collective-permute-start.8 = (bf16[96,256]{1,0:T(8,128)(2,1)}, bf16[96,256]{1,0:T(8,128)(2,1)}, u32[]{:S(2)}, u32[]{:S(2)}) collective-permute-start(bf16[96,256]{1,0:T(8,128)(2,1)} %get-tuple-element.76), channel_id=1, source_target_pairs={{0,16},{16,0},{1,17},{17,1},{2,18},{18,2},{3,19},{19,3},{4,20},{20... | collective-permute-start | bytes 147464 | tf_op jit(solution)/shard_map/ppermute | solution.py:57
  76.1 6.6 %collective-permute-start.9 = (bf16[96,256]{1,0:T(8,128)(2,1)}, bf16[96,256]{1,0:T(8,128)(2,1)}, u32[]{:S(2)}, u32[]{:S(2)}) collective-permute-start(bf16[96,256]{1,0:T(8,128)(2,1)} %get-tuple-element.77), channel_id=1, source_target_pairs={{0,4},{4,8},{8,12},{1,5},{5,9},{9,13},{2,6},{6,10},{10,14},{3,7},{... | collective-permute-start | bytes 147464 | tf_op jit(solution)/shard_map/ppermute | solution.py:57
  81.3 6.3 %collective-permute-start.10 = (bf16[96,256]{1,0:T(8,128)(2,1)}, bf16[96,256]{1,0:T(8,128)(2,1)}, u32[]{:S(2)}, u32[]{:S(2)}) collective-permute-start(bf16[96,256]{1,0:T(8,128)(2,1)} %get-tuple-element.78), channel_id=1, source_target_pairs={{4,0},{8,4},{12,8},{5,1},{9,5},{13,9},{6,2},{10,6},{14,10},{7,3},{... | collective-permute-start | bytes 147464 | tf_op jit(solution)/shard_map/ppermute | solution.py:57
  91.3 11.8 %collective-permute-start.15 = (bf16[432,128]{1,0:T(8,128)(2,1)S(1)}, bf16[432,128]{1,0:T(8,128)(2,1)S(1)}, u32[]{:S(2)}, u32[]{:S(2)}) collective-permute-start(bf16[432,128]{1,0:T(8,128)(2,1)S(1)} %pad_maximum_fusion.2), channel_id=1, source_target_pairs={{0,4},{4,8},{8,12},{12,0},{1,5},{5,9},{9,13},{13,1},{2,6},{6,10},{... | collective-permute-start | bytes 331784 | tf_op jit(solution)/shard_map/ppermute | solution.py:445
  92.3 10.8 %collective-permute-start.16 = (bf16[432,128]{1,0:T(8,128)(2,1)S(1)}, bf16[432,128]{1,0:T(8,128)(2,1)S(1)}, u32[]{:S(2)}, u32[]{:S(2)}) collective-permute-start(bf16[432,128]{1,0:T(8,128)(2,1)S(1)} %pad_maximum_fusion.3), channel_id=1, source_target_pairs={{0,8},{4,12},{8,0},{12,4},{1,9},{5,13},{9,1},{13,5},{2,10},{6,14},... | collective-permute-start | bytes 331784 | tf_op jit(solution)/shard_map/ppermute | solution.py:445
  93.5 9.7 %collective-permute-start.17 = (bf16[432,128]{1,0:T(8,128)(2,1)S(1)}, bf16[432,128]{1,0:T(8,128)(2,1)S(1)}, u32[]{:S(2)}, u32[]{:S(2)}) collective-permute-start(bf16[432,128]{1,0:T(8,128)(2,1)S(1)} %pad_maximum_fusion.4), channel_id=1, source_target_pairs={{0,12},{4,0},{8,4},{12,8},{1,13},{5,1},{9,5},{13,9},{2,14},{6,2},{... | collective-permute-start | bytes 331784 | tf_op jit(solution)/shard_map/ppermute | solution.py:445
  96.4 2.6 %collective-permute-start.13 = (bf16[96,256]{1,0:T(8,128)(2,1)}, bf16[96,256]{1,0:T(8,128)(2,1)S(1)}, u32[]{:S(2)}, u32[]{:S(2)}) collective-permute-start(bf16[96,256]{1,0:T(8,128)(2,1)} %copy-done.4), channel_id=1, source_target_pairs={{0,1},{1,2},{2,3},{4,5},{5,6},{6,7},{8,9},{9,10},{10,11},{12,13},{... | collective-permute-start | bytes 147464 | tf_op jit(solution)/shard_map/ppermute | solution.py:57
  97.7 5.4 %collective-permute-start.14 = (bf16[96,256]{1,0:T(8,128)(2,1)}, bf16[96,256]{1,0:T(8,128)(2,1)S(1)}, u32[]{:S(2)}, u32[]{:S(2)}) collective-permute-start(bf16[96,256]{1,0:T(8,128)(2,1)} %copy-done.3), channel_id=1, source_target_pairs={{1,0},{2,1},{3,2},{5,4},{6,5},{7,6},{9,8},{10,9},{11,10},{13,12},{... | collective-permute-start | bytes 147464 | tf_op jit(solution)/shard_map/ppermute | solution.py:57
  104.1 10.9 %collective-permute-start.20 = (bf16[432,128]{1,0:T(8,128)(2,1)S(1)}, bf16[432,128]{1,0:T(8,128)(2,1)S(1)}, u32[]{:S(2)}, u32[]{:S(2)}) collective-permute-start(bf16[432,128]{1,0:T(8,128)(2,1)S(1)} %fusion.3), channel_id=1, source_target_pairs={{0,12},{4,0},{8,4},{12,8},{1,13},{5,1},{9,5},{13,9},{2,14},{6,2},{... | collective-permute-start | bytes 331784 | tf_op jit(solution)/shard_map/ppermute | solution.py:445
  105.0 11.5 %collective-permute-start.19 = (bf16[432,128]{1,0:T(8,128)(2,1)S(1)}, bf16[432,128]{1,0:T(8,128)(2,1)S(1)}, u32[]{:S(2)}, u32[]{:S(2)}) collective-permute-start(bf16[432,128]{1,0:T(8,128)(2,1)S(1)} %fusion.3), channel_id=1, source_target_pairs={{0,8},{4,12},{8,0},{12,4},{1,9},{5,13},{9,1},{13,5},{2,10},{6,14},... | collective-permute-start | bytes 331784 | tf_op jit(solution)/shard_map/ppermute | solution.py:445
  105.7 10.8 %collective-permute-start.18 = (bf16[432,128]{1,0:T(8,128)(2,1)S(1)}, bf16[432,128]{1,0:T(8,128)(2,1)S(1)}, u32[]{:S(2)}, u32[]{:S(2)}) collective-permute-start(bf16[432,128]{1,0:T(8,128)(2,1)S(1)} %fusion.3), channel_id=1, source_target_pairs={{0,4},{4,8},{8,12},{12,0},{1,5},{5,9},{9,13},{13,1},{2,6},{6,10},{... | collective-permute-start | bytes 331784 | tf_op jit(solution)/shard_map/ppermute | solution.py:445
  107.2 20.1 %copy-start.2 = (s32[1,1,1,6,96]{4,2,3,1,0:T(1,128)S(1)}, s32[1,1,1,6,96]{4,2,3,1,0:T(1,128)}, u32[]{:S(2)}) copy-start(s32[1,1,1,6,96]{4,2,3,1,0:T(1,128)} %param.10) | copy-start | bytes 6916
  116.7 7.9 %collective-permute-start.22 = (bf16[864,128]{1,0:T(8,128)(2,1)S(1)}, bf16[864,128]{1,0:T(8,128)(2,1)S(1)}, u32[]{:S(2)}, u32[]{:S(2)}) collective-permute-start(bf16[864,128]{1,0:T(8,128)(2,1)S(1)} %pad_maximum_fusion.1), channel_id=1, source_target_pairs={{0,16},{16,0},{1,17},{17,1},{2,18},{18,2},{3,19},{19,3},{4,20},{20... | collective-permute-start | bytes 663560 | tf_op jit(solution)/shard_map/ppermute | solution.py:379
  118.2 7.6 %collective-permute-start.21 = (bf16[864,128]{1,0:T(8,128)(2,1)S(1)}, bf16[864,128]{1,0:T(8,128)(2,1)S(1)}, u32[]{:S(2)}, u32[]{:S(2)}) collective-permute-start(bf16[864,128]{1,0:T(8,128)(2,1)S(1)} %pad_maximum_fusion), channel_id=1, source_target_pairs={{0,2},{1,3},{2,0},{3,1},{4,6},{5,7},{6,4},{7,5},{8,10},{9,11},{10,... | collective-permute-start | bytes 663560 | tf_op jit(solution)/shard_map/ppermute | solution.py:379
  124.6 14.0 %collective-permute-start.26 = (bf16[1728,128]{1,0:T(8,128)(2,1)S(1)}, bf16[1728,128]{1,0:T(8,128)(2,1)S(1)}, u32[]{:S(2)}, u32[]{:S(2)}) collective-permute-start(bf16[1728,128]{1,0:T(8,128)(2,1)S(1)} %constant_dynamic-update-slice_fusion.5.refs_2_), channel_id=1, source_target_pairs={{0,1},{1,0},{2,3},{3,2},{4,5},{5,4},{6,7},{7,6},{8,9},{9,8},{10,11... | collective-permute-start | bytes 1327112 | tf_op jit(solution)/shard_map/ppermute | solution.py:379
  124.7 13.1 %collective-permute-start.24 = (bf16[1728,128]{1,0:T(8,128)(2,1)S(1)}, bf16[1728,128]{1,0:T(8,128)(2,1)S(1)}, u32[]{:S(2)}, u32[]{:S(2)}) collective-permute-start(bf16[1728,128]{1,0:T(8,128)(2,1)S(1)} %constant_dynamic-update-slice_fusion.5.refs_2_), channel_id=1, source_target_pairs={{0,2},{1,3},{2,0},{3,1},{4,6},{5,7},{6,4},{7,5},{8,10},{9,11},{10,... | collective-permute-start | bytes 1327112 | tf_op jit(solution)/shard_map/ppermute | solution.py:379
  125.9 12.7 %collective-permute-start.25 = (bf16[1728,128]{1,0:T(8,128)(2,1)S(1)}, bf16[1728,128]{1,0:T(8,128)(2,1)S(1)}, u32[]{:S(2)}, u32[]{:S(2)}) collective-permute-start(bf16[1728,128]{1,0:T(8,128)(2,1)S(1)} %constant_dynamic-update-slice_fusion.refs_1_), channel_id=1, source_target_pairs={{0,1},{1,0},{2,3},{3,2},{4,5},{5,4},{6,7},{7,6},{8,9},{9,8},{10,11... | collective-permute-start | bytes 1327112 | tf_op jit(solution)/shard_map/ppermute | solution.py:379
  126.0 12.6 %collective-permute-start.23 = (bf16[1728,128]{1,0:T(8,128)(2,1)S(1)}, bf16[1728,128]{1,0:T(8,128)(2,1)S(1)}, u32[]{:S(2)}, u32[]{:S(2)}) collective-permute-start(bf16[1728,128]{1,0:T(8,128)(2,1)S(1)} %constant_dynamic-update-slice_fusion.refs_1_), channel_id=1, source_target_pairs={{0,16},{16,0},{1,17},{17,1},{2,18},{18,2},{3,19},{19,3},{4,20},{20... | collective-permute-start | bytes 1327112 | tf_op jit(solution)/shard_map/ppermute | solution.py:379
  140.6 1.9 %collective-permute-start.27 = (bf16[1728,128]{1,0:T(8,128)(2,1)S(1)}, bf16[1728,128]{1,0:T(8,128)(2,1)S(1)}, u32[]{:S(2)}, u32[]{:S(2)}) collective-permute-start(bf16[1728,128]{1,0:T(8,128)(2,1)S(1)} %collective-permute-done.23.refs_1_), channel_id=1, source_target_pairs={{0,1},{1,0},{2,3},{3,2},{4,5},{5,4},{6,7},{7,6},{8,9},{9,8},{10,11... | collective-permute-start | bytes 1327112 | tf_op jit(solution)/shard_map/ppermute | solution.py:379
  140.7 2.4 %collective-permute-start.28 = (bf16[1728,128]{1,0:T(8,128)(2,1)S(1)}, bf16[1728,128]{1,0:T(8,128)(2,1)S(1)}, u32[]{:S(2)}, u32[]{:S(2)}) collective-permute-start(bf16[1728,128]{1,0:T(8,128)(2,1)S(1)} %collective-permute-done.24.refs_2_), channel_id=1, source_target_pairs={{0,1},{1,0},{2,3},{3,2},{4,5},{5,4},{6,7},{7,6},{8,9},{9,8},{10,11... | collective-permute-start | bytes 1327112 | tf_op jit(solution)/shard_map/ppermute | solution.py:379

commit v6 on v5

--- a/solution.py
+++ b/solution.py
@@ -37,37 +37,32 @@
 def routes():
     out = []
     for i, axis in enumerate(AXES):
-        if lax.axis_size(axis) == 2:
-            out.append(("pair", i))
-        else:
-            out.extend([("up", i), ("down", i)])
+        out.append((0, i))
+        if lax.axis_size(axis) > 2:
+            out.append((1, i))
     return out
 
 
 def exchange(arrays, ways):
     got = []
-    for array, (kind, i) in zip(arrays, ways):
+    for array, (odd, i) in zip(arrays, ways):
         n = lax.axis_size(AXES[i])
-        if kind == "pair":
-            pairs = [(0, 1), (1, 0)]
-        elif kind == "up":
-            pairs = [(j, j + 1) for j in range(n - 1)]
-        else:
-            pairs = [(j + 1, j) for j in range(n - 1)]
+        pairs = [p for j in range(odd, n - 1, 2) for p in ((j, j + 1), (j + 1, j))]
         got.append(lax.ppermute(array, AXES[i], pairs))
     return got
+
+
+def towards(flags, way, lower, upper):
+    odd, i = way
+    return jnp.where(flags[1 + i] == odd, upper, lower)
 
 
 def send_kernel(ways, flags, rows_ref, own_ref, *outs):
     face = rows_ref.shape[2]
     own = own_ref.shape[0]
     places = lax.broadcasted_iota(jnp.int32, (own, face), 0)
-    for out, (kind, i) in zip(outs, ways):
-        lower, upper = rows_ref[2 * i], rows_ref[2 * i + 1]
-        if kind == "pair":
-            rows = jnp.where(flags[1 + i] > 0, lower, upper)
-        else:
-            rows = upper if kind == "up" else lower
+    for out, way in zip(outs, ways):
+        rows = towards(flags, way, rows_ref[2 * way[1]], rows_ref[2 * way[1] + 1])
         out[...] = dot(one_hot(places == rows), own_ref[...], TN).astype(BF)
 
 
@@ -148,18 +143,12 @@
     w_copy.start()
     up_copy.start()
     face = faces[0].shape[0]
-    for came, (kind, i) in zip(faces, ways):
-        low, high = own + 2 * i * face, own + (2 * i + 1) * face
-        if kind == "pair":
-            value = came[...].astype(F32)
-            blank = jnp.zeros_like(value)
-            last = flags[1 + i] > 0
-            ext[pl.ds(low, face), :] = jnp.where(last, value, blank).astype(BF)
-            ext[pl.ds(high, face), :] = jnp.where(last, blank, value).astype(BF)
-        elif kind == "up":
-            ext[pl.ds(low, face), :] = came[...]
-        else:
-            ext[pl.ds(high, face), :] = came[...]
+    for i in range(len(AXES)):
+        mine = [came[...].astype(F32) for came, way in zip(faces, ways) if way[1] == i]
+        mine = mine if len(mine) == 2 else mine + [jnp.zeros_like(mine[0])]
+        even = flags[1 + i] == 0
+        ext[pl.ds(own + 2 * i * face, face), :] = jnp.where(even, mine[1], mine[0]).astype(BF)
+        ext[pl.ds(own + (2 * i + 1) * face, face), :] = jnp.where(even, mine[0], mine[1]).astype(BF)
     own_copy.wait()
     lanes = lax.broadcasted_iota(jnp.int32, (step, rows), 1)
 
@@ -303,13 +292,10 @@
     total = scratch[4]
     face = outs[0].shape[0]
     backward_body(start, 0, count, 3 * face, row_hbm, gp_hbm, w_hbm, None, *scratch)
-    for out, (kind, i) in zip(outs, ways):
-        lower = total[pl.ds(2 * i * face, face), :]
-        upper = total[pl.ds((2 * i + 1) * face, face), :]
-        if kind == "pair":
-            out[...] = jnp.where(flags[1 + i] > 0, lower, upper).astype(BF)
-        else:
-            out[...] = (upper if kind == "up" else lower).astype(BF)
+    for out, way in zip(outs, ways):
+        lower = total[pl.ds(2 * way[1] * face, face), :]
+        upper = total[pl.ds((2 * way[1] + 1) * face, face), :]
+        out[...] = towards(flags, way, lower, upper).astype(BF)
 
 
 def backward_faces(ways, flags, row, gp, weight, face):
@@ -352,12 +338,8 @@
     own = out_ref.shape[0]
     places = lax.broadcasted_iota(jnp.int32, (own, face), 0)
     total = scratch[4][...]
-    for came, (kind, i) in zip(faces, ways):
-        lower, upper = rows_ref[2 * i], rows_ref[2 * i + 1]
-        if kind == "pair":
-            rows = jnp.where(flags[1 + i] > 0, lower, upper)
-        else:
-            rows = lower if kind == "up" else upper
+    for came, way in zip(faces, ways):
+        rows = towards(flags, way, rows_ref[2 * way[1]], rows_ref[2 * way[1] + 1])
         total = total + dot(one_hot(places == rows), came[...])
     out_ref[...] = total.astype(BF)
 
@@ -501,16 +483,15 @@
     taps = weight.shape[0]
     block = 128
     ways = routes()
-    last = [lax.axis_index(a) == lax.axis_size(a) - 1 for a in AXES]
-    flags = jnp.stack([side("gz", 0)] + last).astype(jnp.int32)
+    flags = jnp.stack([side("gz", 0)] + [lax.axis_index(a) & 1 for a in AXES]).astype(jnp.int32)
     faces = exchange(send(ways, flags, sends, own_features), ways)
     col, row = invert(single(in_rows), single(out_rows), single(tap_pair_exists), block)
     activated, gp, keep, give = forward(ways, flags, col, own_features, faces, weight, upstream[0, 0, 0])
     devices = lax.axis_size("gx") * lax.axis_size("gy") * lax.axis_size("gz")
     split = 12
     state = {"turn": 0, "returned": {}}
-    early = [j for j, (_, i) in enumerate(ways) if i != 2]
-    late = [j for j, (_, i) in enumerate(ways) if i == 2]
+    late = [j for j, way in enumerate(ways) if way in ((0, 0), (1, 2))]
+    early = [j for j in range(len(ways)) if j not in late]
 
     def tied(out, work, came):
         held = lax.optimization_barrier((gp, *out))

time: 146 us -> 137 us (0.938)
  starting transfers between devices: 39.4 us -> 34.4 us
  waiting for transfers between devices: 22.8 us -> 19.2 us
    ppermute x10, starting transfers between devices: 19.9 us -> 12.8 us  [exchange(): got.append(lax.ppermute(array, AXES[i], pairs))]
    ppermute x10, waiting for transfers between devices: 9.2 us -> 4.69 us  [exchange(): got.append(lax.ppermute(array, AXES[i], pairs))]
    ppermute x6, starting transfers between devices: 8.11 us -> 10.5 us  [reduce_all(): lax.ppermute(y, 'gy', [(j, (j + s) % n) for j in range(n)])]
    ppermute x6, waiting for transfers between devices: 1.49 us -> 3.44 us  [reduce_all(): lax.ppermute(y, 'gy', [(j, (j + s) % n) for j in range(n)])]
  transfers between devices with their start and end apart: 29 -> 29, of which waited for: 10 -> 10; matrix products, arithmetic and copies ran while one was open for 1% -> 1% of each run, Pallas kernels for 24% -> 25%
where the time goes in v6:
time: 137 us; the launch traced here: 136 us
  Pallas kernels  68.5 us (50%)
  starting transfers between devices  34.4 us (25%)
  waiting for transfers between devices  19.2 us (14%)
  other arithmetic  9.65 us (7%)
  local copies, waits for them, and re-layouts  3.6 us (3%)
    pallas_call x1, Pallas kernels, forward(): pl.pallas_call(lambda *refs: forward_kernel(ways, 256, *refs), in_specs=[...  29.1 us
    pallas_call x1, Pallas kernels, backward_faces(): pl.pallas_call(lambda *refs: faces_kernel(ways, own, taps, *refs), in_spe...  12.8 us
    ppermute x10, starting transfers between devices, exchange(): got.append(lax.ppermute(array, AXES[i], pairs))  12.8 us
    ppermute x13, waiting for transfers between devices, swap(): return lax.ppermute(x, axis, [(j, j ^ 1 << bit) for j in range(n)])  11 us
    ppermute x13, starting transfers between devices, swap(): return lax.ppermute(x, axis, [(j, j ^ 1 << bit) for j in range(n)])  11 us
    ppermute x6, starting transfers between devices, reduce_all(): lax.ppermute(y, 'gy', [(j, (j + s) % n) for j in range(n)])  10.5 us
    pallas_call x1, Pallas kernels, finish(): pl.pallas_call(lambda *refs: finish_kernel(ways, first, count, *refs), in...  10.5 us
    pallas_call x1, Pallas kernels, backward_own(): pl.pallas_call(lambda *refs: own_kernel(first, count, *refs), in_specs=[H...  7.84 us
  transfers between devices with their start and end apart: 29, of which 10 were waited for; matrix products, arithmetic and copies ran while one was open for 1% of the time, Pallas kernels for 25%

profile of v6, /device:TPU:0, one launch (start us, length us, event | category | flops | bytes accessed | tf_op | source)
XLA Modules:
  0.0 136.4 jit_solution(14961700230038322847)
XLA Ops:
  0.6 0.1 fusion.4
  0.7 1.0 copy-done
  1.7 0.7 copy-done.1
  2.4 1.0 send.1
  3.4 3.0 %collective-permute-start = (bf16[96,256]{1,0:T(8,128)(2,1)S(1)}, bf16[96,256]{1,0:T(8,128)(2,1)S(1)}, u32[]{:S(2)}, u32[]{:S(2)}) collective-permute-start(bf16[96,256]{1,0:T(8,128)(2,1)S(1)} %get-tuple-element.55), channel_id=1, source_target_pairs={{0,16},{16,0},{1,17},{17,1},{2,18},{18,2},{3,19},{19,3},{4,20},{20... | collective-permute-start | bytes 147464 | tf_op jit(solution)/shard_map/ppermute | solution.py:51
  6.4 1.6 %collective-permute-start.1 = (bf16[96,256]{1,0:T(8,128)(2,1)S(1)}, bf16[96,256]{1,0:T(8,128)(2,1)S(1)}, u32[]{:S(2)}, u32[]{:S(2)}) collective-permute-start(bf16[96,256]{1,0:T(8,128)(2,1)S(1)} %get-tuple-element.56), channel_id=1, source_target_pairs={{0,4},{4,0},{8,12},{12,8},{1,5},{5,1},{9,13},{13,9},{2,6},{6,2},{1... | collective-permute-start | bytes 147464 | tf_op jit(solution)/shard_map/ppermute | solution.py:51
  8.0 0.7 collective-permute-start.2
  8.7 0.7 collective-permute-start.4
  9.4 3.3 %invert.1 = (f32[27,128,16]{2,1,0:T(8,128)S(1)}, f32[27,16,128]{2,1,0:T(8,128)}) custom-call(s32[27,1,768]{2,1,0:T(1,128)} %bitcast.27, s32[27,1,768]{2,1,0:T(1,128)} %bitcast.28, s32[27,1,768]{2,1,0:T(1,128)} %bitcast.29), custom_call_target="tpu_custom_call" | custom-call | tf_op jit(solution)/shard_map/invert/pallas_call | solution.py:111
  12.7 29.1 %forward.1 = (bf16[768,256]{1,0:T(8,128)(2,1)}, bf16[768,256]{1,0:T(8,128)(2,1)}, f32[6912,128]{1,0:T(8,128)S(1)}, bf16[6912,128]{1,0:T(8,128)(2,1)}) custom-call(s32[4]{0:T(128)S(1)} %get-tuple-element.138.refs_0_, f32[27,128,16]{2,1,0:T(8,128)S(1)} %get-tuple-element.54.refs_1_, bf16[768,256]{1,0:T(8,128)(2,1)} %bitcast.19, bf16[6912,256]{1,0:T(8,128)(2,1)} %bitcast.23, ...), custom_call_target="tpu_custom_call" | custom-call | tf_op jit(solution)/shard_map/forward/pallas_call | solution.py:212
  41.8 2.9 %collective-permute-start.5 = (bf16[6912,128]{1,0:T(8,128)(2,1)}, bf16[6912,128]{1,0:T(8,128)(2,1)}, u32[]{:S(2)}, u32[]{:S(2)}) collective-permute-start(bf16[6912,128]{1,0:T(8,128)(2,1)} %get-tuple-element.64), channel_id=1, source_target_pairs={{0,1},{1,0},{2,3},{3,2},{4,5},{5,4},{6,7},{7,6},{8,9},{9,8},{10,11... | collective-permute-start | bytes 5308424 | tf_op jit(solution)/shard_map/ppermute | solution.py:361
  44.8 3.7 %collective-permute-done.5 = bf16[6912,128]{1,0:T(8,128)(2,1)} collective-permute-done((bf16[6912,128]{1,0:T(8,128)(2,1)}, bf16[6912,128]{1,0:T(8,128)(2,1)}, u32[]{:S(2)}, u32[]{:S(2)}) %collective-permute-start.5) | collective-permute-done | bytes 1769504 | tf_op jit(solution)/shard_map/ppermute | solution.py:361
  48.4 2.3 %add_convert_fusion = (bf16[1728,128]{1,0:T(8,128)(2,1)}, bf16[1728,128]{1,0:T(8,128)(2,1)}) fusion(f32[6912,128]{1,0:T(8,128)S(1)} %get-tuple-element.63, s32[]{:T(128)S(6)} %select_n.140, bf16[6912,128]{1,0:T(8,128)(2,1)} %collective-permute-done.5, s32[]{:T(128)S(6)} %select_n.139), kind=kLoop, calls=%fused_computation | loop fusion | flops 1327104 | bytes 3538952 | tf_op jit(solution)/shard_map/convert_element_type | solution.py:419
  50.7 0.8 collective-permute-start.7
  51.5 0.6 collective-permute-start.6
  52.1 12.8 %backward_faces.1 = (bf16[96,256]{1,0:T(8,128)(2,1)S(1)}, bf16[96,256]{1,0:T(8,128)(2,1)}, bf16[96,256]{1,0:T(8,128)(2,1)}, bf16[96,256]{1,0:T(8,128)(2,1)}, bf16[96,256]{1,0:T(8,128)(2,1)S(1)}) custom-call(s32[4]{0:T(128)S(1)} %get-tuple-element.138.refs_0_, f32[27,16,128]{2,1,0:T(8,128)} %get-tuple-element.61.refs_1_.refs_0_.refs_2_, ...), custom_call_target="tpu_custom_call" | custom-call | tf_op jit(solution)/shard_map/backward_faces/pallas_call | solution.py:304
  65.0 0.6 copy-done.3
  65.6 0.6 copy-done.4
  66.2 2.2 %add_convert_fusion.2 = (bf16[864,128]{1,0:T(8,128)(2,1)}, bf16[864,128]{1,0:T(8,128)(2,1)}) fusion(f32[6912,128]{1,0:T(8,128)S(1)} %get-tuple-element.63, s32[]{:T(128)S(6)} %select_n.144, bf16[1728,128]{1,0:T(8,128)(2,1)} %collective-permute-done.7, s32[]{:T(128)S(6)} %select_n.145, bf16[6912,128]{1,0:T(8,128)(2,1)} %collective-permute-done.5, ...), kind=kLoop, calls=%fused_computation.2 | loop fusion | flops 1105920 | bytes 2211856 | tf_op jit(solution)/shard_map/convert_element_type | solution.py:419
  68.4 1.5 %collective-permute-start.12 = (bf16[864,128]{1,0:T(8,128)(2,1)}, bf16[864,128]{1,0:T(8,128)(2,1)}, u32[]{:S(2)}, u32[]{:S(2)}) collective-permute-start(bf16[864,128]{1,0:T(8,128)(2,1)} %get-tuple-element.113), channel_id=1, source_target_pairs={{0,16},{16,0},{1,17},{17,1},{2,18},{18,2},{3,19},{19,3},{4,20},{20... | collective-permute-start | bytes 663560 | tf_op jit(solution)/shard_map/ppermute | solution.py:361
  69.8 1.2 collective-permute-start.11
  71.1 4.4 %collective-permute-start.8 = (bf16[96,256]{1,0:T(8,128)(2,1)}, bf16[96,256]{1,0:T(8,128)(2,1)}, u32[]{:S(2)}, u32[]{:S(2)}) collective-permute-start(bf16[96,256]{1,0:T(8,128)(2,1)} %get-tuple-element.76), channel_id=1, source_target_pairs={{0,4},{4,0},{8,12},{12,8},{1,5},{5,1},{9,13},{13,9},{2,6},{6,2},{1... | collective-permute-start | bytes 147464 | tf_op jit(solution)/shard_map/ppermute | solution.py:51
  75.5 1.3 collective-permute-start.9
  76.7 1.1 collective-permute-done.8.refs_7_
  77.9 0.4 collective-permute-done.10.refs_9_
  78.3 1.9 %add_convert_fusion.4 = (bf16[216,128]{1,0:T(8,128)(2,1)S(1)}, bf16[216,128]{1,0:T(8,128)(2,1)S(1)}, bf16[216,128]{1,0:T(8,128)(2,1)S(1)}, f32[216,128]{1,0:T(8,128)}) fusion(f32[6912,128]{1,0:T(8,128)S(1)} %get-tuple-element.63, s32[]{:T(128)S(6)} %select_n.165, bf16[864,128]{1,0:T(8,128)(2,1)} %collective-permute-done.12, s32[]{:T(128)S(6)} %select_n.164, ...), kind=kLoop, calls=%fused_computation.14 | loop fusion | flops 746496 | bytes 1382448 | tf_op jit(solution)/shard_map/convert.1
  80.2 1.9 %add_convert_fusion.5 = (bf16[216,128]{1,0:T(8,128)(2,1)S(1)}, bf16[216,128]{1,0:T(8,128)(2,1)S(1)}, bf16[216,128]{1,0:T(8,128)(2,1)S(1)}, f32[216,128]{1,0:T(8,128)}) fusion(f32[6912,128]{1,0:T(8,128)S(1)} %get-tuple-element.63, s32[]{:T(128)S(6)} %select_n.162, bf16[864,128]{1,0:T(8,128)(2,1)} %collective-permute-done.11, s32[]{:T(128)S(6)} %select_n.164, ...), kind=kLoop, calls=%fused_computation.15 | loop fusion | flops 746496 | bytes 1382448 | tf_op jit(solution)/shard_map/convert
  82.0 3.6 %collective-permute-start.15 = (bf16[432,128]{1,0:T(8,128)(2,1)S(1)}, bf16[432,128]{1,0:T(8,128)(2,1)S(1)}, u32[]{:S(2)}, u32[]{:S(2)}) collective-permute-start(bf16[432,128]{1,0:T(8,128)(2,1)S(1)} %pad_maximum_fusion.2), channel_id=1, source_target_pairs={{0,4},{4,8},{8,12},{12,0},{1,5},{5,9},{9,13},{13,1},{2,6},{6,10},{... | collective-permute-start | bytes 331784 | tf_op jit(solution)/shard_map/ppermute | solution.py:427
  85.6 0.1 collective-permute-start.16
  85.7 2.4 %collective-permute-start.17 = (bf16[432,128]{1,0:T(8,128)(2,1)S(1)}, bf16[432,128]{1,0:T(8,128)(2,1)S(1)}, u32[]{:S(2)}, u32[]{:S(2)}) collective-permute-start(bf16[432,128]{1,0:T(8,128)(2,1)S(1)} %pad_maximum_fusion.4), channel_id=1, source_target_pairs={{0,12},{4,0},{8,4},{12,8},{1,13},{5,1},{9,5},{13,9},{2,14},{6,2},{... | collective-permute-start | bytes 331784 | tf_op jit(solution)/shard_map/ppermute | solution.py:427
  88.1 0.5 collective-permute-start.13
  88.6 0.7 collective-permute-start.14
  89.3 3.1 %collective-permute-done.13.refs_6_ = bf16[96,256]{1,0:T(8,128)(2,1)S(1)} collective-permute-done((bf16[96,256]{1,0:T(8,128)(2,1)}, bf16[96,256]{1,0:T(8,128)(2,1)S(1)}, u32[]{:S(2)}, u32[]{:S(2)}) %collective-permute-start.13) | collective-permute-done | bytes 49184 | tf_op jit(solution)/shard_map/ppermute | solution.py:51
  92.4 1.4 %collective-permute-done.16 = bf16[432,128]{1,0:T(8,128)(2,1)S(1)} collective-permute-done((bf16[432,128]{1,0:T(8,128)(2,1)S(1)}, bf16[432,128]{1,0:T(8,128)(2,1)S(1)}, u32[]{:S(2)}, u32[]{:S(2)}) %collective-permute-start.16) | collective-permute-done | bytes 110624 | tf_op jit(solution)/shard_map/ppermute | solution.py:427
  93.8 1.0 fusion.3
  94.9 3.9 %collective-permute-start.20 = (bf16[432,128]{1,0:T(8,128)(2,1)S(1)}, bf16[432,128]{1,0:T(8,128)(2,1)S(1)}, u32[]{:S(2)}, u32[]{:S(2)}) collective-permute-start(bf16[432,128]{1,0:T(8,128)(2,1)S(1)} %fusion.3), channel_id=1, source_target_pairs={{0,12},{4,0},{8,4},{12,8},{1,13},{5,1},{9,5},{13,9},{2,14},{6,2},{... | collective-permute-start | bytes 331784 | tf_op jit(solution)/shard_map/ppermute | solution.py:427
  98.7 0.5 collective-permute-start.19
  99.2 0.2 collective-permute-start.18
  99.4 7.8 %backward_own.1.refs_5_ = f32[768,256]{1,0:T(8,128)} custom-call(f32[27,16,128]{2,1,0:T(8,128)} %get-tuple-element.61.refs_1_.refs_0_.refs_2_, bf16[768,256]{1,0:T(8,128)(2,1)} %get-tuple-element.92.refs_2_.refs_1_.refs_3_, bf16[27,256,256]{2,1,0:T(8,128)(2,1)} %refs_4_.1), custom_call_target="tpu_custom_call" | custom-call | tf_op jit(solution)/shard_map/backward_own/pallas_call | solution.py:323
  107.3 2.0 %collective-permute-done.19 = bf16[432,128]{1,0:T(8,128)(2,1)S(1)} collective-permute-done((bf16[432,128]{1,0:T(8,128)(2,1)S(1)}, bf16[432,128]{1,0:T(8,128)(2,1)S(1)}, u32[]{:S(2)}, u32[]{:S(2)}) %collective-permute-start.19) | collective-permute-done | bytes 110624 | tf_op jit(solution)/shard_map/ppermute | solution.py:427
  109.4 0.6 collective-permute-start.22
  110.0 0.9 collective-permute-start.21
  111.0 0.1 broadcast_add_fusion.4
  111.0 5.0 %collective-permute-done.22 = bf16[864,128]{1,0:T(8,128)(2,1)S(1)} collective-permute-done((bf16[864,128]{1,0:T(8,128)(2,1)S(1)}, bf16[864,128]{1,0:T(8,128)(2,1)S(1)}, u32[]{:S(2)}, u32[]{:S(2)}) %collective-permute-start.22) | collective-permute-done | bytes 221216 | tf_op jit(solution)/shard_map/ppermute | solution.py:361
  116.0 0.1 collective-permute-start.26
  116.1 0.9 collective-permute-start.24
  117.1 0.2 collective-permute-start.25
  117.3 0.7 collective-permute-start.23
  118.0 0.1 broadcast_add_fusion.6
  118.1 0.1 broadcast_add_fusion
  118.2 0.1 add.552
  118.3 0.1 add.547
  118.3 0.1 add_multiply_fusion.2
  118.4 0.1 concatenate.62.refs_0_
  118.5 10.5 %finish.1 = bf16[768,256]{1,0:T(8,128)(2,1)} custom-call(s32[4]{0:T(128)S(1)} %get-tuple-element.138.refs_0_, s32[6,1,96]{2,1,0:T(1,128)S(1)} %bitcast.22, f32[27,16,128]{2,1,0:T(8,128)} %get-tuple-element.61.refs_1_.refs_0_.refs_2_, bf16[768,256]{1,0:T(8,128)(2,1)} %get-tuple-element.92.refs_2_.refs_1_.refs_3_, bf16[27,256,256]{2,1,0:T(8,128)(2,1)} %refs_4_.1, ...), custom_call_target="tpu_custom_call" | custom-call | tf_op jit(solution)/shard_map/finish/pallas_call | solution.py:348
  129.0 0.7 collective-permute-done.23.refs_1_
  129.7 2.0 %place.2.refs_5_ = bf16[6912,256]{1,0:T(8,128)(2,1)} custom-call(s32[36]{0:T(128)S(1)} %concatenate.62.refs_0_, bf16[1728,128]{1,0:T(8,128)(2,1)S(1)} %constant_dynamic-update-slice_fusion.refs_1_, bf16[1728,128]{1,0:T(8,128)(2,1)S(1)} %constant_dynamic-update-slice_fusion.5.refs_2_, bf16[1728,128]{1,0:T(8,128)(2,1)S(1)} %collective-permute-done.25.refs_3_, ...), custom_call_target="tpu_custom_call" | custom-call | tf_op jit(solution)/shard_map/place/pallas_call | solution.py:388
  131.8 0.5 collective-permute-start.28
  132.3 0.1 add.542
  132.4 0.1 add.536
  132.5 0.1 concatenate.61.refs_0_
  132.6 1.0 collective-permute-done.27.refs_3_
  133.6 0.6 collective-permute-done.28.refs_4_
  134.2 2.0 %place.3 = bf16[6912,256]{1,0:T(8,128)(2,1)} custom-call(s32[36]{0:T(128)S(1)} %concatenate.61.refs_0_, bf16[1728,128]{1,0:T(8,128)(2,1)S(1)} %collective-permute-done.23.refs_1_, bf16[1728,128]{1,0:T(8,128)(2,1)S(1)} %collective-permute-done.24.refs_2_, bf16[1728,128]{1,0:T(8,128)(2,1)S(1)} %collective-permute-done.27.refs_3_, ...), custom_call_target="tpu_custom_call", output_to_operand_aliasing={{}: (5, {})} | custom-call | tf_op jit(solution)/shard_map/place/pallas_call | solution.py:388
  (39 shorter events, 0.5 us)
Async XLA Ops:
  0.7 1.0 copy-start
  1.7 0.7 copy-start.1
  3.4 9.3 %collective-permute-start = (bf16[96,256]{1,0:T(8,128)(2,1)S(1)}, bf16[96,256]{1,0:T(8,128)(2,1)S(1)}, u32[]{:S(2)}, u32[]{:S(2)}) collective-permute-start(bf16[96,256]{1,0:T(8,128)(2,1)S(1)} %get-tuple-element.55), channel_id=1, source_target_pairs={{0,16},{16,0},{1,17},{17,1},{2,18},{18,2},{3,19},{19,3},{4,20},{20... | collective-permute-start | bytes 147464 | tf_op jit(solution)/shard_map/ppermute | solution.py:51
  6.4 6.3 %collective-permute-start.1 = (bf16[96,256]{1,0:T(8,128)(2,1)S(1)}, bf16[96,256]{1,0:T(8,128)(2,1)S(1)}, u32[]{:S(2)}, u32[]{:S(2)}) collective-permute-start(bf16[96,256]{1,0:T(8,128)(2,1)S(1)} %get-tuple-element.56), channel_id=1, source_target_pairs={{0,4},{4,0},{8,12},{12,8},{1,5},{5,1},{9,13},{13,9},{2,6},{6,2},{1... | collective-permute-start | bytes 147464 | tf_op jit(solution)/shard_map/ppermute | solution.py:51
  8.0 4.7 %collective-permute-start.2 = (bf16[96,256]{1,0:T(8,128)(2,1)S(1)}, bf16[96,256]{1,0:T(8,128)(2,1)S(1)}, u32[]{:S(2)}, u32[]{:S(2)}) collective-permute-start(bf16[96,256]{1,0:T(8,128)(2,1)S(1)} %get-tuple-element.57), channel_id=1, source_target_pairs={{4,8},{8,4},{5,9},{9,5},{6,10},{10,6},{7,11},{11,7},{20,24},{24,20... | collective-permute-start | bytes 147464 | tf_op jit(solution)/shard_map/ppermute | solution.py:51
  8.6 4.1 %collective-permute-start.3 = (bf16[96,256]{1,0:T(8,128)(2,1)S(1)}, bf16[96,256]{1,0:T(8,128)(2,1)S(1)}, u32[]{:S(2)}, u32[]{:S(2)}) collective-permute-start(bf16[96,256]{1,0:T(8,128)(2,1)S(1)} %get-tuple-element.58), channel_id=1, source_target_pairs={{0,1},{1,0},{2,3},{3,2},{4,5},{5,4},{6,7},{7,6},{8,9},{9,8},{10,11... | collective-permute-start | bytes 147464 | tf_op jit(solution)/shard_map/ppermute | solution.py:51
  8.7 4.0 %collective-permute-start.4 = (bf16[96,256]{1,0:T(8,128)(2,1)S(1)}, bf16[96,256]{1,0:T(8,128)(2,1)S(1)}, u32[]{:S(2)}, u32[]{:S(2)}) collective-permute-start(bf16[96,256]{1,0:T(8,128)(2,1)S(1)} %get-tuple-element.59), channel_id=1, source_target_pairs={{1,2},{2,1},{5,6},{6,5},{9,10},{10,9},{13,14},{14,13},{17,18},{18,... | collective-permute-start | bytes 147464 | tf_op jit(solution)/shard_map/ppermute | solution.py:51
  41.8 6.6 %collective-permute-start.5 = (bf16[6912,128]{1,0:T(8,128)(2,1)}, bf16[6912,128]{1,0:T(8,128)(2,1)}, u32[]{:S(2)}, u32[]{:S(2)}) collective-permute-start(bf16[6912,128]{1,0:T(8,128)(2,1)} %get-tuple-element.64), channel_id=1, source_target_pairs={{0,1},{1,0},{2,3},{3,2},{4,5},{5,4},{6,7},{7,6},{8,9},{9,8},{10,11... | collective-permute-start | bytes 5308424 | tf_op jit(solution)/shard_map/ppermute | solution.py:361
  50.7 15.5 %collective-permute-start.7 = (bf16[1728,128]{1,0:T(8,128)(2,1)}, bf16[1728,128]{1,0:T(8,128)(2,1)}, u32[]{:S(2)}, u32[]{:S(2)}) collective-permute-start(bf16[1728,128]{1,0:T(8,128)(2,1)} %get-tuple-element.115), channel_id=1, source_target_pairs={{0,2},{1,3},{2,0},{3,1},{4,6},{5,7},{6,4},{7,5},{8,10},{9,11},{10,... | collective-permute-start | bytes 1327112 | tf_op jit(solution)/shard_map/ppermute | solution.py:361
  51.5 14.6 %collective-permute-start.6 = (bf16[1728,128]{1,0:T(8,128)(2,1)}, bf16[1728,128]{1,0:T(8,128)(2,1)}, u32[]{:S(2)}, u32[]{:S(2)}) collective-permute-start(bf16[1728,128]{1,0:T(8,128)(2,1)} %get-tuple-element.116), channel_id=1, source_target_pairs={{0,16},{16,0},{1,17},{17,1},{2,18},{18,2},{3,19},{19,3},{4,20},{20... | collective-permute-start | bytes 1327112 | tf_op jit(solution)/shard_map/ppermute | solution.py:361
  64.9 0.6 copy-start.3
  65.6 0.6 copy-start.4
  68.4 9.9 %collective-permute-start.12 = (bf16[864,128]{1,0:T(8,128)(2,1)}, bf16[864,128]{1,0:T(8,128)(2,1)}, u32[]{:S(2)}, u32[]{:S(2)}) collective-permute-start(bf16[864,128]{1,0:T(8,128)(2,1)} %get-tuple-element.113), channel_id=1, source_target_pairs={{0,16},{16,0},{1,17},{17,1},{2,18},{18,2},{3,19},{19,3},{4,20},{20... | collective-permute-start | bytes 663560 | tf_op jit(solution)/shard_map/ppermute | solution.py:361
  69.8 8.5 %collective-permute-start.11 = (bf16[864,128]{1,0:T(8,128)(2,1)}, bf16[864,128]{1,0:T(8,128)(2,1)}, u32[]{:S(2)}, u32[]{:S(2)}) collective-permute-start(bf16[864,128]{1,0:T(8,128)(2,1)} %get-tuple-element.114), channel_id=1, source_target_pairs={{0,2},{1,3},{2,0},{3,1},{4,6},{5,7},{6,4},{7,5},{8,10},{9,11},{10,... | collective-permute-start | bytes 663560 | tf_op jit(solution)/shard_map/ppermute | solution.py:361
  71.1 6.8 %collective-permute-start.8 = (bf16[96,256]{1,0:T(8,128)(2,1)}, bf16[96,256]{1,0:T(8,128)(2,1)}, u32[]{:S(2)}, u32[]{:S(2)}) collective-permute-start(bf16[96,256]{1,0:T(8,128)(2,1)} %get-tuple-element.76), channel_id=1, source_target_pairs={{0,4},{4,0},{8,12},{12,8},{1,5},{5,1},{9,13},{13,9},{2,6},{6,2},{1... | collective-permute-start | bytes 147464 | tf_op jit(solution)/shard_map/ppermute | solution.py:51
  75.5 2.4 %collective-permute-start.9 = (bf16[96,256]{1,0:T(8,128)(2,1)}, bf16[96,256]{1,0:T(8,128)(2,1)}, u32[]{:S(2)}, u32[]{:S(2)}) collective-permute-start(bf16[96,256]{1,0:T(8,128)(2,1)} %get-tuple-element.77), channel_id=1, source_target_pairs={{4,8},{8,4},{5,9},{9,5},{6,10},{10,6},{7,11},{11,7},{20,24},{24,20... | collective-permute-start | bytes 147464 | tf_op jit(solution)/shard_map/ppermute | solution.py:51
  76.7 1.6 %collective-permute-start.10 = (bf16[96,256]{1,0:T(8,128)(2,1)}, bf16[96,256]{1,0:T(8,128)(2,1)}, u32[]{:S(2)}, u32[]{:S(2)}) collective-permute-start(bf16[96,256]{1,0:T(8,128)(2,1)} %get-tuple-element.78), channel_id=1, source_target_pairs={{0,1},{1,0},{2,3},{3,2},{4,5},{5,4},{6,7},{7,6},{8,9},{9,8},{10,11... | collective-permute-start | bytes 147464 | tf_op jit(solution)/shard_map/ppermute | solution.py:51
  82.0 10.4 %collective-permute-start.15 = (bf16[432,128]{1,0:T(8,128)(2,1)S(1)}, bf16[432,128]{1,0:T(8,128)(2,1)S(1)}, u32[]{:S(2)}, u32[]{:S(2)}) collective-permute-start(bf16[432,128]{1,0:T(8,128)(2,1)S(1)} %pad_maximum_fusion.2), channel_id=1, source_target_pairs={{0,4},{4,8},{8,12},{12,0},{1,5},{5,9},{9,13},{13,1},{2,6},{6,10},{... | collective-permute-start | bytes 331784 | tf_op jit(solution)/shard_map/ppermute | solution.py:427
  85.6 8.2 %collective-permute-start.16 = (bf16[432,128]{1,0:T(8,128)(2,1)S(1)}, bf16[432,128]{1,0:T(8,128)(2,1)S(1)}, u32[]{:S(2)}, u32[]{:S(2)}) collective-permute-start(bf16[432,128]{1,0:T(8,128)(2,1)S(1)} %pad_maximum_fusion.3), channel_id=1, source_target_pairs={{0,8},{4,12},{8,0},{12,4},{1,9},{5,13},{9,1},{13,5},{2,10},{6,14},... | collective-permute-start | bytes 331784 | tf_op jit(solution)/shard_map/ppermute | solution.py:427
  85.7 8.1 %collective-permute-start.17 = (bf16[432,128]{1,0:T(8,128)(2,1)S(1)}, bf16[432,128]{1,0:T(8,128)(2,1)S(1)}, u32[]{:S(2)}, u32[]{:S(2)}) collective-permute-start(bf16[432,128]{1,0:T(8,128)(2,1)S(1)} %pad_maximum_fusion.4), channel_id=1, source_target_pairs={{0,12},{4,0},{8,4},{12,8},{1,13},{5,1},{9,5},{13,9},{2,14},{6,2},{... | collective-permute-start | bytes 331784 | tf_op jit(solution)/shard_map/ppermute | solution.py:427
  88.1 4.3 %collective-permute-start.13 = (bf16[96,256]{1,0:T(8,128)(2,1)}, bf16[96,256]{1,0:T(8,128)(2,1)S(1)}, u32[]{:S(2)}, u32[]{:S(2)}) collective-permute-start(bf16[96,256]{1,0:T(8,128)(2,1)} %copy-done.4), channel_id=1, source_target_pairs={{0,16},{16,0},{1,17},{17,1},{2,18},{18,2},{3,19},{19,3},{4,20},{20... | collective-permute-start | bytes 147464 | tf_op jit(solution)/shard_map/ppermute | solution.py:51
  88.6 3.8 %collective-permute-start.14 = (bf16[96,256]{1,0:T(8,128)(2,1)}, bf16[96,256]{1,0:T(8,128)(2,1)S(1)}, u32[]{:S(2)}, u32[]{:S(2)}) collective-permute-start(bf16[96,256]{1,0:T(8,128)(2,1)} %copy-done.3), channel_id=1, source_target_pairs={{1,2},{2,1},{5,6},{6,5},{9,10},{10,9},{13,14},{14,13},{17,18},{18,... | collective-permute-start | bytes 147464 | tf_op jit(solution)/shard_map/ppermute | solution.py:51
  94.9 12.4 %collective-permute-start.20 = (bf16[432,128]{1,0:T(8,128)(2,1)S(1)}, bf16[432,128]{1,0:T(8,128)(2,1)S(1)}, u32[]{:S(2)}, u32[]{:S(2)}) collective-permute-start(bf16[432,128]{1,0:T(8,128)(2,1)S(1)} %fusion.3), channel_id=1, source_target_pairs={{0,12},{4,0},{8,4},{12,8},{1,13},{5,1},{9,5},{13,9},{2,14},{6,2},{... | collective-permute-start | bytes 331784 | tf_op jit(solution)/shard_map/ppermute | solution.py:427
  98.7 10.5 %collective-permute-start.19 = (bf16[432,128]{1,0:T(8,128)(2,1)S(1)}, bf16[432,128]{1,0:T(8,128)(2,1)S(1)}, u32[]{:S(2)}, u32[]{:S(2)}) collective-permute-start(bf16[432,128]{1,0:T(8,128)(2,1)S(1)} %fusion.3), channel_id=1, source_target_pairs={{0,8},{4,12},{8,0},{12,4},{1,9},{5,13},{9,1},{13,5},{2,10},{6,14},... | collective-permute-start | bytes 331784 | tf_op jit(solution)/shard_map/ppermute | solution.py:427
  99.2 10.1 %collective-permute-start.18 = (bf16[432,128]{1,0:T(8,128)(2,1)S(1)}, bf16[432,128]{1,0:T(8,128)(2,1)S(1)}, u32[]{:S(2)}, u32[]{:S(2)}) collective-permute-start(bf16[432,128]{1,0:T(8,128)(2,1)S(1)} %fusion.3), channel_id=1, source_target_pairs={{0,4},{4,8},{8,12},{12,0},{1,5},{5,9},{9,13},{13,1},{2,6},{6,10},{... | collective-permute-start | bytes 331784 | tf_op jit(solution)/shard_map/ppermute | solution.py:427
  99.4 19.1 %copy-start.2 = (s32[1,1,1,6,96]{4,2,3,1,0:T(1,128)S(1)}, s32[1,1,1,6,96]{4,2,3,1,0:T(1,128)}, u32[]{:S(2)}) copy-start(s32[1,1,1,6,96]{4,2,3,1,0:T(1,128)} %param.10) | copy-start | bytes 6916
  109.4 6.6 %collective-permute-start.22 = (bf16[864,128]{1,0:T(8,128)(2,1)S(1)}, bf16[864,128]{1,0:T(8,128)(2,1)S(1)}, u32[]{:S(2)}, u32[]{:S(2)}) collective-permute-start(bf16[864,128]{1,0:T(8,128)(2,1)S(1)} %pad_maximum_fusion.1), channel_id=1, source_target_pairs={{0,16},{16,0},{1,17},{17,1},{2,18},{18,2},{3,19},{19,3},{4,20},{20... | collective-permute-start | bytes 663560 | tf_op jit(solution)/shard_map/ppermute | solution.py:361
  110.0 7.0 %collective-permute-start.21 = (bf16[864,128]{1,0:T(8,128)(2,1)S(1)}, bf16[864,128]{1,0:T(8,128)(2,1)S(1)}, u32[]{:S(2)}, u32[]{:S(2)}) collective-permute-start(bf16[864,128]{1,0:T(8,128)(2,1)S(1)} %pad_maximum_fusion), channel_id=1, source_target_pairs={{0,2},{1,3},{2,0},{3,1},{4,6},{5,7},{6,4},{7,5},{8,10},{9,11},{10,... | collective-permute-start | bytes 663560 | tf_op jit(solution)/shard_map/ppermute | solution.py:361
  116.0 13.7 %collective-permute-start.26 = (bf16[1728,128]{1,0:T(8,128)(2,1)S(1)}, bf16[1728,128]{1,0:T(8,128)(2,1)S(1)}, u32[]{:S(2)}, u32[]{:S(2)}) collective-permute-start(bf16[1728,128]{1,0:T(8,128)(2,1)S(1)} %constant_dynamic-update-slice_fusion.5.refs_2_), channel_id=1, source_target_pairs={{0,1},{1,0},{2,3},{3,2},{4,5},{5,4},{6,7},{7,6},{8,9},{9,8},{10,11... | collective-permute-start | bytes 1327112 | tf_op jit(solution)/shard_map/ppermute | solution.py:361
  116.1 12.9 %collective-permute-start.24 = (bf16[1728,128]{1,0:T(8,128)(2,1)S(1)}, bf16[1728,128]{1,0:T(8,128)(2,1)S(1)}, u32[]{:S(2)}, u32[]{:S(2)}) collective-permute-start(bf16[1728,128]{1,0:T(8,128)(2,1)S(1)} %constant_dynamic-update-slice_fusion.5.refs_2_), channel_id=1, source_target_pairs={{0,2},{1,3},{2,0},{3,1},{4,6},{5,7},{6,4},{7,5},{8,10},{9,11},{10,... | collective-permute-start | bytes 1327112 | tf_op jit(solution)/shard_map/ppermute | solution.py:361
  117.1 12.7 %collective-permute-start.25 = (bf16[1728,128]{1,0:T(8,128)(2,1)S(1)}, bf16[1728,128]{1,0:T(8,128)(2,1)S(1)}, u32[]{:S(2)}, u32[]{:S(2)}) collective-permute-start(bf16[1728,128]{1,0:T(8,128)(2,1)S(1)} %constant_dynamic-update-slice_fusion.refs_1_), channel_id=1, source_target_pairs={{0,1},{1,0},{2,3},{3,2},{4,5},{5,4},{6,7},{7,6},{8,9},{9,8},{10,11... | collective-permute-start | bytes 1327112 | tf_op jit(solution)/shard_map/ppermute | solution.py:361
  117.3 12.4 %collective-permute-start.23 = (bf16[1728,128]{1,0:T(8,128)(2,1)S(1)}, bf16[1728,128]{1,0:T(8,128)(2,1)S(1)}, u32[]{:S(2)}, u32[]{:S(2)}) collective-permute-start(bf16[1728,128]{1,0:T(8,128)(2,1)S(1)} %constant_dynamic-update-slice_fusion.refs_1_), channel_id=1, source_target_pairs={{0,16},{16,0},{1,17},{17,1},{2,18},{18,2},{3,19},{19,3},{4,20},{20... | collective-permute-start | bytes 1327112 | tf_op jit(solution)/shard_map/ppermute | solution.py:361
  131.7 1.9 %collective-permute-start.27 = (bf16[1728,128]{1,0:T(8,128)(2,1)S(1)}, bf16[1728,128]{1,0:T(8,128)(2,1)S(1)}, u32[]{:S(2)}, u32[]{:S(2)}) collective-permute-start(bf16[1728,128]{1,0:T(8,128)(2,1)S(1)} %collective-permute-done.23.refs_1_), channel_id=1, source_target_pairs={{0,1},{1,0},{2,3},{3,2},{4,5},{5,4},{6,7},{7,6},{8,9},{9,8},{10,11... | collective-permute-start | bytes 1327112 | tf_op jit(solution)/shard_map/ppermute | solution.py:361
  131.8 2.4 %collective-permute-start.28 = (bf16[1728,128]{1,0:T(8,128)(2,1)S(1)}, bf16[1728,128]{1,0:T(8,128)(2,1)S(1)}, u32[]{:S(2)}, u32[]{:S(2)}) collective-permute-start(bf16[1728,128]{1,0:T(8,128)(2,1)S(1)} %collective-permute-done.24.refs_2_), channel_id=1, source_target_pairs={{0,1},{1,0},{2,3},{3,2},{4,5},{5,4},{6,7},{7,6},{8,9},{9,8},{10,11... | collective-permute-start | bytes 1327112 | tf_op jit(solution)/shard_map/ppermute | solution.py:361

commit v7 on v6

--- a/solution.py
+++ b/solution.py
@@ -43,6 +43,15 @@
     return out
 
 
+def slots():
+    out, count = [], 0
+    for axis in AXES:
+        size = 1 if lax.axis_size(axis) == 2 else 2
+        out.append(tuple(range(count, count + size)))
+        count += size
+    return out, count
+
+
 def exchange(arrays, ways):
     got = []
     for array, (odd, i) in zip(arrays, ways):
@@ -57,7 +66,16 @@
     return jnp.where(flags[1 + i] == odd, upper, lower)
 
 
-def send_kernel(ways, flags, rows_ref, own_ref, *outs):
+def send_kernel(ways, flags, rows_hbm, own_hbm, *rest):
+    outs, (rows_ref, own_ref, sems) = rest[: len(ways)], rest[len(ways) :]
+    copies = [
+        pltpu.make_async_copy(own_hbm, own_ref, sems.at[0]),
+        pltpu.make_async_copy(rows_hbm, rows_ref, sems.at[1]),
+    ]
+    for copy in copies:
+        copy.start()
+    for copy in copies:
+        copy.wait()
     face = rows_ref.shape[2]
     own = own_ref.shape[0]
     places = lax.broadcasted_iota(jnp.int32, (own, face), 0)
@@ -70,15 +88,20 @@
     shape = jax.ShapeDtypeStruct((rows.shape[2], own_features.shape[1]), BF)
     return pl.pallas_call(
         lambda *refs: send_kernel(ways, *refs),
-        in_specs=[SMEM, VMEM, VMEM],
+        in_specs=[SMEM, HBM, HBM],
         out_specs=[VMEM] * len(ways),
         out_shape=[shape] * len(ways),
+        scratch_shapes=[
+            pltpu.VMEM(rows.shape, jnp.int32),
+            pltpu.VMEM(own_features.shape, BF),
+            pltpu.SemaphoreType.DMA((2,)),
+        ],
         compiler_params=params(8),
         name="send",
-    )(flags, rows, own_features)
-
-
-def invert_kernel(block, in_hbm, out_hbm, live_hbm, col_ref, row_hbm, tables, row_ref, sems):
+    )(flags, hold(rows), hold(own_features))
+
+
+def invert_kernel(block, face, pairs, flags, in_hbm, out_hbm, live_hbm, col_ref, row_hbm, tables, row_ref, sems):
     copies = [
         pltpu.make_async_copy(hbm, tables.at[j], sems.at[j])
         for j, hbm in enumerate((in_hbm, out_hbm, live_hbm))
@@ -92,7 +115,14 @@
         copy.wait()
     for k in range(taps):
         target = tables[1, k]
-        source = jnp.where(tables[2, k] > 0, tables[0, k], MISSING)
+        source = tables[0, k]
+        live = tables[2, k] > 0
+        for i in pairs:
+            dead = own + (2 * i + flags[1 + i]) * face
+            beyond = source >= dead + face
+            live = jnp.logical_and(live, jnp.logical_or(beyond, source < dead))
+            source = jnp.where(beyond, source - face, source)
+        source = jnp.where(live, source, MISSING)
         high = target // block
         hot = one_hot(lows == target - high * block)
         big = (source // 16) * 16
@@ -106,11 +136,12 @@
     copy.wait()
 
 
-def invert(in_rows, out_rows, live, block):
+def invert(flags, in_rows, out_rows, live, face, block):
+    pairs = [i for i in reversed(range(len(AXES))) if lax.axis_size(AXES[i]) == 2]
     taps, _, own = in_rows.shape
     return pl.pallas_call(
-        lambda *refs: invert_kernel(block, *refs),
-        in_specs=[HBM, HBM, HBM],
+        lambda *refs: invert_kernel(block, face, pairs, *refs),
+        in_specs=[SMEM, HBM, HBM, HBM],
         out_specs=[VMEM, HBM],
         out_shape=(
             jax.ShapeDtypeStruct((taps, block, 16), F32),
@@ -123,13 +154,13 @@
         ],
         compiler_params=params(12),
         name="invert",
-    )(hold(in_rows), hold(out_rows), hold(live))
-
-
-def forward_kernel(ways, step, flags, col_ref, own_hbm, w_hbm, up_hbm, *rest):
+    )(flags, hold(in_rows), hold(out_rows), hold(live))
+
+
+def forward_kernel(ways, where, step, flags, col_ref, own_hbm, w_hbm, up_hbm, *rest):
     faces = rest[: len(ways)]
-    act_hbm, gp_hbm, keep_hbm, give_hbm = rest[len(ways) : len(ways) + 4]
-    ext, got, got_t, weights, turned, up, act, gp, keep, give, sems = rest[len(ways) + 4 :]
+    act_hbm, gp_hbm, keep_hbm, *give_hbm = rest[len(ways) : len(ways) + 5]
+    ext, got, got_t, weights, turned, up, act, gp, keep, give, sems = rest[len(ways) + 5 :]
     taps = col_ref.shape[0]
     own, ch = up.shape
     rows = ext.shape[0]
@@ -143,12 +174,14 @@
     w_copy.start()
     up_copy.start()
     face = faces[0].shape[0]
-    for i in range(len(AXES)):
-        mine = [came[...].astype(F32) for came, way in zip(faces, ways) if way[1] == i]
-        mine = mine if len(mine) == 2 else mine + [jnp.zeros_like(mine[0])]
-        even = flags[1 + i] == 0
-        ext[pl.ds(own + 2 * i * face, face), :] = jnp.where(even, mine[1], mine[0]).astype(BF)
-        ext[pl.ds(own + (2 * i + 1) * face, face), :] = jnp.where(even, mine[0], mine[1]).astype(BF)
+    for i, places in enumerate(where):
+        mine = [came[...] for came, way in zip(faces, ways) if way[1] == i]
+        if len(places) == 2:
+            mine = [value.astype(F32) for value in mine]
+            even = flags[1 + i] == 0
+            mine = [jnp.where(even, mine[1], mine[0]).astype(BF), jnp.where(even, mine[0], mine[1]).astype(BF)]
+        for place, value in zip(places, mine):
+            ext[pl.ds(own + place * face, face), :] = value
     own_copy.wait()
     lanes = lax.broadcasted_iota(jnp.int32, (step, rows), 1)
 
@@ -192,12 +225,13 @@
         give[pl.ds(at, ch), :] = r[:, half:].astype(BF)
         return carried
 
-    bounds = [0, 9, 18, taps] if taps > 18 else [0, taps]
-    for j in range(len(bounds) - 1):
-        lax.fori_loop(bounds[j], bounds[j + 1], one, 0, unroll=3)
-        part = pl.ds(bounds[j] * ch, (bounds[j + 1] - bounds[j]) * ch)
-        for source, target, sem in ((give, give_hbm, 5 + j), (keep, keep_hbm, 8 + j)):
-            copy = pltpu.make_async_copy(source.at[part, :], target.at[part, :], sems.at[sem])
+    middle = taps * ch // 2
+    bounds = [0, (taps + 1) // 2, taps]
+    for j in range(2):
+        lax.fori_loop(bounds[j], bounds[j + 1], one, 0, unroll=2)
+        part = pl.ds(j * middle, middle)
+        for source, target, sem in ((give, give_hbm[j], 5 + j), (keep, keep_hbm.at[part, :], 7 + j)):
+            copy = pltpu.make_async_copy(source.at[part, :], target, sems.at[sem])
             copy.start()
             out_copies.append(copy)
     for copy in out_copies:
@@ -207,17 +241,19 @@
 def forward(ways, flags, col, own_features, faces, weight, upstream):
     taps, block, _ = col.shape
     own, ch = own_features.shape
-    rows = own + 6 * faces[0].shape[0]
+    where, faced = slots()
+    rows = own + faced * faces[0].shape[0]
     like = jax.ShapeDtypeStruct
     return pl.pallas_call(
-        lambda *refs: forward_kernel(ways, 256, *refs),
+        lambda *refs: forward_kernel(ways, where, 256, *refs),
         in_specs=[SMEM, VMEM, HBM, HBM, HBM] + [VMEM] * len(faces),
-        out_specs=[HBM, HBM, ANY, ANY],
+        out_specs=[HBM, HBM, ANY, ANY, ANY],
         out_shape=[
             pltpu.HBM((own, ch), BF),
             pltpu.HBM((own, ch), BF),
             like((taps * ch, ch // 2), F32),
-            like((taps * ch, ch // 2), BF),
+            like((taps * ch // 2, ch // 2), BF),
+            like((taps * ch // 2, ch // 2), BF),
         ],
         scratch_shapes=[
             pltpu.VMEM((rows, ch), BF),
@@ -287,73 +323,96 @@
     ]
 
 
-def faces_kernel(ways, start, count, flags, row_hbm, gp_hbm, w_hbm, *rest):
-    outs, scratch = rest[: len(ways)], rest[len(ways) :]
+def faces_kernel(ways, where, start, count, flags, row_hbm, gp_hbm, w_hbm, *rest):
+    outs, staged, sems, scratch = rest[: len(ways)], rest[len(ways)], rest[len(ways) + 1], rest[len(ways) + 2 :]
     total = scratch[4]
     face = outs[0].shape[0]
-    backward_body(start, 0, count, 3 * face, row_hbm, gp_hbm, w_hbm, None, *scratch)
-    for out, way in zip(outs, ways):
-        lower = total[pl.ds(2 * way[1] * face, face), :]
-        upper = total[pl.ds((2 * way[1] + 1) * face, face), :]
-        out[...] = towards(flags, way, lower, upper).astype(BF)
+    backward_body(start, 0, count, total.shape[0] // 2, row_hbm, gp_hbm, w_hbm, None, *scratch)
+    copies = []
+    for j, way in enumerate(ways):
+        values = [total[pl.ds(place * face, face), :] for place in where[way[1]]]
+        value = towards(flags, way, *values) if len(values) == 2 else values[0]
+        staged[j] = value.astype(BF)
+        copies.append(pltpu.make_async_copy(staged.at[j], outs[j], sems.at[j]))
+        copies[-1].start()
+    for copy in copies:
+        copy.wait()
 
 
 def backward_faces(ways, flags, row, gp, weight, face):
     taps = row.shape[0]
     own, ch = gp.shape
+    where, faced = slots()
     return pl.pallas_call(
-        lambda *refs: faces_kernel(ways, own, taps, *refs),
+        lambda *refs: faces_kernel(ways, where, own, taps, *refs),
         in_specs=[SMEM, HBM, HBM, HBM],
-        out_specs=[VMEM] * len(ways),
-        out_shape=[jax.ShapeDtypeStruct((face, ch), BF)] * len(ways),
-        scratch_shapes=backward_scratch(row, gp, 6 * face, taps),
+        out_specs=[HBM] * len(ways),
+        out_shape=[pltpu.HBM((face, ch), BF)] * len(ways),
+        scratch_shapes=[pltpu.VMEM((len(ways), face, ch), BF), pltpu.SemaphoreType.DMA((len(ways),))]
+        + backward_scratch(row, gp, faced * face, taps),
         compiler_params=params(18),
         name="backward_faces",
     )(flags, hold(row), hold(gp), hold(weight))
 
 
-def own_kernel(first, count, row_hbm, gp_hbm, w_hbm, out_hbm, *scratch):
-    backward_body(0, first, count, 384, row_hbm, gp_hbm, w_hbm, None, *scratch)
+def own_kernel(first, count, row_hbm, gp_hbm, w_hbm, *rest):
+    *before, out_hbm = rest[:-6]
+    scratch = rest[-6:]
+    backward_body(0, first, count, 384, row_hbm, gp_hbm, w_hbm, before[0] if before else None, *scratch)
     copy = pltpu.make_async_copy(scratch[4], out_hbm, scratch[5].at[2])
     copy.start()
     copy.wait()
 
 
-def backward_own(row, gp, weight, first, count):
+def backward_own(row, gp, weight, first, count, before):
+    args = [row, gp, weight] + before
     return pl.pallas_call(
         lambda *refs: own_kernel(first, count, *refs),
-        in_specs=[HBM, HBM, HBM],
+        in_specs=[HBM] * len(args),
         out_specs=HBM,
         out_shape=pltpu.HBM(gp.shape, F32),
         scratch_shapes=backward_scratch(row, gp, gp.shape[0], count),
         compiler_params=params(14),
         name="backward_own",
-    )(hold(row), hold(gp), hold(weight))
-
-
-def finish_kernel(ways, first, count, flags, rows_ref, row_hbm, gp_hbm, w_hbm, before_hbm, *rest):
-    faces, out_ref, scratch = rest[: len(ways)], rest[len(ways)], rest[len(ways) + 1 :]
+    )(*[hold(x) for x in args])
+
+
+def finish_kernel(ways, first, count, flags, rows_hbm, row_hbm, gp_hbm, w_hbm, before_hbm, *rest):
+    faces_hbm, out_ref, rows_ref, faces, sems = rest[: len(ways)], *rest[len(ways) : len(ways) + 4]
+    scratch = rest[len(ways) + 4 :]
+    copies = [pltpu.make_async_copy(rows_hbm, rows_ref, sems.at[len(ways)])]
+    for j in range(len(ways)):
+        copies.append(pltpu.make_async_copy(faces_hbm[j], faces.at[j], sems.at[j]))
+    for copy in copies:
+        copy.start()
     backward_body(0, first, count, 384, row_hbm, gp_hbm, w_hbm, before_hbm, *scratch)
     face = rows_ref.shape[2]
     own = out_ref.shape[0]
     places = lax.broadcasted_iota(jnp.int32, (own, face), 0)
     total = scratch[4][...]
-    for came, way in zip(faces, ways):
+    for copy in copies:
+        copy.wait()
+    for j, way in enumerate(ways):
         rows = towards(flags, way, rows_ref[2 * way[1]], rows_ref[2 * way[1] + 1])
-        total = total + dot(one_hot(places == rows), came[...])
+        total = total + dot(one_hot(places == rows), faces[j])
     out_ref[...] = total.astype(BF)
 
 
 def finish(ways, flags, rows, row, gp, weight, first, count, before, returned):
     return pl.pallas_call(
         lambda *refs: finish_kernel(ways, first, count, *refs),
-        in_specs=[SMEM, VMEM, HBM, HBM, HBM, HBM] + [VMEM] * len(returned),
+        in_specs=[SMEM] + [HBM] * (5 + len(returned)),
         out_specs=VMEM,
         out_shape=jax.ShapeDtypeStruct(gp.shape, BF),
-        scratch_shapes=backward_scratch(row, gp, gp.shape[0], count),
+        scratch_shapes=[
+            pltpu.VMEM(rows.shape, jnp.int32),
+            pltpu.VMEM((len(ways),) + returned[0].shape, BF),
+            pltpu.SemaphoreType.DMA((len(ways) + 1,)),
+        ]
+        + backward_scratch(row, gp, gp.shape[0], count),
         compiler_params=params(16),
         name="finish",
-    )(flags, rows, hold(row), hold(gp), hold(weight), hold(before), *returned)
+    )(flags, *[hold(x) for x in [rows, row, gp, weight, before] + returned])
 
 
 def swap(x, axis, bit):
@@ -402,8 +461,7 @@
     plane = [bits("gx", 0) + bits("gz", 1), bits("gz", 1) + bits("gx", 0)]
     turns = len(plane[0])
     rows, ch = keep.shape
-    came = swap(give, "gz", 0)
-    terms = [[(keep, i * (rows // 2)), (came, i * (rows // 2))] for i in range(2)]
+    terms = [[(keep, i * (rows // 2)), (swap(give[i], "gz", 0), 0)] for i in range(2)]
 
     def total(i, extra, size):
         out = None
@@ -416,7 +474,10 @@
     for turn in range(turns):
         size = size // 2
         mine = [side(*plane[i][turn]) for i in range(2)]
-        out = [total(i, (1 - mine[i]) * size, size).astype(BF) for i in range(2)]
+        out = [total(0, (1 - mine[0]) * size, size).astype(BF)]
+        held = lax.optimization_barrier((out[0], terms[1][-1][0]))
+        out, terms[1][-1] = [held[0]], (held[1], terms[1][-1][1])
+        out.append(total(1, (1 - mine[1]) * size, size).astype(BF))
         came = beside(out, [swap(out[i], *plane[i][turn]) for i in range(2)])
         for i in range(2):
             terms[i] = [(a, start + mine[i] * size) for a, start in terms[i]] + [(came[i], 0)]
@@ -485,11 +546,13 @@
     ways = routes()
     flags = jnp.stack([side("gz", 0)] + [lax.axis_index(a) & 1 for a in AXES]).astype(jnp.int32)
     faces = exchange(send(ways, flags, sends, own_features), ways)
-    col, row = invert(single(in_rows), single(out_rows), single(tap_pair_exists), block)
-    activated, gp, keep, give = forward(ways, flags, col, own_features, faces, weight, upstream[0, 0, 0])
+    col, row = invert(
+        flags, single(in_rows), single(out_rows), single(tap_pair_exists), sends.shape[2], block
+    )
+    activated, gp, keep, *give = forward(ways, flags, col, own_features, faces, weight, upstream[0, 0, 0])
     devices = lax.axis_size("gx") * lax.axis_size("gy") * lax.axis_size("gz")
-    split = 12
-    state = {"turn": 0, "returned": {}}
+    split = (0, 6, 18)
+    state = {"turn": 0, "returned": {}, "grad": []}
     late = [j for j, way in enumerate(ways) if way in ((0, 0), (1, 2))]
     early = [j for j in range(len(ways)) if j not in late]
 
@@ -513,12 +576,15 @@
             for j, face in zip(picks, held):
                 state["returned"][j] = face
             came = list(held[len(picks) :])
-        elif turn == 3:
-            work = lambda g: [backward_own(row, g, weight, 0, split)]
-            (state["grad"],), came = tied(out, work, came)
-        elif turn == 5:
+        if turn in (2, 3):
+            first, after = split[turn - 2 : turn]
+            work = lambda g: [backward_own(row, g, weight, first, after - first, state["grad"])]
+            made, came = tied(out, work, came)
+            state["grad"] = [made[0]]
+        if turn == 5:
             faces = [state["returned"][j] for j in range(len(ways))]
-            work = lambda g: [finish(ways, flags, sends, row, g, weight, split, taps - split, state["grad"], faces)]
+            first = split[-1]
+            work = lambda g: [finish(ways, flags, sends, row, g, weight, first, taps - first, state["grad"][0], faces)]
             (state["done"],), came = tied(out, work, came)
         return came
 

time: 137 us -> 134 us (0.978)
  local copies, waits for them, and re-layouts: 3.6 us -> 0.7 us
  starting transfers between devices: 34.4 us -> 32.1 us
  other arithmetic: 9.65 us -> 11.3 us
    pallas_call x1 -> x2, Pallas kernels: 7.84 us -> 12.8 us  [backward_own(): pl.pallas_call(lambda *refs: own_kernel(first, count, *refs), in_specs=[H...]
    ppermute x13 -> x14, waiting for transfers between devices: 11 us -> 14.6 us  [swap(): return lax.ppermute(x, axis, [(j, j ^ 1 << bit) for j in range(n)])]
    ppermute x10, waiting for transfers between devices: 4.69 us -> 1.38 us  [exchange(): got.append(lax.ppermute(array, AXES[i], pairs))]
    convert_element_type x2 -> x4, other arithmetic: 4.48 us -> 7.4 us  [the longest x2 3.71 us: reduce_all(): out.append(total(1, (1 - mine[1]) * size, size).astype(BF))]
    unnamed x10 -> x4, local copies, waits for them, and re-layouts: 2.9 us -> 0.01 us
    pallas_call x1, Pallas kernels: 10.5 us -> 7.73 us  [finish(): pl.pallas_call(lambda *refs: finish_kernel(ways, first, count, *refs), in...]
    ppermute x6, starting transfers between devices: 10.5 us -> 8.73 us  [reduce_all(): lax.ppermute(y, 'gy', [(j, (j + s) % n) for j in range(n)])]
    pallas_call x4, Pallas kernels: 46.2 us -> 44.5 us  [the longest x1 27.2 us: forward(): pl.pallas_call(lambda *refs: forward_kernel(ways, where, 256, *refs), in_...]
  transfers between devices with their start and end apart: 29 -> 30, of which waited for: 10 -> 11; matrix products, arithmetic and copies ran while one was open for 1% -> 3% of each run, Pallas kernels for 25% -> 27%
where the time goes in v7:
time: 134 us; the launch traced here: 133 us
  Pallas kernels  69.1 us (52%)
  starting transfers between devices  32.1 us (24%)
  waiting for transfers between devices  18.5 us (14%)
  other arithmetic  11.3 us (8%)
    pallas_call x1, Pallas kernels, forward(): pl.pallas_call(lambda *refs: forward_kernel(ways, where, 256, *refs), in_...  27.2 us
    ppermute x14, waiting for transfers between devices, swap(): return lax.ppermute(x, axis, [(j, j ^ 1 << bit) for j in range(n)])  14.6 us
    ppermute x10, starting transfers between devices, exchange(): got.append(lax.ppermute(array, AXES[i], pairs))  13.5 us
    pallas_call x2, Pallas kernels, backward_own(): pl.pallas_call(lambda *refs: own_kernel(first, count, *refs), in_specs=[H...  12.8 us
    pallas_call x1, Pallas kernels, backward_faces(): pl.pallas_call(lambda *refs: faces_kernel(ways, where, own, taps, *refs),...  11.4 us
    ppermute x14, starting transfers between devices, swap(): return lax.ppermute(x, axis, [(j, j ^ 1 << bit) for j in range(n)])  9.86 us
    ppermute x6, starting transfers between devices, reduce_all(): lax.ppermute(y, 'gy', [(j, (j + s) % n) for j in range(n)])  8.73 us
    pallas_call x1, Pallas kernels, finish(): pl.pallas_call(lambda *refs: finish_kernel(ways, first, count, *refs), in...  7.73 us
  transfers between devices with their start and end apart: 30, of which 11 were waited for; matrix products, arithmetic and copies ran while one was open for 3% of the time, Pallas kernels for 27%

profile of v7, /device:TPU:0, one launch (start us, length us, event | category | flops | bytes accessed | tf_op | source)
XLA Modules:
  0.0 133.0 jit_solution(9398184512128503868)
XLA Ops:
  0.6 0.1 fusion.4
  0.7 2.0 %send.1 = (bf16[96,256]{1,0:T(8,128)(2,1)S(1)}, bf16[96,256]{1,0:T(8,128)(2,1)S(1)}, bf16[96,256]{1,0:T(8,128)(2,1)S(1)}, bf16[96,256]{1,0:T(8,128)(2,1)S(1)}, bf16[96,256]{1,0:T(8,128)(2,1)S(1)}) custom-call(s32[4]{0:T(128)S(1)} %get-tuple-element.154.refs_0_, s32[6,1,96]{2,1,0:T(1,128)} %bitcast.28, bf16[768,256]{1,0:T(8,128)(2,1)} %bitcast.21), custom_call_target="tpu_custom_call" | custom-call | tf_op jit(solution)/shard_map/send/pallas_call | solution.py:89
  2.7 3.0 %collective-permute-start = (bf16[96,256]{1,0:T(8,128)(2,1)S(1)}, bf16[96,256]{1,0:T(8,128)(2,1)S(1)}, u32[]{:S(2)}, u32[]{:S(2)}) collective-permute-start(bf16[96,256]{1,0:T(8,128)(2,1)S(1)} %get-tuple-element.65), channel_id=1, source_target_pairs={{0,16},{16,0},{1,17},{17,1},{2,18},{18,2},{3,19},{19,3},{4,20},{20... | collective-permute-start | bytes 147464 | tf_op jit(solution)/shard_map/ppermute | solution.py:60
  5.7 1.6 %collective-permute-start.1 = (bf16[96,256]{1,0:T(8,128)(2,1)S(1)}, bf16[96,256]{1,0:T(8,128)(2,1)S(1)}, u32[]{:S(2)}, u32[]{:S(2)}) collective-permute-start(bf16[96,256]{1,0:T(8,128)(2,1)S(1)} %get-tuple-element.66), channel_id=1, source_target_pairs={{0,4},{4,0},{8,12},{12,8},{1,5},{5,1},{9,13},{13,9},{2,6},{6,2},{1... | collective-permute-start | bytes 147464 | tf_op jit(solution)/shard_map/ppermute | solution.py:60
  7.3 0.7 collective-permute-start.2
  8.1 0.7 collective-permute-start.4
  8.7 3.9 %invert.1 = (f32[27,128,16]{2,1,0:T(8,128)S(1)}, f32[27,16,128]{2,1,0:T(8,128)}) custom-call(s32[4]{0:T(128)S(1)} %get-tuple-element.154.refs_0_, s32[27,1,768]{2,1,0:T(1,128)} %bitcast.25, s32[27,1,768]{2,1,0:T(1,128)} %bitcast.26, s32[27,1,768]{2,1,0:T(1,128)} %bitcast.27), custom_call_target="tpu_custom_call" | custom-call | tf_op jit(solution)/shard_map/invert/pallas_call | solution.py:142
  12.7 27.2 %forward.1 = (bf16[768,256]{1,0:T(8,128)(2,1)}, bf16[768,256]{1,0:T(8,128)(2,1)}, f32[6912,128]{1,0:T(8,128)S(1)}, bf16[3456,128]{1,0:T(8,128)(2,1)}, bf16[3456,128]{1,0:T(8,128)(2,1)}) custom-call(s32[4]{0:T(128)S(1)} %get-tuple-element.154.refs_0_, f32[27,128,16]{2,1,0:T(8,128)S(1)} %get-tuple-element.64.refs_1_, bf16[768,256]{1,0:T(8,128)(2,1)} %bitcast.22, ...), custom_call_target="tpu_custom_call" | custom-call | tf_op jit(solution)/shard_map/forward/pallas_call | solution.py:247
  39.9 3.0 %collective-permute-start.5 = (bf16[3456,128]{1,0:T(8,128)(2,1)}, bf16[3456,128]{1,0:T(8,128)(2,1)}, u32[]{:S(2)}, u32[]{:S(2)}) collective-permute-start(bf16[3456,128]{1,0:T(8,128)(2,1)} %get-tuple-element.74), channel_id=1, source_target_pairs={{0,1},{1,0},{2,3},{3,2},{4,5},{5,4},{6,7},{7,6},{8,9},{9,8},{10,11... | collective-permute-start | bytes 2654216 | tf_op jit(solution)/shard_map/ppermute | solution.py:420
  42.8 0.1 collective-permute-start.6
  42.9 2.3 %collective-permute-done.5 = bf16[3456,128]{1,0:T(8,128)(2,1)} collective-permute-done((bf16[3456,128]{1,0:T(8,128)(2,1)}, bf16[3456,128]{1,0:T(8,128)(2,1)}, u32[]{:S(2)}, u32[]{:S(2)}) %collective-permute-start.5) | collective-permute-done | bytes 884768 | tf_op jit(solution)/shard_map/ppermute | solution.py:420
  45.2 1.9 %add_convert_fusion.1 = bf16[1728,128]{1,0:T(8,128)(2,1)} fusion(f32[6912,128]{1,0:T(8,128)S(1)} %get-tuple-element.73, s32[]{:T(128)S(6)} %select_n.164, bf16[3456,128]{1,0:T(8,128)(2,1)} %collective-permute-done.5, s32[]{:T(128)S(6)} %select_n.165), kind=kLoop, calls=%fused_computation.1 | loop fusion | flops 663552 | bytes 1769480 | tf_op jit(solution)/shard_map/convert_element_type | solution.py:477
  47.1 1.9 %add_convert_fusion = bf16[1728,128]{1,0:T(8,128)(2,1)} fusion(f32[6912,128]{1,0:T(8,128)S(1)} %get-tuple-element.73, s32[]{:T(128)S(6)} %select_n.166, bf16[3456,128]{1,0:T(8,128)(2,1)} %collective-permute-done.6, s32[]{:T(128)S(6)} %select_n.167), kind=kLoop, calls=%fused_computation | loop fusion | flops 663552 | bytes 1769480 | tf_op jit(solution)/shard_map/convert_element_type | solution.py:480
  49.0 0.9 collective-permute-start.8
  49.9 0.5 collective-permute-start.7
  50.4 11.4 %backward_faces.1 = (bf16[96,256]{1,0:T(8,128)(2,1)}, bf16[96,256]{1,0:T(8,128)(2,1)}, bf16[96,256]{1,0:T(8,128)(2,1)}, bf16[96,256]{1,0:T(8,128)(2,1)}, bf16[96,256]{1,0:T(8,128)(2,1)}) custom-call(s32[4]{0:T(128)S(1)} %get-tuple-element.154.refs_0_, f32[27,16,128]{2,1,0:T(8,128)} %get-tuple-element.71.refs_1_.refs_0_.refs_2_, ...), custom_call_target="tpu_custom_call" | custom-call | tf_op jit(solution)/shard_map/backward_faces/pallas_call | solution.py:346
  61.9 0.2 collective-permute-done.7
  62.1 1.8 %add_convert_fusion.3 = bf16[864,128]{1,0:T(8,128)(2,1)} fusion(f32[6912,128]{1,0:T(8,128)S(1)} %get-tuple-element.73, s32[]{:T(128)S(6)} %select_n.169, bf16[1728,128]{1,0:T(8,128)(2,1)} %collective-permute-done.7, s32[]{:T(128)S(6)} %select_n.171, bf16[3456,128]{1,0:T(8,128)(2,1)} %collective-permute-done.5, s32[]{:T(128)S(6)} %select_n.170), kind=kLoop, calls=%fused_computation.3 | loop fusion | flops 552960 | bytes 1105932 | tf_op jit(solution)/shard_map/convert_element_type | solution.py:477
  63.9 1.8 %add_convert_fusion.2 = bf16[864,128]{1,0:T(8,128)(2,1)} fusion(f32[6912,128]{1,0:T(8,128)S(1)} %get-tuple-element.73, s32[]{:T(128)S(6)} %select_n.172, bf16[1728,128]{1,0:T(8,128)(2,1)} %collective-permute-done.8, s32[]{:T(128)S(6)} %select_n.174, bf16[3456,128]{1,0:T(8,128)(2,1)} %collective-permute-done.6, s32[]{:T(128)S(6)} %select_n.173), kind=kLoop, calls=%fused_computation.2 | loop fusion | flops 552960 | bytes 1105932 | tf_op jit(solution)/shard_map/convert_element_type | solution.py:480
  65.7 1.2 collective-permute-start.13
  66.9 1.2 collective-permute-start.12
  68.2 4.4 %collective-permute-start.9 = (bf16[96,256]{1,0:T(8,128)(2,1)}, bf16[96,256]{1,0:T(8,128)(2,1)}, u32[]{:S(2)}, u32[]{:S(2)}) collective-permute-start(bf16[96,256]{1,0:T(8,128)(2,1)} %get-tuple-element.91), channel_id=1, source_target_pairs={{0,4},{4,0},{8,12},{12,8},{1,5},{5,1},{9,13},{13,9},{2,6},{6,2},{1... | collective-permute-start | bytes 147464 | tf_op jit(solution)/shard_map/ppermute | solution.py:60
  72.6 1.3 collective-permute-start.10
  73.8 0.1 broadcast_add_fusion.4
  74.0 0.9 collective-permute-done.9.refs_7_
  75.0 0.4 collective-permute-done.11.refs_9_
  75.4 1.1 add_convert_fusion.4
  76.5 1.1 add_convert_fusion.5
  77.7 3.5 %collective-permute-start.16 = (bf16[432,128]{1,0:T(8,128)(2,1)S(1)}, bf16[432,128]{1,0:T(8,128)(2,1)S(1)}, u32[]{:S(2)}, u32[]{:S(2)}) collective-permute-start(bf16[432,128]{1,0:T(8,128)(2,1)S(1)} %pad_maximum_fusion.2), channel_id=1, source_target_pairs={{0,4},{4,8},{8,12},{12,0},{1,5},{5,9},{9,13},{13,1},{2,6},{6,10},{... | collective-permute-start | bytes 331784 | tf_op jit(solution)/shard_map/ppermute | solution.py:488
  81.2 0.1 collective-permute-start.17
  81.3 2.4 %collective-permute-start.18 = (bf16[432,128]{1,0:T(8,128)(2,1)S(1)}, bf16[432,128]{1,0:T(8,128)(2,1)S(1)}, u32[]{:S(2)}, u32[]{:S(2)}) collective-permute-start(bf16[432,128]{1,0:T(8,128)(2,1)S(1)} %pad_maximum_fusion.4), channel_id=1, source_target_pairs={{0,12},{4,0},{8,4},{12,8},{1,13},{5,1},{9,5},{13,9},{2,14},{6,2},{... | collective-permute-start | bytes 331784 | tf_op jit(solution)/shard_map/ppermute | solution.py:488
  83.8 1.0 collective-permute-start.14
  84.8 0.9 collective-permute-start.15
  85.6 1.0 convert_add_fusion.1
  86.7 5.0 %backward_own.2.refs_3_ = f32[768,256]{1,0:T(8,128)} custom-call(f32[27,16,128]{2,1,0:T(8,128)} %get-tuple-element.71.refs_1_.refs_0_.refs_2_, bf16[768,256]{1,0:T(8,128)(2,1)} %get-tuple-element.112.refs_2_.refs_1_.refs_3_, bf16[27,256,256]{2,1,0:T(8,128)(2,1)} %refs_4_.1), custom_call_target="tpu_custom_call" | custom-call | tf_op jit(solution)/shard_map/backward_own/pallas_call | solution.py:369
  91.7 0.1 fusion.3
  91.8 2.1 %collective-permute-start.21 = (bf16[432,128]{1,0:T(8,128)(2,1)S(1)}, bf16[432,128]{1,0:T(8,128)(2,1)S(1)}, u32[]{:S(2)}, u32[]{:S(2)}) collective-permute-start(bf16[432,128]{1,0:T(8,128)(2,1)S(1)} %fusion.3), channel_id=1, source_target_pairs={{0,12},{4,0},{8,4},{12,8},{1,13},{5,1},{9,5},{13,9},{2,14},{6,2},{... | collective-permute-start | bytes 331784 | tf_op jit(solution)/shard_map/ppermute | solution.py:488
  93.9 0.6 collective-permute-start.19
  94.5 7.8 %backward_own.3.refs_5_ = f32[768,256]{1,0:T(8,128)} custom-call(f32[27,16,128]{2,1,0:T(8,128)} %get-tuple-element.71.refs_1_.refs_0_.refs_2_, bf16[768,256]{1,0:T(8,128)(2,1)} %get-tuple-element.112.refs_2_.refs_1_.refs_3_, bf16[27,256,256]{2,1,0:T(8,128)(2,1)} %refs_4_.1, f32[768,256]{1,0:T(8,128)} %backward_own.2.refs_3_), custom_call_target="tpu_custom_call" | custom-call | tf_op jit(solution)/shard_map/backward_own/pallas_call | solution.py:369
  102.4 2.5 %collective-permute-done.20 = bf16[432,128]{1,0:T(8,128)(2,1)S(1)} collective-permute-done((bf16[432,128]{1,0:T(8,128)(2,1)S(1)}, bf16[432,128]{1,0:T(8,128)(2,1)S(1)}, u32[]{:S(2)}, u32[]{:S(2)}) %collective-permute-start.20) | collective-permute-done | bytes 110624 | tf_op jit(solution)/shard_map/ppermute | solution.py:488
  105.1 1.3 collective-permute-start.23
  106.4 0.1 collective-permute-start.22
  106.5 0.1 broadcast_add_fusion.5
  106.5 6.1 %collective-permute-done.23 = bf16[864,128]{1,0:T(8,128)(2,1)S(1)} collective-permute-done((bf16[864,128]{1,0:T(8,128)(2,1)S(1)}, bf16[864,128]{1,0:T(8,128)(2,1)S(1)}, u32[]{:S(2)}, u32[]{:S(2)}) %collective-permute-start.23) | collective-permute-done | bytes 221216 | tf_op jit(solution)/shard_map/ppermute | solution.py:420
  112.6 0.1 collective-permute-start.27
  112.8 0.8 collective-permute-done.22
  113.7 0.9 collective-permute-start.24
  114.6 0.1 broadcast_add_fusion.7
  114.7 0.1 broadcast_add_fusion
  114.8 0.1 add.601
  114.8 0.1 add.596
  114.9 0.1 add_multiply_fusion.2
  115.0 0.1 concatenate.62.refs_0_
  115.1 7.7 %finish.1 = bf16[768,256]{1,0:T(8,128)(2,1)} custom-call(s32[4]{0:T(128)S(1)} %get-tuple-element.154.refs_0_, s32[6,1,96]{2,1,0:T(1,128)} %bitcast.29, f32[27,16,128]{2,1,0:T(8,128)} %get-tuple-element.71.refs_1_.refs_0_.refs_2_, bf16[768,256]{1,0:T(8,128)(2,1)} %get-tuple-element.112.refs_2_.refs_1_.refs_3_, bf16[27,256,256]{2,1,0:T(8,128)(2,1)} %refs_4_.1, ...), custom_call_target="tpu_custom_call" | custom-call | tf_op jit(solution)/shard_map/finish/pallas_call | solution.py:402
  122.8 2.5 %collective-permute-done.25.refs_2_ = bf16[1728,128]{1,0:T(8,128)(2,1)S(1)} collective-permute-done((bf16[1728,128]{1,0:T(8,128)(2,1)S(1)}, bf16[1728,128]{1,0:T(8,128)(2,1)S(1)}, u32[]{:S(2)}, u32[]{:S(2)}) %collective-permute-start.25) | collective-permute-done | bytes 442400 | tf_op jit(solution)/shard_map/ppermute | solution.py:420
  125.3 1.0 collective-permute-done.24.refs_1_
  126.3 2.0 %place.2.refs_5_ = bf16[6912,256]{1,0:T(8,128)(2,1)} custom-call(s32[36]{0:T(128)S(1)} %concatenate.62.refs_0_, bf16[1728,128]{1,0:T(8,128)(2,1)S(1)} %constant_dynamic-update-slice_fusion.refs_1_, bf16[1728,128]{1,0:T(8,128)(2,1)S(1)} %constant_dynamic-update-slice_fusion.5.refs_2_, bf16[1728,128]{1,0:T(8,128)(2,1)S(1)} %collective-permute-done.26.refs_3_, ...), custom_call_target="tpu_custom_call" | custom-call | tf_op jit(solution)/shard_map/place/pallas_call | solution.py:447
  128.4 0.5 collective-permute-start.29
  128.9 0.1 add.591
  129.0 0.1 add.585
  129.1 0.1 concatenate.61.refs_0_
  129.2 1.0 collective-permute-done.28.refs_3_
  130.2 0.6 collective-permute-done.29.refs_4_
  130.8 2.0 %place.3 = bf16[6912,256]{1,0:T(8,128)(2,1)} custom-call(s32[36]{0:T(128)S(1)} %concatenate.61.refs_0_, bf16[1728,128]{1,0:T(8,128)(2,1)S(1)} %collective-permute-done.24.refs_1_, bf16[1728,128]{1,0:T(8,128)(2,1)S(1)} %collective-permute-done.25.refs_2_, bf16[1728,128]{1,0:T(8,128)(2,1)S(1)} %collective-permute-done.28.refs_3_, ...), custom_call_target="tpu_custom_call", output_to_operand_aliasing={{}: (5, {})} | custom-call | tf_op jit(solution)/shard_map/place/pallas_call | solution.py:447
  (40 shorter events, 0.7 us)
Async XLA Ops:
  2.7 9.9 %collective-permute-start = (bf16[96,256]{1,0:T(8,128)(2,1)S(1)}, bf16[96,256]{1,0:T(8,128)(2,1)S(1)}, u32[]{:S(2)}, u32[]{:S(2)}) collective-permute-start(bf16[96,256]{1,0:T(8,128)(2,1)S(1)} %get-tuple-element.65), channel_id=1, source_target_pairs={{0,16},{16,0},{1,17},{17,1},{2,18},{18,2},{3,19},{19,3},{4,20},{20... | collective-permute-start | bytes 147464 | tf_op jit(solution)/shard_map/ppermute | solution.py:60
  5.7 6.9 %collective-permute-start.1 = (bf16[96,256]{1,0:T(8,128)(2,1)S(1)}, bf16[96,256]{1,0:T(8,128)(2,1)S(1)}, u32[]{:S(2)}, u32[]{:S(2)}) collective-permute-start(bf16[96,256]{1,0:T(8,128)(2,1)S(1)} %get-tuple-element.66), channel_id=1, source_target_pairs={{0,4},{4,0},{8,12},{12,8},{1,5},{5,1},{9,13},{13,9},{2,6},{6,2},{1... | collective-permute-start | bytes 147464 | tf_op jit(solution)/shard_map/ppermute | solution.py:60
  7.3 5.3 %collective-permute-start.2 = (bf16[96,256]{1,0:T(8,128)(2,1)S(1)}, bf16[96,256]{1,0:T(8,128)(2,1)S(1)}, u32[]{:S(2)}, u32[]{:S(2)}) collective-permute-start(bf16[96,256]{1,0:T(8,128)(2,1)S(1)} %get-tuple-element.67), channel_id=1, source_target_pairs={{4,8},{8,4},{5,9},{9,5},{6,10},{10,6},{7,11},{11,7},{20,24},{24,20... | collective-permute-start | bytes 147464 | tf_op jit(solution)/shard_map/ppermute | solution.py:60
  8.0 4.7 %collective-permute-start.3 = (bf16[96,256]{1,0:T(8,128)(2,1)S(1)}, bf16[96,256]{1,0:T(8,128)(2,1)S(1)}, u32[]{:S(2)}, u32[]{:S(2)}) collective-permute-start(bf16[96,256]{1,0:T(8,128)(2,1)S(1)} %get-tuple-element.68), channel_id=1, source_target_pairs={{0,1},{1,0},{2,3},{3,2},{4,5},{5,4},{6,7},{7,6},{8,9},{9,8},{10,11... | collective-permute-start | bytes 147464 | tf_op jit(solution)/shard_map/ppermute | solution.py:60
  8.1 4.6 %collective-permute-start.4 = (bf16[96,256]{1,0:T(8,128)(2,1)S(1)}, bf16[96,256]{1,0:T(8,128)(2,1)S(1)}, u32[]{:S(2)}, u32[]{:S(2)}) collective-permute-start(bf16[96,256]{1,0:T(8,128)(2,1)S(1)} %get-tuple-element.69), channel_id=1, source_target_pairs={{1,2},{2,1},{5,6},{6,5},{9,10},{10,9},{13,14},{14,13},{17,18},{18,... | collective-permute-start | bytes 147464 | tf_op jit(solution)/shard_map/ppermute | solution.py:60
  39.9 5.3 %collective-permute-start.5 = (bf16[3456,128]{1,0:T(8,128)(2,1)}, bf16[3456,128]{1,0:T(8,128)(2,1)}, u32[]{:S(2)}, u32[]{:S(2)}) collective-permute-start(bf16[3456,128]{1,0:T(8,128)(2,1)} %get-tuple-element.74), channel_id=1, source_target_pairs={{0,1},{1,0},{2,3},{3,2},{4,5},{5,4},{6,7},{7,6},{8,9},{9,8},{10,11... | collective-permute-start | bytes 2654216 | tf_op jit(solution)/shard_map/ppermute | solution.py:420
  42.8 4.3 %collective-permute-start.6 = (bf16[3456,128]{1,0:T(8,128)(2,1)}, bf16[3456,128]{1,0:T(8,128)(2,1)}, u32[]{:S(2)}, u32[]{:S(2)}) collective-permute-start(bf16[3456,128]{1,0:T(8,128)(2,1)} %get-tuple-element.75), channel_id=1, source_target_pairs={{0,1},{1,0},{2,3},{3,2},{4,5},{5,4},{6,7},{7,6},{8,9},{9,8},{10,11... | collective-permute-start | bytes 2654216 | tf_op jit(solution)/shard_map/ppermute | solution.py:420
  49.0 12.8 %collective-permute-start.8 = (bf16[1728,128]{1,0:T(8,128)(2,1)}, bf16[1728,128]{1,0:T(8,128)(2,1)}, u32[]{:S(2)}, u32[]{:S(2)}) collective-permute-start(bf16[1728,128]{1,0:T(8,128)(2,1)} %add_convert_fusion), channel_id=1, source_target_pairs={{0,2},{1,3},{2,0},{3,1},{4,6},{5,7},{6,4},{7,5},{8,10},{9,11},{10,... | collective-permute-start | bytes 1327112 | tf_op jit(solution)/shard_map/ppermute | solution.py:420
  49.9 12.2 %collective-permute-start.7 = (bf16[1728,128]{1,0:T(8,128)(2,1)}, bf16[1728,128]{1,0:T(8,128)(2,1)}, u32[]{:S(2)}, u32[]{:S(2)}) collective-permute-start(bf16[1728,128]{1,0:T(8,128)(2,1)} %add_convert_fusion.1), channel_id=1, source_target_pairs={{0,16},{16,0},{1,17},{17,1},{2,18},{18,2},{3,19},{19,3},{4,20},{20... | collective-permute-start | bytes 1327112 | tf_op jit(solution)/shard_map/ppermute | solution.py:420
  65.7 9.7 %collective-permute-start.13 = (bf16[864,128]{1,0:T(8,128)(2,1)}, bf16[864,128]{1,0:T(8,128)(2,1)}, u32[]{:S(2)}, u32[]{:S(2)}) collective-permute-start(bf16[864,128]{1,0:T(8,128)(2,1)} %add_convert_fusion.2), channel_id=1, source_target_pairs={{0,16},{16,0},{1,17},{17,1},{2,18},{18,2},{3,19},{19,3},{4,20},{20... | collective-permute-start | bytes 663560 | tf_op jit(solution)/shard_map/ppermute | solution.py:420
  66.9 8.5 %collective-permute-start.12 = (bf16[864,128]{1,0:T(8,128)(2,1)}, bf16[864,128]{1,0:T(8,128)(2,1)}, u32[]{:S(2)}, u32[]{:S(2)}) collective-permute-start(bf16[864,128]{1,0:T(8,128)(2,1)} %add_convert_fusion.3), channel_id=1, source_target_pairs={{0,2},{1,3},{2,0},{3,1},{4,6},{5,7},{6,4},{7,5},{8,10},{9,11},{10,... | collective-permute-start | bytes 663560 | tf_op jit(solution)/shard_map/ppermute | solution.py:420
  68.2 6.8 %collective-permute-start.9 = (bf16[96,256]{1,0:T(8,128)(2,1)}, bf16[96,256]{1,0:T(8,128)(2,1)}, u32[]{:S(2)}, u32[]{:S(2)}) collective-permute-start(bf16[96,256]{1,0:T(8,128)(2,1)} %get-tuple-element.91), channel_id=1, source_target_pairs={{0,4},{4,0},{8,12},{12,8},{1,5},{5,1},{9,13},{13,9},{2,6},{6,2},{1... | collective-permute-start | bytes 147464 | tf_op jit(solution)/shard_map/ppermute | solution.py:60
  72.6 2.4 %collective-permute-start.10 = (bf16[96,256]{1,0:T(8,128)(2,1)}, bf16[96,256]{1,0:T(8,128)(2,1)}, u32[]{:S(2)}, u32[]{:S(2)}) collective-permute-start(bf16[96,256]{1,0:T(8,128)(2,1)} %get-tuple-element.92), channel_id=1, source_target_pairs={{4,8},{8,4},{5,9},{9,5},{6,10},{10,6},{7,11},{11,7},{20,24},{24,20... | collective-permute-start | bytes 147464 | tf_op jit(solution)/shard_map/ppermute | solution.py:60
  73.8 1.6 %collective-permute-start.11 = (bf16[96,256]{1,0:T(8,128)(2,1)}, bf16[96,256]{1,0:T(8,128)(2,1)}, u32[]{:S(2)}, u32[]{:S(2)}) collective-permute-start(bf16[96,256]{1,0:T(8,128)(2,1)} %get-tuple-element.93), channel_id=1, source_target_pairs={{0,1},{1,0},{2,3},{3,2},{4,5},{5,4},{6,7},{7,6},{8,9},{9,8},{10,11... | collective-permute-start | bytes 147464 | tf_op jit(solution)/shard_map/ppermute | solution.py:60
  77.7 14.0 %collective-permute-start.16 = (bf16[432,128]{1,0:T(8,128)(2,1)S(1)}, bf16[432,128]{1,0:T(8,128)(2,1)S(1)}, u32[]{:S(2)}, u32[]{:S(2)}) collective-permute-start(bf16[432,128]{1,0:T(8,128)(2,1)S(1)} %pad_maximum_fusion.2), channel_id=1, source_target_pairs={{0,4},{4,8},{8,12},{12,0},{1,5},{5,9},{9,13},{13,1},{2,6},{6,10},{... | collective-permute-start | bytes 331784 | tf_op jit(solution)/shard_map/ppermute | solution.py:488
  81.2 10.5 %collective-permute-start.17 = (bf16[432,128]{1,0:T(8,128)(2,1)S(1)}, bf16[432,128]{1,0:T(8,128)(2,1)S(1)}, u32[]{:S(2)}, u32[]{:S(2)}) collective-permute-start(bf16[432,128]{1,0:T(8,128)(2,1)S(1)} %pad_maximum_fusion.3), channel_id=1, source_target_pairs={{0,8},{4,12},{8,0},{12,4},{1,9},{5,13},{9,1},{13,5},{2,10},{6,14},... | collective-permute-start | bytes 331784 | tf_op jit(solution)/shard_map/ppermute | solution.py:488
  81.3 10.4 %collective-permute-start.18 = (bf16[432,128]{1,0:T(8,128)(2,1)S(1)}, bf16[432,128]{1,0:T(8,128)(2,1)S(1)}, u32[]{:S(2)}, u32[]{:S(2)}) collective-permute-start(bf16[432,128]{1,0:T(8,128)(2,1)S(1)} %pad_maximum_fusion.4), channel_id=1, source_target_pairs={{0,12},{4,0},{8,4},{12,8},{1,13},{5,1},{9,5},{13,9},{2,14},{6,2},{... | collective-permute-start | bytes 331784 | tf_op jit(solution)/shard_map/ppermute | solution.py:488
  83.8 7.9 %collective-permute-start.14 = (bf16[96,256]{1,0:T(8,128)(2,1)}, bf16[96,256]{1,0:T(8,128)(2,1)S(1)}, u32[]{:S(2)}, u32[]{:S(2)}) collective-permute-start(bf16[96,256]{1,0:T(8,128)(2,1)} %get-tuple-element.99), channel_id=1, source_target_pairs={{0,16},{16,0},{1,17},{17,1},{2,18},{18,2},{3,19},{19,3},{4,20},{20... | collective-permute-start | bytes 147464 | tf_op jit(solution)/shard_map/ppermute | solution.py:60
  84.8 6.9 %collective-permute-start.15 = (bf16[96,256]{1,0:T(8,128)(2,1)}, bf16[96,256]{1,0:T(8,128)(2,1)S(1)}, u32[]{:S(2)}, u32[]{:S(2)}) collective-permute-start(bf16[96,256]{1,0:T(8,128)(2,1)} %get-tuple-element.100), channel_id=1, source_target_pairs={{1,2},{2,1},{5,6},{6,5},{9,10},{10,9},{13,14},{14,13},{17,18},{18,... | collective-permute-start | bytes 147464 | tf_op jit(solution)/shard_map/ppermute | solution.py:60
  91.7 13.3 %copy-start = (bf16[96,256]{1,0:T(8,128)(2,1)}, bf16[96,256]{1,0:T(8,128)(2,1)S(1)}, u32[]{:S(2)}) copy-start(bf16[96,256]{1,0:T(8,128)(2,1)S(1)} %collective-permute-done.14.refs_6_) | copy-start | bytes 147460
  91.7 13.3 %copy-start.1 = (bf16[96,256]{1,0:T(8,128)(2,1)}, bf16[96,256]{1,0:T(8,128)(2,1)S(1)}, u32[]{:S(2)}) copy-start(bf16[96,256]{1,0:T(8,128)(2,1)S(1)} %collective-permute-done.15.refs_10_) | copy-start | bytes 147460
  91.8 10.6 %collective-permute-start.21 = (bf16[432,128]{1,0:T(8,128)(2,1)S(1)}, bf16[432,128]{1,0:T(8,128)(2,1)S(1)}, u32[]{:S(2)}, u32[]{:S(2)}) collective-permute-start(bf16[432,128]{1,0:T(8,128)(2,1)S(1)} %fusion.3), channel_id=1, source_target_pairs={{0,12},{4,0},{8,4},{12,8},{1,13},{5,1},{9,5},{13,9},{2,14},{6,2},{... | collective-permute-start | bytes 331784 | tf_op jit(solution)/shard_map/ppermute | solution.py:488
  93.9 11.0 %collective-permute-start.20 = (bf16[432,128]{1,0:T(8,128)(2,1)S(1)}, bf16[432,128]{1,0:T(8,128)(2,1)S(1)}, u32[]{:S(2)}, u32[]{:S(2)}) collective-permute-start(bf16[432,128]{1,0:T(8,128)(2,1)S(1)} %fusion.3), channel_id=1, source_target_pairs={{0,8},{4,12},{8,0},{12,4},{1,9},{5,13},{9,1},{13,5},{2,10},{6,14},... | collective-permute-start | bytes 331784 | tf_op jit(solution)/shard_map/ppermute | solution.py:488
  93.9 11.0 %collective-permute-start.19 = (bf16[432,128]{1,0:T(8,128)(2,1)S(1)}, bf16[432,128]{1,0:T(8,128)(2,1)S(1)}, u32[]{:S(2)}, u32[]{:S(2)}) collective-permute-start(bf16[432,128]{1,0:T(8,128)(2,1)S(1)} %fusion.3), channel_id=1, source_target_pairs={{0,4},{4,8},{8,12},{12,0},{1,5},{5,9},{9,13},{13,1},{2,6},{6,10},{... | collective-permute-start | bytes 331784 | tf_op jit(solution)/shard_map/ppermute | solution.py:488
  105.1 7.5 %collective-permute-start.23 = (bf16[864,128]{1,0:T(8,128)(2,1)S(1)}, bf16[864,128]{1,0:T(8,128)(2,1)S(1)}, u32[]{:S(2)}, u32[]{:S(2)}) collective-permute-start(bf16[864,128]{1,0:T(8,128)(2,1)S(1)} %pad_maximum_fusion.1), channel_id=1, source_target_pairs={{0,16},{16,0},{1,17},{17,1},{2,18},{18,2},{3,19},{19,3},{4,20},{20... | collective-permute-start | bytes 663560 | tf_op jit(solution)/shard_map/ppermute | solution.py:420
  106.4 7.2 %collective-permute-start.22 = (bf16[864,128]{1,0:T(8,128)(2,1)S(1)}, bf16[864,128]{1,0:T(8,128)(2,1)S(1)}, u32[]{:S(2)}, u32[]{:S(2)}) collective-permute-start(bf16[864,128]{1,0:T(8,128)(2,1)S(1)} %pad_maximum_fusion), channel_id=1, source_target_pairs={{0,2},{1,3},{2,0},{3,1},{4,6},{5,7},{6,4},{7,5},{8,10},{9,11},{10,... | collective-permute-start | bytes 663560 | tf_op jit(solution)/shard_map/ppermute | solution.py:420
  112.6 13.7 %collective-permute-start.27 = (bf16[1728,128]{1,0:T(8,128)(2,1)S(1)}, bf16[1728,128]{1,0:T(8,128)(2,1)S(1)}, u32[]{:S(2)}, u32[]{:S(2)}) collective-permute-start(bf16[1728,128]{1,0:T(8,128)(2,1)S(1)} %constant_dynamic-update-slice_fusion.5.refs_2_), channel_id=1, source_target_pairs={{0,1},{1,0},{2,3},{3,2},{4,5},{5,4},{6,7},{7,6},{8,9},{9,8},{10,11... | collective-permute-start | bytes 1327112 | tf_op jit(solution)/shard_map/ppermute | solution.py:420
  112.7 12.6 %collective-permute-start.25 = (bf16[1728,128]{1,0:T(8,128)(2,1)S(1)}, bf16[1728,128]{1,0:T(8,128)(2,1)S(1)}, u32[]{:S(2)}, u32[]{:S(2)}) collective-permute-start(bf16[1728,128]{1,0:T(8,128)(2,1)S(1)} %constant_dynamic-update-slice_fusion.5.refs_2_), channel_id=1, source_target_pairs={{0,2},{1,3},{2,0},{3,1},{4,6},{5,7},{6,4},{7,5},{8,10},{9,11},{10,... | collective-permute-start | bytes 1327112 | tf_op jit(solution)/shard_map/ppermute | solution.py:420
  113.6 12.7 %collective-permute-start.26 = (bf16[1728,128]{1,0:T(8,128)(2,1)S(1)}, bf16[1728,128]{1,0:T(8,128)(2,1)S(1)}, u32[]{:S(2)}, u32[]{:S(2)}) collective-permute-start(bf16[1728,128]{1,0:T(8,128)(2,1)S(1)} %constant_dynamic-update-slice_fusion.refs_1_), channel_id=1, source_target_pairs={{0,1},{1,0},{2,3},{3,2},{4,5},{5,4},{6,7},{7,6},{8,9},{9,8},{10,11... | collective-permute-start | bytes 1327112 | tf_op jit(solution)/shard_map/ppermute | solution.py:420
  113.7 12.6 %collective-permute-start.24 = (bf16[1728,128]{1,0:T(8,128)(2,1)S(1)}, bf16[1728,128]{1,0:T(8,128)(2,1)S(1)}, u32[]{:S(2)}, u32[]{:S(2)}) collective-permute-start(bf16[1728,128]{1,0:T(8,128)(2,1)S(1)} %constant_dynamic-update-slice_fusion.refs_1_), channel_id=1, source_target_pairs={{0,16},{16,0},{1,17},{17,1},{2,18},{18,2},{3,19},{19,3},{4,20},{20... | collective-permute-start | bytes 1327112 | tf_op jit(solution)/shard_map/ppermute | solution.py:420
  128.3 1.9 %collective-permute-start.28 = (bf16[1728,128]{1,0:T(8,128)(2,1)S(1)}, bf16[1728,128]{1,0:T(8,128)(2,1)S(1)}, u32[]{:S(2)}, u32[]{:S(2)}) collective-permute-start(bf16[1728,128]{1,0:T(8,128)(2,1)S(1)} %collective-permute-done.24.refs_1_), channel_id=1, source_target_pairs={{0,1},{1,0},{2,3},{3,2},{4,5},{5,4},{6,7},{7,6},{8,9},{9,8},{10,11... | collective-permute-start | bytes 1327112 | tf_op jit(solution)/shard_map/ppermute | solution.py:420
  128.4 2.4 %collective-permute-start.29 = (bf16[1728,128]{1,0:T(8,128)(2,1)S(1)}, bf16[1728,128]{1,0:T(8,128)(2,1)S(1)}, u32[]{:S(2)}, u32[]{:S(2)}) collective-permute-start(bf16[1728,128]{1,0:T(8,128)(2,1)S(1)} %collective-permute-done.25.refs_2_), channel_id=1, source_target_pairs={{0,1},{1,0},{2,3},{3,2},{4,5},{5,4},{6,7},{7,6},{8,9},{9,8},{10,11... | collective-permute-start | bytes 1327112 | tf_op jit(solution)/shard_map/ppermute | solution.py:420

commit v8 on v7

--- a/solution.py
+++ b/solution.py
@@ -228,7 +228,7 @@
     middle = taps * ch // 2
     bounds = [0, (taps + 1) // 2, taps]
     for j in range(2):
-        lax.fori_loop(bounds[j], bounds[j + 1], one, 0, unroll=2)
+        lax.fori_loop(bounds[j], bounds[j + 1], one, 0, unroll=7 if (bounds[j + 1] - bounds[j]) % 7 == 0 else True)
         part = pl.ds(j * middle, middle)
         for source, target, sem in ((give, give_hbm[j], 5 + j), (keep, keep_hbm.at[part, :], 7 + j)):
             copy = pltpu.make_async_copy(source.at[part, :], target, sems.at[sem])
@@ -303,7 +303,7 @@
             got[pl.ds(r, step), pl.ds(at, ch)] = dot(jnp.concatenate(hots, axis=1), gp[...]).astype(BF)
         return carried
 
-    lax.fori_loop(0, count, gather, 0, unroll=3)
+    lax.fori_loop(0, count, gather, 0, unroll=next(u for u in (9, 6, 3, 1) if count % u == 0))
     for copy in later:
         copy.wait()
     for r in range(0, size, step):
@@ -474,10 +474,7 @@
     for turn in range(turns):
         size = size // 2
         mine = [side(*plane[i][turn]) for i in range(2)]
-        out = [total(0, (1 - mine[0]) * size, size).astype(BF)]
-        held = lax.optimization_barrier((out[0], terms[1][-1][0]))
-        out, terms[1][-1] = [held[0]], (held[1], terms[1][-1][1])
-        out.append(total(1, (1 - mine[1]) * size, size).astype(BF))
+        out = [total(i, (1 - mine[i]) * size, size).astype(BF) for i in range(2)]
         came = beside(out, [swap(out[i], *plane[i][turn]) for i in range(2)])
         for i in range(2):
             terms[i] = [(a, start + mine[i] * size) for a, start in terms[i]] + [(came[i], 0)]
@@ -517,8 +514,6 @@
             return jnp.concatenate(out + out + [lanes]).astype(jnp.int32)
 
         half = place(spots(0), pieces + twins, size, rows, None)
-        came = lax.optimization_barrier((half, *came))
-        half, came = came[0], list(came[1:])
         last = cross(came)
         return place(spots(1), came + last, size, rows, half)
     last = cross(came)
@@ -551,7 +546,7 @@
     )
     activated, gp, keep, *give = forward(ways, flags, col, own_features, faces, weight, upstream[0, 0, 0])
     devices = lax.axis_size("gx") * lax.axis_size("gy") * lax.axis_size("gz")
-    split = (0, 6, 18)
+    split = (0, 3, 15)
     state = {"turn": 0, "returned": {}, "grad": []}
     late = [j for j, way in enumerate(ways) if way in ((0, 0), (1, 2))]
     early = [j for j in range(len(ways)) if j not in late]

time: 134 us -> 130 us (0.970)
  Pallas kernels: 69.1 us -> 65.9 us
  waiting for transfers between devices: 18.5 us -> 15.8 us
  local copies, waits for them, and re-layouts: 0.7 us -> 3.23 us
  other arithmetic: 11.3 us -> 9.36 us
  starting transfers between devices: 32.1 us -> 33.5 us
    ppermute x14, waiting for transfers between devices: 14.6 us -> 11.5 us  [swap(): return lax.ppermute(x, axis, [(j, j ^ 1 << bit) for j in range(n)])]
    convert_element_type x4 -> x2, other arithmetic: 7.4 us -> 4.46 us  [reduce_all(): out = [total(i, (1 - mine[i]) * size, size).astype(BF) for i in range(2)]]
    pallas_call x2, Pallas kernels: 12.8 us -> 11.1 us  [backward_own(): pl.pallas_call(lambda *refs: own_kernel(first, count, *refs), in_specs=[H...]
    pallas_call x1, Pallas kernels: 27.2 us -> 25.5 us  [forward(): pl.pallas_call(lambda *refs: forward_kernel(ways, where, 256, *refs), in_...]
    concatenate x2, local copies, waits for them, and re-layouts: 0.16 us -> 1.5 us  [spots(): return jnp.concatenate(out + out + [lanes]).astype(jnp.int32)]
  transfers between devices with their start and end apart: 30 -> 30, of which waited for: 11 -> 11; matrix products, arithmetic and copies ran while one was open for 3% -> 4% of each run, Pallas kernels for 27% -> 28%
where the time goes in v8:
time: 130 us; the launch traced here: 129 us
  Pallas kernels  65.9 us (51%)
  starting transfers between devices  33.5 us (26%)
  waiting for transfers between devices  15.8 us (12%)
  other arithmetic  9.36 us (7%)
  local copies, waits for them, and re-layouts  3.23 us (2%)
    pallas_call x1, Pallas kernels, forward(): pl.pallas_call(lambda *refs: forward_kernel(ways, where, 256, *refs), in_...  25.5 us
    ppermute x10, starting transfers between devices, exchange(): got.append(lax.ppermute(array, AXES[i], pairs))  13.8 us
    ppermute x14, waiting for transfers between devices, swap(): return lax.ppermute(x, axis, [(j, j ^ 1 << bit) for j in range(n)])  11.5 us
    pallas_call x2, Pallas kernels, backward_own(): pl.pallas_call(lambda *refs: own_kernel(first, count, *refs), in_specs=[H...  11.1 us
    pallas_call x1, Pallas kernels, backward_faces(): pl.pallas_call(lambda *refs: faces_kernel(ways, where, own, taps, *refs),...  10.6 us
    ppermute x14, starting transfers between devices, swap(): return lax.ppermute(x, axis, [(j, j ^ 1 << bit) for j in range(n)])  10.4 us
    ppermute x6, starting transfers between devices, reduce_all(): lax.ppermute(y, 'gy', [(j, (j + s) % n) for j in range(n)])  9.31 us
    pallas_call x1, Pallas kernels, finish(): pl.pallas_call(lambda *refs: finish_kernel(ways, first, count, *refs), in...  8.85 us
  transfers between devices with their start and end apart: 30, of which 11 were waited for; matrix products, arithmetic and copies ran while one was open for 4% of the time, Pallas kernels for 28%

profile of v8, /device:TPU:0, one launch (start us, length us, event | category | flops | bytes accessed | tf_op | source)
XLA Modules:
  0.0 129.0 jit_solution(12636196342900426299)
XLA Ops:
  0.6 0.1 fusion.4
  0.7 2.0 %send.1 = (bf16[96,256]{1,0:T(8,128)(2,1)S(1)}, bf16[96,256]{1,0:T(8,128)(2,1)S(1)}, bf16[96,256]{1,0:T(8,128)(2,1)S(1)}, bf16[96,256]{1,0:T(8,128)(2,1)S(1)}, bf16[96,256]{1,0:T(8,128)(2,1)S(1)}) custom-call(s32[4]{0:T(128)S(1)} %get-tuple-element.144.refs_0_, s32[6,1,96]{2,1,0:T(1,128)} %bitcast.28, bf16[768,256]{1,0:T(8,128)(2,1)} %bitcast.21), custom_call_target="tpu_custom_call" | custom-call | tf_op jit(solution)/shard_map/send/pallas_call | solution.py:89
  2.7 3.0 %collective-permute-start = (bf16[96,256]{1,0:T(8,128)(2,1)S(1)}, bf16[96,256]{1,0:T(8,128)(2,1)S(1)}, u32[]{:S(2)}, u32[]{:S(2)}) collective-permute-start(bf16[96,256]{1,0:T(8,128)(2,1)S(1)} %get-tuple-element.58), channel_id=1, source_target_pairs={{0,16},{16,0},{1,17},{17,1},{2,18},{18,2},{3,19},{19,3},{4,20},{20... | collective-permute-start | bytes 147464 | tf_op jit(solution)/shard_map/ppermute | solution.py:60
  5.7 1.6 %collective-permute-start.1 = (bf16[96,256]{1,0:T(8,128)(2,1)S(1)}, bf16[96,256]{1,0:T(8,128)(2,1)S(1)}, u32[]{:S(2)}, u32[]{:S(2)}) collective-permute-start(bf16[96,256]{1,0:T(8,128)(2,1)S(1)} %get-tuple-element.59), channel_id=1, source_target_pairs={{0,4},{4,0},{8,12},{12,8},{1,5},{5,1},{9,13},{13,9},{2,6},{6,2},{1... | collective-permute-start | bytes 147464 | tf_op jit(solution)/shard_map/ppermute | solution.py:60
  7.3 0.7 collective-permute-start.2
  8.0 0.1 collective-permute-start.3
  8.1 0.7 collective-permute-start.4
  8.7 3.9 %invert.1 = (f32[27,128,16]{2,1,0:T(8,128)S(1)}, f32[27,16,128]{2,1,0:T(8,128)}) custom-call(s32[4]{0:T(128)S(1)} %get-tuple-element.144.refs_0_, s32[27,1,768]{2,1,0:T(1,128)} %bitcast.25, s32[27,1,768]{2,1,0:T(1,128)} %bitcast.26, s32[27,1,768]{2,1,0:T(1,128)} %bitcast.27), custom_call_target="tpu_custom_call" | custom-call | tf_op jit(solution)/shard_map/invert/pallas_call | solution.py:142
  12.7 25.5 %forward.1 = (bf16[768,256]{1,0:T(8,128)(2,1)}, bf16[768,256]{1,0:T(8,128)(2,1)}, f32[6912,128]{1,0:T(8,128)S(1)}, bf16[3456,128]{1,0:T(8,128)(2,1)}, bf16[3456,128]{1,0:T(8,128)(2,1)}) custom-call(s32[4]{0:T(128)S(1)} %get-tuple-element.144.refs_0_, f32[27,128,16]{2,1,0:T(8,128)S(1)} %get-tuple-element.57.refs_1_, bf16[768,256]{1,0:T(8,128)(2,1)} %bitcast.22, ...), custom_call_target="tpu_custom_call" | custom-call | tf_op jit(solution)/shard_map/forward/pallas_call | solution.py:247
  38.2 3.0 %collective-permute-start.5 = (bf16[3456,128]{1,0:T(8,128)(2,1)}, bf16[3456,128]{1,0:T(8,128)(2,1)}, u32[]{:S(2)}, u32[]{:S(2)}) collective-permute-start(bf16[3456,128]{1,0:T(8,128)(2,1)} %get-tuple-element.67), channel_id=1, source_target_pairs={{0,1},{1,0},{2,3},{3,2},{4,5},{5,4},{6,7},{7,6},{8,9},{9,8},{10,11... | collective-permute-start | bytes 2654216 | tf_op jit(solution)/shard_map/ppermute | solution.py:420
  41.2 0.1 collective-permute-start.6
  41.2 2.3 %collective-permute-done.5 = bf16[3456,128]{1,0:T(8,128)(2,1)} collective-permute-done((bf16[3456,128]{1,0:T(8,128)(2,1)}, bf16[3456,128]{1,0:T(8,128)(2,1)}, u32[]{:S(2)}, u32[]{:S(2)}) %collective-permute-start.5) | collective-permute-done | bytes 884768 | tf_op jit(solution)/shard_map/ppermute | solution.py:420
  43.6 1.3 collective-permute-done.6
  44.8 2.3 %add_convert_fusion = (bf16[1728,128]{1,0:T(8,128)(2,1)}, bf16[1728,128]{1,0:T(8,128)(2,1)}) fusion(f32[6912,128]{1,0:T(8,128)S(1)} %get-tuple-element.66, s32[]{:T(128)S(6)} %select_n.166, bf16[3456,128]{1,0:T(8,128)(2,1)} %collective-permute-done.6, s32[]{:T(128)S(6)} %select_n.167, bf16[3456,128]{1,0:T(8,128)(2,1)} %collective-permute-done.5, ...), kind=kLoop, calls=%fused_computation | loop fusion | flops 1327104 | bytes 3538960 | tf_op jit(solution)/shard_map/convert_element_type | solution.py:477
  47.1 0.8 collective-permute-start.8
  47.9 0.5 collective-permute-start.7
  48.5 10.6 %backward_faces.1 = (bf16[96,256]{1,0:T(8,128)(2,1)}, bf16[96,256]{1,0:T(8,128)(2,1)}, bf16[96,256]{1,0:T(8,128)(2,1)}, bf16[96,256]{1,0:T(8,128)(2,1)}, bf16[96,256]{1,0:T(8,128)(2,1)}) custom-call(s32[4]{0:T(128)S(1)} %get-tuple-element.144.refs_0_, f32[27,16,128]{2,1,0:T(8,128)} %get-tuple-element.64.refs_1_.refs_0_.refs_2_, ...), custom_call_target="tpu_custom_call" | custom-call | tf_op jit(solution)/shard_map/backward_faces/pallas_call | solution.py:346
  59.1 0.8 collective-permute-done.8
  59.9 0.3 collective-permute-done.7
  60.2 2.2 %add_convert_fusion.2 = (bf16[864,128]{1,0:T(8,128)(2,1)}, bf16[864,128]{1,0:T(8,128)(2,1)}) fusion(f32[6912,128]{1,0:T(8,128)S(1)} %get-tuple-element.66, s32[]{:T(128)S(6)} %select_n.172, bf16[1728,128]{1,0:T(8,128)(2,1)} %collective-permute-done.8, s32[]{:T(128)S(6)} %select_n.174, bf16[3456,128]{1,0:T(8,128)(2,1)} %collective-permute-done.6, ...), kind=kLoop, calls=%fused_computation.2 | loop fusion | flops 1105920 | bytes 2211864 | tf_op jit(solution)/shard_map/convert_element_type | solution.py:477
  62.4 0.5 collective-permute-start.13
  62.9 1.4 %collective-permute-start.12 = (bf16[864,128]{1,0:T(8,128)(2,1)}, bf16[864,128]{1,0:T(8,128)(2,1)}, u32[]{:S(2)}, u32[]{:S(2)}) collective-permute-start(bf16[864,128]{1,0:T(8,128)(2,1)} %get-tuple-element.120), channel_id=1, source_target_pairs={{0,2},{1,3},{2,0},{3,1},{4,6},{5,7},{6,4},{7,5},{8,10},{9,11},{10,... | collective-permute-start | bytes 663560 | tf_op jit(solution)/shard_map/ppermute | solution.py:420
  64.3 4.4 %collective-permute-start.9 = (bf16[96,256]{1,0:T(8,128)(2,1)}, bf16[96,256]{1,0:T(8,128)(2,1)}, u32[]{:S(2)}, u32[]{:S(2)}) collective-permute-start(bf16[96,256]{1,0:T(8,128)(2,1)} %get-tuple-element.80), channel_id=1, source_target_pairs={{0,4},{4,0},{8,12},{12,8},{1,5},{5,1},{9,13},{13,9},{2,6},{6,2},{1... | collective-permute-start | bytes 147464 | tf_op jit(solution)/shard_map/ppermute | solution.py:60
  68.7 1.3 collective-permute-start.10
  70.0 1.1 collective-permute-done.9.refs_7_
  71.1 0.5 collective-permute-done.11.refs_9_
  71.6 1.1 add_convert_fusion.5
  72.7 1.1 add_convert_fusion.4
  73.8 3.5 %collective-permute-start.16 = (bf16[432,128]{1,0:T(8,128)(2,1)S(1)}, bf16[432,128]{1,0:T(8,128)(2,1)S(1)}, u32[]{:S(2)}, u32[]{:S(2)}) collective-permute-start(bf16[432,128]{1,0:T(8,128)(2,1)S(1)} %pad_maximum_fusion.2), channel_id=1, source_target_pairs={{0,4},{4,8},{8,12},{12,0},{1,5},{5,9},{9,13},{13,1},{2,6},{6,10},{... | collective-permute-start | bytes 331784 | tf_op jit(solution)/shard_map/ppermute | solution.py:485
  77.4 0.1 collective-permute-start.17
  77.5 2.4 %collective-permute-start.18 = (bf16[432,128]{1,0:T(8,128)(2,1)S(1)}, bf16[432,128]{1,0:T(8,128)(2,1)S(1)}, u32[]{:S(2)}, u32[]{:S(2)}) collective-permute-start(bf16[432,128]{1,0:T(8,128)(2,1)S(1)} %pad_maximum_fusion.4), channel_id=1, source_target_pairs={{0,12},{4,0},{8,4},{12,8},{1,13},{5,1},{9,5},{13,9},{2,14},{6,2},{... | collective-permute-start | bytes 331784 | tf_op jit(solution)/shard_map/ppermute | solution.py:485
  79.9 1.5 %collective-permute-start.14 = (bf16[96,256]{1,0:T(8,128)(2,1)}, bf16[96,256]{1,0:T(8,128)(2,1)S(1)}, u32[]{:S(2)}, u32[]{:S(2)}) collective-permute-start(bf16[96,256]{1,0:T(8,128)(2,1)} %get-tuple-element.88), channel_id=1, source_target_pairs={{0,16},{16,0},{1,17},{17,1},{2,18},{18,2},{3,19},{19,3},{4,20},{20... | collective-permute-start | bytes 147464 | tf_op jit(solution)/shard_map/ppermute | solution.py:60
  81.4 0.7 collective-permute-start.15
  82.1 1.0 convert_add_fusion.1
  83.1 3.5 %backward_own.2.refs_3_ = f32[768,256]{1,0:T(8,128)} custom-call(f32[27,16,128]{2,1,0:T(8,128)} %get-tuple-element.64.refs_1_.refs_0_.refs_2_, bf16[768,256]{1,0:T(8,128)(2,1)} %get-tuple-element.101.refs_2_.refs_1_.refs_3_, bf16[27,256,256]{2,1,0:T(8,128)(2,1)} %refs_4_.1), custom_call_target="tpu_custom_call" | custom-call | tf_op jit(solution)/shard_map/backward_own/pallas_call | solution.py:369
  86.7 0.1 fusion.3
  86.8 2.6 %collective-permute-start.21 = (bf16[432,128]{1,0:T(8,128)(2,1)S(1)}, bf16[432,128]{1,0:T(8,128)(2,1)S(1)}, u32[]{:S(2)}, u32[]{:S(2)}) collective-permute-start(bf16[432,128]{1,0:T(8,128)(2,1)S(1)} %fusion.3), channel_id=1, source_target_pairs={{0,12},{4,0},{8,4},{12,8},{1,13},{5,1},{9,5},{13,9},{2,14},{6,2},{... | collective-permute-start | bytes 331784 | tf_op jit(solution)/shard_map/ppermute | solution.py:485
  89.4 0.6 collective-permute-start.20
  90.1 7.5 %backward_own.3.refs_5_ = f32[768,256]{1,0:T(8,128)} custom-call(f32[27,16,128]{2,1,0:T(8,128)} %get-tuple-element.64.refs_1_.refs_0_.refs_2_, bf16[768,256]{1,0:T(8,128)(2,1)} %get-tuple-element.101.refs_2_.refs_1_.refs_3_, bf16[27,256,256]{2,1,0:T(8,128)(2,1)} %refs_4_.1, f32[768,256]{1,0:T(8,128)} %backward_own.2.refs_3_), custom_call_target="tpu_custom_call" | custom-call | tf_op jit(solution)/shard_map/backward_own/pallas_call | solution.py:369
  97.7 2.7 %collective-permute-done.20 = bf16[432,128]{1,0:T(8,128)(2,1)S(1)} collective-permute-done((bf16[432,128]{1,0:T(8,128)(2,1)S(1)}, bf16[432,128]{1,0:T(8,128)(2,1)S(1)}, u32[]{:S(2)}, u32[]{:S(2)}) %collective-permute-start.20) | collective-permute-done | bytes 110624 | tf_op jit(solution)/shard_map/ppermute | solution.py:485
  100.5 1.4 %collective-permute-start.23 = (bf16[864,128]{1,0:T(8,128)(2,1)S(1)}, bf16[864,128]{1,0:T(8,128)(2,1)S(1)}, u32[]{:S(2)}, u32[]{:S(2)}) collective-permute-start(bf16[864,128]{1,0:T(8,128)(2,1)S(1)} %pad_maximum_fusion.1), channel_id=1, source_target_pairs={{0,16},{16,0},{1,17},{17,1},{2,18},{18,2},{3,19},{19,3},{4,20},{20... | collective-permute-start | bytes 663560 | tf_op jit(solution)/shard_map/ppermute | solution.py:420
  101.9 0.7 collective-permute-start.22
  102.6 5.4 %collective-permute-done.23 = bf16[864,128]{1,0:T(8,128)(2,1)S(1)} collective-permute-done((bf16[864,128]{1,0:T(8,128)(2,1)S(1)}, bf16[864,128]{1,0:T(8,128)(2,1)S(1)}, u32[]{:S(2)}, u32[]{:S(2)}) %collective-permute-start.23) | collective-permute-done | bytes 221216 | tf_op jit(solution)/shard_map/ppermute | solution.py:420
  108.1 0.1 collective-permute-start.25
  108.1 0.8 collective-permute-done.22
  109.0 0.9 collective-permute-start.24
  110.0 0.1 broadcast_add_fusion.4
  110.0 0.0 collective-permute-start.29
  110.1 0.5 collective-permute-start.28
  110.5 8.9 %finish.1 = bf16[768,256]{1,0:T(8,128)(2,1)} custom-call(s32[4]{0:T(128)S(1)} %get-tuple-element.144.refs_0_, s32[6,1,96]{2,1,0:T(1,128)} %bitcast.29, f32[27,16,128]{2,1,0:T(8,128)} %get-tuple-element.64.refs_1_.refs_0_.refs_2_, bf16[768,256]{1,0:T(8,128)(2,1)} %get-tuple-element.101.refs_2_.refs_1_.refs_3_, bf16[27,256,256]{2,1,0:T(8,128)(2,1)} %refs_4_.1, ...), custom_call_target="tpu_custom_call" | custom-call | tf_op jit(solution)/shard_map/finish/pallas_call | solution.py:402
  119.4 0.1 collective-permute-done.25.refs_2_
  119.5 0.5 collective-permute-done.24.refs_1_
  119.9 0.5 collective-permute-start.27
  120.5 0.1 broadcast_add_fusion.6
  120.5 0.6 broadcast_add_fusion
  121.2 0.1 add.601
  121.2 0.1 add.591
  121.3 0.8 add.596
  122.1 0.6 add.585
  122.7 0.6 add_multiply_fusion.2
  123.3 0.7 concatenate.62.refs_0_
  124.0 0.8 concatenate.61.refs_0_
  124.8 2.0 %place.2.refs_5_ = bf16[6912,256]{1,0:T(8,128)(2,1)} custom-call(s32[36]{0:T(128)S(1)} %concatenate.62.refs_0_, bf16[1728,128]{1,0:T(8,128)(2,1)S(1)} %constant_dynamic-update-slice_fusion.refs_1_, bf16[1728,128]{1,0:T(8,128)(2,1)S(1)} %constant_dynamic-update-slice_fusion.5.refs_2_, bf16[1728,128]{1,0:T(8,128)(2,1)S(1)} %collective-permute-done.28.refs_3_, ...), custom_call_target="tpu_custom_call" | custom-call | tf_op jit(solution)/shard_map/place/pallas_call | solution.py:447
  126.8 2.0 %place.3 = bf16[6912,256]{1,0:T(8,128)(2,1)} custom-call(s32[36]{0:T(128)S(1)} %concatenate.61.refs_0_, bf16[1728,128]{1,0:T(8,128)(2,1)S(1)} %collective-permute-done.24.refs_1_, bf16[1728,128]{1,0:T(8,128)(2,1)S(1)} %collective-permute-done.25.refs_2_, bf16[1728,128]{1,0:T(8,128)(2,1)S(1)} %collective-permute-done.26.refs_3_, ...), custom_call_target="tpu_custom_call", output_to_operand_aliasing={{}: (5, {})} | custom-call | tf_op jit(solution)/shard_map/place/pallas_call | solution.py:447
  (37 shorter events, 0.3 us)
Async XLA Ops:
  2.7 9.9 %collective-permute-start = (bf16[96,256]{1,0:T(8,128)(2,1)S(1)}, bf16[96,256]{1,0:T(8,128)(2,1)S(1)}, u32[]{:S(2)}, u32[]{:S(2)}) collective-permute-start(bf16[96,256]{1,0:T(8,128)(2,1)S(1)} %get-tuple-element.58), channel_id=1, source_target_pairs={{0,16},{16,0},{1,17},{17,1},{2,18},{18,2},{3,19},{19,3},{4,20},{20... | collective-permute-start | bytes 147464 | tf_op jit(solution)/shard_map/ppermute | solution.py:60
  5.7 6.9 %collective-permute-start.1 = (bf16[96,256]{1,0:T(8,128)(2,1)S(1)}, bf16[96,256]{1,0:T(8,128)(2,1)S(1)}, u32[]{:S(2)}, u32[]{:S(2)}) collective-permute-start(bf16[96,256]{1,0:T(8,128)(2,1)S(1)} %get-tuple-element.59), channel_id=1, source_target_pairs={{0,4},{4,0},{8,12},{12,8},{1,5},{5,1},{9,13},{13,9},{2,6},{6,2},{1... | collective-permute-start | bytes 147464 | tf_op jit(solution)/shard_map/ppermute | solution.py:60
  7.3 5.3 %collective-permute-start.2 = (bf16[96,256]{1,0:T(8,128)(2,1)S(1)}, bf16[96,256]{1,0:T(8,128)(2,1)S(1)}, u32[]{:S(2)}, u32[]{:S(2)}) collective-permute-start(bf16[96,256]{1,0:T(8,128)(2,1)S(1)} %get-tuple-element.60), channel_id=1, source_target_pairs={{4,8},{8,4},{5,9},{9,5},{6,10},{10,6},{7,11},{11,7},{20,24},{24,20... | collective-permute-start | bytes 147464 | tf_op jit(solution)/shard_map/ppermute | solution.py:60
  8.0 4.7 %collective-permute-start.3 = (bf16[96,256]{1,0:T(8,128)(2,1)S(1)}, bf16[96,256]{1,0:T(8,128)(2,1)S(1)}, u32[]{:S(2)}, u32[]{:S(2)}) collective-permute-start(bf16[96,256]{1,0:T(8,128)(2,1)S(1)} %get-tuple-element.61), channel_id=1, source_target_pairs={{0,1},{1,0},{2,3},{3,2},{4,5},{5,4},{6,7},{7,6},{8,9},{9,8},{10,11... | collective-permute-start | bytes 147464 | tf_op jit(solution)/shard_map/ppermute | solution.py:60
  8.1 4.6 %collective-permute-start.4 = (bf16[96,256]{1,0:T(8,128)(2,1)S(1)}, bf16[96,256]{1,0:T(8,128)(2,1)S(1)}, u32[]{:S(2)}, u32[]{:S(2)}) collective-permute-start(bf16[96,256]{1,0:T(8,128)(2,1)S(1)} %get-tuple-element.62), channel_id=1, source_target_pairs={{1,2},{2,1},{5,6},{6,5},{9,10},{10,9},{13,14},{14,13},{17,18},{18,... | collective-permute-start | bytes 147464 | tf_op jit(solution)/shard_map/ppermute | solution.py:60
  38.2 5.4 %collective-permute-start.5 = (bf16[3456,128]{1,0:T(8,128)(2,1)}, bf16[3456,128]{1,0:T(8,128)(2,1)}, u32[]{:S(2)}, u32[]{:S(2)}) collective-permute-start(bf16[3456,128]{1,0:T(8,128)(2,1)} %get-tuple-element.67), channel_id=1, source_target_pairs={{0,1},{1,0},{2,3},{3,2},{4,5},{5,4},{6,7},{7,6},{8,9},{9,8},{10,11... | collective-permute-start | bytes 2654216 | tf_op jit(solution)/shard_map/ppermute | solution.py:420
  41.2 3.7 %collective-permute-start.6 = (bf16[3456,128]{1,0:T(8,128)(2,1)}, bf16[3456,128]{1,0:T(8,128)(2,1)}, u32[]{:S(2)}, u32[]{:S(2)}) collective-permute-start(bf16[3456,128]{1,0:T(8,128)(2,1)} %get-tuple-element.68), channel_id=1, source_target_pairs={{0,1},{1,0},{2,3},{3,2},{4,5},{5,4},{6,7},{7,6},{8,9},{9,8},{10,11... | collective-permute-start | bytes 2654216 | tf_op jit(solution)/shard_map/ppermute | solution.py:420
  47.1 12.8 %collective-permute-start.8 = (bf16[1728,128]{1,0:T(8,128)(2,1)}, bf16[1728,128]{1,0:T(8,128)(2,1)}, u32[]{:S(2)}, u32[]{:S(2)}) collective-permute-start(bf16[1728,128]{1,0:T(8,128)(2,1)} %get-tuple-element.121), channel_id=1, source_target_pairs={{0,2},{1,3},{2,0},{3,1},{4,6},{5,7},{6,4},{7,5},{8,10},{9,11},{10,... | collective-permute-start | bytes 1327112 | tf_op jit(solution)/shard_map/ppermute | solution.py:420
  47.9 12.2 %collective-permute-start.7 = (bf16[1728,128]{1,0:T(8,128)(2,1)}, bf16[1728,128]{1,0:T(8,128)(2,1)}, u32[]{:S(2)}, u32[]{:S(2)}) collective-permute-start(bf16[1728,128]{1,0:T(8,128)(2,1)} %get-tuple-element.122), channel_id=1, source_target_pairs={{0,16},{16,0},{1,17},{17,1},{2,18},{18,2},{3,19},{19,3},{4,20},{20... | collective-permute-start | bytes 1327112 | tf_op jit(solution)/shard_map/ppermute | solution.py:420
  62.4 9.2 %collective-permute-start.13 = (bf16[864,128]{1,0:T(8,128)(2,1)}, bf16[864,128]{1,0:T(8,128)(2,1)}, u32[]{:S(2)}, u32[]{:S(2)}) collective-permute-start(bf16[864,128]{1,0:T(8,128)(2,1)} %get-tuple-element.119), channel_id=1, source_target_pairs={{0,16},{16,0},{1,17},{17,1},{2,18},{18,2},{3,19},{19,3},{4,20},{20... | collective-permute-start | bytes 663560 | tf_op jit(solution)/shard_map/ppermute | solution.py:420
  62.9 8.6 %collective-permute-start.12 = (bf16[864,128]{1,0:T(8,128)(2,1)}, bf16[864,128]{1,0:T(8,128)(2,1)}, u32[]{:S(2)}, u32[]{:S(2)}) collective-permute-start(bf16[864,128]{1,0:T(8,128)(2,1)} %get-tuple-element.120), channel_id=1, source_target_pairs={{0,2},{1,3},{2,0},{3,1},{4,6},{5,7},{6,4},{7,5},{8,10},{9,11},{10,... | collective-permute-start | bytes 663560 | tf_op jit(solution)/shard_map/ppermute | solution.py:420
  64.3 6.8 %collective-permute-start.9 = (bf16[96,256]{1,0:T(8,128)(2,1)}, bf16[96,256]{1,0:T(8,128)(2,1)}, u32[]{:S(2)}, u32[]{:S(2)}) collective-permute-start(bf16[96,256]{1,0:T(8,128)(2,1)} %get-tuple-element.80), channel_id=1, source_target_pairs={{0,4},{4,0},{8,12},{12,8},{1,5},{5,1},{9,13},{13,9},{2,6},{6,2},{1... | collective-permute-start | bytes 147464 | tf_op jit(solution)/shard_map/ppermute | solution.py:60
  68.7 2.4 %collective-permute-start.10 = (bf16[96,256]{1,0:T(8,128)(2,1)}, bf16[96,256]{1,0:T(8,128)(2,1)}, u32[]{:S(2)}, u32[]{:S(2)}) collective-permute-start(bf16[96,256]{1,0:T(8,128)(2,1)} %get-tuple-element.81), channel_id=1, source_target_pairs={{4,8},{8,4},{5,9},{9,5},{6,10},{10,6},{7,11},{11,7},{20,24},{24,20... | collective-permute-start | bytes 147464 | tf_op jit(solution)/shard_map/ppermute | solution.py:60
  70.0 1.6 %collective-permute-start.11 = (bf16[96,256]{1,0:T(8,128)(2,1)}, bf16[96,256]{1,0:T(8,128)(2,1)}, u32[]{:S(2)}, u32[]{:S(2)}) collective-permute-start(bf16[96,256]{1,0:T(8,128)(2,1)} %get-tuple-element.82), channel_id=1, source_target_pairs={{0,1},{1,0},{2,3},{3,2},{4,5},{5,4},{6,7},{7,6},{8,9},{9,8},{10,11... | collective-permute-start | bytes 147464 | tf_op jit(solution)/shard_map/ppermute | solution.py:60
  73.8 12.8 %collective-permute-start.16 = (bf16[432,128]{1,0:T(8,128)(2,1)S(1)}, bf16[432,128]{1,0:T(8,128)(2,1)S(1)}, u32[]{:S(2)}, u32[]{:S(2)}) collective-permute-start(bf16[432,128]{1,0:T(8,128)(2,1)S(1)} %pad_maximum_fusion.2), channel_id=1, source_target_pairs={{0,4},{4,8},{8,12},{12,0},{1,5},{5,9},{9,13},{13,1},{2,6},{6,10},{... | collective-permute-start | bytes 331784 | tf_op jit(solution)/shard_map/ppermute | solution.py:485
  77.4 9.3 %collective-permute-start.17 = (bf16[432,128]{1,0:T(8,128)(2,1)S(1)}, bf16[432,128]{1,0:T(8,128)(2,1)S(1)}, u32[]{:S(2)}, u32[]{:S(2)}) collective-permute-start(bf16[432,128]{1,0:T(8,128)(2,1)S(1)} %pad_maximum_fusion.3), channel_id=1, source_target_pairs={{0,8},{4,12},{8,0},{12,4},{1,9},{5,13},{9,1},{13,5},{2,10},{6,14},... | collective-permute-start | bytes 331784 | tf_op jit(solution)/shard_map/ppermute | solution.py:485
  77.5 9.2 %collective-permute-start.18 = (bf16[432,128]{1,0:T(8,128)(2,1)S(1)}, bf16[432,128]{1,0:T(8,128)(2,1)S(1)}, u32[]{:S(2)}, u32[]{:S(2)}) collective-permute-start(bf16[432,128]{1,0:T(8,128)(2,1)S(1)} %pad_maximum_fusion.4), channel_id=1, source_target_pairs={{0,12},{4,0},{8,4},{12,8},{1,13},{5,1},{9,5},{13,9},{2,14},{6,2},{... | collective-permute-start | bytes 331784 | tf_op jit(solution)/shard_map/ppermute | solution.py:485
  79.9 6.7 %collective-permute-start.14 = (bf16[96,256]{1,0:T(8,128)(2,1)}, bf16[96,256]{1,0:T(8,128)(2,1)S(1)}, u32[]{:S(2)}, u32[]{:S(2)}) collective-permute-start(bf16[96,256]{1,0:T(8,128)(2,1)} %get-tuple-element.88), channel_id=1, source_target_pairs={{0,16},{16,0},{1,17},{17,1},{2,18},{18,2},{3,19},{19,3},{4,20},{20... | collective-permute-start | bytes 147464 | tf_op jit(solution)/shard_map/ppermute | solution.py:60
  81.4 5.3 %collective-permute-start.15 = (bf16[96,256]{1,0:T(8,128)(2,1)}, bf16[96,256]{1,0:T(8,128)(2,1)S(1)}, u32[]{:S(2)}, u32[]{:S(2)}) collective-permute-start(bf16[96,256]{1,0:T(8,128)(2,1)} %get-tuple-element.89), channel_id=1, source_target_pairs={{1,2},{2,1},{5,6},{6,5},{9,10},{10,9},{13,14},{14,13},{17,18},{18,... | collective-permute-start | bytes 147464 | tf_op jit(solution)/shard_map/ppermute | solution.py:60
  86.6 13.8 %copy-start = (bf16[96,256]{1,0:T(8,128)(2,1)}, bf16[96,256]{1,0:T(8,128)(2,1)S(1)}, u32[]{:S(2)}) copy-start(bf16[96,256]{1,0:T(8,128)(2,1)S(1)} %collective-permute-done.14.refs_6_) | copy-start | bytes 147460
  86.7 13.8 %copy-start.1 = (bf16[96,256]{1,0:T(8,128)(2,1)}, bf16[96,256]{1,0:T(8,128)(2,1)S(1)}, u32[]{:S(2)}) copy-start(bf16[96,256]{1,0:T(8,128)(2,1)S(1)} %collective-permute-done.15.refs_10_) | copy-start | bytes 147460
  86.8 10.9 %collective-permute-start.21 = (bf16[432,128]{1,0:T(8,128)(2,1)S(1)}, bf16[432,128]{1,0:T(8,128)(2,1)S(1)}, u32[]{:S(2)}, u32[]{:S(2)}) collective-permute-start(bf16[432,128]{1,0:T(8,128)(2,1)S(1)} %fusion.3), channel_id=1, source_target_pairs={{0,12},{4,0},{8,4},{12,8},{1,13},{5,1},{9,5},{13,9},{2,14},{6,2},{... | collective-permute-start | bytes 331784 | tf_op jit(solution)/shard_map/ppermute | solution.py:485
  89.4 10.9 %collective-permute-start.20 = (bf16[432,128]{1,0:T(8,128)(2,1)S(1)}, bf16[432,128]{1,0:T(8,128)(2,1)S(1)}, u32[]{:S(2)}, u32[]{:S(2)}) collective-permute-start(bf16[432,128]{1,0:T(8,128)(2,1)S(1)} %fusion.3), channel_id=1, source_target_pairs={{0,8},{4,12},{8,0},{12,4},{1,9},{5,13},{9,1},{13,5},{2,10},{6,14},... | collective-permute-start | bytes 331784 | tf_op jit(solution)/shard_map/ppermute | solution.py:485
  90.1 10.3 %collective-permute-start.19 = (bf16[432,128]{1,0:T(8,128)(2,1)S(1)}, bf16[432,128]{1,0:T(8,128)(2,1)S(1)}, u32[]{:S(2)}, u32[]{:S(2)}) collective-permute-start(bf16[432,128]{1,0:T(8,128)(2,1)S(1)} %fusion.3), channel_id=1, source_target_pairs={{0,4},{4,8},{8,12},{12,0},{1,5},{5,9},{9,13},{13,1},{2,6},{6,10},{... | collective-permute-start | bytes 331784 | tf_op jit(solution)/shard_map/ppermute | solution.py:485
  100.5 7.5 %collective-permute-start.23 = (bf16[864,128]{1,0:T(8,128)(2,1)S(1)}, bf16[864,128]{1,0:T(8,128)(2,1)S(1)}, u32[]{:S(2)}, u32[]{:S(2)}) collective-permute-start(bf16[864,128]{1,0:T(8,128)(2,1)S(1)} %pad_maximum_fusion.1), channel_id=1, source_target_pairs={{0,16},{16,0},{1,17},{17,1},{2,18},{18,2},{3,19},{19,3},{4,20},{20... | collective-permute-start | bytes 663560 | tf_op jit(solution)/shard_map/ppermute | solution.py:420
  101.9 7.1 %collective-permute-start.22 = (bf16[864,128]{1,0:T(8,128)(2,1)S(1)}, bf16[864,128]{1,0:T(8,128)(2,1)S(1)}, u32[]{:S(2)}, u32[]{:S(2)}) collective-permute-start(bf16[864,128]{1,0:T(8,128)(2,1)S(1)} %pad_maximum_fusion), channel_id=1, source_target_pairs={{0,2},{1,3},{2,0},{3,1},{4,6},{5,7},{6,4},{7,5},{8,10},{9,11},{10,... | collective-permute-start | bytes 663560 | tf_op jit(solution)/shard_map/ppermute | solution.py:420
  108.1 11.4 %collective-permute-start.25 = (bf16[1728,128]{1,0:T(8,128)(2,1)S(1)}, bf16[1728,128]{1,0:T(8,128)(2,1)S(1)}, u32[]{:S(2)}, u32[]{:S(2)}) collective-permute-start(bf16[1728,128]{1,0:T(8,128)(2,1)S(1)} %constant_dynamic-update-slice_fusion.5.refs_2_), channel_id=1, source_target_pairs={{0,2},{1,3},{2,0},{3,1},{4,6},{5,7},{6,4},{7,5},{8,10},{9,11},{10,... | collective-permute-start | bytes 1327112 | tf_op jit(solution)/shard_map/ppermute | solution.py:420
  109.0 10.9 %collective-permute-start.24 = (bf16[1728,128]{1,0:T(8,128)(2,1)S(1)}, bf16[1728,128]{1,0:T(8,128)(2,1)S(1)}, u32[]{:S(2)}, u32[]{:S(2)}) collective-permute-start(bf16[1728,128]{1,0:T(8,128)(2,1)S(1)} %constant_dynamic-update-slice_fusion.refs_1_), channel_id=1, source_target_pairs={{0,16},{16,0},{1,17},{17,1},{2,18},{18,2},{3,19},{19,3},{4,20},{20... | collective-permute-start | bytes 1327112 | tf_op jit(solution)/shard_map/ppermute | solution.py:420
  110.0 14.8 %collective-permute-start.29 = (bf16[1728,128]{1,0:T(8,128)(2,1)S(1)}, bf16[1728,128]{1,0:T(8,128)(2,1)S(1)}, u32[]{:S(2)}, u32[]{:S(2)}) collective-permute-start(bf16[1728,128]{1,0:T(8,128)(2,1)S(1)} %constant_dynamic-update-slice_fusion.5.refs_2_), channel_id=1, source_target_pairs={{0,1},{1,0},{2,3},{3,2},{4,5},{5,4},{6,7},{7,6},{8,9},{9,8},{10,11... | collective-permute-start | bytes 1327112 | tf_op jit(solution)/shard_map/ppermute | solution.py:420
  110.1 14.7 %collective-permute-start.28 = (bf16[1728,128]{1,0:T(8,128)(2,1)S(1)}, bf16[1728,128]{1,0:T(8,128)(2,1)S(1)}, u32[]{:S(2)}, u32[]{:S(2)}) collective-permute-start(bf16[1728,128]{1,0:T(8,128)(2,1)S(1)} %constant_dynamic-update-slice_fusion.refs_1_), channel_id=1, source_target_pairs={{0,1},{1,0},{2,3},{3,2},{4,5},{5,4},{6,7},{7,6},{8,9},{9,8},{10,11... | collective-permute-start | bytes 1327112 | tf_op jit(solution)/shard_map/ppermute | solution.py:420
  119.9 6.9 %collective-permute-start.26 = (bf16[1728,128]{1,0:T(8,128)(2,1)S(1)}, bf16[1728,128]{1,0:T(8,128)(2,1)S(1)}, u32[]{:S(2)}, u32[]{:S(2)}) collective-permute-start(bf16[1728,128]{1,0:T(8,128)(2,1)S(1)} %collective-permute-done.24.refs_1_), channel_id=1, source_target_pairs={{0,1},{1,0},{2,3},{3,2},{4,5},{5,4},{6,7},{7,6},{8,9},{9,8},{10,11... | collective-permute-start | bytes 1327112 | tf_op jit(solution)/shard_map/ppermute | solution.py:420
  119.9 6.9 %collective-permute-start.27 = (bf16[1728,128]{1,0:T(8,128)(2,1)S(1)}, bf16[1728,128]{1,0:T(8,128)(2,1)S(1)}, u32[]{:S(2)}, u32[]{:S(2)}) collective-permute-start(bf16[1728,128]{1,0:T(8,128)(2,1)S(1)} %collective-permute-done.25.refs_2_), channel_id=1, source_target_pairs={{0,1},{1,0},{2,3},{3,2},{4,5},{5,4},{6,7},{7,6},{8,9},{9,8},{10,11... | collective-permute-start | bytes 1327112 | tf_op jit(solution)/shard_map/ppermute | solution.py:420

commit v9 on v8

--- a/solution.py
+++ b/solution.py
@@ -101,22 +101,14 @@
     )(flags, hold(rows), hold(own_features))
 
 
-def invert_kernel(block, face, pairs, flags, in_hbm, out_hbm, live_hbm, col_ref, row_hbm, tables, row_ref, sems):
-    copies = [
-        pltpu.make_async_copy(hbm, tables.at[j], sems.at[j])
-        for j, hbm in enumerate((in_hbm, out_hbm, live_hbm))
-    ]
-    for copy in copies:
-        copy.start()
-    taps, _, own = in_hbm.shape
+def invert_kernel(block, face, pairs, flags, in_ref, out_ref, live_ref, col_ref, row_hbm, row_ref, sem):
+    taps, _, own = in_ref.shape
     lows = lax.broadcasted_iota(jnp.int32, (block, own), 0)
     ranks = lax.broadcasted_iota(jnp.int32, (16, own), 0)
-    for copy in copies:
-        copy.wait()
     for k in range(taps):
-        target = tables[1, k]
-        source = tables[0, k]
-        live = tables[2, k] > 0
+        target = out_ref[k]
+        source = in_ref[k]
+        live = live_ref[k] > 0
         for i in pairs:
             dead = own + (2 * i + flags[1 + i]) * face
             beyond = source >= dead + face
@@ -131,7 +123,7 @@
         col = dot(hot, spread, NT)
         col_ref[k] = col
         row_ref[k] = col.T
-    copy = pltpu.make_async_copy(row_ref, row_hbm, sems.at[3])
+    copy = pltpu.make_async_copy(row_ref, row_hbm, sem)
     copy.start()
     copy.wait()
 
@@ -141,20 +133,19 @@
     taps, _, own = in_rows.shape
     return pl.pallas_call(
         lambda *refs: invert_kernel(block, face, pairs, *refs),
-        in_specs=[SMEM, HBM, HBM, HBM],
+        in_specs=[SMEM, VMEM, VMEM, VMEM],
         out_specs=[VMEM, HBM],
         out_shape=(
             jax.ShapeDtypeStruct((taps, block, 16), F32),
             pltpu.HBM((taps, 16, block), F32),
         ),
         scratch_shapes=[
-            pltpu.VMEM((3, taps, 1, own), jnp.int32),
             pltpu.VMEM((taps, 16, block), F32),
-            pltpu.SemaphoreType.DMA((4,)),
+            pltpu.SemaphoreType.DMA,
         ],
         compiler_params=params(12),
         name="invert",
-    )(flags, hold(in_rows), hold(out_rows), hold(live))
+    )(flags, in_rows, out_rows, live)
 
 
 def forward_kernel(ways, where, step, flags, col_ref, own_hbm, w_hbm, up_hbm, *rest):
@@ -303,7 +294,7 @@
             got[pl.ds(r, step), pl.ds(at, ch)] = dot(jnp.concatenate(hots, axis=1), gp[...]).astype(BF)
         return carried
 
-    lax.fori_loop(0, count, gather, 0, unroll=next(u for u in (9, 6, 3, 1) if count % u == 0))
+    lax.fori_loop(0, count, gather, 0, unroll=next(u for u in (9, 6, 5, 3, 1) if count % u == 0))
     for copy in later:
         copy.wait()
     for r in range(0, size, step):
@@ -424,28 +415,35 @@
     return (lax.axis_index(axis) >> bit) & 1
 
 
-def place_kernel(size, spots_ref, *refs):
-    count = len(refs) - 2
-    arrays, out, sem = refs[: count - (count % 2)], refs[-2], refs[-1]
+def place_kernel(size, turns, n, flip, spots, *refs):
+    arrays, out, sem = refs[:4], refs[-2], refs[-1]
+    half, ch = out.shape[0] // 2, out.shape[1] // 2
+    at, odd = spots[2 * turns], spots[2 * turns + 1]
     copies = []
     for a, array in enumerate(arrays):
-        blocks = array.shape[0] // size
-        for b in range(blocks):
-            at = pl.multiple_of(spots_ref[a * blocks + b], 8)
-            lane = pl.multiple_of(spots_ref[len(arrays) * blocks + a], 128)
-            target = out.at[pl.ds(at, size), pl.ds(lane, array.shape[1])]
-            copies.append(pltpu.make_async_copy(array.at[pl.ds(b * size, size), :], target, sem.at[a * blocks + b]))
-    for copy in copies:
-        copy.start()
+        i, twin = a % 2, a // 2
+        side_of = lambda t, r: jnp.bitwise_xor(spots[i * turns + t], r)
+        lane = pl.multiple_of((odd if twin == 0 else 1 - odd) * ch, 128)
+        for b in range(array.shape[0] // size):
+            s, rest = b % n, b // n
+            row = i * half + side_of(0, flip) * (half // 2)
+            for t in range(turns - 1, 0, -1):
+                row = row + side_of(t, rest % 2) * (half >> (t + 1))
+                rest = rest // 2
+            row = row + jnp.where(at >= s, at - s, at - s + n) * size
+            target = out.at[pl.ds(pl.multiple_of(row, 8), size), pl.ds(lane, ch)]
+            copies.append(pltpu.make_async_copy(array.at[pl.ds(b * size, size), :], target, sem.at[len(copies)]))
+            copies[-1].start()
     for copy in copies:
         copy.wait()
 
 
-def place(spots, arrays, size, rows, before):
+def place(spots, arrays, size, turns, rows, flip, before):
     blocks = len(arrays) * (arrays[0].shape[0] // size)
+    n = lax.axis_size("gy")
     args = list(arrays) + ([] if before is None else [before])
     return pl.pallas_call(
-        lambda *refs: place_kernel(size, *refs),
+        lambda *refs: place_kernel(size, turns, n, flip, *refs),
         in_specs=[SMEM] + [ANY] * len(arrays) + [HBM] * (len(args) - len(arrays)),
         out_specs=HBM,
         out_shape=jax.ShapeDtypeStruct((rows, 2 * arrays[0].shape[1]), BF),
@@ -461,6 +459,7 @@
     plane = [bits("gx", 0) + bits("gz", 1), bits("gz", 1) + bits("gx", 0)]
     turns = len(plane[0])
     rows, ch = keep.shape
+    sides = [[side(*plane[i][t]) for t in range(turns)] for i in range(2)]
     terms = [[(keep, i * (rows // 2)), (swap(give[i], "gz", 0), 0)] for i in range(2)]
 
     def total(i, extra, size):
@@ -498,24 +497,11 @@
     cross = lambda arrays: [swap(y, "gz", 0) for y in arrays]
     came = beside(pieces, [swap(pieces[i], *plane[i][0]) for i in range(2)])
     twins = cross(pieces)
-    sides = [[side(*plane[i][t]) for t in range(turns)] for i in range(2)]
     if size % 8 == 0:
-        lanes = jnp.stack([odd, odd, 1 - odd, 1 - odd]) * ch
-
-        def spots(flip):
-            out = []
-            for i in range(2):
-                base = jnp.asarray(i * (rows // 2) + (sides[i][0] ^ flip) * (rows // 4))[None]
-                for t in range(1, turns):
-                    order = jnp.stack([sides[i][t], 1 - sides[i][t]]) * (rows // (4 << t))
-                    base = (base[:, None] + order[None, :]).reshape(-1)
-                order = ((at - jnp.arange(n)) % n) * size
-                out.append((base[:, None] + order[None, :]).reshape(-1))
-            return jnp.concatenate(out + out + [lanes]).astype(jnp.int32)
-
-        half = place(spots(0), pieces + twins, size, rows, None)
+        spots = jnp.stack(sides[0] + sides[1] + [at, odd]).astype(jnp.int32)
+        half = place(spots, pieces + twins, size, turns, rows, 0, None)
         last = cross(came)
-        return place(spots(1), came + last, size, rows, half)
+        return place(spots, came + last, size, turns, rows, 1, half)
     last = cross(came)
 
     def ordered(i, first, second):
@@ -546,7 +532,7 @@
     )
     activated, gp, keep, *give = forward(ways, flags, col, own_features, faces, weight, upstream[0, 0, 0])
     devices = lax.axis_size("gx") * lax.axis_size("gy") * lax.axis_size("gz")
-    split = (0, 3, 15)
+    split = (0, 3, 18)
     state = {"turn": 0, "returned": {}, "grad": []}
     late = [j for j, way in enumerate(ways) if way in ((0, 0), (1, 2))]
     early = [j for j in range(len(ways)) if j not in late]

time: 130 us -> 127 us (0.977)
  other arithmetic: 9.36 us -> 7.98 us
    unnamed x4 -> x10, local copies, waits for them, and re-layouts: 0.01 us -> 2.66 us
    ppermute x14, waiting for transfers between devices: 11.5 us -> 13.1 us  [swap(): return lax.ppermute(x, axis, [(j, j ^ 1 << bit) for j in range(n)])]
    add x4 -> x0, local copies, waits for them, and re-layouts: 1.51 us -> none  [spots(): out.append((base[:, None] + order[None, :]).reshape(-1))]
    concatenate x2 -> x0, local copies, waits for them, and re-layouts: 1.5 us -> none  [spots(): return jnp.concatenate(out + out + [lanes]).astype(jnp.int32)]
    ppermute x6, waiting for transfers between devices: 2.69 us -> 1.23 us  [reduce_all(): lax.ppermute(y, 'gy', [(j, (j + s) % n) for j in range(n)])]
    pallas_call x2, Pallas kernels: 11.1 us -> 12.5 us  [backward_own(): pl.pallas_call(lambda *refs: own_kernel(first, count, *refs), in_specs=[H...]
    pallas_call x1, Pallas kernels: 8.85 us -> 7.43 us  [finish(): pl.pallas_call(lambda *refs: finish_kernel(ways, first, count, *refs), in...]
  transfers between devices with their start and end apart: 30 -> 30, of which waited for: 11 -> 11; matrix products, arithmetic and copies ran while one was open for 4% -> 1% of each run, Pallas kernels for 28% -> 28%
where the time goes in v9:
time: 127 us; the launch traced here: 126 us
  Pallas kernels  64.9 us (51%)
  starting transfers between devices  33.5 us (26%)
  waiting for transfers between devices  15.9 us (13%)
  other arithmetic  7.98 us (6%)
  local copies, waits for them, and re-layouts  2.96 us (2%)
    pallas_call x1, Pallas kernels, forward(): pl.pallas_call(lambda *refs: forward_kernel(ways, where, 256, *refs), in_...  25.5 us
    ppermute x10, starting transfers between devices, exchange(): got.append(lax.ppermute(array, AXES[i], pairs))  13.8 us
    ppermute x14, waiting for transfers between devices, swap(): return lax.ppermute(x, axis, [(j, j ^ 1 << bit) for j in range(n)])  13.1 us
    pallas_call x2, Pallas kernels, backward_own(): pl.pallas_call(lambda *refs: own_kernel(first, count, *refs), in_specs=[H...  12.5 us
    pallas_call x1, Pallas kernels, backward_faces(): pl.pallas_call(lambda *refs: faces_kernel(ways, where, own, taps, *refs),...  10.6 us
    ppermute x14, starting transfers between devices, swap(): return lax.ppermute(x, axis, [(j, j ^ 1 << bit) for j in range(n)])  10.4 us
    ppermute x6, starting transfers between devices, reduce_all(): lax.ppermute(y, 'gy', [(j, (j + s) % n) for j in range(n)])  9.33 us
    pallas_call x1, Pallas kernels, finish(): pl.pallas_call(lambda *refs: finish_kernel(ways, first, count, *refs), in...  7.43 us
  transfers between devices with their start and end apart: 30, of which 11 were waited for; matrix products, arithmetic and copies ran while one was open for 1% of the time, Pallas kernels for 28%

profile of v9, /device:TPU:0, one launch (start us, length us, event | category | flops | bytes accessed | tf_op | source)
XLA Modules:
  0.0 126.4 jit_solution(12933659759678582126)
XLA Ops:
  0.6 0.1 pad_add_fusion.refs_0_
  0.7 2.0 %send.1 = (bf16[96,256]{1,0:T(8,128)(2,1)S(1)}, bf16[96,256]{1,0:T(8,128)(2,1)S(1)}, bf16[96,256]{1,0:T(8,128)(2,1)S(1)}, bf16[96,256]{1,0:T(8,128)(2,1)S(1)}, bf16[96,256]{1,0:T(8,128)(2,1)S(1)}) custom-call(s32[4]{0:T(128)S(1)} %pad_add_fusion.refs_0_, s32[6,1,96]{2,1,0:T(1,128)} %bitcast.26, bf16[768,256]{1,0:T(8,128)(2,1)} %bitcast.22), custom_call_target="tpu_custom_call" | custom-call | tf_op jit(solution)/shard_map/send/pallas_call | solution.py:89
  2.7 3.0 %collective-permute-start = (bf16[96,256]{1,0:T(8,128)(2,1)S(1)}, bf16[96,256]{1,0:T(8,128)(2,1)S(1)}, u32[]{:S(2)}, u32[]{:S(2)}) collective-permute-start(bf16[96,256]{1,0:T(8,128)(2,1)S(1)} %get-tuple-element.58), channel_id=1, source_target_pairs={{0,16},{16,0},{1,17},{17,1},{2,18},{18,2},{3,19},{19,3},{4,20},{20... | collective-permute-start | bytes 147464 | tf_op jit(solution)/shard_map/ppermute | solution.py:60
  5.7 1.6 %collective-permute-start.1 = (bf16[96,256]{1,0:T(8,128)(2,1)S(1)}, bf16[96,256]{1,0:T(8,128)(2,1)S(1)}, u32[]{:S(2)}, u32[]{:S(2)}) collective-permute-start(bf16[96,256]{1,0:T(8,128)(2,1)S(1)} %get-tuple-element.59), channel_id=1, source_target_pairs={{0,4},{4,0},{8,12},{12,8},{1,5},{5,1},{9,13},{13,9},{2,6},{6,2},{1... | collective-permute-start | bytes 147464 | tf_op jit(solution)/shard_map/ppermute | solution.py:60
  7.3 0.7 collective-permute-start.2
  8.0 0.1 collective-permute-start.3
  8.1 0.7 collective-permute-start.4
  8.7 0.0 copy-start
  8.7 0.9 copy-done
  9.6 0.9 copy-done.1
  10.5 0.9 copy-done.2
  11.4 2.9 %invert.1 = (f32[27,128,16]{2,1,0:T(8,128)S(1)}, f32[27,16,128]{2,1,0:T(8,128)}) custom-call(s32[4]{0:T(128)S(1)} %pad_add_fusion.refs_0_, s32[27,1,768]{2,1,0:T(1,128)S(1)} %bitcast.17, s32[27,1,768]{2,1,0:T(1,128)S(1)} %bitcast.18, s32[27,1,768]{2,1,0:T(1,128)S(1)} %bitcast.19), custom_call_target="tpu_custom_call" | custom-call | tf_op jit(solution)/shard_map/invert/pallas_call | solution.py:134
  14.3 0.0 collective-permute-done.2.refs_7_
  14.3 0.0 collective-permute-done.3.refs_8_
  14.3 25.5 %forward.1 = (bf16[768,256]{1,0:T(8,128)(2,1)}, bf16[768,256]{1,0:T(8,128)(2,1)}, f32[6912,128]{1,0:T(8,128)S(1)}, bf16[3456,128]{1,0:T(8,128)(2,1)}, bf16[3456,128]{1,0:T(8,128)(2,1)}) custom-call(s32[4]{0:T(128)S(1)} %pad_add_fusion.refs_0_, f32[27,128,16]{2,1,0:T(8,128)S(1)} %get-tuple-element.57.refs_1_, bf16[768,256]{1,0:T(8,128)(2,1)} %bitcast.23, ...), custom_call_target="tpu_custom_call" | custom-call | tf_op jit(solution)/shard_map/forward/pallas_call | solution.py:238
  39.8 2.9 %collective-permute-start.5 = (bf16[3456,128]{1,0:T(8,128)(2,1)}, bf16[3456,128]{1,0:T(8,128)(2,1)}, u32[]{:S(2)}, u32[]{:S(2)}) collective-permute-start(bf16[3456,128]{1,0:T(8,128)(2,1)} %get-tuple-element.67), channel_id=1, source_target_pairs={{0,1},{1,0},{2,3},{3,2},{4,5},{5,4},{6,7},{7,6},{8,9},{9,8},{10,11... | collective-permute-start | bytes 2654216 | tf_op jit(solution)/shard_map/ppermute | solution.py:411
  42.8 0.1 collective-permute-start.6
  42.8 2.3 %collective-permute-done.5 = bf16[3456,128]{1,0:T(8,128)(2,1)} collective-permute-done((bf16[3456,128]{1,0:T(8,128)(2,1)}, bf16[3456,128]{1,0:T(8,128)(2,1)}, u32[]{:S(2)}, u32[]{:S(2)}) %collective-permute-start.5) | collective-permute-done | bytes 884768 | tf_op jit(solution)/shard_map/ppermute | solution.py:411
  45.2 1.3 %collective-permute-done.6 = bf16[3456,128]{1,0:T(8,128)(2,1)} collective-permute-done((bf16[3456,128]{1,0:T(8,128)(2,1)}, bf16[3456,128]{1,0:T(8,128)(2,1)}, u32[]{:S(2)}, u32[]{:S(2)}) %collective-permute-start.6) | collective-permute-done | bytes 884768 | tf_op jit(solution)/shard_map/ppermute | solution.py:411
  46.4 2.3 %add_convert_fusion = (bf16[1728,128]{1,0:T(8,128)(2,1)}, bf16[1728,128]{1,0:T(8,128)(2,1)}) fusion(f32[6912,128]{1,0:T(8,128)S(1)} %get-tuple-element.66, s32[]{:T(128)S(6)} %select_n.150, bf16[3456,128]{1,0:T(8,128)(2,1)} %collective-permute-done.6, s32[]{:T(128)S(6)} %select_n.151, bf16[3456,128]{1,0:T(8,128)(2,1)} %collective-permute-done.5, ...), kind=kLoop, calls=%fused_computation | loop fusion | flops 1327104 | bytes 3538960 | tf_op jit(solution)/shard_map/convert_element_type | solution.py:476
  48.7 0.8 collective-permute-start.8
  49.5 0.5 collective-permute-start.7
  50.1 10.6 %backward_faces.1 = (bf16[96,256]{1,0:T(8,128)(2,1)}, bf16[96,256]{1,0:T(8,128)(2,1)}, bf16[96,256]{1,0:T(8,128)(2,1)}, bf16[96,256]{1,0:T(8,128)(2,1)}, bf16[96,256]{1,0:T(8,128)(2,1)}) custom-call(s32[4]{0:T(128)S(1)} %pad_add_fusion.refs_0_, f32[27,16,128]{2,1,0:T(8,128)} %get-tuple-element.64.refs_1_.refs_0_.refs_2_, ...), custom_call_target="tpu_custom_call" | custom-call | tf_op jit(solution)/shard_map/backward_faces/pallas_call | solution.py:337
  60.7 0.8 collective-permute-done.8
  61.5 0.3 collective-permute-done.7
  61.8 2.2 %add_convert_fusion.2 = (bf16[864,128]{1,0:T(8,128)(2,1)}, bf16[864,128]{1,0:T(8,128)(2,1)}) fusion(f32[6912,128]{1,0:T(8,128)S(1)} %get-tuple-element.66, s32[]{:T(128)S(6)} %select_n.156, bf16[1728,128]{1,0:T(8,128)(2,1)} %collective-permute-done.8, s32[]{:T(128)S(6)} %select_n.158, bf16[3456,128]{1,0:T(8,128)(2,1)} %collective-permute-done.6, ...), kind=kLoop, calls=%fused_computation.2 | loop fusion | flops 1105920 | bytes 2211864 | tf_op jit(solution)/shard_map/convert_element_type | solution.py:476
  64.0 0.5 collective-permute-start.13
  64.5 1.4 %collective-permute-start.12 = (bf16[864,128]{1,0:T(8,128)(2,1)}, bf16[864,128]{1,0:T(8,128)(2,1)}, u32[]{:S(2)}, u32[]{:S(2)}) collective-permute-start(bf16[864,128]{1,0:T(8,128)(2,1)} %get-tuple-element.120), channel_id=1, source_target_pairs={{0,2},{1,3},{2,0},{3,1},{4,6},{5,7},{6,4},{7,5},{8,10},{9,11},{10,... | collective-permute-start | bytes 663560 | tf_op jit(solution)/shard_map/ppermute | solution.py:411
  65.9 4.4 %collective-permute-start.9 = (bf16[96,256]{1,0:T(8,128)(2,1)}, bf16[96,256]{1,0:T(8,128)(2,1)}, u32[]{:S(2)}, u32[]{:S(2)}) collective-permute-start(bf16[96,256]{1,0:T(8,128)(2,1)} %get-tuple-element.80), channel_id=1, source_target_pairs={{0,4},{4,0},{8,12},{12,8},{1,5},{5,1},{9,13},{13,9},{2,6},{6,2},{1... | collective-permute-start | bytes 147464 | tf_op jit(solution)/shard_map/ppermute | solution.py:60
  70.3 1.3 %collective-permute-start.10 = (bf16[96,256]{1,0:T(8,128)(2,1)}, bf16[96,256]{1,0:T(8,128)(2,1)}, u32[]{:S(2)}, u32[]{:S(2)}) collective-permute-start(bf16[96,256]{1,0:T(8,128)(2,1)} %get-tuple-element.81), channel_id=1, source_target_pairs={{4,8},{8,4},{5,9},{9,5},{6,10},{10,6},{7,11},{11,7},{20,24},{24,20... | collective-permute-start | bytes 147464 | tf_op jit(solution)/shard_map/ppermute | solution.py:60
  71.6 1.1 collective-permute-done.9.refs_7_
  72.7 0.5 collective-permute-done.11.refs_9_
  73.2 0.0 collective-permute-done.13
  73.2 0.0 collective-permute-done.12
  73.2 1.1 add_convert_fusion.5
  74.3 1.1 add_convert_fusion.4
  75.5 3.5 %collective-permute-start.16 = (bf16[432,128]{1,0:T(8,128)(2,1)S(1)}, bf16[432,128]{1,0:T(8,128)(2,1)S(1)}, u32[]{:S(2)}, u32[]{:S(2)}) collective-permute-start(bf16[432,128]{1,0:T(8,128)(2,1)S(1)} %pad_maximum_fusion.2), channel_id=1, source_target_pairs={{0,4},{4,8},{8,12},{12,0},{1,5},{5,9},{9,13},{13,1},{2,6},{6,10},{... | collective-permute-start | bytes 331784 | tf_op jit(solution)/shard_map/ppermute | solution.py:484
  79.0 0.1 collective-permute-start.17
  79.1 2.4 %collective-permute-start.18 = (bf16[432,128]{1,0:T(8,128)(2,1)S(1)}, bf16[432,128]{1,0:T(8,128)(2,1)S(1)}, u32[]{:S(2)}, u32[]{:S(2)}) collective-permute-start(bf16[432,128]{1,0:T(8,128)(2,1)S(1)} %pad_maximum_fusion.4), channel_id=1, source_target_pairs={{0,12},{4,0},{8,4},{12,8},{1,13},{5,1},{9,5},{13,9},{2,14},{6,2},{... | collective-permute-start | bytes 331784 | tf_op jit(solution)/shard_map/ppermute | solution.py:484
  81.5 1.5 %collective-permute-start.14 = (bf16[96,256]{1,0:T(8,128)(2,1)}, bf16[96,256]{1,0:T(8,128)(2,1)S(1)}, u32[]{:S(2)}, u32[]{:S(2)}) collective-permute-start(bf16[96,256]{1,0:T(8,128)(2,1)} %get-tuple-element.88), channel_id=1, source_target_pairs={{0,16},{16,0},{1,17},{17,1},{2,18},{18,2},{3,19},{19,3},{4,20},{20... | collective-permute-start | bytes 147464 | tf_op jit(solution)/shard_map/ppermute | solution.py:60
  83.0 0.7 collective-permute-start.15
  83.7 1.0 convert_add_fusion.1
  84.7 3.5 %backward_own.2.refs_3_ = f32[768,256]{1,0:T(8,128)} custom-call(f32[27,16,128]{2,1,0:T(8,128)} %get-tuple-element.64.refs_1_.refs_0_.refs_2_, bf16[768,256]{1,0:T(8,128)(2,1)} %get-tuple-element.101.refs_2_.refs_1_.refs_3_, bf16[27,256,256]{2,1,0:T(8,128)(2,1)} %refs_4_.1), custom_call_target="tpu_custom_call" | custom-call | tf_op jit(solution)/shard_map/backward_own/pallas_call | solution.py:360
  88.2 0.0 collective-permute-done.14.refs_6_
  88.3 0.0 collective-permute-done.17
  88.3 0.1 fusion.3
  88.4 2.6 %collective-permute-start.21 = (bf16[432,128]{1,0:T(8,128)(2,1)S(1)}, bf16[432,128]{1,0:T(8,128)(2,1)S(1)}, u32[]{:S(2)}, u32[]{:S(2)}) collective-permute-start(bf16[432,128]{1,0:T(8,128)(2,1)S(1)} %fusion.3), channel_id=1, source_target_pairs={{0,12},{4,0},{8,4},{12,8},{1,13},{5,1},{9,5},{13,9},{2,14},{6,2},{... | collective-permute-start | bytes 331784 | tf_op jit(solution)/shard_map/ppermute | solution.py:484
  91.0 0.7 collective-permute-start.20
  91.7 9.0 %backward_own.3.refs_5_ = f32[768,256]{1,0:T(8,128)} custom-call(f32[27,16,128]{2,1,0:T(8,128)} %get-tuple-element.64.refs_1_.refs_0_.refs_2_, bf16[768,256]{1,0:T(8,128)(2,1)} %get-tuple-element.101.refs_2_.refs_1_.refs_3_, bf16[27,256,256]{2,1,0:T(8,128)(2,1)} %refs_4_.1, f32[768,256]{1,0:T(8,128)} %backward_own.2.refs_3_), custom_call_target="tpu_custom_call" | custom-call | tf_op jit(solution)/shard_map/backward_own/pallas_call | solution.py:360
  100.7 1.2 collective-permute-done.20
  102.1 1.4 %collective-permute-start.23 = (bf16[864,128]{1,0:T(8,128)(2,1)S(1)}, bf16[864,128]{1,0:T(8,128)(2,1)S(1)}, u32[]{:S(2)}, u32[]{:S(2)}) collective-permute-start(bf16[864,128]{1,0:T(8,128)(2,1)S(1)} %pad_maximum_fusion.1), channel_id=1, source_target_pairs={{0,16},{16,0},{1,17},{17,1},{2,18},{18,2},{3,19},{19,3},{4,20},{20... | collective-permute-start | bytes 663560 | tf_op jit(solution)/shard_map/ppermute | solution.py:411
  103.5 0.7 collective-permute-start.22
  104.2 5.4 %collective-permute-done.23 = bf16[864,128]{1,0:T(8,128)(2,1)S(1)} collective-permute-done((bf16[864,128]{1,0:T(8,128)(2,1)S(1)}, bf16[864,128]{1,0:T(8,128)(2,1)S(1)}, u32[]{:S(2)}, u32[]{:S(2)}) %collective-permute-start.23) | collective-permute-done | bytes 221216 | tf_op jit(solution)/shard_map/ppermute | solution.py:411
  109.7 0.1 collective-permute-start.25
  109.8 0.9 collective-permute-done.22
  110.7 0.9 collective-permute-start.24
  111.6 0.5 collective-permute-start.28
  112.1 7.4 %finish.1 = bf16[768,256]{1,0:T(8,128)(2,1)} custom-call(s32[4]{0:T(128)S(1)} %pad_add_fusion.refs_0_, s32[6,1,96]{2,1,0:T(1,128)} %bitcast.27, f32[27,16,128]{2,1,0:T(8,128)} %get-tuple-element.64.refs_1_.refs_0_.refs_2_, bf16[768,256]{1,0:T(8,128)(2,1)} %get-tuple-element.101.refs_2_.refs_1_.refs_3_, bf16[27,256,256]{2,1,0:T(8,128)(2,1)} %refs_4_.1, ...), custom_call_target="tpu_custom_call" | custom-call | tf_op jit(solution)/shard_map/finish/pallas_call | solution.py:393
  119.5 1.6 %collective-permute-done.25.refs_2_ = bf16[1728,128]{1,0:T(8,128)(2,1)S(1)} collective-permute-done((bf16[1728,128]{1,0:T(8,128)(2,1)S(1)}, bf16[1728,128]{1,0:T(8,128)(2,1)S(1)}, u32[]{:S(2)}, u32[]{:S(2)}) %collective-permute-start.25) | collective-permute-done | bytes 442400 | tf_op jit(solution)/shard_map/ppermute | solution.py:411
  121.1 0.5 collective-permute-done.24.refs_1_
  121.6 0.5 collective-permute-start.27
  122.1 0.1 stack.38.refs_0_
  122.2 2.0 %place.2.refs_5_ = bf16[6912,256]{1,0:T(8,128)(2,1)} custom-call(s32[6]{0:T(128)S(1)} %stack.38.refs_0_, bf16[1728,128]{1,0:T(8,128)(2,1)S(1)} %constant_dynamic-update-slice_fusion.refs_1_, bf16[1728,128]{1,0:T(8,128)(2,1)S(1)} %constant_dynamic-update-slice_fusion.5.refs_2_, bf16[1728,128]{1,0:T(8,128)(2,1)S(1)} %collective-permute-done.28.refs_3_, ...), custom_call_target="tpu_custom_call" | custom-call | tf_op jit(solution)/shard_map/place/pallas_call | solution.py:445
  124.2 2.0 %place.3 = bf16[6912,256]{1,0:T(8,128)(2,1)} custom-call(s32[6]{0:T(128)S(1)} %stack.38.refs_0_, bf16[1728,128]{1,0:T(8,128)(2,1)S(1)} %collective-permute-done.24.refs_1_, bf16[1728,128]{1,0:T(8,128)(2,1)S(1)} %collective-permute-done.25.refs_2_, bf16[1728,128]{1,0:T(8,128)(2,1)S(1)} %collective-permute-done.26.refs_3_, ...), custom_call_target="tpu_custom_call", output_to_operand_aliasing={{}: (5, {})} | custom-call | tf_op jit(solution)/shard_map/place/pallas_call | solution.py:445
  (34 shorter events, 0.3 us)
Async XLA Ops:
  2.7 11.5 %collective-permute-start = (bf16[96,256]{1,0:T(8,128)(2,1)S(1)}, bf16[96,256]{1,0:T(8,128)(2,1)S(1)}, u32[]{:S(2)}, u32[]{:S(2)}) collective-permute-start(bf16[96,256]{1,0:T(8,128)(2,1)S(1)} %get-tuple-element.58), channel_id=1, source_target_pairs={{0,16},{16,0},{1,17},{17,1},{2,18},{18,2},{3,19},{19,3},{4,20},{20... | collective-permute-start | bytes 147464 | tf_op jit(solution)/shard_map/ppermute | solution.py:60
  5.7 8.5 %collective-permute-start.1 = (bf16[96,256]{1,0:T(8,128)(2,1)S(1)}, bf16[96,256]{1,0:T(8,128)(2,1)S(1)}, u32[]{:S(2)}, u32[]{:S(2)}) collective-permute-start(bf16[96,256]{1,0:T(8,128)(2,1)S(1)} %get-tuple-element.59), channel_id=1, source_target_pairs={{0,4},{4,0},{8,12},{12,8},{1,5},{5,1},{9,13},{13,9},{2,6},{6,2},{1... | collective-permute-start | bytes 147464 | tf_op jit(solution)/shard_map/ppermute | solution.py:60
  7.3 7.0 %collective-permute-start.2 = (bf16[96,256]{1,0:T(8,128)(2,1)S(1)}, bf16[96,256]{1,0:T(8,128)(2,1)S(1)}, u32[]{:S(2)}, u32[]{:S(2)}) collective-permute-start(bf16[96,256]{1,0:T(8,128)(2,1)S(1)} %get-tuple-element.60), channel_id=1, source_target_pairs={{4,8},{8,4},{5,9},{9,5},{6,10},{10,6},{7,11},{11,7},{20,24},{24,20... | collective-permute-start | bytes 147464 | tf_op jit(solution)/shard_map/ppermute | solution.py:60
  8.0 6.3 %collective-permute-start.3 = (bf16[96,256]{1,0:T(8,128)(2,1)S(1)}, bf16[96,256]{1,0:T(8,128)(2,1)S(1)}, u32[]{:S(2)}, u32[]{:S(2)}) collective-permute-start(bf16[96,256]{1,0:T(8,128)(2,1)S(1)} %get-tuple-element.61), channel_id=1, source_target_pairs={{0,1},{1,0},{2,3},{3,2},{4,5},{5,4},{6,7},{7,6},{8,9},{9,8},{10,11... | collective-permute-start | bytes 147464 | tf_op jit(solution)/shard_map/ppermute | solution.py:60
  8.1 6.3 %collective-permute-start.4 = (bf16[96,256]{1,0:T(8,128)(2,1)S(1)}, bf16[96,256]{1,0:T(8,128)(2,1)S(1)}, u32[]{:S(2)}, u32[]{:S(2)}) collective-permute-start(bf16[96,256]{1,0:T(8,128)(2,1)S(1)} %get-tuple-element.62), channel_id=1, source_target_pairs={{1,2},{2,1},{5,6},{6,5},{9,10},{10,9},{13,14},{14,13},{17,18},{18,... | collective-permute-start | bytes 147464 | tf_op jit(solution)/shard_map/ppermute | solution.py:60
  8.7 0.9 copy-start
  9.6 0.9 copy-start.1
  10.5 0.9 copy-start.2
  39.8 5.3 %collective-permute-start.5 = (bf16[3456,128]{1,0:T(8,128)(2,1)}, bf16[3456,128]{1,0:T(8,128)(2,1)}, u32[]{:S(2)}, u32[]{:S(2)}) collective-permute-start(bf16[3456,128]{1,0:T(8,128)(2,1)} %get-tuple-element.67), channel_id=1, source_target_pairs={{0,1},{1,0},{2,3},{3,2},{4,5},{5,4},{6,7},{7,6},{8,9},{9,8},{10,11... | collective-permute-start | bytes 2654216 | tf_op jit(solution)/shard_map/ppermute | solution.py:411
  42.8 3.7 %collective-permute-start.6 = (bf16[3456,128]{1,0:T(8,128)(2,1)}, bf16[3456,128]{1,0:T(8,128)(2,1)}, u32[]{:S(2)}, u32[]{:S(2)}) collective-permute-start(bf16[3456,128]{1,0:T(8,128)(2,1)} %get-tuple-element.68), channel_id=1, source_target_pairs={{0,1},{1,0},{2,3},{3,2},{4,5},{5,4},{6,7},{7,6},{8,9},{9,8},{10,11... | collective-permute-start | bytes 2654216 | tf_op jit(solution)/shard_map/ppermute | solution.py:411
  48.7 12.8 %collective-permute-start.8 = (bf16[1728,128]{1,0:T(8,128)(2,1)}, bf16[1728,128]{1,0:T(8,128)(2,1)}, u32[]{:S(2)}, u32[]{:S(2)}) collective-permute-start(bf16[1728,128]{1,0:T(8,128)(2,1)} %get-tuple-element.121), channel_id=1, source_target_pairs={{0,2},{1,3},{2,0},{3,1},{4,6},{5,7},{6,4},{7,5},{8,10},{9,11},{10,... | collective-permute-start | bytes 1327112 | tf_op jit(solution)/shard_map/ppermute | solution.py:411
  49.5 12.2 %collective-permute-start.7 = (bf16[1728,128]{1,0:T(8,128)(2,1)}, bf16[1728,128]{1,0:T(8,128)(2,1)}, u32[]{:S(2)}, u32[]{:S(2)}) collective-permute-start(bf16[1728,128]{1,0:T(8,128)(2,1)} %get-tuple-element.122), channel_id=1, source_target_pairs={{0,16},{16,0},{1,17},{17,1},{2,18},{18,2},{3,19},{19,3},{4,20},{20... | collective-permute-start | bytes 1327112 | tf_op jit(solution)/shard_map/ppermute | solution.py:411
  64.0 9.2 %collective-permute-start.13 = (bf16[864,128]{1,0:T(8,128)(2,1)}, bf16[864,128]{1,0:T(8,128)(2,1)}, u32[]{:S(2)}, u32[]{:S(2)}) collective-permute-start(bf16[864,128]{1,0:T(8,128)(2,1)} %get-tuple-element.119), channel_id=1, source_target_pairs={{0,16},{16,0},{1,17},{17,1},{2,18},{18,2},{3,19},{19,3},{4,20},{20... | collective-permute-start | bytes 663560 | tf_op jit(solution)/shard_map/ppermute | solution.py:411
  64.5 8.7 %collective-permute-start.12 = (bf16[864,128]{1,0:T(8,128)(2,1)}, bf16[864,128]{1,0:T(8,128)(2,1)}, u32[]{:S(2)}, u32[]{:S(2)}) collective-permute-start(bf16[864,128]{1,0:T(8,128)(2,1)} %get-tuple-element.120), channel_id=1, source_target_pairs={{0,2},{1,3},{2,0},{3,1},{4,6},{5,7},{6,4},{7,5},{8,10},{9,11},{10,... | collective-permute-start | bytes 663560 | tf_op jit(solution)/shard_map/ppermute | solution.py:411
  65.9 6.8 %collective-permute-start.9 = (bf16[96,256]{1,0:T(8,128)(2,1)}, bf16[96,256]{1,0:T(8,128)(2,1)}, u32[]{:S(2)}, u32[]{:S(2)}) collective-permute-start(bf16[96,256]{1,0:T(8,128)(2,1)} %get-tuple-element.80), channel_id=1, source_target_pairs={{0,4},{4,0},{8,12},{12,8},{1,5},{5,1},{9,13},{13,9},{2,6},{6,2},{1... | collective-permute-start | bytes 147464 | tf_op jit(solution)/shard_map/ppermute | solution.py:60
  70.3 2.4 %collective-permute-start.10 = (bf16[96,256]{1,0:T(8,128)(2,1)}, bf16[96,256]{1,0:T(8,128)(2,1)}, u32[]{:S(2)}, u32[]{:S(2)}) collective-permute-start(bf16[96,256]{1,0:T(8,128)(2,1)} %get-tuple-element.81), channel_id=1, source_target_pairs={{4,8},{8,4},{5,9},{9,5},{6,10},{10,6},{7,11},{11,7},{20,24},{24,20... | collective-permute-start | bytes 147464 | tf_op jit(solution)/shard_map/ppermute | solution.py:60
  71.6 1.6 %collective-permute-start.11 = (bf16[96,256]{1,0:T(8,128)(2,1)}, bf16[96,256]{1,0:T(8,128)(2,1)}, u32[]{:S(2)}, u32[]{:S(2)}) collective-permute-start(bf16[96,256]{1,0:T(8,128)(2,1)} %get-tuple-element.82), channel_id=1, source_target_pairs={{0,1},{1,0},{2,3},{3,2},{4,5},{5,4},{6,7},{7,6},{8,9},{9,8},{10,11... | collective-permute-start | bytes 147464 | tf_op jit(solution)/shard_map/ppermute | solution.py:60
  75.5 12.8 %collective-permute-start.16 = (bf16[432,128]{1,0:T(8,128)(2,1)S(1)}, bf16[432,128]{1,0:T(8,128)(2,1)S(1)}, u32[]{:S(2)}, u32[]{:S(2)}) collective-permute-start(bf16[432,128]{1,0:T(8,128)(2,1)S(1)} %pad_maximum_fusion.2), channel_id=1, source_target_pairs={{0,4},{4,8},{8,12},{12,0},{1,5},{5,9},{9,13},{13,1},{2,6},{6,10},{... | collective-permute-start | bytes 331784 | tf_op jit(solution)/shard_map/ppermute | solution.py:484
  79.0 9.3 %collective-permute-start.17 = (bf16[432,128]{1,0:T(8,128)(2,1)S(1)}, bf16[432,128]{1,0:T(8,128)(2,1)S(1)}, u32[]{:S(2)}, u32[]{:S(2)}) collective-permute-start(bf16[432,128]{1,0:T(8,128)(2,1)S(1)} %pad_maximum_fusion.3), channel_id=1, source_target_pairs={{0,8},{4,12},{8,0},{12,4},{1,9},{5,13},{9,1},{13,5},{2,10},{6,14},... | collective-permute-start | bytes 331784 | tf_op jit(solution)/shard_map/ppermute | solution.py:484
  79.1 9.2 %collective-permute-start.18 = (bf16[432,128]{1,0:T(8,128)(2,1)S(1)}, bf16[432,128]{1,0:T(8,128)(2,1)S(1)}, u32[]{:S(2)}, u32[]{:S(2)}) collective-permute-start(bf16[432,128]{1,0:T(8,128)(2,1)S(1)} %pad_maximum_fusion.4), channel_id=1, source_target_pairs={{0,12},{4,0},{8,4},{12,8},{1,13},{5,1},{9,5},{13,9},{2,14},{6,2},{... | collective-permute-start | bytes 331784 | tf_op jit(solution)/shard_map/ppermute | solution.py:484
  81.5 6.7 %collective-permute-start.14 = (bf16[96,256]{1,0:T(8,128)(2,1)}, bf16[96,256]{1,0:T(8,128)(2,1)S(1)}, u32[]{:S(2)}, u32[]{:S(2)}) collective-permute-start(bf16[96,256]{1,0:T(8,128)(2,1)} %get-tuple-element.88), channel_id=1, source_target_pairs={{0,16},{16,0},{1,17},{17,1},{2,18},{18,2},{3,19},{19,3},{4,20},{20... | collective-permute-start | bytes 147464 | tf_op jit(solution)/shard_map/ppermute | solution.py:60
  83.0 5.3 %collective-permute-start.15 = (bf16[96,256]{1,0:T(8,128)(2,1)}, bf16[96,256]{1,0:T(8,128)(2,1)S(1)}, u32[]{:S(2)}, u32[]{:S(2)}) collective-permute-start(bf16[96,256]{1,0:T(8,128)(2,1)} %get-tuple-element.89), channel_id=1, source_target_pairs={{1,2},{2,1},{5,6},{6,5},{9,10},{10,9},{13,14},{14,13},{17,18},{18,... | collective-permute-start | bytes 147464 | tf_op jit(solution)/shard_map/ppermute | solution.py:60
  88.3 13.8 %copy-start.3 = (bf16[96,256]{1,0:T(8,128)(2,1)}, bf16[96,256]{1,0:T(8,128)(2,1)S(1)}, u32[]{:S(2)}) copy-start(bf16[96,256]{1,0:T(8,128)(2,1)S(1)} %collective-permute-done.14.refs_6_) | copy-start | bytes 147460
  88.3 13.8 %copy-start.4 = (bf16[96,256]{1,0:T(8,128)(2,1)}, bf16[96,256]{1,0:T(8,128)(2,1)S(1)}, u32[]{:S(2)}) copy-start(bf16[96,256]{1,0:T(8,128)(2,1)S(1)} %collective-permute-done.15.refs_10_) | copy-start | bytes 147460
  88.4 12.3 %collective-permute-start.21 = (bf16[432,128]{1,0:T(8,128)(2,1)S(1)}, bf16[432,128]{1,0:T(8,128)(2,1)S(1)}, u32[]{:S(2)}, u32[]{:S(2)}) collective-permute-start(bf16[432,128]{1,0:T(8,128)(2,1)S(1)} %fusion.3), channel_id=1, source_target_pairs={{0,12},{4,0},{8,4},{12,8},{1,13},{5,1},{9,5},{13,9},{2,14},{6,2},{... | collective-permute-start | bytes 331784 | tf_op jit(solution)/shard_map/ppermute | solution.py:484
  91.0 10.9 %collective-permute-start.20 = (bf16[432,128]{1,0:T(8,128)(2,1)S(1)}, bf16[432,128]{1,0:T(8,128)(2,1)S(1)}, u32[]{:S(2)}, u32[]{:S(2)}) collective-permute-start(bf16[432,128]{1,0:T(8,128)(2,1)S(1)} %fusion.3), channel_id=1, source_target_pairs={{0,8},{4,12},{8,0},{12,4},{1,9},{5,13},{9,1},{13,5},{2,10},{6,14},... | collective-permute-start | bytes 331784 | tf_op jit(solution)/shard_map/ppermute | solution.py:484
  91.7 10.2 %collective-permute-start.19 = (bf16[432,128]{1,0:T(8,128)(2,1)S(1)}, bf16[432,128]{1,0:T(8,128)(2,1)S(1)}, u32[]{:S(2)}, u32[]{:S(2)}) collective-permute-start(bf16[432,128]{1,0:T(8,128)(2,1)S(1)} %fusion.3), channel_id=1, source_target_pairs={{0,4},{4,8},{8,12},{12,0},{1,5},{5,9},{9,13},{13,1},{2,6},{6,10},{... | collective-permute-start | bytes 331784 | tf_op jit(solution)/shard_map/ppermute | solution.py:484
  102.1 7.5 %collective-permute-start.23 = (bf16[864,128]{1,0:T(8,128)(2,1)S(1)}, bf16[864,128]{1,0:T(8,128)(2,1)S(1)}, u32[]{:S(2)}, u32[]{:S(2)}) collective-permute-start(bf16[864,128]{1,0:T(8,128)(2,1)S(1)} %pad_maximum_fusion.1), channel_id=1, source_target_pairs={{0,16},{16,0},{1,17},{17,1},{2,18},{18,2},{3,19},{19,3},{4,20},{20... | collective-permute-start | bytes 663560 | tf_op jit(solution)/shard_map/ppermute | solution.py:411
  103.5 7.1 %collective-permute-start.22 = (bf16[864,128]{1,0:T(8,128)(2,1)S(1)}, bf16[864,128]{1,0:T(8,128)(2,1)S(1)}, u32[]{:S(2)}, u32[]{:S(2)}) collective-permute-start(bf16[864,128]{1,0:T(8,128)(2,1)S(1)} %pad_maximum_fusion), channel_id=1, source_target_pairs={{0,2},{1,3},{2,0},{3,1},{4,6},{5,7},{6,4},{7,5},{8,10},{9,11},{10,... | collective-permute-start | bytes 663560 | tf_op jit(solution)/shard_map/ppermute | solution.py:411
  109.7 11.4 %collective-permute-start.25 = (bf16[1728,128]{1,0:T(8,128)(2,1)S(1)}, bf16[1728,128]{1,0:T(8,128)(2,1)S(1)}, u32[]{:S(2)}, u32[]{:S(2)}) collective-permute-start(bf16[1728,128]{1,0:T(8,128)(2,1)S(1)} %constant_dynamic-update-slice_fusion.5.refs_2_), channel_id=1, source_target_pairs={{0,2},{1,3},{2,0},{3,1},{4,6},{5,7},{6,4},{7,5},{8,10},{9,11},{10,... | collective-permute-start | bytes 1327112 | tf_op jit(solution)/shard_map/ppermute | solution.py:411
  110.7 10.9 %collective-permute-start.24 = (bf16[1728,128]{1,0:T(8,128)(2,1)S(1)}, bf16[1728,128]{1,0:T(8,128)(2,1)S(1)}, u32[]{:S(2)}, u32[]{:S(2)}) collective-permute-start(bf16[1728,128]{1,0:T(8,128)(2,1)S(1)} %constant_dynamic-update-slice_fusion.refs_1_), channel_id=1, source_target_pairs={{0,16},{16,0},{1,17},{17,1},{2,18},{18,2},{3,19},{19,3},{4,20},{20... | collective-permute-start | bytes 1327112 | tf_op jit(solution)/shard_map/ppermute | solution.py:411
  111.6 10.6 %collective-permute-start.29 = (bf16[1728,128]{1,0:T(8,128)(2,1)S(1)}, bf16[1728,128]{1,0:T(8,128)(2,1)S(1)}, u32[]{:S(2)}, u32[]{:S(2)}) collective-permute-start(bf16[1728,128]{1,0:T(8,128)(2,1)S(1)} %constant_dynamic-update-slice_fusion.5.refs_2_), channel_id=1, source_target_pairs={{0,1},{1,0},{2,3},{3,2},{4,5},{5,4},{6,7},{7,6},{8,9},{9,8},{10,11... | collective-permute-start | bytes 1327112 | tf_op jit(solution)/shard_map/ppermute | solution.py:411
  111.6 10.6 %collective-permute-start.28 = (bf16[1728,128]{1,0:T(8,128)(2,1)S(1)}, bf16[1728,128]{1,0:T(8,128)(2,1)S(1)}, u32[]{:S(2)}, u32[]{:S(2)}) collective-permute-start(bf16[1728,128]{1,0:T(8,128)(2,1)S(1)} %constant_dynamic-update-slice_fusion.refs_1_), channel_id=1, source_target_pairs={{0,1},{1,0},{2,3},{3,2},{4,5},{5,4},{6,7},{7,6},{8,9},{9,8},{10,11... | collective-permute-start | bytes 1327112 | tf_op jit(solution)/shard_map/ppermute | solution.py:411
  121.6 2.6 %collective-permute-start.26 = (bf16[1728,128]{1,0:T(8,128)(2,1)S(1)}, bf16[1728,128]{1,0:T(8,128)(2,1)S(1)}, u32[]{:S(2)}, u32[]{:S(2)}) collective-permute-start(bf16[1728,128]{1,0:T(8,128)(2,1)S(1)} %collective-permute-done.24.refs_1_), channel_id=1, source_target_pairs={{0,1},{1,0},{2,3},{3,2},{4,5},{5,4},{6,7},{7,6},{8,9},{9,8},{10,11... | collective-permute-start | bytes 1327112 | tf_op jit(solution)/shard_map/ppermute | solution.py:411
  121.6 2.6 %collective-permute-start.27 = (bf16[1728,128]{1,0:T(8,128)(2,1)S(1)}, bf16[1728,128]{1,0:T(8,128)(2,1)S(1)}, u32[]{:S(2)}, u32[]{:S(2)}) collective-permute-start(bf16[1728,128]{1,0:T(8,128)(2,1)S(1)} %collective-permute-done.25.refs_2_), channel_id=1, source_target_pairs={{0,1},{1,0},{2,3},{3,2},{4,5},{5,4},{6,7},{7,6},{8,9},{9,8},{10,11... | collective-permute-start | bytes 1327112 | tf_op jit(solution)/shard_map/ppermute | solution.py:411

commit v10 on v9

--- a/solution.py
+++ b/solution.py
@@ -101,14 +101,22 @@
     )(flags, hold(rows), hold(own_features))
 
 
-def invert_kernel(block, face, pairs, flags, in_ref, out_ref, live_ref, col_ref, row_hbm, row_ref, sem):
-    taps, _, own = in_ref.shape
+def invert_kernel(block, face, pairs, flags, in_hbm, out_hbm, live_hbm, col_ref, row_hbm, tables, row_ref, sems):
+    copies = [
+        pltpu.make_async_copy(hbm, tables.at[j], sems.at[j])
+        for j, hbm in enumerate((in_hbm, out_hbm, live_hbm))
+    ]
+    for copy in copies:
+        copy.start()
+    taps, _, own = in_hbm.shape
     lows = lax.broadcasted_iota(jnp.int32, (block, own), 0)
     ranks = lax.broadcasted_iota(jnp.int32, (16, own), 0)
+    for copy in copies:
+        copy.wait()
     for k in range(taps):
-        target = out_ref[k]
-        source = in_ref[k]
-        live = live_ref[k] > 0
+        target = tables[1, k]
+        source = tables[0, k]
+        live = tables[2, k] > 0
         for i in pairs:
             dead = own + (2 * i + flags[1 + i]) * face
             beyond = source >= dead + face
@@ -123,7 +131,7 @@
         col = dot(hot, spread, NT)
         col_ref[k] = col
         row_ref[k] = col.T
-    copy = pltpu.make_async_copy(row_ref, row_hbm, sem)
+    copy = pltpu.make_async_copy(row_ref, row_hbm, sems.at[3])
     copy.start()
     copy.wait()
 
@@ -133,19 +141,20 @@
     taps, _, own = in_rows.shape
     return pl.pallas_call(
         lambda *refs: invert_kernel(block, face, pairs, *refs),
-        in_specs=[SMEM, VMEM, VMEM, VMEM],
+        in_specs=[SMEM, HBM, HBM, HBM],
         out_specs=[VMEM, HBM],
         out_shape=(
             jax.ShapeDtypeStruct((taps, block, 16), F32),
             pltpu.HBM((taps, 16, block), F32),
         ),
         scratch_shapes=[
+            pltpu.VMEM((3, taps, 1, own), jnp.int32),
             pltpu.VMEM((taps, 16, block), F32),
-            pltpu.SemaphoreType.DMA,
+            pltpu.SemaphoreType.DMA((4,)),
         ],
         compiler_params=params(12),
         name="invert",
-    )(flags, in_rows, out_rows, live)
+    )(flags, hold(in_rows), hold(out_rows), hold(live))
 
 
 def forward_kernel(ways, where, step, flags, col_ref, own_hbm, w_hbm, up_hbm, *rest):
@@ -532,7 +541,7 @@
     )
     activated, gp, keep, *give = forward(ways, flags, col, own_features, faces, weight, upstream[0, 0, 0])
     devices = lax.axis_size("gx") * lax.axis_size("gy") * lax.axis_size("gz")
-    split = (0, 3, 18)
+    split = (0, 15, 18)
     state = {"turn": 0, "returned": {}, "grad": []}
     late = [j for j, way in enumerate(ways) if way in ((0, 0), (1, 2))]
     early = [j for j in range(len(ways)) if j not in late]
@@ -557,8 +566,8 @@
             for j, face in zip(picks, held):
                 state["returned"][j] = face
             came = list(held[len(picks) :])
-        if turn in (2, 3):
-            first, after = split[turn - 2 : turn]
+        if turn in (3, 4):
+            first, after = split[turn - 3 : turn - 1]
             work = lambda g: [backward_own(row, g, weight, first, after - first, state["grad"])]
             made, came = tied(out, work, came)
             state["grad"] = [made[0]]

time: 127 us -> 124 us (0.976)
  waiting for transfers between devices: 15.9 us -> 11.4 us
  starting transfers between devices: 33.5 us -> 36.8 us
  local copies, waits for them, and re-layouts: 2.96 us -> 0.3 us
    ppermute x14, waiting for transfers between devices: 13.1 us -> 6.21 us  [swap(): return lax.ppermute(x, axis, [(j, j ^ 1 << bit) for j in range(n)])]
    unnamed x10 -> x8, local copies, waits for them, and re-layouts: 2.66 us -> 0.16 us
    ppermute x14, starting transfers between devices: 10.4 us -> 12.6 us  [swap(): return lax.ppermute(x, axis, [(j, j ^ 1 << bit) for j in range(n)])]
  transfers between devices with their start and end apart: 30 -> 30, of which waited for: 11 -> 12; matrix products, arithmetic and copies ran while one was open for 1% -> 1% of each run, Pallas kernels for 28% -> 29%
where the time goes in v10:
time: 124 us; the launch traced here: 123 us
  Pallas kernels  65.9 us (53%)
  starting transfers between devices  36.8 us (30%)
  waiting for transfers between devices  11.4 us (9%)
  other arithmetic  7.96 us (6%)
    pallas_call x1, Pallas kernels, forward(): pl.pallas_call(lambda *refs: forward_kernel(ways, where, 256, *refs), in_...  25.5 us
    ppermute x10, starting transfers between devices, exchange(): got.append(lax.ppermute(array, AXES[i], pairs))  13.8 us
    ppermute x14, starting transfers between devices, swap(): return lax.ppermute(x, axis, [(j, j ^ 1 << bit) for j in range(n)])  12.6 us
    pallas_call x2, Pallas kernels, backward_own(): pl.pallas_call(lambda *refs: own_kernel(first, count, *refs), in_specs=[H...  12.5 us
    pallas_call x1, Pallas kernels, backward_faces(): pl.pallas_call(lambda *refs: faces_kernel(ways, where, own, taps, *refs),...  10.6 us
    ppermute x6, starting transfers between devices, reduce_all(): lax.ppermute(y, 'gy', [(j, (j + s) % n) for j in range(n)])  10.4 us
    pallas_call x1, Pallas kernels, finish(): pl.pallas_call(lambda *refs: finish_kernel(ways, first, count, *refs), in...  7.42 us
    ppermute x14, waiting for transfers between devices, swap(): return lax.ppermute(x, axis, [(j, j ^ 1 << bit) for j in range(n)])  6.21 us
  transfers between devices with their start and end apart: 30, of which 12 were waited for; matrix products, arithmetic and copies ran while one was open for 1% of the time, Pallas kernels for 29%

profile of v10, /device:TPU:0, one launch (start us, length us, event | category | flops | bytes accessed | tf_op | source)
XLA Modules:
  0.0 123.5 jit_solution(6461972628291376622)
XLA Ops:
  0.6 0.1 pad_add_fusion.refs_0_
  0.7 2.0 %send.1 = (bf16[96,256]{1,0:T(8,128)(2,1)S(1)}, bf16[96,256]{1,0:T(8,128)(2,1)S(1)}, bf16[96,256]{1,0:T(8,128)(2,1)S(1)}, bf16[96,256]{1,0:T(8,128)(2,1)S(1)}, bf16[96,256]{1,0:T(8,128)(2,1)S(1)}) custom-call(s32[4]{0:T(128)S(1)} %pad_add_fusion.refs_0_, s32[6,1,96]{2,1,0:T(1,128)} %bitcast.26, bf16[768,256]{1,0:T(8,128)(2,1)} %bitcast.19), custom_call_target="tpu_custom_call" | custom-call | tf_op jit(solution)/shard_map/send/pallas_call | solution.py:89
  2.7 3.0 %collective-permute-start = (bf16[96,256]{1,0:T(8,128)(2,1)S(1)}, bf16[96,256]{1,0:T(8,128)(2,1)S(1)}, u32[]{:S(2)}, u32[]{:S(2)}) collective-permute-start(bf16[96,256]{1,0:T(8,128)(2,1)S(1)} %get-tuple-element.57), channel_id=1, source_target_pairs={{0,16},{16,0},{1,17},{17,1},{2,18},{18,2},{3,19},{19,3},{4,20},{20... | collective-permute-start | bytes 147464 | tf_op jit(solution)/shard_map/ppermute | solution.py:60
  5.7 1.6 %collective-permute-start.1 = (bf16[96,256]{1,0:T(8,128)(2,1)S(1)}, bf16[96,256]{1,0:T(8,128)(2,1)S(1)}, u32[]{:S(2)}, u32[]{:S(2)}) collective-permute-start(bf16[96,256]{1,0:T(8,128)(2,1)S(1)} %get-tuple-element.58), channel_id=1, source_target_pairs={{0,4},{4,0},{8,12},{12,8},{1,5},{5,1},{9,13},{13,9},{2,6},{6,2},{1... | collective-permute-start | bytes 147464 | tf_op jit(solution)/shard_map/ppermute | solution.py:60
  7.3 0.7 collective-permute-start.2
  8.0 0.1 collective-permute-start.3
  8.1 0.7 collective-permute-start.4
  8.7 3.9 %invert.1 = (f32[27,128,16]{2,1,0:T(8,128)S(1)}, f32[27,16,128]{2,1,0:T(8,128)}) custom-call(s32[4]{0:T(128)S(1)} %pad_add_fusion.refs_0_, s32[27,1,768]{2,1,0:T(1,128)} %bitcast.23, s32[27,1,768]{2,1,0:T(1,128)} %bitcast.24, s32[27,1,768]{2,1,0:T(1,128)} %bitcast.25), custom_call_target="tpu_custom_call" | custom-call | tf_op jit(solution)/shard_map/invert/pallas_call | solution.py:142
  12.6 0.0 collective-permute-done.2.refs_7_
  12.7 25.5 %forward.1 = (bf16[768,256]{1,0:T(8,128)(2,1)}, bf16[768,256]{1,0:T(8,128)(2,1)}, f32[6912,128]{1,0:T(8,128)S(1)}, bf16[3456,128]{1,0:T(8,128)(2,1)}, bf16[3456,128]{1,0:T(8,128)(2,1)}) custom-call(s32[4]{0:T(128)S(1)} %pad_add_fusion.refs_0_, f32[27,128,16]{2,1,0:T(8,128)S(1)} %get-tuple-element.56.refs_1_, bf16[768,256]{1,0:T(8,128)(2,1)} %bitcast.20, ...), custom_call_target="tpu_custom_call" | custom-call | tf_op jit(solution)/shard_map/forward/pallas_call | solution.py:247
  38.2 2.9 %collective-permute-start.5 = (bf16[3456,128]{1,0:T(8,128)(2,1)}, bf16[3456,128]{1,0:T(8,128)(2,1)}, u32[]{:S(2)}, u32[]{:S(2)}) collective-permute-start(bf16[3456,128]{1,0:T(8,128)(2,1)} %get-tuple-element.66), channel_id=1, source_target_pairs={{0,1},{1,0},{2,3},{3,2},{4,5},{5,4},{6,7},{7,6},{8,9},{9,8},{10,11... | collective-permute-start | bytes 2654216 | tf_op jit(solution)/shard_map/ppermute | solution.py:420
  41.1 0.1 collective-permute-start.6
  41.2 2.3 %collective-permute-done.5 = bf16[3456,128]{1,0:T(8,128)(2,1)} collective-permute-done((bf16[3456,128]{1,0:T(8,128)(2,1)}, bf16[3456,128]{1,0:T(8,128)(2,1)}, u32[]{:S(2)}, u32[]{:S(2)}) %collective-permute-start.5) | collective-permute-done | bytes 884768 | tf_op jit(solution)/shard_map/ppermute | solution.py:420
  43.5 1.3 %collective-permute-done.6 = bf16[3456,128]{1,0:T(8,128)(2,1)} collective-permute-done((bf16[3456,128]{1,0:T(8,128)(2,1)}, bf16[3456,128]{1,0:T(8,128)(2,1)}, u32[]{:S(2)}, u32[]{:S(2)}) %collective-permute-start.6) | collective-permute-done | bytes 884768 | tf_op jit(solution)/shard_map/ppermute | solution.py:420
  44.8 2.3 %add_convert_fusion = (bf16[1728,128]{1,0:T(8,128)(2,1)}, bf16[1728,128]{1,0:T(8,128)(2,1)}) fusion(f32[6912,128]{1,0:T(8,128)S(1)} %get-tuple-element.65, s32[]{:T(128)S(6)} %select_n.150, bf16[3456,128]{1,0:T(8,128)(2,1)} %collective-permute-done.6, s32[]{:T(128)S(6)} %select_n.151, bf16[3456,128]{1,0:T(8,128)(2,1)} %collective-permute-done.5, ...), kind=kLoop, calls=%fused_computation | loop fusion | flops 1327104 | bytes 3538960 | tf_op jit(solution)/shard_map/convert_element_type | solution.py:485
  47.0 0.9 collective-permute-start.8
  47.9 0.5 collective-permute-start.7
  48.4 10.6 %backward_faces.1 = (bf16[96,256]{1,0:T(8,128)(2,1)}, bf16[96,256]{1,0:T(8,128)(2,1)}, bf16[96,256]{1,0:T(8,128)(2,1)}, bf16[96,256]{1,0:T(8,128)(2,1)}, bf16[96,256]{1,0:T(8,128)(2,1)}) custom-call(s32[4]{0:T(128)S(1)} %pad_add_fusion.refs_0_, f32[27,16,128]{2,1,0:T(8,128)} %get-tuple-element.63.refs_1_.refs_0_.refs_2_, ...), custom_call_target="tpu_custom_call" | custom-call | tf_op jit(solution)/shard_map/backward_faces/pallas_call | solution.py:346
  59.0 0.8 collective-permute-done.8
  59.8 0.3 collective-permute-done.7
  60.1 2.2 %add_convert_fusion.2 = (bf16[864,128]{1,0:T(8,128)(2,1)}, bf16[864,128]{1,0:T(8,128)(2,1)}) fusion(f32[6912,128]{1,0:T(8,128)S(1)} %get-tuple-element.65, s32[]{:T(128)S(6)} %select_n.156, bf16[1728,128]{1,0:T(8,128)(2,1)} %collective-permute-done.8, s32[]{:T(128)S(6)} %select_n.158, bf16[3456,128]{1,0:T(8,128)(2,1)} %collective-permute-done.6, ...), kind=kLoop, calls=%fused_computation.2 | loop fusion | flops 1105920 | bytes 2211864 | tf_op jit(solution)/shard_map/convert_element_type | solution.py:485
  62.3 0.5 collective-permute-start.13
  62.8 1.4 %collective-permute-start.12 = (bf16[864,128]{1,0:T(8,128)(2,1)}, bf16[864,128]{1,0:T(8,128)(2,1)}, u32[]{:S(2)}, u32[]{:S(2)}) collective-permute-start(bf16[864,128]{1,0:T(8,128)(2,1)} %get-tuple-element.118), channel_id=1, source_target_pairs={{0,2},{1,3},{2,0},{3,1},{4,6},{5,7},{6,4},{7,5},{8,10},{9,11},{10,... | collective-permute-start | bytes 663560 | tf_op jit(solution)/shard_map/ppermute | solution.py:420
  64.3 4.4 %collective-permute-start.9 = (bf16[96,256]{1,0:T(8,128)(2,1)}, bf16[96,256]{1,0:T(8,128)(2,1)}, u32[]{:S(2)}, u32[]{:S(2)}) collective-permute-start(bf16[96,256]{1,0:T(8,128)(2,1)} %get-tuple-element.79), channel_id=1, source_target_pairs={{0,4},{4,0},{8,12},{12,8},{1,5},{5,1},{9,13},{13,9},{2,6},{6,2},{1... | collective-permute-start | bytes 147464 | tf_op jit(solution)/shard_map/ppermute | solution.py:60
  68.7 1.3 %collective-permute-start.10 = (bf16[96,256]{1,0:T(8,128)(2,1)}, bf16[96,256]{1,0:T(8,128)(2,1)}, u32[]{:S(2)}, u32[]{:S(2)}) collective-permute-start(bf16[96,256]{1,0:T(8,128)(2,1)} %get-tuple-element.80), channel_id=1, source_target_pairs={{4,8},{8,4},{5,9},{9,5},{6,10},{10,6},{7,11},{11,7},{20,24},{24,20... | collective-permute-start | bytes 147464 | tf_op jit(solution)/shard_map/ppermute | solution.py:60
  69.9 1.1 collective-permute-done.9.refs_7_
  71.1 0.4 collective-permute-done.11.refs_9_
  71.5 1.1 add_convert_fusion.5
  72.6 1.1 add_convert_fusion.4
  73.8 3.5 %collective-permute-start.16 = (bf16[432,128]{1,0:T(8,128)(2,1)S(1)}, bf16[432,128]{1,0:T(8,128)(2,1)S(1)}, u32[]{:S(2)}, u32[]{:S(2)}) collective-permute-start(bf16[432,128]{1,0:T(8,128)(2,1)S(1)} %pad_maximum_fusion.2), channel_id=1, source_target_pairs={{0,4},{4,8},{8,12},{12,0},{1,5},{5,9},{9,13},{13,1},{2,6},{6,10},{... | collective-permute-start | bytes 331784 | tf_op jit(solution)/shard_map/ppermute | solution.py:493
  77.4 0.1 collective-permute-start.17
  77.4 2.4 %collective-permute-start.18 = (bf16[432,128]{1,0:T(8,128)(2,1)S(1)}, bf16[432,128]{1,0:T(8,128)(2,1)S(1)}, u32[]{:S(2)}, u32[]{:S(2)}) collective-permute-start(bf16[432,128]{1,0:T(8,128)(2,1)S(1)} %pad_maximum_fusion.4), channel_id=1, source_target_pairs={{0,12},{4,0},{8,4},{12,8},{1,13},{5,1},{9,5},{13,9},{2,14},{6,2},{... | collective-permute-start | bytes 331784 | tf_op jit(solution)/shard_map/ppermute | solution.py:493
  79.9 1.5 %collective-permute-start.14 = (bf16[96,256]{1,0:T(8,128)(2,1)}, bf16[96,256]{1,0:T(8,128)(2,1)S(1)}, u32[]{:S(2)}, u32[]{:S(2)}) collective-permute-start(bf16[96,256]{1,0:T(8,128)(2,1)} %get-tuple-element.86), channel_id=1, source_target_pairs={{0,16},{16,0},{1,17},{17,1},{2,18},{18,2},{3,19},{19,3},{4,20},{20... | collective-permute-start | bytes 147464 | tf_op jit(solution)/shard_map/ppermute | solution.py:60
  81.3 0.7 collective-permute-start.15
  82.0 1.0 convert_add_fusion.1
  83.0 1.1 collective-permute-done.14.refs_6_
  84.2 0.0 collective-permute-done.15.refs_10_
  84.2 0.0 collective-permute-done.16
  84.2 1.4 %collective-permute-done.17 = bf16[432,128]{1,0:T(8,128)(2,1)S(1)} collective-permute-done((bf16[432,128]{1,0:T(8,128)(2,1)S(1)}, bf16[432,128]{1,0:T(8,128)(2,1)S(1)}, u32[]{:S(2)}, u32[]{:S(2)}) %collective-permute-start.17) | collective-permute-done | bytes 110624 | tf_op jit(solution)/shard_map/ppermute | solution.py:493
  85.6 0.0 collective-permute-done.18
  85.6 0.1 fusion.3
  85.7 3.7 %collective-permute-start.21 = (bf16[432,128]{1,0:T(8,128)(2,1)S(1)}, bf16[432,128]{1,0:T(8,128)(2,1)S(1)}, u32[]{:S(2)}, u32[]{:S(2)}) collective-permute-start(bf16[432,128]{1,0:T(8,128)(2,1)S(1)} %fusion.3), channel_id=1, source_target_pairs={{0,12},{4,0},{8,4},{12,8},{1,13},{5,1},{9,5},{13,9},{2,14},{6,2},{... | collective-permute-start | bytes 331784 | tf_op jit(solution)/shard_map/ppermute | solution.py:493
  89.4 0.7 collective-permute-start.20
  90.0 0.0 collective-permute-start.19
  90.1 9.0 %backward_own.2.refs_3_ = f32[768,256]{1,0:T(8,128)} custom-call(f32[27,16,128]{2,1,0:T(8,128)} %get-tuple-element.63.refs_1_.refs_0_.refs_2_, bf16[768,256]{1,0:T(8,128)(2,1)} %get-tuple-element.99.refs_2_.refs_1_.refs_3_, bf16[27,256,256]{2,1,0:T(8,128)(2,1)} %refs_4_.1), custom_call_target="tpu_custom_call" | custom-call | tf_op jit(solution)/shard_map/backward_own/pallas_call | solution.py:369
  99.0 0.0 collective-permute-done.21
  99.0 1.1 collective-permute-done.20
  100.3 0.7 collective-permute-start.22
  101.0 1.6 %collective-permute-start.23 = (bf16[864,128]{1,0:T(8,128)(2,1)S(1)}, bf16[864,128]{1,0:T(8,128)(2,1)S(1)}, u32[]{:S(2)}, u32[]{:S(2)}) collective-permute-start(bf16[864,128]{1,0:T(8,128)(2,1)S(1)} %pad_maximum_fusion.1), channel_id=1, source_target_pairs={{0,16},{16,0},{1,17},{17,1},{2,18},{18,2},{3,19},{19,3},{4,20},{20... | collective-permute-start | bytes 663560 | tf_op jit(solution)/shard_map/ppermute | solution.py:420
  102.5 3.6 %backward_own.3.refs_5_ = f32[768,256]{1,0:T(8,128)} custom-call(f32[27,16,128]{2,1,0:T(8,128)} %get-tuple-element.63.refs_1_.refs_0_.refs_2_, bf16[768,256]{1,0:T(8,128)(2,1)} %get-tuple-element.99.refs_2_.refs_1_.refs_3_, bf16[27,256,256]{2,1,0:T(8,128)(2,1)} %refs_4_.1, f32[768,256]{1,0:T(8,128)} %backward_own.2.refs_3_), custom_call_target="tpu_custom_call" | custom-call | tf_op jit(solution)/shard_map/backward_own/pallas_call | solution.py:369
  106.1 0.7 collective-permute-done.22
  106.9 0.4 collective-permute-done.23
  107.3 1.5 %collective-permute-start.25 = (bf16[1728,128]{1,0:T(8,128)(2,1)S(1)}, bf16[1728,128]{1,0:T(8,128)(2,1)S(1)}, u32[]{:S(2)}, u32[]{:S(2)}) collective-permute-start(bf16[1728,128]{1,0:T(8,128)(2,1)S(1)} %constant_dynamic-update-slice_fusion.5.refs_2_), channel_id=1, source_target_pairs={{0,2},{1,3},{2,0},{3,1},{4,6},{5,7},{6,4},{7,5},{8,10},{9,11},{10,... | collective-permute-start | bytes 1327112 | tf_op jit(solution)/shard_map/ppermute | solution.py:420
  108.8 1.5 %collective-permute-start.24 = (bf16[1728,128]{1,0:T(8,128)(2,1)S(1)}, bf16[1728,128]{1,0:T(8,128)(2,1)S(1)}, u32[]{:S(2)}, u32[]{:S(2)}) collective-permute-start(bf16[1728,128]{1,0:T(8,128)(2,1)S(1)} %constant_dynamic-update-slice_fusion.refs_1_), channel_id=1, source_target_pairs={{0,16},{16,0},{1,17},{17,1},{2,18},{18,2},{3,19},{19,3},{4,20},{20... | collective-permute-start | bytes 1327112 | tf_op jit(solution)/shard_map/ppermute | solution.py:420
  110.4 0.0 collective-permute-start.29
  110.4 0.5 collective-permute-start.28
  110.9 7.4 %finish.1 = bf16[768,256]{1,0:T(8,128)(2,1)} custom-call(s32[4]{0:T(128)S(1)} %pad_add_fusion.refs_0_, s32[6,1,96]{2,1,0:T(1,128)} %bitcast.27, f32[27,16,128]{2,1,0:T(8,128)} %get-tuple-element.63.refs_1_.refs_0_.refs_2_, bf16[768,256]{1,0:T(8,128)(2,1)} %get-tuple-element.99.refs_2_.refs_1_.refs_3_, bf16[27,256,256]{2,1,0:T(8,128)(2,1)} %refs_4_.1, ...), custom_call_target="tpu_custom_call" | custom-call | tf_op jit(solution)/shard_map/finish/pallas_call | solution.py:402
  118.3 0.0 collective-permute-done.25.refs_2_
  118.3 0.3 collective-permute-done.24.refs_1_
  118.6 0.5 collective-permute-start.27
  119.2 0.1 stack.38.refs_0_
  119.2 2.0 %place.2.refs_5_ = bf16[6912,256]{1,0:T(8,128)(2,1)} custom-call(s32[6]{0:T(128)S(1)} %stack.38.refs_0_, bf16[1728,128]{1,0:T(8,128)(2,1)S(1)} %constant_dynamic-update-slice_fusion.refs_1_, bf16[1728,128]{1,0:T(8,128)(2,1)S(1)} %constant_dynamic-update-slice_fusion.5.refs_2_, bf16[1728,128]{1,0:T(8,128)(2,1)S(1)} %collective-permute-done.28.refs_3_, ...), custom_call_target="tpu_custom_call" | custom-call | tf_op jit(solution)/shard_map/place/pallas_call | solution.py:454
  121.3 0.0 collective-permute-done.26.refs_3_
  121.3 2.0 %place.3 = bf16[6912,256]{1,0:T(8,128)(2,1)} custom-call(s32[6]{0:T(128)S(1)} %stack.38.refs_0_, bf16[1728,128]{1,0:T(8,128)(2,1)S(1)} %collective-permute-done.24.refs_1_, bf16[1728,128]{1,0:T(8,128)(2,1)S(1)} %collective-permute-done.25.refs_2_, bf16[1728,128]{1,0:T(8,128)(2,1)S(1)} %collective-permute-done.26.refs_3_, ...), custom_call_target="tpu_custom_call", output_to_operand_aliasing={{}: (5, {})} | custom-call | tf_op jit(solution)/shard_map/place/pallas_call | solution.py:454
  (28 shorter events, 0.3 us)
Async XLA Ops:
  2.7 9.9 %collective-permute-start = (bf16[96,256]{1,0:T(8,128)(2,1)S(1)}, bf16[96,256]{1,0:T(8,128)(2,1)S(1)}, u32[]{:S(2)}, u32[]{:S(2)}) collective-permute-start(bf16[96,256]{1,0:T(8,128)(2,1)S(1)} %get-tuple-element.57), channel_id=1, source_target_pairs={{0,16},{16,0},{1,17},{17,1},{2,18},{18,2},{3,19},{19,3},{4,20},{20... | collective-permute-start | bytes 147464 | tf_op jit(solution)/shard_map/ppermute | solution.py:60
  5.7 6.9 %collective-permute-start.1 = (bf16[96,256]{1,0:T(8,128)(2,1)S(1)}, bf16[96,256]{1,0:T(8,128)(2,1)S(1)}, u32[]{:S(2)}, u32[]{:S(2)}) collective-permute-start(bf16[96,256]{1,0:T(8,128)(2,1)S(1)} %get-tuple-element.58), channel_id=1, source_target_pairs={{0,4},{4,0},{8,12},{12,8},{1,5},{5,1},{9,13},{13,9},{2,6},{6,2},{1... | collective-permute-start | bytes 147464 | tf_op jit(solution)/shard_map/ppermute | solution.py:60
  7.3 5.3 %collective-permute-start.2 = (bf16[96,256]{1,0:T(8,128)(2,1)S(1)}, bf16[96,256]{1,0:T(8,128)(2,1)S(1)}, u32[]{:S(2)}, u32[]{:S(2)}) collective-permute-start(bf16[96,256]{1,0:T(8,128)(2,1)S(1)} %get-tuple-element.59), channel_id=1, source_target_pairs={{4,8},{8,4},{5,9},{9,5},{6,10},{10,6},{7,11},{11,7},{20,24},{24,20... | collective-permute-start | bytes 147464 | tf_op jit(solution)/shard_map/ppermute | solution.py:60
  8.0 4.7 %collective-permute-start.3 = (bf16[96,256]{1,0:T(8,128)(2,1)S(1)}, bf16[96,256]{1,0:T(8,128)(2,1)S(1)}, u32[]{:S(2)}, u32[]{:S(2)}) collective-permute-start(bf16[96,256]{1,0:T(8,128)(2,1)S(1)} %get-tuple-element.60), channel_id=1, source_target_pairs={{0,1},{1,0},{2,3},{3,2},{4,5},{5,4},{6,7},{7,6},{8,9},{9,8},{10,11... | collective-permute-start | bytes 147464 | tf_op jit(solution)/shard_map/ppermute | solution.py:60
  8.1 4.6 %collective-permute-start.4 = (bf16[96,256]{1,0:T(8,128)(2,1)S(1)}, bf16[96,256]{1,0:T(8,128)(2,1)S(1)}, u32[]{:S(2)}, u32[]{:S(2)}) collective-permute-start(bf16[96,256]{1,0:T(8,128)(2,1)S(1)} %get-tuple-element.61), channel_id=1, source_target_pairs={{1,2},{2,1},{5,6},{6,5},{9,10},{10,9},{13,14},{14,13},{17,18},{18,... | collective-permute-start | bytes 147464 | tf_op jit(solution)/shard_map/ppermute | solution.py:60
  38.2 5.3 %collective-permute-start.5 = (bf16[3456,128]{1,0:T(8,128)(2,1)}, bf16[3456,128]{1,0:T(8,128)(2,1)}, u32[]{:S(2)}, u32[]{:S(2)}) collective-permute-start(bf16[3456,128]{1,0:T(8,128)(2,1)} %get-tuple-element.66), channel_id=1, source_target_pairs={{0,1},{1,0},{2,3},{3,2},{4,5},{5,4},{6,7},{7,6},{8,9},{9,8},{10,11... | collective-permute-start | bytes 2654216 | tf_op jit(solution)/shard_map/ppermute | solution.py:420
  41.1 3.7 %collective-permute-start.6 = (bf16[3456,128]{1,0:T(8,128)(2,1)}, bf16[3456,128]{1,0:T(8,128)(2,1)}, u32[]{:S(2)}, u32[]{:S(2)}) collective-permute-start(bf16[3456,128]{1,0:T(8,128)(2,1)} %get-tuple-element.67), channel_id=1, source_target_pairs={{0,1},{1,0},{2,3},{3,2},{4,5},{5,4},{6,7},{7,6},{8,9},{9,8},{10,11... | collective-permute-start | bytes 2654216 | tf_op jit(solution)/shard_map/ppermute | solution.py:420
  47.0 12.8 %collective-permute-start.8 = (bf16[1728,128]{1,0:T(8,128)(2,1)}, bf16[1728,128]{1,0:T(8,128)(2,1)}, u32[]{:S(2)}, u32[]{:S(2)}) collective-permute-start(bf16[1728,128]{1,0:T(8,128)(2,1)} %get-tuple-element.119), channel_id=1, source_target_pairs={{0,2},{1,3},{2,0},{3,1},{4,6},{5,7},{6,4},{7,5},{8,10},{9,11},{10,... | collective-permute-start | bytes 1327112 | tf_op jit(solution)/shard_map/ppermute | solution.py:420
  47.9 12.2 %collective-permute-start.7 = (bf16[1728,128]{1,0:T(8,128)(2,1)}, bf16[1728,128]{1,0:T(8,128)(2,1)}, u32[]{:S(2)}, u32[]{:S(2)}) collective-permute-start(bf16[1728,128]{1,0:T(8,128)(2,1)} %get-tuple-element.120), channel_id=1, source_target_pairs={{0,16},{16,0},{1,17},{17,1},{2,18},{18,2},{3,19},{19,3},{4,20},{20... | collective-permute-start | bytes 1327112 | tf_op jit(solution)/shard_map/ppermute | solution.py:420
  62.3 9.2 %collective-permute-start.13 = (bf16[864,128]{1,0:T(8,128)(2,1)}, bf16[864,128]{1,0:T(8,128)(2,1)}, u32[]{:S(2)}, u32[]{:S(2)}) collective-permute-start(bf16[864,128]{1,0:T(8,128)(2,1)} %get-tuple-element.117), channel_id=1, source_target_pairs={{0,16},{16,0},{1,17},{17,1},{2,18},{18,2},{3,19},{19,3},{4,20},{20... | collective-permute-start | bytes 663560 | tf_op jit(solution)/shard_map/ppermute | solution.py:420
  62.8 8.7 %collective-permute-start.12 = (bf16[864,128]{1,0:T(8,128)(2,1)}, bf16[864,128]{1,0:T(8,128)(2,1)}, u32[]{:S(2)}, u32[]{:S(2)}) collective-permute-start(bf16[864,128]{1,0:T(8,128)(2,1)} %get-tuple-element.118), channel_id=1, source_target_pairs={{0,2},{1,3},{2,0},{3,1},{4,6},{5,7},{6,4},{7,5},{8,10},{9,11},{10,... | collective-permute-start | bytes 663560 | tf_op jit(solution)/shard_map/ppermute | solution.py:420
  64.3 6.8 %collective-permute-start.9 = (bf16[96,256]{1,0:T(8,128)(2,1)}, bf16[96,256]{1,0:T(8,128)(2,1)}, u32[]{:S(2)}, u32[]{:S(2)}) collective-permute-start(bf16[96,256]{1,0:T(8,128)(2,1)} %get-tuple-element.79), channel_id=1, source_target_pairs={{0,4},{4,0},{8,12},{12,8},{1,5},{5,1},{9,13},{13,9},{2,6},{6,2},{1... | collective-permute-start | bytes 147464 | tf_op jit(solution)/shard_map/ppermute | solution.py:60
  68.7 2.4 %collective-permute-start.10 = (bf16[96,256]{1,0:T(8,128)(2,1)}, bf16[96,256]{1,0:T(8,128)(2,1)}, u32[]{:S(2)}, u32[]{:S(2)}) collective-permute-start(bf16[96,256]{1,0:T(8,128)(2,1)} %get-tuple-element.80), channel_id=1, source_target_pairs={{4,8},{8,4},{5,9},{9,5},{6,10},{10,6},{7,11},{11,7},{20,24},{24,20... | collective-permute-start | bytes 147464 | tf_op jit(solution)/shard_map/ppermute | solution.py:60
  69.9 1.6 %collective-permute-start.11 = (bf16[96,256]{1,0:T(8,128)(2,1)}, bf16[96,256]{1,0:T(8,128)(2,1)}, u32[]{:S(2)}, u32[]{:S(2)}) collective-permute-start(bf16[96,256]{1,0:T(8,128)(2,1)} %get-tuple-element.81), channel_id=1, source_target_pairs={{0,1},{1,0},{2,3},{3,2},{4,5},{5,4},{6,7},{7,6},{8,9},{9,8},{10,11... | collective-permute-start | bytes 147464 | tf_op jit(solution)/shard_map/ppermute | solution.py:60
  73.8 10.4 %collective-permute-start.16 = (bf16[432,128]{1,0:T(8,128)(2,1)S(1)}, bf16[432,128]{1,0:T(8,128)(2,1)S(1)}, u32[]{:S(2)}, u32[]{:S(2)}) collective-permute-start(bf16[432,128]{1,0:T(8,128)(2,1)S(1)} %pad_maximum_fusion.2), channel_id=1, source_target_pairs={{0,4},{4,8},{8,12},{12,0},{1,5},{5,9},{9,13},{13,1},{2,6},{6,10},{... | collective-permute-start | bytes 331784 | tf_op jit(solution)/shard_map/ppermute | solution.py:493
  77.4 8.3 %collective-permute-start.17 = (bf16[432,128]{1,0:T(8,128)(2,1)S(1)}, bf16[432,128]{1,0:T(8,128)(2,1)S(1)}, u32[]{:S(2)}, u32[]{:S(2)}) collective-permute-start(bf16[432,128]{1,0:T(8,128)(2,1)S(1)} %pad_maximum_fusion.3), channel_id=1, source_target_pairs={{0,8},{4,12},{8,0},{12,4},{1,9},{5,13},{9,1},{13,5},{2,10},{6,14},... | collective-permute-start | bytes 331784 | tf_op jit(solution)/shard_map/ppermute | solution.py:493
  77.4 8.2 %collective-permute-start.18 = (bf16[432,128]{1,0:T(8,128)(2,1)S(1)}, bf16[432,128]{1,0:T(8,128)(2,1)S(1)}, u32[]{:S(2)}, u32[]{:S(2)}) collective-permute-start(bf16[432,128]{1,0:T(8,128)(2,1)S(1)} %pad_maximum_fusion.4), channel_id=1, source_target_pairs={{0,12},{4,0},{8,4},{12,8},{1,13},{5,1},{9,5},{13,9},{2,14},{6,2},{... | collective-permute-start | bytes 331784 | tf_op jit(solution)/shard_map/ppermute | solution.py:493
  79.9 4.3 %collective-permute-start.14 = (bf16[96,256]{1,0:T(8,128)(2,1)}, bf16[96,256]{1,0:T(8,128)(2,1)S(1)}, u32[]{:S(2)}, u32[]{:S(2)}) collective-permute-start(bf16[96,256]{1,0:T(8,128)(2,1)} %get-tuple-element.86), channel_id=1, source_target_pairs={{0,16},{16,0},{1,17},{17,1},{2,18},{18,2},{3,19},{19,3},{4,20},{20... | collective-permute-start | bytes 147464 | tf_op jit(solution)/shard_map/ppermute | solution.py:60
  81.3 2.8 %collective-permute-start.15 = (bf16[96,256]{1,0:T(8,128)(2,1)}, bf16[96,256]{1,0:T(8,128)(2,1)S(1)}, u32[]{:S(2)}, u32[]{:S(2)}) collective-permute-start(bf16[96,256]{1,0:T(8,128)(2,1)} %get-tuple-element.87), channel_id=1, source_target_pairs={{1,2},{2,1},{5,6},{6,5},{9,10},{10,9},{13,14},{14,13},{17,18},{18,... | collective-permute-start | bytes 147464 | tf_op jit(solution)/shard_map/ppermute | solution.py:60
  84.2 16.1 %copy-start = (bf16[96,256]{1,0:T(8,128)(2,1)}, bf16[96,256]{1,0:T(8,128)(2,1)S(1)}, u32[]{:S(2)}) copy-start(bf16[96,256]{1,0:T(8,128)(2,1)S(1)} %collective-permute-done.14.refs_6_) | copy-start | bytes 147460
  84.2 16.1 %copy-start.1 = (bf16[96,256]{1,0:T(8,128)(2,1)}, bf16[96,256]{1,0:T(8,128)(2,1)S(1)}, u32[]{:S(2)}) copy-start(bf16[96,256]{1,0:T(8,128)(2,1)S(1)} %collective-permute-done.15.refs_10_) | copy-start | bytes 147460
  85.7 13.4 %collective-permute-start.21 = (bf16[432,128]{1,0:T(8,128)(2,1)S(1)}, bf16[432,128]{1,0:T(8,128)(2,1)S(1)}, u32[]{:S(2)}, u32[]{:S(2)}) collective-permute-start(bf16[432,128]{1,0:T(8,128)(2,1)S(1)} %fusion.3), channel_id=1, source_target_pairs={{0,12},{4,0},{8,4},{12,8},{1,13},{5,1},{9,5},{13,9},{2,14},{6,2},{... | collective-permute-start | bytes 331784 | tf_op jit(solution)/shard_map/ppermute | solution.py:493
  89.4 10.7 %collective-permute-start.20 = (bf16[432,128]{1,0:T(8,128)(2,1)S(1)}, bf16[432,128]{1,0:T(8,128)(2,1)S(1)}, u32[]{:S(2)}, u32[]{:S(2)}) collective-permute-start(bf16[432,128]{1,0:T(8,128)(2,1)S(1)} %fusion.3), channel_id=1, source_target_pairs={{0,8},{4,12},{8,0},{12,4},{1,9},{5,13},{9,1},{13,5},{2,10},{6,14},... | collective-permute-start | bytes 331784 | tf_op jit(solution)/shard_map/ppermute | solution.py:493
  90.0 10.1 %collective-permute-start.19 = (bf16[432,128]{1,0:T(8,128)(2,1)S(1)}, bf16[432,128]{1,0:T(8,128)(2,1)S(1)}, u32[]{:S(2)}, u32[]{:S(2)}) collective-permute-start(bf16[432,128]{1,0:T(8,128)(2,1)S(1)} %fusion.3), channel_id=1, source_target_pairs={{0,4},{4,8},{8,12},{12,0},{1,5},{5,9},{9,13},{13,1},{2,6},{6,10},{... | collective-permute-start | bytes 331784 | tf_op jit(solution)/shard_map/ppermute | solution.py:493
  100.3 6.6 %collective-permute-start.22 = (bf16[864,128]{1,0:T(8,128)(2,1)S(1)}, bf16[864,128]{1,0:T(8,128)(2,1)S(1)}, u32[]{:S(2)}, u32[]{:S(2)}) collective-permute-start(bf16[864,128]{1,0:T(8,128)(2,1)S(1)} %pad_maximum_fusion), channel_id=1, source_target_pairs={{0,2},{1,3},{2,0},{3,1},{4,6},{5,7},{6,4},{7,5},{8,10},{9,11},{10,... | collective-permute-start | bytes 663560 | tf_op jit(solution)/shard_map/ppermute | solution.py:420
  101.0 6.3 %collective-permute-start.23 = (bf16[864,128]{1,0:T(8,128)(2,1)S(1)}, bf16[864,128]{1,0:T(8,128)(2,1)S(1)}, u32[]{:S(2)}, u32[]{:S(2)}) collective-permute-start(bf16[864,128]{1,0:T(8,128)(2,1)S(1)} %pad_maximum_fusion.1), channel_id=1, source_target_pairs={{0,16},{16,0},{1,17},{17,1},{2,18},{18,2},{3,19},{19,3},{4,20},{20... | collective-permute-start | bytes 663560 | tf_op jit(solution)/shard_map/ppermute | solution.py:420
  107.3 11.0 %collective-permute-start.25 = (bf16[1728,128]{1,0:T(8,128)(2,1)S(1)}, bf16[1728,128]{1,0:T(8,128)(2,1)S(1)}, u32[]{:S(2)}, u32[]{:S(2)}) collective-permute-start(bf16[1728,128]{1,0:T(8,128)(2,1)S(1)} %constant_dynamic-update-slice_fusion.5.refs_2_), channel_id=1, source_target_pairs={{0,2},{1,3},{2,0},{3,1},{4,6},{5,7},{6,4},{7,5},{8,10},{9,11},{10,... | collective-permute-start | bytes 1327112 | tf_op jit(solution)/shard_map/ppermute | solution.py:420
  108.8 9.8 %collective-permute-start.24 = (bf16[1728,128]{1,0:T(8,128)(2,1)S(1)}, bf16[1728,128]{1,0:T(8,128)(2,1)S(1)}, u32[]{:S(2)}, u32[]{:S(2)}) collective-permute-start(bf16[1728,128]{1,0:T(8,128)(2,1)S(1)} %constant_dynamic-update-slice_fusion.refs_1_), channel_id=1, source_target_pairs={{0,16},{16,0},{1,17},{17,1},{2,18},{18,2},{3,19},{19,3},{4,20},{20... | collective-permute-start | bytes 1327112 | tf_op jit(solution)/shard_map/ppermute | solution.py:420
  110.4 8.9 %collective-permute-start.29 = (bf16[1728,128]{1,0:T(8,128)(2,1)S(1)}, bf16[1728,128]{1,0:T(8,128)(2,1)S(1)}, u32[]{:S(2)}, u32[]{:S(2)}) collective-permute-start(bf16[1728,128]{1,0:T(8,128)(2,1)S(1)} %constant_dynamic-update-slice_fusion.5.refs_2_), channel_id=1, source_target_pairs={{0,1},{1,0},{2,3},{3,2},{4,5},{5,4},{6,7},{7,6},{8,9},{9,8},{10,11... | collective-permute-start | bytes 1327112 | tf_op jit(solution)/shard_map/ppermute | solution.py:420
  110.4 8.9 %collective-permute-start.28 = (bf16[1728,128]{1,0:T(8,128)(2,1)S(1)}, bf16[1728,128]{1,0:T(8,128)(2,1)S(1)}, u32[]{:S(2)}, u32[]{:S(2)}) collective-permute-start(bf16[1728,128]{1,0:T(8,128)(2,1)S(1)} %constant_dynamic-update-slice_fusion.refs_1_), channel_id=1, source_target_pairs={{0,1},{1,0},{2,3},{3,2},{4,5},{5,4},{6,7},{7,6},{8,9},{9,8},{10,11... | collective-permute-start | bytes 1327112 | tf_op jit(solution)/shard_map/ppermute | solution.py:420
  118.6 2.6 %collective-permute-start.26 = (bf16[1728,128]{1,0:T(8,128)(2,1)S(1)}, bf16[1728,128]{1,0:T(8,128)(2,1)S(1)}, u32[]{:S(2)}, u32[]{:S(2)}) collective-permute-start(bf16[1728,128]{1,0:T(8,128)(2,1)S(1)} %collective-permute-done.24.refs_1_), channel_id=1, source_target_pairs={{0,1},{1,0},{2,3},{3,2},{4,5},{5,4},{6,7},{7,6},{8,9},{9,8},{10,11... | collective-permute-start | bytes 1327112 | tf_op jit(solution)/shard_map/ppermute | solution.py:420
  118.6 2.6 %collective-permute-start.27 = (bf16[1728,128]{1,0:T(8,128)(2,1)S(1)}, bf16[1728,128]{1,0:T(8,128)(2,1)S(1)}, u32[]{:S(2)}, u32[]{:S(2)}) collective-permute-start(bf16[1728,128]{1,0:T(8,128)(2,1)S(1)} %collective-permute-done.25.refs_2_), channel_id=1, source_target_pairs={{0,1},{1,0},{2,3},{3,2},{4,5},{5,4},{6,7},{7,6},{8,9},{9,8},{10,11... | collective-permute-start | bytes 1327112 | tf_op jit(solution)/shard_map/ppermute | solution.py:420

commit v11 on v10

--- a/solution.py
+++ b/solution.py
@@ -541,10 +541,10 @@
     )
     activated, gp, keep, *give = forward(ways, flags, col, own_features, faces, weight, upstream[0, 0, 0])
     devices = lax.axis_size("gx") * lax.axis_size("gy") * lax.axis_size("gz")
-    split = (0, 15, 18)
     state = {"turn": 0, "returned": {}, "grad": []}
-    late = [j for j, way in enumerate(ways) if way in ((0, 0), (1, 2))]
-    early = [j for j in range(len(ways)) if j not in late]
+    when = {(0, 0): 2, (1, 2): 2, (0, 2): 3, (0, 1): 4, (1, 1): 4}
+    back_at = {turn: [j for j, way in enumerate(ways) if when.get(way, 4) == turn] for turn in (2, 3, 4)}
+    own_at = {1: (0, 3), 2: (3, 6), 3: (6, 18)}
 
     def tied(out, work, came):
         held = lax.optimization_barrier((gp, *out))
@@ -558,22 +558,22 @@
         if turn == 0:
             work = lambda g: backward_faces(ways, flags, row, g, weight, sends.shape[2])
             state["back"], came = tied(out, work, came)
-        elif turn in (1, 2):
-            picks = early if turn == 1 else late
+        if back_at.get(turn):
+            picks = back_at[turn]
             held = lax.optimization_barrier((*[state["back"][j] for j in picks], *out))
             got = exchange(held[: len(picks)], [ways[j] for j in picks])
             held = lax.optimization_barrier((*got, *came))
             for j, face in zip(picks, held):
                 state["returned"][j] = face
             came = list(held[len(picks) :])
-        if turn in (3, 4):
-            first, after = split[turn - 3 : turn - 1]
+        if turn in own_at:
+            first, after = own_at[turn]
             work = lambda g: [backward_own(row, g, weight, first, after - first, state["grad"])]
             made, came = tied(out, work, came)
             state["grad"] = [made[0]]
         if turn == 5:
             faces = [state["returned"][j] for j in range(len(ways))]
-            first = split[-1]
+            first = own_at[3][1]
             work = lambda g: [finish(ways, flags, sends, row, g, weight, first, taps - first, state["grad"][0], faces)]
             (state["done"],), came = tied(out, work, came)
         return came

time: 124 us -> 125 us (level)
  Pallas kernels: 65.9 us -> 68 us
  starting transfers between devices: 36.8 us -> 35.1 us
    ppermute x14, waiting for transfers between devices: 6.21 us -> 10.7 us  [swap(): return lax.ppermute(x, axis, [(j, j ^ 1 << bit) for j in range(n)])]
    ppermute x6, waiting for transfers between devices: 2.49 us -> 0.02 us  [reduce_all(): lax.ppermute(y, 'gy', [(j, (j + s) % n) for j in range(n)])]
    pallas_call x2 -> x3, Pallas kernels: 12.5 us -> 14.6 us  [backward_own(): pl.pallas_call(lambda *refs: own_kernel(first, count, *refs), in_specs=[H...]
    ppermute x10, waiting for transfers between devices: 2.72 us -> 1.17 us  [exchange(): got.append(lax.ppermute(array, AXES[i], pairs))]
  transfers between devices with their start and end apart: 30 -> 30, of which waited for: 12 -> 11; matrix products, arithmetic and copies ran while one was open for 1% -> 1% of each run, Pallas kernels for 29% -> 31%
where the time goes in v11:
time: 125 us; the launch traced here: 124 us
  Pallas kernels  68 us (54%)
  starting transfers between devices  35.1 us (28%)
  waiting for transfers between devices  11.8 us (9%)
  other arithmetic  7.9 us (6%)
    pallas_call x1, Pallas kernels, forward(): pl.pallas_call(lambda *refs: forward_kernel(ways, where, 256, *refs), in_...  25.5 us
    pallas_call x3, Pallas kernels, backward_own(): pl.pallas_call(lambda *refs: own_kernel(first, count, *refs), in_specs=[H...  14.6 us
    ppermute x10, starting transfers between devices, exchange(): got.append(lax.ppermute(array, AXES[i], pairs))  13.4 us
    ppermute x14, starting transfers between devices, swap(): return lax.ppermute(x, axis, [(j, j ^ 1 << bit) for j in range(n)])  12.1 us
    ppermute x14, waiting for transfers between devices, swap(): return lax.ppermute(x, axis, [(j, j ^ 1 << bit) for j in range(n)])  10.7 us
    pallas_call x1, Pallas kernels, backward_faces(): pl.pallas_call(lambda *refs: faces_kernel(ways, where, own, taps, *refs),...  10.6 us
    ppermute x6, starting transfers between devices, reduce_all(): lax.ppermute(y, 'gy', [(j, (j + s) % n) for j in range(n)])  9.64 us
    pallas_call x1, Pallas kernels, finish(): pl.pallas_call(lambda *refs: finish_kernel(ways, first, count, *refs), in...  7.42 us
  transfers between devices with their start and end apart: 30, of which 11 were waited for; matrix products, arithmetic and copies ran while one was open for 1% of the time, Pallas kernels for 31%

profile of v11, /device:TPU:0, one launch (start us, length us, event | category | flops | bytes accessed | tf_op | source)
XLA Modules:
  0.0 124.5 jit_solution(946154899218652043)
XLA Ops:
  0.6 0.1 pad_add_fusion.refs_0_
  0.7 2.0 %send.1 = (bf16[96,256]{1,0:T(8,128)(2,1)S(1)}, bf16[96,256]{1,0:T(8,128)(2,1)S(1)}, bf16[96,256]{1,0:T(8,128)(2,1)S(1)}, bf16[96,256]{1,0:T(8,128)(2,1)S(1)}, bf16[96,256]{1,0:T(8,128)(2,1)S(1)}) custom-call(s32[4]{0:T(128)S(1)} %pad_add_fusion.refs_0_, s32[6,1,96]{2,1,0:T(1,128)} %bitcast.26, bf16[768,256]{1,0:T(8,128)(2,1)} %bitcast.19), custom_call_target="tpu_custom_call" | custom-call | tf_op jit(solution)/shard_map/send/pallas_call | solution.py:89
  2.7 3.0 %collective-permute-start = (bf16[96,256]{1,0:T(8,128)(2,1)S(1)}, bf16[96,256]{1,0:T(8,128)(2,1)S(1)}, u32[]{:S(2)}, u32[]{:S(2)}) collective-permute-start(bf16[96,256]{1,0:T(8,128)(2,1)S(1)} %get-tuple-element.65), channel_id=1, source_target_pairs={{0,16},{16,0},{1,17},{17,1},{2,18},{18,2},{3,19},{19,3},{4,20},{20... | collective-permute-start | bytes 147464 | tf_op jit(solution)/shard_map/ppermute | solution.py:60
  5.7 1.6 %collective-permute-start.1 = (bf16[96,256]{1,0:T(8,128)(2,1)S(1)}, bf16[96,256]{1,0:T(8,128)(2,1)S(1)}, u32[]{:S(2)}, u32[]{:S(2)}) collective-permute-start(bf16[96,256]{1,0:T(8,128)(2,1)S(1)} %get-tuple-element.66), channel_id=1, source_target_pairs={{0,4},{4,0},{8,12},{12,8},{1,5},{5,1},{9,13},{13,9},{2,6},{6,2},{1... | collective-permute-start | bytes 147464 | tf_op jit(solution)/shard_map/ppermute | solution.py:60
  7.3 0.7 collective-permute-start.2
  8.0 0.1 collective-permute-start.3
  8.1 0.7 collective-permute-start.4
  8.7 3.9 %invert.1 = (f32[27,128,16]{2,1,0:T(8,128)S(1)}, f32[27,16,128]{2,1,0:T(8,128)}) custom-call(s32[4]{0:T(128)S(1)} %pad_add_fusion.refs_0_, s32[27,1,768]{2,1,0:T(1,128)} %bitcast.23, s32[27,1,768]{2,1,0:T(1,128)} %bitcast.24, s32[27,1,768]{2,1,0:T(1,128)} %bitcast.25), custom_call_target="tpu_custom_call" | custom-call | tf_op jit(solution)/shard_map/invert/pallas_call | solution.py:142
  12.6 0.0 collective-permute-done.2.refs_7_
  12.7 0.0 collective-permute-done.3.refs_8_
  12.7 25.5 %forward.1 = (bf16[768,256]{1,0:T(8,128)(2,1)}, bf16[768,256]{1,0:T(8,128)(2,1)}, f32[6912,128]{1,0:T(8,128)S(1)}, bf16[3456,128]{1,0:T(8,128)(2,1)}, bf16[3456,128]{1,0:T(8,128)(2,1)}) custom-call(s32[4]{0:T(128)S(1)} %pad_add_fusion.refs_0_, f32[27,128,16]{2,1,0:T(8,128)S(1)} %get-tuple-element.64.refs_1_, bf16[768,256]{1,0:T(8,128)(2,1)} %bitcast.20, ...), custom_call_target="tpu_custom_call" | custom-call | tf_op jit(solution)/shard_map/forward/pallas_call | solution.py:247
  38.1 2.9 %collective-permute-start.5 = (bf16[3456,128]{1,0:T(8,128)(2,1)}, bf16[3456,128]{1,0:T(8,128)(2,1)}, u32[]{:S(2)}, u32[]{:S(2)}) collective-permute-start(bf16[3456,128]{1,0:T(8,128)(2,1)} %get-tuple-element.74), channel_id=1, source_target_pairs={{0,1},{1,0},{2,3},{3,2},{4,5},{5,4},{6,7},{7,6},{8,9},{9,8},{10,11... | collective-permute-start | bytes 2654216 | tf_op jit(solution)/shard_map/ppermute | solution.py:420
  41.1 0.1 collective-permute-start.6
  41.2 2.3 %collective-permute-done.5 = bf16[3456,128]{1,0:T(8,128)(2,1)} collective-permute-done((bf16[3456,128]{1,0:T(8,128)(2,1)}, bf16[3456,128]{1,0:T(8,128)(2,1)}, u32[]{:S(2)}, u32[]{:S(2)}) %collective-permute-start.5) | collective-permute-done | bytes 884768 | tf_op jit(solution)/shard_map/ppermute | solution.py:420
  43.5 1.3 %collective-permute-done.6 = bf16[3456,128]{1,0:T(8,128)(2,1)} collective-permute-done((bf16[3456,128]{1,0:T(8,128)(2,1)}, bf16[3456,128]{1,0:T(8,128)(2,1)}, u32[]{:S(2)}, u32[]{:S(2)}) %collective-permute-start.6) | collective-permute-done | bytes 884768 | tf_op jit(solution)/shard_map/ppermute | solution.py:420
  44.7 2.2 %add_convert_fusion = (bf16[1728,128]{1,0:T(8,128)(2,1)}, bf16[1728,128]{1,0:T(8,128)(2,1)}) fusion(f32[6912,128]{1,0:T(8,128)S(1)} %get-tuple-element.73, s32[]{:T(128)S(6)} %select_n.150, bf16[3456,128]{1,0:T(8,128)(2,1)} %collective-permute-done.6, s32[]{:T(128)S(6)} %select_n.151, bf16[3456,128]{1,0:T(8,128)(2,1)} %collective-permute-done.5, ...), kind=kLoop, calls=%fused_computation | loop fusion | flops 1327104 | bytes 3538960 | tf_op jit(solution)/shard_map/convert_element_type | solution.py:485
  47.0 0.9 collective-permute-start.8
  47.8 0.5 collective-permute-start.7
  48.4 10.6 %backward_faces.1 = (bf16[96,256]{1,0:T(8,128)(2,1)}, bf16[96,256]{1,0:T(8,128)(2,1)}, bf16[96,256]{1,0:T(8,128)(2,1)}, bf16[96,256]{1,0:T(8,128)(2,1)}, bf16[96,256]{1,0:T(8,128)(2,1)}) custom-call(s32[4]{0:T(128)S(1)} %pad_add_fusion.refs_0_, f32[27,16,128]{2,1,0:T(8,128)} %get-tuple-element.71.refs_1_.refs_0_.refs_2_, ...), custom_call_target="tpu_custom_call" | custom-call | tf_op jit(solution)/shard_map/backward_faces/pallas_call | solution.py:346
  59.0 0.7 collective-permute-done.8
  59.7 0.3 collective-permute-done.7
  60.1 2.2 %add_convert_fusion.2 = (bf16[864,128]{1,0:T(8,128)(2,1)}, bf16[864,128]{1,0:T(8,128)(2,1)}) fusion(f32[6912,128]{1,0:T(8,128)S(1)} %get-tuple-element.73, s32[]{:T(128)S(6)} %select_n.156, bf16[1728,128]{1,0:T(8,128)(2,1)} %collective-permute-done.8, s32[]{:T(128)S(6)} %select_n.158, bf16[3456,128]{1,0:T(8,128)(2,1)} %collective-permute-done.6, ...), kind=kLoop, calls=%fused_computation.2 | loop fusion | flops 1105920 | bytes 2211864 | tf_op jit(solution)/shard_map/convert_element_type | solution.py:485
  62.3 0.5 collective-permute-start.10
  62.8 1.4 %collective-permute-start.9 = (bf16[864,128]{1,0:T(8,128)(2,1)}, bf16[864,128]{1,0:T(8,128)(2,1)}, u32[]{:S(2)}, u32[]{:S(2)}) collective-permute-start(bf16[864,128]{1,0:T(8,128)(2,1)} %get-tuple-element.134), channel_id=1, source_target_pairs={{0,2},{1,3},{2,0},{3,1},{4,6},{5,7},{6,4},{7,5},{8,10},{9,11},{10,... | collective-permute-start | bytes 663560 | tf_op jit(solution)/shard_map/ppermute | solution.py:420
  64.2 3.5 %backward_own.3.refs_3_ = f32[768,256]{1,0:T(8,128)} custom-call(f32[27,16,128]{2,1,0:T(8,128)} %get-tuple-element.71.refs_1_.refs_0_.refs_2_, bf16[768,256]{1,0:T(8,128)(2,1)} %get-tuple-element.115.refs_2_.refs_1_.refs_3_, bf16[27,256,256]{2,1,0:T(8,128)(2,1)} %refs_4_.1), custom_call_target="tpu_custom_call" | custom-call | tf_op jit(solution)/shard_map/backward_own/pallas_call | solution.py:369
  67.7 1.4 %collective-permute-done.10 = bf16[864,128]{1,0:T(8,128)(2,1)} collective-permute-done((bf16[864,128]{1,0:T(8,128)(2,1)}, bf16[864,128]{1,0:T(8,128)(2,1)}, u32[]{:S(2)}, u32[]{:S(2)}) %collective-permute-start.10) | collective-permute-done | bytes 221216 | tf_op jit(solution)/shard_map/ppermute | solution.py:420
  69.1 0.5 collective-permute-done.9
  69.7 1.1 add_convert_fusion.5
  70.8 1.1 add_convert_fusion.4
  71.9 4.4 %collective-permute-start.13 = (bf16[432,128]{1,0:T(8,128)(2,1)S(1)}, bf16[432,128]{1,0:T(8,128)(2,1)S(1)}, u32[]{:S(2)}, u32[]{:S(2)}) collective-permute-start(bf16[432,128]{1,0:T(8,128)(2,1)S(1)} %pad_maximum_fusion.2), channel_id=1, source_target_pairs={{0,4},{4,8},{8,12},{12,0},{1,5},{5,9},{9,13},{13,1},{2,6},{6,10},{... | collective-permute-start | bytes 331784 | tf_op jit(solution)/shard_map/ppermute | solution.py:493
  76.4 0.1 collective-permute-start.14
  76.5 2.4 %collective-permute-start.15 = (bf16[432,128]{1,0:T(8,128)(2,1)S(1)}, bf16[432,128]{1,0:T(8,128)(2,1)S(1)}, u32[]{:S(2)}, u32[]{:S(2)}) collective-permute-start(bf16[432,128]{1,0:T(8,128)(2,1)S(1)} %pad_maximum_fusion.4), channel_id=1, source_target_pairs={{0,12},{4,0},{8,4},{12,8},{1,13},{5,1},{9,5},{13,9},{2,14},{6,2},{... | collective-permute-start | bytes 331784 | tf_op jit(solution)/shard_map/ppermute | solution.py:493
  78.9 1.2 collective-permute-start.11
  80.1 0.7 collective-permute-start.12
  80.8 1.0 convert_add_fusion.1
  81.8 3.5 %backward_own.4.refs_3_ = f32[768,256]{1,0:T(8,128)} custom-call(f32[27,16,128]{2,1,0:T(8,128)} %get-tuple-element.71.refs_1_.refs_0_.refs_2_, bf16[768,256]{1,0:T(8,128)(2,1)} %get-tuple-element.115.refs_2_.refs_1_.refs_3_, bf16[27,256,256]{2,1,0:T(8,128)(2,1)} %refs_4_.1, f32[768,256]{1,0:T(8,128)} %backward_own.3.refs_3_), custom_call_target="tpu_custom_call" | custom-call | tf_op jit(solution)/shard_map/backward_own/pallas_call | solution.py:369
  85.4 0.0 collective-permute-done.11.refs_6_
  85.4 0.0 collective-permute-done.12.refs_10_
  85.4 0.0 collective-permute-done.14
  85.4 0.0 collective-permute-done.15
  85.4 0.1 fusion.3
  85.5 2.1 %collective-permute-start.19 = (bf16[432,128]{1,0:T(8,128)(2,1)S(1)}, bf16[432,128]{1,0:T(8,128)(2,1)S(1)}, u32[]{:S(2)}, u32[]{:S(2)}) collective-permute-start(bf16[432,128]{1,0:T(8,128)(2,1)S(1)} %fusion.3), channel_id=1, source_target_pairs={{0,12},{4,0},{8,4},{12,8},{1,13},{5,1},{9,5},{13,9},{2,14},{6,2},{... | collective-permute-start | bytes 331784 | tf_op jit(solution)/shard_map/ppermute | solution.py:493
  87.6 0.2 collective-permute-start.18
  87.8 0.4 collective-permute-start.17
  88.2 2.2 %collective-permute-start.16 = (bf16[96,256]{1,0:T(8,128)(2,1)S(1)}, bf16[96,256]{1,0:T(8,128)(2,1)S(1)}, u32[]{:S(2)}, u32[]{:S(2)}) collective-permute-start(bf16[96,256]{1,0:T(8,128)(2,1)S(1)} %copy-done.7), channel_id=1, source_target_pairs={{0,1},{1,0},{2,3},{3,2},{4,5},{5,4},{6,7},{7,6},{8,9},{9,8},{10,11... | collective-permute-start | bytes 147464 | tf_op jit(solution)/shard_map/ppermute | solution.py:60
  90.5 7.5 %backward_own.5.refs_5_ = f32[768,256]{1,0:T(8,128)} custom-call(f32[27,16,128]{2,1,0:T(8,128)} %get-tuple-element.71.refs_1_.refs_0_.refs_2_, bf16[768,256]{1,0:T(8,128)(2,1)} %get-tuple-element.115.refs_2_.refs_1_.refs_3_, bf16[27,256,256]{2,1,0:T(8,128)(2,1)} %refs_4_.1, f32[768,256]{1,0:T(8,128)} %backward_own.4.refs_3_), custom_call_target="tpu_custom_call" | custom-call | tf_op jit(solution)/shard_map/backward_own/pallas_call | solution.py:369
  98.1 0.0 collective-permute-done.18
  98.3 0.5 collective-permute-start.22
  98.8 1.2 collective-permute-start.23
  100.0 2.5 %collective-permute-start.20 = (bf16[96,256]{1,0:T(8,128)(2,1)S(1)}, bf16[96,256]{1,0:T(8,128)(2,1)S(1)}, u32[]{:S(2)}, u32[]{:S(2)}) collective-permute-start(bf16[96,256]{1,0:T(8,128)(2,1)S(1)} %copy-done.6), channel_id=1, source_target_pairs={{0,4},{4,0},{8,12},{12,8},{1,5},{5,1},{9,13},{13,9},{2,6},{6,2},{1... | collective-permute-start | bytes 147464 | tf_op jit(solution)/shard_map/ppermute | solution.py:60
  102.5 0.9 collective-permute-start.21
  103.4 1.1 collective-permute-done.20.refs_7_
  104.6 1.7 %collective-permute-done.22 = bf16[864,128]{1,0:T(8,128)(2,1)S(1)} collective-permute-done((bf16[864,128]{1,0:T(8,128)(2,1)S(1)}, bf16[864,128]{1,0:T(8,128)(2,1)S(1)}, u32[]{:S(2)}, u32[]{:S(2)}) %collective-permute-start.22) | collective-permute-done | bytes 221216 | tf_op jit(solution)/shard_map/ppermute | solution.py:420
  106.3 0.2 collective-permute-done.23
  106.5 1.7 %collective-permute-start.25 = (bf16[1728,128]{1,0:T(8,128)(2,1)S(1)}, bf16[1728,128]{1,0:T(8,128)(2,1)S(1)}, u32[]{:S(2)}, u32[]{:S(2)}) collective-permute-start(bf16[1728,128]{1,0:T(8,128)(2,1)S(1)} %constant_dynamic-update-slice_fusion.5.refs_2_), channel_id=1, source_target_pairs={{0,2},{1,3},{2,0},{3,1},{4,6},{5,7},{6,4},{7,5},{8,10},{9,11},{10,... | collective-permute-start | bytes 1327112 | tf_op jit(solution)/shard_map/ppermute | solution.py:420
  108.2 1.2 collective-permute-start.24
  109.5 0.5 collective-permute-start.28
  110.0 7.4 %finish.1 = bf16[768,256]{1,0:T(8,128)(2,1)} custom-call(s32[4]{0:T(128)S(1)} %pad_add_fusion.refs_0_, s32[6,1,96]{2,1,0:T(1,128)} %bitcast.27, f32[27,16,128]{2,1,0:T(8,128)} %get-tuple-element.71.refs_1_.refs_0_.refs_2_, bf16[768,256]{1,0:T(8,128)(2,1)} %get-tuple-element.115.refs_2_.refs_1_.refs_3_, bf16[27,256,256]{2,1,0:T(8,128)(2,1)} %refs_4_.1, ...), custom_call_target="tpu_custom_call" | custom-call | tf_op jit(solution)/shard_map/finish/pallas_call | solution.py:402
  117.4 0.9 collective-permute-done.25.refs_2_
  118.3 1.3 %collective-permute-done.24.refs_1_ = bf16[1728,128]{1,0:T(8,128)(2,1)S(1)} collective-permute-done((bf16[1728,128]{1,0:T(8,128)(2,1)S(1)}, bf16[1728,128]{1,0:T(8,128)(2,1)S(1)}, u32[]{:S(2)}, u32[]{:S(2)}) %collective-permute-start.24) | collective-permute-done | bytes 442400 | tf_op jit(solution)/shard_map/ppermute | solution.py:420
  119.6 0.5 collective-permute-start.27
  120.1 0.1 stack.38.refs_0_
  120.2 2.0 %place.2.refs_5_ = bf16[6912,256]{1,0:T(8,128)(2,1)} custom-call(s32[6]{0:T(128)S(1)} %stack.38.refs_0_, bf16[1728,128]{1,0:T(8,128)(2,1)S(1)} %constant_dynamic-update-slice_fusion.refs_1_, bf16[1728,128]{1,0:T(8,128)(2,1)S(1)} %constant_dynamic-update-slice_fusion.5.refs_2_, bf16[1728,128]{1,0:T(8,128)(2,1)S(1)} %collective-permute-done.28.refs_3_, ...), custom_call_target="tpu_custom_call" | custom-call | tf_op jit(solution)/shard_map/place/pallas_call | solution.py:454
  122.3 2.0 %place.3 = bf16[6912,256]{1,0:T(8,128)(2,1)} custom-call(s32[6]{0:T(128)S(1)} %stack.38.refs_0_, bf16[1728,128]{1,0:T(8,128)(2,1)S(1)} %collective-permute-done.24.refs_1_, bf16[1728,128]{1,0:T(8,128)(2,1)S(1)} %collective-permute-done.25.refs_2_, bf16[1728,128]{1,0:T(8,128)(2,1)S(1)} %collective-permute-done.26.refs_3_, ...), custom_call_target="tpu_custom_call", output_to_operand_aliasing={{}: (5, {})} | custom-call | tf_op jit(solution)/shard_map/place/pallas_call | solution.py:454
  (45 shorter events, 0.3 us)
Async XLA Ops:
  2.7 9.9 %collective-permute-start = (bf16[96,256]{1,0:T(8,128)(2,1)S(1)}, bf16[96,256]{1,0:T(8,128)(2,1)S(1)}, u32[]{:S(2)}, u32[]{:S(2)}) collective-permute-start(bf16[96,256]{1,0:T(8,128)(2,1)S(1)} %get-tuple-element.65), channel_id=1, source_target_pairs={{0,16},{16,0},{1,17},{17,1},{2,18},{18,2},{3,19},{19,3},{4,20},{20... | collective-permute-start | bytes 147464 | tf_op jit(solution)/shard_map/ppermute | solution.py:60
  5.7 6.9 %collective-permute-start.1 = (bf16[96,256]{1,0:T(8,128)(2,1)S(1)}, bf16[96,256]{1,0:T(8,128)(2,1)S(1)}, u32[]{:S(2)}, u32[]{:S(2)}) collective-permute-start(bf16[96,256]{1,0:T(8,128)(2,1)S(1)} %get-tuple-element.66), channel_id=1, source_target_pairs={{0,4},{4,0},{8,12},{12,8},{1,5},{5,1},{9,13},{13,9},{2,6},{6,2},{1... | collective-permute-start | bytes 147464 | tf_op jit(solution)/shard_map/ppermute | solution.py:60
  7.3 5.3 %collective-permute-start.2 = (bf16[96,256]{1,0:T(8,128)(2,1)S(1)}, bf16[96,256]{1,0:T(8,128)(2,1)S(1)}, u32[]{:S(2)}, u32[]{:S(2)}) collective-permute-start(bf16[96,256]{1,0:T(8,128)(2,1)S(1)} %get-tuple-element.67), channel_id=1, source_target_pairs={{4,8},{8,4},{5,9},{9,5},{6,10},{10,6},{7,11},{11,7},{20,24},{24,20... | collective-permute-start | bytes 147464 | tf_op jit(solution)/shard_map/ppermute | solution.py:60
  8.0 4.7 %collective-permute-start.3 = (bf16[96,256]{1,0:T(8,128)(2,1)S(1)}, bf16[96,256]{1,0:T(8,128)(2,1)S(1)}, u32[]{:S(2)}, u32[]{:S(2)}) collective-permute-start(bf16[96,256]{1,0:T(8,128)(2,1)S(1)} %get-tuple-element.68), channel_id=1, source_target_pairs={{0,1},{1,0},{2,3},{3,2},{4,5},{5,4},{6,7},{7,6},{8,9},{9,8},{10,11... | collective-permute-start | bytes 147464 | tf_op jit(solution)/shard_map/ppermute | solution.py:60
  8.1 4.6 %collective-permute-start.4 = (bf16[96,256]{1,0:T(8,128)(2,1)S(1)}, bf16[96,256]{1,0:T(8,128)(2,1)S(1)}, u32[]{:S(2)}, u32[]{:S(2)}) collective-permute-start(bf16[96,256]{1,0:T(8,128)(2,1)S(1)} %get-tuple-element.69), channel_id=1, source_target_pairs={{1,2},{2,1},{5,6},{6,5},{9,10},{10,9},{13,14},{14,13},{17,18},{18,... | collective-permute-start | bytes 147464 | tf_op jit(solution)/shard_map/ppermute | solution.py:60
  38.1 5.3 %collective-permute-start.5 = (bf16[3456,128]{1,0:T(8,128)(2,1)}, bf16[3456,128]{1,0:T(8,128)(2,1)}, u32[]{:S(2)}, u32[]{:S(2)}) collective-permute-start(bf16[3456,128]{1,0:T(8,128)(2,1)} %get-tuple-element.74), channel_id=1, source_target_pairs={{0,1},{1,0},{2,3},{3,2},{4,5},{5,4},{6,7},{7,6},{8,9},{9,8},{10,11... | collective-permute-start | bytes 2654216 | tf_op jit(solution)/shard_map/ppermute | solution.py:420
  41.1 3.7 %collective-permute-start.6 = (bf16[3456,128]{1,0:T(8,128)(2,1)}, bf16[3456,128]{1,0:T(8,128)(2,1)}, u32[]{:S(2)}, u32[]{:S(2)}) collective-permute-start(bf16[3456,128]{1,0:T(8,128)(2,1)} %get-tuple-element.75), channel_id=1, source_target_pairs={{0,1},{1,0},{2,3},{3,2},{4,5},{5,4},{6,7},{7,6},{8,9},{9,8},{10,11... | collective-permute-start | bytes 2654216 | tf_op jit(solution)/shard_map/ppermute | solution.py:420
  47.0 12.8 %collective-permute-start.8 = (bf16[1728,128]{1,0:T(8,128)(2,1)}, bf16[1728,128]{1,0:T(8,128)(2,1)}, u32[]{:S(2)}, u32[]{:S(2)}) collective-permute-start(bf16[1728,128]{1,0:T(8,128)(2,1)} %get-tuple-element.135), channel_id=1, source_target_pairs={{0,2},{1,3},{2,0},{3,1},{4,6},{5,7},{6,4},{7,5},{8,10},{9,11},{10,... | collective-permute-start | bytes 1327112 | tf_op jit(solution)/shard_map/ppermute | solution.py:420
  47.8 12.2 %collective-permute-start.7 = (bf16[1728,128]{1,0:T(8,128)(2,1)}, bf16[1728,128]{1,0:T(8,128)(2,1)}, u32[]{:S(2)}, u32[]{:S(2)}) collective-permute-start(bf16[1728,128]{1,0:T(8,128)(2,1)} %get-tuple-element.136), channel_id=1, source_target_pairs={{0,16},{16,0},{1,17},{17,1},{2,18},{18,2},{3,19},{19,3},{4,20},{20... | collective-permute-start | bytes 1327112 | tf_op jit(solution)/shard_map/ppermute | solution.py:420
  62.3 6.9 %collective-permute-start.10 = (bf16[864,128]{1,0:T(8,128)(2,1)}, bf16[864,128]{1,0:T(8,128)(2,1)}, u32[]{:S(2)}, u32[]{:S(2)}) collective-permute-start(bf16[864,128]{1,0:T(8,128)(2,1)} %get-tuple-element.133), channel_id=1, source_target_pairs={{0,16},{16,0},{1,17},{17,1},{2,18},{18,2},{3,19},{19,3},{4,20},{20... | collective-permute-start | bytes 663560 | tf_op jit(solution)/shard_map/ppermute | solution.py:420
  62.8 6.9 %collective-permute-start.9 = (bf16[864,128]{1,0:T(8,128)(2,1)}, bf16[864,128]{1,0:T(8,128)(2,1)}, u32[]{:S(2)}, u32[]{:S(2)}) collective-permute-start(bf16[864,128]{1,0:T(8,128)(2,1)} %get-tuple-element.134), channel_id=1, source_target_pairs={{0,2},{1,3},{2,0},{3,1},{4,6},{5,7},{6,4},{7,5},{8,10},{9,11},{10,... | collective-permute-start | bytes 663560 | tf_op jit(solution)/shard_map/ppermute | solution.py:420
  64.2 14.7 %copy-start.9 = (bf16[96,256]{1,0:T(8,128)(2,1)S(1)}, bf16[96,256]{1,0:T(8,128)(2,1)}, u32[]{:S(2)}) copy-start(bf16[96,256]{1,0:T(8,128)(2,1)} %get-tuple-element.91) | copy-start | bytes 147460
  64.2 15.9 %copy-start.8 = (bf16[96,256]{1,0:T(8,128)(2,1)S(1)}, bf16[96,256]{1,0:T(8,128)(2,1)}, u32[]{:S(2)}) copy-start(bf16[96,256]{1,0:T(8,128)(2,1)} %get-tuple-element.92) | copy-start | bytes 147460
  71.9 13.5 %collective-permute-start.13 = (bf16[432,128]{1,0:T(8,128)(2,1)S(1)}, bf16[432,128]{1,0:T(8,128)(2,1)S(1)}, u32[]{:S(2)}, u32[]{:S(2)}) collective-permute-start(bf16[432,128]{1,0:T(8,128)(2,1)S(1)} %pad_maximum_fusion.2), channel_id=1, source_target_pairs={{0,4},{4,8},{8,12},{12,0},{1,5},{5,9},{9,13},{13,1},{2,6},{6,10},{... | collective-permute-start | bytes 331784 | tf_op jit(solution)/shard_map/ppermute | solution.py:493
  76.4 9.0 %collective-permute-start.14 = (bf16[432,128]{1,0:T(8,128)(2,1)S(1)}, bf16[432,128]{1,0:T(8,128)(2,1)S(1)}, u32[]{:S(2)}, u32[]{:S(2)}) collective-permute-start(bf16[432,128]{1,0:T(8,128)(2,1)S(1)} %pad_maximum_fusion.3), channel_id=1, source_target_pairs={{0,8},{4,12},{8,0},{12,4},{1,9},{5,13},{9,1},{13,5},{2,10},{6,14},... | collective-permute-start | bytes 331784 | tf_op jit(solution)/shard_map/ppermute | solution.py:493
  76.5 11.7 %copy-start.7 = (bf16[96,256]{1,0:T(8,128)(2,1)S(1)}, bf16[96,256]{1,0:T(8,128)(2,1)}, u32[]{:S(2)}) copy-start(bf16[96,256]{1,0:T(8,128)(2,1)} %get-tuple-element.102) | copy-start | bytes 147460
  76.5 8.9 %collective-permute-start.15 = (bf16[432,128]{1,0:T(8,128)(2,1)S(1)}, bf16[432,128]{1,0:T(8,128)(2,1)S(1)}, u32[]{:S(2)}, u32[]{:S(2)}) collective-permute-start(bf16[432,128]{1,0:T(8,128)(2,1)S(1)} %pad_maximum_fusion.4), channel_id=1, source_target_pairs={{0,12},{4,0},{8,4},{12,8},{1,13},{5,1},{9,5},{13,9},{2,14},{6,2},{... | collective-permute-start | bytes 331784 | tf_op jit(solution)/shard_map/ppermute | solution.py:493
  78.9 6.4 %collective-permute-start.11 = (bf16[96,256]{1,0:T(8,128)(2,1)S(1)}, bf16[96,256]{1,0:T(8,128)(2,1)S(1)}, u32[]{:S(2)}, u32[]{:S(2)}) collective-permute-start(bf16[96,256]{1,0:T(8,128)(2,1)S(1)} %copy-done.9), channel_id=1, source_target_pairs={{0,16},{16,0},{1,17},{17,1},{2,18},{18,2},{3,19},{19,3},{4,20},{20... | collective-permute-start | bytes 147464 | tf_op jit(solution)/shard_map/ppermute | solution.py:60
  80.1 5.3 %collective-permute-start.12 = (bf16[96,256]{1,0:T(8,128)(2,1)S(1)}, bf16[96,256]{1,0:T(8,128)(2,1)S(1)}, u32[]{:S(2)}, u32[]{:S(2)}) collective-permute-start(bf16[96,256]{1,0:T(8,128)(2,1)S(1)} %copy-done.8), channel_id=1, source_target_pairs={{1,2},{2,1},{5,6},{6,5},{9,10},{10,9},{13,14},{14,13},{17,18},{18,... | collective-permute-start | bytes 147464 | tf_op jit(solution)/shard_map/ppermute | solution.py:60
  85.4 12.8 %copy-start = (bf16[96,256]{1,0:T(8,128)(2,1)}, bf16[96,256]{1,0:T(8,128)(2,1)S(1)}, u32[]{:S(2)}) copy-start(bf16[96,256]{1,0:T(8,128)(2,1)S(1)} %collective-permute-done.11.refs_6_) | copy-start | bytes 147460
  85.4 12.8 %copy-start.1 = (bf16[96,256]{1,0:T(8,128)(2,1)}, bf16[96,256]{1,0:T(8,128)(2,1)S(1)}, u32[]{:S(2)}) copy-start(bf16[96,256]{1,0:T(8,128)(2,1)S(1)} %collective-permute-done.12.refs_10_) | copy-start | bytes 147460
  85.5 12.5 %collective-permute-start.19 = (bf16[432,128]{1,0:T(8,128)(2,1)S(1)}, bf16[432,128]{1,0:T(8,128)(2,1)S(1)}, u32[]{:S(2)}, u32[]{:S(2)}) collective-permute-start(bf16[432,128]{1,0:T(8,128)(2,1)S(1)} %fusion.3), channel_id=1, source_target_pairs={{0,12},{4,0},{8,4},{12,8},{1,13},{5,1},{9,5},{13,9},{2,14},{6,2},{... | collective-permute-start | bytes 331784 | tf_op jit(solution)/shard_map/ppermute | solution.py:493
  87.6 10.5 %collective-permute-start.18 = (bf16[432,128]{1,0:T(8,128)(2,1)S(1)}, bf16[432,128]{1,0:T(8,128)(2,1)S(1)}, u32[]{:S(2)}, u32[]{:S(2)}) collective-permute-start(bf16[432,128]{1,0:T(8,128)(2,1)S(1)} %fusion.3), channel_id=1, source_target_pairs={{0,8},{4,12},{8,0},{12,4},{1,9},{5,13},{9,1},{13,5},{2,10},{6,14},... | collective-permute-start | bytes 331784 | tf_op jit(solution)/shard_map/ppermute | solution.py:493
  87.8 10.3 %collective-permute-start.17 = (bf16[432,128]{1,0:T(8,128)(2,1)S(1)}, bf16[432,128]{1,0:T(8,128)(2,1)S(1)}, u32[]{:S(2)}, u32[]{:S(2)}) collective-permute-start(bf16[432,128]{1,0:T(8,128)(2,1)S(1)} %fusion.3), channel_id=1, source_target_pairs={{0,4},{4,8},{8,12},{12,0},{1,5},{5,9},{9,13},{13,1},{2,6},{6,10},{... | collective-permute-start | bytes 331784 | tf_op jit(solution)/shard_map/ppermute | solution.py:493
  88.2 9.8 %collective-permute-start.16 = (bf16[96,256]{1,0:T(8,128)(2,1)S(1)}, bf16[96,256]{1,0:T(8,128)(2,1)S(1)}, u32[]{:S(2)}, u32[]{:S(2)}) collective-permute-start(bf16[96,256]{1,0:T(8,128)(2,1)S(1)} %copy-done.7), channel_id=1, source_target_pairs={{0,1},{1,0},{2,3},{3,2},{4,5},{5,4},{6,7},{7,6},{8,9},{9,8},{10,11... | collective-permute-start | bytes 147464 | tf_op jit(solution)/shard_map/ppermute | solution.py:60
  90.5 9.5 %copy-start.6 = (bf16[96,256]{1,0:T(8,128)(2,1)S(1)}, bf16[96,256]{1,0:T(8,128)(2,1)}, u32[]{:S(2)}) copy-start(bf16[96,256]{1,0:T(8,128)(2,1)} %get-tuple-element.111) | copy-start | bytes 147460
  90.5 12.0 %copy-start.5 = (bf16[96,256]{1,0:T(8,128)(2,1)S(1)}, bf16[96,256]{1,0:T(8,128)(2,1)}, u32[]{:S(2)}) copy-start(bf16[96,256]{1,0:T(8,128)(2,1)} %get-tuple-element.112) | copy-start | bytes 147460
  98.0 11.9 %copy-start.2 = (bf16[96,256]{1,0:T(8,128)(2,1)}, bf16[96,256]{1,0:T(8,128)(2,1)S(1)}, u32[]{:S(2)}) copy-start(bf16[96,256]{1,0:T(8,128)(2,1)S(1)} %collective-permute-done.16.refs_9_) | copy-start | bytes 147460
  98.3 8.0 %collective-permute-start.22 = (bf16[864,128]{1,0:T(8,128)(2,1)S(1)}, bf16[864,128]{1,0:T(8,128)(2,1)S(1)}, u32[]{:S(2)}, u32[]{:S(2)}) collective-permute-start(bf16[864,128]{1,0:T(8,128)(2,1)S(1)} %pad_maximum_fusion), channel_id=1, source_target_pairs={{0,2},{1,3},{2,0},{3,1},{4,6},{5,7},{6,4},{7,5},{8,10},{9,11},{10,... | collective-permute-start | bytes 663560 | tf_op jit(solution)/shard_map/ppermute | solution.py:420
  98.8 7.6 %collective-permute-start.23 = (bf16[864,128]{1,0:T(8,128)(2,1)S(1)}, bf16[864,128]{1,0:T(8,128)(2,1)S(1)}, u32[]{:S(2)}, u32[]{:S(2)}) collective-permute-start(bf16[864,128]{1,0:T(8,128)(2,1)S(1)} %pad_maximum_fusion.1), channel_id=1, source_target_pairs={{0,16},{16,0},{1,17},{17,1},{2,18},{18,2},{3,19},{19,3},{4,20},{20... | collective-permute-start | bytes 663560 | tf_op jit(solution)/shard_map/ppermute | solution.py:420
  100.0 4.5 %collective-permute-start.20 = (bf16[96,256]{1,0:T(8,128)(2,1)S(1)}, bf16[96,256]{1,0:T(8,128)(2,1)S(1)}, u32[]{:S(2)}, u32[]{:S(2)}) collective-permute-start(bf16[96,256]{1,0:T(8,128)(2,1)S(1)} %copy-done.6), channel_id=1, source_target_pairs={{0,4},{4,0},{8,12},{12,8},{1,5},{5,1},{9,13},{13,9},{2,6},{6,2},{1... | collective-permute-start | bytes 147464 | tf_op jit(solution)/shard_map/ppermute | solution.py:60
  102.5 2.1 %collective-permute-start.21 = (bf16[96,256]{1,0:T(8,128)(2,1)S(1)}, bf16[96,256]{1,0:T(8,128)(2,1)S(1)}, u32[]{:S(2)}, u32[]{:S(2)}) collective-permute-start(bf16[96,256]{1,0:T(8,128)(2,1)S(1)} %copy-done.5), channel_id=1, source_target_pairs={{4,8},{8,4},{5,9},{9,5},{6,10},{10,6},{7,11},{11,7},{20,24},{24,20... | collective-permute-start | bytes 147464 | tf_op jit(solution)/shard_map/ppermute | solution.py:60
  104.5 5.4 %copy-start.3 = (bf16[96,256]{1,0:T(8,128)(2,1)}, bf16[96,256]{1,0:T(8,128)(2,1)S(1)}, u32[]{:S(2)}) copy-start(bf16[96,256]{1,0:T(8,128)(2,1)S(1)} %collective-permute-done.20.refs_7_) | copy-start | bytes 147460
  104.6 5.4 %copy-start.4 = (bf16[96,256]{1,0:T(8,128)(2,1)}, bf16[96,256]{1,0:T(8,128)(2,1)S(1)}, u32[]{:S(2)}) copy-start(bf16[96,256]{1,0:T(8,128)(2,1)S(1)} %collective-permute-done.21.refs_8_) | copy-start | bytes 147460
  106.5 11.8 %collective-permute-start.25 = (bf16[1728,128]{1,0:T(8,128)(2,1)S(1)}, bf16[1728,128]{1,0:T(8,128)(2,1)S(1)}, u32[]{:S(2)}, u32[]{:S(2)}) collective-permute-start(bf16[1728,128]{1,0:T(8,128)(2,1)S(1)} %constant_dynamic-update-slice_fusion.5.refs_2_), channel_id=1, source_target_pairs={{0,2},{1,3},{2,0},{3,1},{4,6},{5,7},{6,4},{7,5},{8,10},{9,11},{10,... | collective-permute-start | bytes 1327112 | tf_op jit(solution)/shard_map/ppermute | solution.py:420
  108.2 11.4 %collective-permute-start.24 = (bf16[1728,128]{1,0:T(8,128)(2,1)S(1)}, bf16[1728,128]{1,0:T(8,128)(2,1)S(1)}, u32[]{:S(2)}, u32[]{:S(2)}) collective-permute-start(bf16[1728,128]{1,0:T(8,128)(2,1)S(1)} %constant_dynamic-update-slice_fusion.refs_1_), channel_id=1, source_target_pairs={{0,16},{16,0},{1,17},{17,1},{2,18},{18,2},{3,19},{19,3},{4,20},{20... | collective-permute-start | bytes 1327112 | tf_op jit(solution)/shard_map/ppermute | solution.py:420
  109.5 10.7 %collective-permute-start.29 = (bf16[1728,128]{1,0:T(8,128)(2,1)S(1)}, bf16[1728,128]{1,0:T(8,128)(2,1)S(1)}, u32[]{:S(2)}, u32[]{:S(2)}) collective-permute-start(bf16[1728,128]{1,0:T(8,128)(2,1)S(1)} %constant_dynamic-update-slice_fusion.5.refs_2_), channel_id=1, source_target_pairs={{0,1},{1,0},{2,3},{3,2},{4,5},{5,4},{6,7},{7,6},{8,9},{9,8},{10,11... | collective-permute-start | bytes 1327112 | tf_op jit(solution)/shard_map/ppermute | solution.py:420
  109.5 10.7 %collective-permute-start.28 = (bf16[1728,128]{1,0:T(8,128)(2,1)S(1)}, bf16[1728,128]{1,0:T(8,128)(2,1)S(1)}, u32[]{:S(2)}, u32[]{:S(2)}) collective-permute-start(bf16[1728,128]{1,0:T(8,128)(2,1)S(1)} %constant_dynamic-update-slice_fusion.refs_1_), channel_id=1, source_target_pairs={{0,1},{1,0},{2,3},{3,2},{4,5},{5,4},{6,7},{7,6},{8,9},{9,8},{10,11... | collective-permute-start | bytes 1327112 | tf_op jit(solution)/shard_map/ppermute | solution.py:420
  119.6 2.6 %collective-permute-start.26 = (bf16[1728,128]{1,0:T(8,128)(2,1)S(1)}, bf16[1728,128]{1,0:T(8,128)(2,1)S(1)}, u32[]{:S(2)}, u32[]{:S(2)}) collective-permute-start(bf16[1728,128]{1,0:T(8,128)(2,1)S(1)} %collective-permute-done.24.refs_1_), channel_id=1, source_target_pairs={{0,1},{1,0},{2,3},{3,2},{4,5},{5,4},{6,7},{7,6},{8,9},{9,8},{10,11... | collective-permute-start | bytes 1327112 | tf_op jit(solution)/shard_map/ppermute | solution.py:420
  119.6 2.6 %collective-permute-start.27 = (bf16[1728,128]{1,0:T(8,128)(2,1)S(1)}, bf16[1728,128]{1,0:T(8,128)(2,1)S(1)}, u32[]{:S(2)}, u32[]{:S(2)}) collective-permute-start(bf16[1728,128]{1,0:T(8,128)(2,1)S(1)} %collective-permute-done.25.refs_2_), channel_id=1, source_target_pairs={{0,1},{1,0},{2,3},{3,2},{4,5},{5,4},{6,7},{7,6},{8,9},{9,8},{10,11... | collective-permute-start | bytes 1327112 | tf_op jit(solution)/shard_map/ppermute | solution.py:420

commit v12 on v10

--- a/solution.py
+++ b/solution.py
@@ -183,7 +183,7 @@
         for place, value in zip(places, mine):
             ext[pl.ds(own + place * face, face), :] = value
     own_copy.wait()
-    lanes = lax.broadcasted_iota(jnp.int32, (step, rows), 1)
+    lanes = lax.broadcasted_iota(jnp.int32, (step, 128), 1)
 
     def gather(k, carried):
         at = pl.multiple_of(k * ch, ch)
@@ -193,7 +193,12 @@
                 for b in range(h * step // block, (h + 1) * step // block)
             ]
             place = jnp.concatenate(places, axis=0).astype(jnp.int32)
-            picked = dot(one_hot(lanes == place), ext[...]).astype(BF)
+            place = jnp.broadcast_to(place, (step, 128)).astype(jnp.int16)
+            hots = []
+            for r in range(0, rows, 128):
+                hot = jnp.where((lanes + r).astype(jnp.int16) == place, jnp.ones((), BF), jnp.zeros((), BF))
+                hots.append(hot[:, : min(128, rows - r)])
+            picked = dot(jnp.concatenate(hots, axis=1), ext[...]).astype(BF)
             got[pl.ds(h * step, step), pl.ds(at, ch)] = picked
             got_t[pl.ds(at, ch), pl.ds(h * step, step)] = picked.T
         return carried
@@ -541,7 +546,7 @@
     )
     activated, gp, keep, *give = forward(ways, flags, col, own_features, faces, weight, upstream[0, 0, 0])
     devices = lax.axis_size("gx") * lax.axis_size("gy") * lax.axis_size("gz")
-    split = (0, 15, 18)
+    split = (0, 3, 15, 18)
     state = {"turn": 0, "returned": {}, "grad": []}
     late = [j for j, way in enumerate(ways) if way in ((0, 0), (1, 2))]
     early = [j for j in range(len(ways)) if j not in late]
@@ -566,8 +571,8 @@
             for j, face in zip(picks, held):
                 state["returned"][j] = face
             came = list(held[len(picks) :])
-        if turn in (3, 4):
-            first, after = split[turn - 3 : turn - 1]
+        if turn in (2, 3, 4):
+            first, after = split[turn - 2 : turn]
             work = lambda g: [backward_own(row, g, weight, first, after - first, state["grad"])]
             made, came = tied(out, work, came)
             state["grad"] = [made[0]]

time: 124 us -> 126 us (1.016)
  Pallas kernels: 65.9 us -> 67.5 us
  starting transfers between devices: 36.8 us -> 35.5 us
    ppermute x14, waiting for transfers between devices: 6.21 us -> 8.38 us  [swap(): return lax.ppermute(x, axis, [(j, j ^ 1 << bit) for j in range(n)])]
    pallas_call x2 -> x3, Pallas kernels: 12.5 us -> 14.6 us  [backward_own(): pl.pallas_call(lambda *refs: own_kernel(first, count, *refs), in_specs=[H...]
  transfers between devices with their start and end apart: 30 -> 30, of which waited for: 12 -> 11; matrix products, arithmetic and copies ran while one was open for 1% -> 1% of each run, Pallas kernels for 29% -> 31%
where the time goes in v12:
time: 126 us; the launch traced here: 125 us
  Pallas kernels  67.5 us (54%)
  starting transfers between devices  35.5 us (28%)
  waiting for transfers between devices  12.6 us (10%)
  other arithmetic  7.96 us (6%)
    pallas_call x1, Pallas kernels, forward(): pl.pallas_call(lambda *refs: forward_kernel(ways, where, 256, *refs), in_...  25 us
    pallas_call x3, Pallas kernels, backward_own(): pl.pallas_call(lambda *refs: own_kernel(first, count, *refs), in_specs=[H...  14.6 us
    ppermute x10, starting transfers between devices, exchange(): got.append(lax.ppermute(array, AXES[i], pairs))  13.8 us
    ppermute x14, starting transfers between devices, swap(): return lax.ppermute(x, axis, [(j, j ^ 1 << bit) for j in range(n)])  12.4 us
    pallas_call x1, Pallas kernels, backward_faces(): pl.pallas_call(lambda *refs: faces_kernel(ways, where, own, taps, *refs),...  10.6 us
    ppermute x6, starting transfers between devices, reduce_all(): lax.ppermute(y, 'gy', [(j, (j + s) % n) for j in range(n)])  9.32 us
    ppermute x14, waiting for transfers between devices, swap(): return lax.ppermute(x, axis, [(j, j ^ 1 << bit) for j in range(n)])  8.38 us
    pallas_call x1, Pallas kernels, finish(): pl.pallas_call(lambda *refs: finish_kernel(ways, first, count, *refs), in...  7.41 us
  transfers between devices with their start and end apart: 30, of which 11 were waited for; matrix products, arithmetic and copies ran while one was open for 1% of the time, Pallas kernels for 31%

profile of v12, /device:TPU:0, one launch (start us, length us, event | category | flops | bytes accessed | tf_op | source)
XLA Modules:
  0.0 125.1 jit_solution(12385366166623086753)
XLA Ops:
  0.6 0.1 pad_add_fusion.refs_0_
  0.7 2.0 %send.1 = (bf16[96,256]{1,0:T(8,128)(2,1)S(1)}, bf16[96,256]{1,0:T(8,128)(2,1)S(1)}, bf16[96,256]{1,0:T(8,128)(2,1)S(1)}, bf16[96,256]{1,0:T(8,128)(2,1)S(1)}, bf16[96,256]{1,0:T(8,128)(2,1)S(1)}) custom-call(s32[4]{0:T(128)S(1)} %pad_add_fusion.refs_0_, s32[6,1,96]{2,1,0:T(1,128)} %bitcast.26, bf16[768,256]{1,0:T(8,128)(2,1)} %bitcast.19), custom_call_target="tpu_custom_call" | custom-call | tf_op jit(solution)/shard_map/send/pallas_call | solution.py:89
  2.7 3.0 %collective-permute-start = (bf16[96,256]{1,0:T(8,128)(2,1)S(1)}, bf16[96,256]{1,0:T(8,128)(2,1)S(1)}, u32[]{:S(2)}, u32[]{:S(2)}) collective-permute-start(bf16[96,256]{1,0:T(8,128)(2,1)S(1)} %get-tuple-element.62), channel_id=1, source_target_pairs={{0,16},{16,0},{1,17},{17,1},{2,18},{18,2},{3,19},{19,3},{4,20},{20... | collective-permute-start | bytes 147464 | tf_op jit(solution)/shard_map/ppermute | solution.py:60
  5.7 1.6 %collective-permute-start.1 = (bf16[96,256]{1,0:T(8,128)(2,1)S(1)}, bf16[96,256]{1,0:T(8,128)(2,1)S(1)}, u32[]{:S(2)}, u32[]{:S(2)}) collective-permute-start(bf16[96,256]{1,0:T(8,128)(2,1)S(1)} %get-tuple-element.63), channel_id=1, source_target_pairs={{0,4},{4,0},{8,12},{12,8},{1,5},{5,1},{9,13},{13,9},{2,6},{6,2},{1... | collective-permute-start | bytes 147464 | tf_op jit(solution)/shard_map/ppermute | solution.py:60
  7.3 0.7 collective-permute-start.2
  8.0 0.1 collective-permute-start.3
  8.1 0.7 collective-permute-start.4
  8.7 3.9 %invert.1 = (f32[27,128,16]{2,1,0:T(8,128)S(1)}, f32[27,16,128]{2,1,0:T(8,128)}) custom-call(s32[4]{0:T(128)S(1)} %pad_add_fusion.refs_0_, s32[27,1,768]{2,1,0:T(1,128)} %bitcast.23, s32[27,1,768]{2,1,0:T(1,128)} %bitcast.24, s32[27,1,768]{2,1,0:T(1,128)} %bitcast.25), custom_call_target="tpu_custom_call" | custom-call | tf_op jit(solution)/shard_map/invert/pallas_call | solution.py:142
  12.6 0.0 collective-permute-done.1.refs_6_
  12.7 0.0 collective-permute-done.4.refs_9_
  12.7 25.0 %forward.1 = (bf16[768,256]{1,0:T(8,128)(2,1)}, bf16[768,256]{1,0:T(8,128)(2,1)}, f32[6912,128]{1,0:T(8,128)S(1)}, bf16[3456,128]{1,0:T(8,128)(2,1)}, bf16[3456,128]{1,0:T(8,128)(2,1)}) custom-call(s32[4]{0:T(128)S(1)} %pad_add_fusion.refs_0_, f32[27,128,16]{2,1,0:T(8,128)S(1)} %get-tuple-element.61.refs_1_, bf16[768,256]{1,0:T(8,128)(2,1)} %bitcast.20, ...), custom_call_target="tpu_custom_call" | custom-call | tf_op jit(solution)/shard_map/forward/pallas_call | solution.py:252
  37.7 2.9 %collective-permute-start.5 = (bf16[3456,128]{1,0:T(8,128)(2,1)}, bf16[3456,128]{1,0:T(8,128)(2,1)}, u32[]{:S(2)}, u32[]{:S(2)}) collective-permute-start(bf16[3456,128]{1,0:T(8,128)(2,1)} %get-tuple-element.71), channel_id=1, source_target_pairs={{0,1},{1,0},{2,3},{3,2},{4,5},{5,4},{6,7},{7,6},{8,9},{9,8},{10,11... | collective-permute-start | bytes 2654216 | tf_op jit(solution)/shard_map/ppermute | solution.py:425
  40.6 0.1 collective-permute-start.6
  40.7 2.3 %collective-permute-done.5 = bf16[3456,128]{1,0:T(8,128)(2,1)} collective-permute-done((bf16[3456,128]{1,0:T(8,128)(2,1)}, bf16[3456,128]{1,0:T(8,128)(2,1)}, u32[]{:S(2)}, u32[]{:S(2)}) %collective-permute-start.5) | collective-permute-done | bytes 884768 | tf_op jit(solution)/shard_map/ppermute | solution.py:425
  43.0 1.3 %collective-permute-done.6 = bf16[3456,128]{1,0:T(8,128)(2,1)} collective-permute-done((bf16[3456,128]{1,0:T(8,128)(2,1)}, bf16[3456,128]{1,0:T(8,128)(2,1)}, u32[]{:S(2)}, u32[]{:S(2)}) %collective-permute-start.6) | collective-permute-done | bytes 884768 | tf_op jit(solution)/shard_map/ppermute | solution.py:425
  44.3 2.3 %add_convert_fusion = (bf16[1728,128]{1,0:T(8,128)(2,1)}, bf16[1728,128]{1,0:T(8,128)(2,1)}) fusion(f32[6912,128]{1,0:T(8,128)S(1)} %get-tuple-element.70, s32[]{:T(128)S(6)} %select_n.150, bf16[3456,128]{1,0:T(8,128)(2,1)} %collective-permute-done.6, s32[]{:T(128)S(6)} %select_n.151, bf16[3456,128]{1,0:T(8,128)(2,1)} %collective-permute-done.5, ...), kind=kLoop, calls=%fused_computation | loop fusion | flops 1327104 | bytes 3538960 | tf_op jit(solution)/shard_map/convert_element_type | solution.py:490
  46.5 0.9 collective-permute-start.8
  47.4 0.5 collective-permute-start.7
  47.9 10.6 %backward_faces.1 = (bf16[96,256]{1,0:T(8,128)(2,1)}, bf16[96,256]{1,0:T(8,128)(2,1)}, bf16[96,256]{1,0:T(8,128)(2,1)}, bf16[96,256]{1,0:T(8,128)(2,1)}, bf16[96,256]{1,0:T(8,128)(2,1)}) custom-call(s32[4]{0:T(128)S(1)} %pad_add_fusion.refs_0_, f32[27,16,128]{2,1,0:T(8,128)} %get-tuple-element.68.refs_1_.refs_0_.refs_2_, ...), custom_call_target="tpu_custom_call" | custom-call | tf_op jit(solution)/shard_map/backward_faces/pallas_call | solution.py:351
  58.5 0.8 collective-permute-done.8
  59.3 0.3 collective-permute-done.7
  59.6 2.2 %add_convert_fusion.2 = (bf16[864,128]{1,0:T(8,128)(2,1)}, bf16[864,128]{1,0:T(8,128)(2,1)}) fusion(f32[6912,128]{1,0:T(8,128)S(1)} %get-tuple-element.70, s32[]{:T(128)S(6)} %select_n.156, bf16[1728,128]{1,0:T(8,128)(2,1)} %collective-permute-done.8, s32[]{:T(128)S(6)} %select_n.158, bf16[3456,128]{1,0:T(8,128)(2,1)} %collective-permute-done.6, ...), kind=kLoop, calls=%fused_computation.2 | loop fusion | flops 1105920 | bytes 2211864 | tf_op jit(solution)/shard_map/convert_element_type | solution.py:490
  61.8 0.5 collective-permute-start.13
  62.4 1.4 %collective-permute-start.12 = (bf16[864,128]{1,0:T(8,128)(2,1)}, bf16[864,128]{1,0:T(8,128)(2,1)}, u32[]{:S(2)}, u32[]{:S(2)}) collective-permute-start(bf16[864,128]{1,0:T(8,128)(2,1)} %get-tuple-element.128), channel_id=1, source_target_pairs={{0,2},{1,3},{2,0},{3,1},{4,6},{5,7},{6,4},{7,5},{8,10},{9,11},{10,... | collective-permute-start | bytes 663560 | tf_op jit(solution)/shard_map/ppermute | solution.py:425
  63.8 4.4 %collective-permute-start.9 = (bf16[96,256]{1,0:T(8,128)(2,1)}, bf16[96,256]{1,0:T(8,128)(2,1)}, u32[]{:S(2)}, u32[]{:S(2)}) collective-permute-start(bf16[96,256]{1,0:T(8,128)(2,1)} %get-tuple-element.84), channel_id=1, source_target_pairs={{0,4},{4,0},{8,12},{12,8},{1,5},{5,1},{9,13},{13,9},{2,6},{6,2},{1... | collective-permute-start | bytes 147464 | tf_op jit(solution)/shard_map/ppermute | solution.py:60
  68.2 1.3 %collective-permute-start.10 = (bf16[96,256]{1,0:T(8,128)(2,1)}, bf16[96,256]{1,0:T(8,128)(2,1)}, u32[]{:S(2)}, u32[]{:S(2)}) collective-permute-start(bf16[96,256]{1,0:T(8,128)(2,1)} %get-tuple-element.85), channel_id=1, source_target_pairs={{4,8},{8,4},{5,9},{9,5},{6,10},{10,6},{7,11},{11,7},{20,24},{24,20... | collective-permute-start | bytes 147464 | tf_op jit(solution)/shard_map/ppermute | solution.py:60
  69.4 0.0 collective-permute-start.11
  69.4 1.1 collective-permute-done.9.refs_7_
  70.6 0.4 collective-permute-done.11.refs_9_
  71.0 0.0 collective-permute-done.12
  71.0 1.1 add_convert_fusion.5
  72.1 1.1 add_convert_fusion.4
  73.3 3.5 %collective-permute-start.16 = (bf16[432,128]{1,0:T(8,128)(2,1)S(1)}, bf16[432,128]{1,0:T(8,128)(2,1)S(1)}, u32[]{:S(2)}, u32[]{:S(2)}) collective-permute-start(bf16[432,128]{1,0:T(8,128)(2,1)S(1)} %pad_maximum_fusion.2), channel_id=1, source_target_pairs={{0,4},{4,8},{8,12},{12,0},{1,5},{5,9},{9,13},{13,1},{2,6},{6,10},{... | collective-permute-start | bytes 331784 | tf_op jit(solution)/shard_map/ppermute | solution.py:498
  76.9 0.1 collective-permute-start.17
  77.0 2.4 %collective-permute-start.18 = (bf16[432,128]{1,0:T(8,128)(2,1)S(1)}, bf16[432,128]{1,0:T(8,128)(2,1)S(1)}, u32[]{:S(2)}, u32[]{:S(2)}) collective-permute-start(bf16[432,128]{1,0:T(8,128)(2,1)S(1)} %pad_maximum_fusion.4), channel_id=1, source_target_pairs={{0,12},{4,0},{8,4},{12,8},{1,13},{5,1},{9,5},{13,9},{2,14},{6,2},{... | collective-permute-start | bytes 331784 | tf_op jit(solution)/shard_map/ppermute | solution.py:498
  79.4 1.5 %collective-permute-start.14 = (bf16[96,256]{1,0:T(8,128)(2,1)}, bf16[96,256]{1,0:T(8,128)(2,1)S(1)}, u32[]{:S(2)}, u32[]{:S(2)}) collective-permute-start(bf16[96,256]{1,0:T(8,128)(2,1)} %get-tuple-element.92), channel_id=1, source_target_pairs={{0,16},{16,0},{1,17},{17,1},{2,18},{18,2},{3,19},{19,3},{4,20},{20... | collective-permute-start | bytes 147464 | tf_op jit(solution)/shard_map/ppermute | solution.py:60
  80.9 0.7 collective-permute-start.15
  81.5 1.0 convert_add_fusion.1
  82.5 3.5 %backward_own.3.refs_3_ = f32[768,256]{1,0:T(8,128)} custom-call(f32[27,16,128]{2,1,0:T(8,128)} %get-tuple-element.68.refs_1_.refs_0_.refs_2_, bf16[768,256]{1,0:T(8,128)(2,1)} %get-tuple-element.109.refs_2_.refs_1_.refs_3_, bf16[27,256,256]{2,1,0:T(8,128)(2,1)} %refs_4_.1), custom_call_target="tpu_custom_call" | custom-call | tf_op jit(solution)/shard_map/backward_own/pallas_call | solution.py:374
  86.1 0.0 collective-permute-done.14.refs_6_
  86.1 0.0 collective-permute-done.17
  86.2 0.0 collective-permute-done.18
  86.2 0.1 fusion.3
  86.2 2.6 %collective-permute-start.21 = (bf16[432,128]{1,0:T(8,128)(2,1)S(1)}, bf16[432,128]{1,0:T(8,128)(2,1)S(1)}, u32[]{:S(2)}, u32[]{:S(2)}) collective-permute-start(bf16[432,128]{1,0:T(8,128)(2,1)S(1)} %fusion.3), channel_id=1, source_target_pairs={{0,12},{4,0},{8,4},{12,8},{1,13},{5,1},{9,5},{13,9},{2,14},{6,2},{... | collective-permute-start | bytes 331784 | tf_op jit(solution)/shard_map/ppermute | solution.py:498
  88.9 0.7 collective-permute-start.20
  89.5 0.0 collective-permute-start.19
  89.6 7.5 %backward_own.4.refs_3_ = f32[768,256]{1,0:T(8,128)} custom-call(f32[27,16,128]{2,1,0:T(8,128)} %get-tuple-element.68.refs_1_.refs_0_.refs_2_, bf16[768,256]{1,0:T(8,128)(2,1)} %get-tuple-element.109.refs_2_.refs_1_.refs_3_, bf16[27,256,256]{2,1,0:T(8,128)(2,1)} %refs_4_.1, f32[768,256]{1,0:T(8,128)} %backward_own.3.refs_3_), custom_call_target="tpu_custom_call" | custom-call | tf_op jit(solution)/shard_map/backward_own/pallas_call | solution.py:374
  97.1 0.0 collective-permute-done.21
  97.1 2.7 %collective-permute-done.20 = bf16[432,128]{1,0:T(8,128)(2,1)S(1)} collective-permute-done((bf16[432,128]{1,0:T(8,128)(2,1)S(1)}, bf16[432,128]{1,0:T(8,128)(2,1)S(1)}, u32[]{:S(2)}, u32[]{:S(2)}) %collective-permute-start.20) | collective-permute-done | bytes 110624 | tf_op jit(solution)/shard_map/ppermute | solution.py:498
  100.0 0.5 collective-permute-start.22
  100.5 1.6 %collective-permute-start.23 = (bf16[864,128]{1,0:T(8,128)(2,1)S(1)}, bf16[864,128]{1,0:T(8,128)(2,1)S(1)}, u32[]{:S(2)}, u32[]{:S(2)}) collective-permute-start(bf16[864,128]{1,0:T(8,128)(2,1)S(1)} %pad_maximum_fusion.1), channel_id=1, source_target_pairs={{0,16},{16,0},{1,17},{17,1},{2,18},{18,2},{3,19},{19,3},{4,20},{20... | collective-permute-start | bytes 663560 | tf_op jit(solution)/shard_map/ppermute | solution.py:425
  102.1 3.5 %backward_own.5.refs_5_ = f32[768,256]{1,0:T(8,128)} custom-call(f32[27,16,128]{2,1,0:T(8,128)} %get-tuple-element.68.refs_1_.refs_0_.refs_2_, bf16[768,256]{1,0:T(8,128)(2,1)} %get-tuple-element.109.refs_2_.refs_1_.refs_3_, bf16[27,256,256]{2,1,0:T(8,128)(2,1)} %refs_4_.1, f32[768,256]{1,0:T(8,128)} %backward_own.4.refs_3_), custom_call_target="tpu_custom_call" | custom-call | tf_op jit(solution)/shard_map/backward_own/pallas_call | solution.py:374
  105.6 1.9 %collective-permute-done.22 = bf16[864,128]{1,0:T(8,128)(2,1)S(1)} collective-permute-done((bf16[864,128]{1,0:T(8,128)(2,1)S(1)}, bf16[864,128]{1,0:T(8,128)(2,1)S(1)}, u32[]{:S(2)}, u32[]{:S(2)}) %collective-permute-start.22) | collective-permute-done | bytes 221216 | tf_op jit(solution)/shard_map/ppermute | solution.py:425
  107.5 0.1 collective-permute-done.23
  107.6 1.8 %collective-permute-start.25 = (bf16[1728,128]{1,0:T(8,128)(2,1)S(1)}, bf16[1728,128]{1,0:T(8,128)(2,1)S(1)}, u32[]{:S(2)}, u32[]{:S(2)}) collective-permute-start(bf16[1728,128]{1,0:T(8,128)(2,1)S(1)} %constant_dynamic-update-slice_fusion.5.refs_2_), channel_id=1, source_target_pairs={{0,2},{1,3},{2,0},{3,1},{4,6},{5,7},{6,4},{7,5},{8,10},{9,11},{10,... | collective-permute-start | bytes 1327112 | tf_op jit(solution)/shard_map/ppermute | solution.py:425
  109.5 1.2 collective-permute-start.24
  110.7 0.5 collective-permute-start.28
  111.2 7.4 %finish.1 = bf16[768,256]{1,0:T(8,128)(2,1)} custom-call(s32[4]{0:T(128)S(1)} %pad_add_fusion.refs_0_, s32[6,1,96]{2,1,0:T(1,128)} %bitcast.27, f32[27,16,128]{2,1,0:T(8,128)} %get-tuple-element.68.refs_1_.refs_0_.refs_2_, bf16[768,256]{1,0:T(8,128)(2,1)} %get-tuple-element.109.refs_2_.refs_1_.refs_3_, bf16[27,256,256]{2,1,0:T(8,128)(2,1)} %refs_4_.1, ...), custom_call_target="tpu_custom_call" | custom-call | tf_op jit(solution)/shard_map/finish/pallas_call | solution.py:407
  118.6 0.3 collective-permute-done.25.refs_2_
  118.9 1.3 %collective-permute-done.24.refs_1_ = bf16[1728,128]{1,0:T(8,128)(2,1)S(1)} collective-permute-done((bf16[1728,128]{1,0:T(8,128)(2,1)S(1)}, bf16[1728,128]{1,0:T(8,128)(2,1)S(1)}, u32[]{:S(2)}, u32[]{:S(2)}) %collective-permute-start.24) | collective-permute-done | bytes 442400 | tf_op jit(solution)/shard_map/ppermute | solution.py:425
  120.3 0.5 collective-permute-start.27
  120.8 0.1 stack.38.refs_0_
  120.9 2.0 %place.2.refs_5_ = bf16[6912,256]{1,0:T(8,128)(2,1)} custom-call(s32[6]{0:T(128)S(1)} %stack.38.refs_0_, bf16[1728,128]{1,0:T(8,128)(2,1)S(1)} %constant_dynamic-update-slice_fusion.refs_1_, bf16[1728,128]{1,0:T(8,128)(2,1)S(1)} %constant_dynamic-update-slice_fusion.5.refs_2_, bf16[1728,128]{1,0:T(8,128)(2,1)S(1)} %collective-permute-done.28.refs_3_, ...), custom_call_target="tpu_custom_call" | custom-call | tf_op jit(solution)/shard_map/place/pallas_call | solution.py:459
  122.9 2.0 %place.3 = bf16[6912,256]{1,0:T(8,128)(2,1)} custom-call(s32[6]{0:T(128)S(1)} %stack.38.refs_0_, bf16[1728,128]{1,0:T(8,128)(2,1)S(1)} %collective-permute-done.24.refs_1_, bf16[1728,128]{1,0:T(8,128)(2,1)S(1)} %collective-permute-done.25.refs_2_, bf16[1728,128]{1,0:T(8,128)(2,1)S(1)} %collective-permute-done.26.refs_3_, ...), custom_call_target="tpu_custom_call", output_to_operand_aliasing={{}: (5, {})} | custom-call | tf_op jit(solution)/shard_map/place/pallas_call | solution.py:459
  (29 shorter events, 0.3 us)
Async XLA Ops:
  2.7 9.9 %collective-permute-start = (bf16[96,256]{1,0:T(8,128)(2,1)S(1)}, bf16[96,256]{1,0:T(8,128)(2,1)S(1)}, u32[]{:S(2)}, u32[]{:S(2)}) collective-permute-start(bf16[96,256]{1,0:T(8,128)(2,1)S(1)} %get-tuple-element.62), channel_id=1, source_target_pairs={{0,16},{16,0},{1,17},{17,1},{2,18},{18,2},{3,19},{19,3},{4,20},{20... | collective-permute-start | bytes 147464 | tf_op jit(solution)/shard_map/ppermute | solution.py:60
  5.7 6.9 %collective-permute-start.1 = (bf16[96,256]{1,0:T(8,128)(2,1)S(1)}, bf16[96,256]{1,0:T(8,128)(2,1)S(1)}, u32[]{:S(2)}, u32[]{:S(2)}) collective-permute-start(bf16[96,256]{1,0:T(8,128)(2,1)S(1)} %get-tuple-element.63), channel_id=1, source_target_pairs={{0,4},{4,0},{8,12},{12,8},{1,5},{5,1},{9,13},{13,9},{2,6},{6,2},{1... | collective-permute-start | bytes 147464 | tf_op jit(solution)/shard_map/ppermute | solution.py:60
  7.3 5.3 %collective-permute-start.2 = (bf16[96,256]{1,0:T(8,128)(2,1)S(1)}, bf16[96,256]{1,0:T(8,128)(2,1)S(1)}, u32[]{:S(2)}, u32[]{:S(2)}) collective-permute-start(bf16[96,256]{1,0:T(8,128)(2,1)S(1)} %get-tuple-element.64), channel_id=1, source_target_pairs={{4,8},{8,4},{5,9},{9,5},{6,10},{10,6},{7,11},{11,7},{20,24},{24,20... | collective-permute-start | bytes 147464 | tf_op jit(solution)/shard_map/ppermute | solution.py:60
  8.0 4.7 %collective-permute-start.3 = (bf16[96,256]{1,0:T(8,128)(2,1)S(1)}, bf16[96,256]{1,0:T(8,128)(2,1)S(1)}, u32[]{:S(2)}, u32[]{:S(2)}) collective-permute-start(bf16[96,256]{1,0:T(8,128)(2,1)S(1)} %get-tuple-element.65), channel_id=1, source_target_pairs={{0,1},{1,0},{2,3},{3,2},{4,5},{5,4},{6,7},{7,6},{8,9},{9,8},{10,11... | collective-permute-start | bytes 147464 | tf_op jit(solution)/shard_map/ppermute | solution.py:60
  8.1 4.6 %collective-permute-start.4 = (bf16[96,256]{1,0:T(8,128)(2,1)S(1)}, bf16[96,256]{1,0:T(8,128)(2,1)S(1)}, u32[]{:S(2)}, u32[]{:S(2)}) collective-permute-start(bf16[96,256]{1,0:T(8,128)(2,1)S(1)} %get-tuple-element.66), channel_id=1, source_target_pairs={{1,2},{2,1},{5,6},{6,5},{9,10},{10,9},{13,14},{14,13},{17,18},{18,... | collective-permute-start | bytes 147464 | tf_op jit(solution)/shard_map/ppermute | solution.py:60
  37.7 5.3 %collective-permute-start.5 = (bf16[3456,128]{1,0:T(8,128)(2,1)}, bf16[3456,128]{1,0:T(8,128)(2,1)}, u32[]{:S(2)}, u32[]{:S(2)}) collective-permute-start(bf16[3456,128]{1,0:T(8,128)(2,1)} %get-tuple-element.71), channel_id=1, source_target_pairs={{0,1},{1,0},{2,3},{3,2},{4,5},{5,4},{6,7},{7,6},{8,9},{9,8},{10,11... | collective-permute-start | bytes 2654216 | tf_op jit(solution)/shard_map/ppermute | solution.py:425
  40.6 3.7 %collective-permute-start.6 = (bf16[3456,128]{1,0:T(8,128)(2,1)}, bf16[3456,128]{1,0:T(8,128)(2,1)}, u32[]{:S(2)}, u32[]{:S(2)}) collective-permute-start(bf16[3456,128]{1,0:T(8,128)(2,1)} %get-tuple-element.72), channel_id=1, source_target_pairs={{0,1},{1,0},{2,3},{3,2},{4,5},{5,4},{6,7},{7,6},{8,9},{9,8},{10,11... | collective-permute-start | bytes 2654216 | tf_op jit(solution)/shard_map/ppermute | solution.py:425
  46.5 12.8 %collective-permute-start.8 = (bf16[1728,128]{1,0:T(8,128)(2,1)}, bf16[1728,128]{1,0:T(8,128)(2,1)}, u32[]{:S(2)}, u32[]{:S(2)}) collective-permute-start(bf16[1728,128]{1,0:T(8,128)(2,1)} %get-tuple-element.129), channel_id=1, source_target_pairs={{0,2},{1,3},{2,0},{3,1},{4,6},{5,7},{6,4},{7,5},{8,10},{9,11},{10,... | collective-permute-start | bytes 1327112 | tf_op jit(solution)/shard_map/ppermute | solution.py:425
  47.4 12.2 %collective-permute-start.7 = (bf16[1728,128]{1,0:T(8,128)(2,1)}, bf16[1728,128]{1,0:T(8,128)(2,1)}, u32[]{:S(2)}, u32[]{:S(2)}) collective-permute-start(bf16[1728,128]{1,0:T(8,128)(2,1)} %get-tuple-element.130), channel_id=1, source_target_pairs={{0,16},{16,0},{1,17},{17,1},{2,18},{18,2},{3,19},{19,3},{4,20},{20... | collective-permute-start | bytes 1327112 | tf_op jit(solution)/shard_map/ppermute | solution.py:425
  61.8 9.2 %collective-permute-start.13 = (bf16[864,128]{1,0:T(8,128)(2,1)}, bf16[864,128]{1,0:T(8,128)(2,1)}, u32[]{:S(2)}, u32[]{:S(2)}) collective-permute-start(bf16[864,128]{1,0:T(8,128)(2,1)} %get-tuple-element.127), channel_id=1, source_target_pairs={{0,16},{16,0},{1,17},{17,1},{2,18},{18,2},{3,19},{19,3},{4,20},{20... | collective-permute-start | bytes 663560 | tf_op jit(solution)/shard_map/ppermute | solution.py:425
  62.4 8.6 %collective-permute-start.12 = (bf16[864,128]{1,0:T(8,128)(2,1)}, bf16[864,128]{1,0:T(8,128)(2,1)}, u32[]{:S(2)}, u32[]{:S(2)}) collective-permute-start(bf16[864,128]{1,0:T(8,128)(2,1)} %get-tuple-element.128), channel_id=1, source_target_pairs={{0,2},{1,3},{2,0},{3,1},{4,6},{5,7},{6,4},{7,5},{8,10},{9,11},{10,... | collective-permute-start | bytes 663560 | tf_op jit(solution)/shard_map/ppermute | solution.py:425
  63.8 6.8 %collective-permute-start.9 = (bf16[96,256]{1,0:T(8,128)(2,1)}, bf16[96,256]{1,0:T(8,128)(2,1)}, u32[]{:S(2)}, u32[]{:S(2)}) collective-permute-start(bf16[96,256]{1,0:T(8,128)(2,1)} %get-tuple-element.84), channel_id=1, source_target_pairs={{0,4},{4,0},{8,12},{12,8},{1,5},{5,1},{9,13},{13,9},{2,6},{6,2},{1... | collective-permute-start | bytes 147464 | tf_op jit(solution)/shard_map/ppermute | solution.py:60
  68.2 2.4 %collective-permute-start.10 = (bf16[96,256]{1,0:T(8,128)(2,1)}, bf16[96,256]{1,0:T(8,128)(2,1)}, u32[]{:S(2)}, u32[]{:S(2)}) collective-permute-start(bf16[96,256]{1,0:T(8,128)(2,1)} %get-tuple-element.85), channel_id=1, source_target_pairs={{4,8},{8,4},{5,9},{9,5},{6,10},{10,6},{7,11},{11,7},{20,24},{24,20... | collective-permute-start | bytes 147464 | tf_op jit(solution)/shard_map/ppermute | solution.py:60
  69.4 1.6 %collective-permute-start.11 = (bf16[96,256]{1,0:T(8,128)(2,1)}, bf16[96,256]{1,0:T(8,128)(2,1)}, u32[]{:S(2)}, u32[]{:S(2)}) collective-permute-start(bf16[96,256]{1,0:T(8,128)(2,1)} %get-tuple-element.86), channel_id=1, source_target_pairs={{0,1},{1,0},{2,3},{3,2},{4,5},{5,4},{6,7},{7,6},{8,9},{9,8},{10,11... | collective-permute-start | bytes 147464 | tf_op jit(solution)/shard_map/ppermute | solution.py:60
  73.3 12.8 %collective-permute-start.16 = (bf16[432,128]{1,0:T(8,128)(2,1)S(1)}, bf16[432,128]{1,0:T(8,128)(2,1)S(1)}, u32[]{:S(2)}, u32[]{:S(2)}) collective-permute-start(bf16[432,128]{1,0:T(8,128)(2,1)S(1)} %pad_maximum_fusion.2), channel_id=1, source_target_pairs={{0,4},{4,8},{8,12},{12,0},{1,5},{5,9},{9,13},{13,1},{2,6},{6,10},{... | collective-permute-start | bytes 331784 | tf_op jit(solution)/shard_map/ppermute | solution.py:498
  76.9 9.3 %collective-permute-start.17 = (bf16[432,128]{1,0:T(8,128)(2,1)S(1)}, bf16[432,128]{1,0:T(8,128)(2,1)S(1)}, u32[]{:S(2)}, u32[]{:S(2)}) collective-permute-start(bf16[432,128]{1,0:T(8,128)(2,1)S(1)} %pad_maximum_fusion.3), channel_id=1, source_target_pairs={{0,8},{4,12},{8,0},{12,4},{1,9},{5,13},{9,1},{13,5},{2,10},{6,14},... | collective-permute-start | bytes 331784 | tf_op jit(solution)/shard_map/ppermute | solution.py:498
  77.0 9.2 %collective-permute-start.18 = (bf16[432,128]{1,0:T(8,128)(2,1)S(1)}, bf16[432,128]{1,0:T(8,128)(2,1)S(1)}, u32[]{:S(2)}, u32[]{:S(2)}) collective-permute-start(bf16[432,128]{1,0:T(8,128)(2,1)S(1)} %pad_maximum_fusion.4), channel_id=1, source_target_pairs={{0,12},{4,0},{8,4},{12,8},{1,13},{5,1},{9,5},{13,9},{2,14},{6,2},{... | collective-permute-start | bytes 331784 | tf_op jit(solution)/shard_map/ppermute | solution.py:498
  79.4 6.7 %collective-permute-start.14 = (bf16[96,256]{1,0:T(8,128)(2,1)}, bf16[96,256]{1,0:T(8,128)(2,1)S(1)}, u32[]{:S(2)}, u32[]{:S(2)}) collective-permute-start(bf16[96,256]{1,0:T(8,128)(2,1)} %get-tuple-element.92), channel_id=1, source_target_pairs={{0,16},{16,0},{1,17},{17,1},{2,18},{18,2},{3,19},{19,3},{4,20},{20... | collective-permute-start | bytes 147464 | tf_op jit(solution)/shard_map/ppermute | solution.py:60
  80.9 5.3 %collective-permute-start.15 = (bf16[96,256]{1,0:T(8,128)(2,1)}, bf16[96,256]{1,0:T(8,128)(2,1)S(1)}, u32[]{:S(2)}, u32[]{:S(2)}) collective-permute-start(bf16[96,256]{1,0:T(8,128)(2,1)} %get-tuple-element.93), channel_id=1, source_target_pairs={{1,2},{2,1},{5,6},{6,5},{9,10},{10,9},{13,14},{14,13},{17,18},{18,... | collective-permute-start | bytes 147464 | tf_op jit(solution)/shard_map/ppermute | solution.py:60
  86.1 13.8 %copy-start = (bf16[96,256]{1,0:T(8,128)(2,1)}, bf16[96,256]{1,0:T(8,128)(2,1)S(1)}, u32[]{:S(2)}) copy-start(bf16[96,256]{1,0:T(8,128)(2,1)S(1)} %collective-permute-done.14.refs_6_) | copy-start | bytes 147460
  86.1 13.8 %copy-start.1 = (bf16[96,256]{1,0:T(8,128)(2,1)}, bf16[96,256]{1,0:T(8,128)(2,1)S(1)}, u32[]{:S(2)}) copy-start(bf16[96,256]{1,0:T(8,128)(2,1)S(1)} %collective-permute-done.15.refs_10_) | copy-start | bytes 147460
  86.2 10.9 %collective-permute-start.21 = (bf16[432,128]{1,0:T(8,128)(2,1)S(1)}, bf16[432,128]{1,0:T(8,128)(2,1)S(1)}, u32[]{:S(2)}, u32[]{:S(2)}) collective-permute-start(bf16[432,128]{1,0:T(8,128)(2,1)S(1)} %fusion.3), channel_id=1, source_target_pairs={{0,12},{4,0},{8,4},{12,8},{1,13},{5,1},{9,5},{13,9},{2,14},{6,2},{... | collective-permute-start | bytes 331784 | tf_op jit(solution)/shard_map/ppermute | solution.py:498
  88.9 10.9 %collective-permute-start.20 = (bf16[432,128]{1,0:T(8,128)(2,1)S(1)}, bf16[432,128]{1,0:T(8,128)(2,1)S(1)}, u32[]{:S(2)}, u32[]{:S(2)}) collective-permute-start(bf16[432,128]{1,0:T(8,128)(2,1)S(1)} %fusion.3), channel_id=1, source_target_pairs={{0,8},{4,12},{8,0},{12,4},{1,9},{5,13},{9,1},{13,5},{2,10},{6,14},... | collective-permute-start | bytes 331784 | tf_op jit(solution)/shard_map/ppermute | solution.py:498
  89.5 10.3 %collective-permute-start.19 = (bf16[432,128]{1,0:T(8,128)(2,1)S(1)}, bf16[432,128]{1,0:T(8,128)(2,1)S(1)}, u32[]{:S(2)}, u32[]{:S(2)}) collective-permute-start(bf16[432,128]{1,0:T(8,128)(2,1)S(1)} %fusion.3), channel_id=1, source_target_pairs={{0,4},{4,8},{8,12},{12,0},{1,5},{5,9},{9,13},{13,1},{2,6},{6,10},{... | collective-permute-start | bytes 331784 | tf_op jit(solution)/shard_map/ppermute | solution.py:498
  100.0 7.5 %collective-permute-start.22 = (bf16[864,128]{1,0:T(8,128)(2,1)S(1)}, bf16[864,128]{1,0:T(8,128)(2,1)S(1)}, u32[]{:S(2)}, u32[]{:S(2)}) collective-permute-start(bf16[864,128]{1,0:T(8,128)(2,1)S(1)} %pad_maximum_fusion), channel_id=1, source_target_pairs={{0,2},{1,3},{2,0},{3,1},{4,6},{5,7},{6,4},{7,5},{8,10},{9,11},{10,... | collective-permute-start | bytes 663560 | tf_op jit(solution)/shard_map/ppermute | solution.py:425
  100.5 7.1 %collective-permute-start.23 = (bf16[864,128]{1,0:T(8,128)(2,1)S(1)}, bf16[864,128]{1,0:T(8,128)(2,1)S(1)}, u32[]{:S(2)}, u32[]{:S(2)}) collective-permute-start(bf16[864,128]{1,0:T(8,128)(2,1)S(1)} %pad_maximum_fusion.1), channel_id=1, source_target_pairs={{0,16},{16,0},{1,17},{17,1},{2,18},{18,2},{3,19},{19,3},{4,20},{20... | collective-permute-start | bytes 663560 | tf_op jit(solution)/shard_map/ppermute | solution.py:425
  107.6 11.3 %collective-permute-start.25 = (bf16[1728,128]{1,0:T(8,128)(2,1)S(1)}, bf16[1728,128]{1,0:T(8,128)(2,1)S(1)}, u32[]{:S(2)}, u32[]{:S(2)}) collective-permute-start(bf16[1728,128]{1,0:T(8,128)(2,1)S(1)} %constant_dynamic-update-slice_fusion.5.refs_2_), channel_id=1, source_target_pairs={{0,2},{1,3},{2,0},{3,1},{4,6},{5,7},{6,4},{7,5},{8,10},{9,11},{10,... | collective-permute-start | bytes 1327112 | tf_op jit(solution)/shard_map/ppermute | solution.py:425
  109.5 10.8 %collective-permute-start.24 = (bf16[1728,128]{1,0:T(8,128)(2,1)S(1)}, bf16[1728,128]{1,0:T(8,128)(2,1)S(1)}, u32[]{:S(2)}, u32[]{:S(2)}) collective-permute-start(bf16[1728,128]{1,0:T(8,128)(2,1)S(1)} %constant_dynamic-update-slice_fusion.refs_1_), channel_id=1, source_target_pairs={{0,16},{16,0},{1,17},{17,1},{2,18},{18,2},{3,19},{19,3},{4,20},{20... | collective-permute-start | bytes 1327112 | tf_op jit(solution)/shard_map/ppermute | solution.py:425
  110.7 10.2 %collective-permute-start.29 = (bf16[1728,128]{1,0:T(8,128)(2,1)S(1)}, bf16[1728,128]{1,0:T(8,128)(2,1)S(1)}, u32[]{:S(2)}, u32[]{:S(2)}) collective-permute-start(bf16[1728,128]{1,0:T(8,128)(2,1)S(1)} %constant_dynamic-update-slice_fusion.5.refs_2_), channel_id=1, source_target_pairs={{0,1},{1,0},{2,3},{3,2},{4,5},{5,4},{6,7},{7,6},{8,9},{9,8},{10,11... | collective-permute-start | bytes 1327112 | tf_op jit(solution)/shard_map/ppermute | solution.py:425
  110.7 10.2 %collective-permute-start.28 = (bf16[1728,128]{1,0:T(8,128)(2,1)S(1)}, bf16[1728,128]{1,0:T(8,128)(2,1)S(1)}, u32[]{:S(2)}, u32[]{:S(2)}) collective-permute-start(bf16[1728,128]{1,0:T(8,128)(2,1)S(1)} %constant_dynamic-update-slice_fusion.refs_1_), channel_id=1, source_target_pairs={{0,1},{1,0},{2,3},{3,2},{4,5},{5,4},{6,7},{7,6},{8,9},{9,8},{10,11... | collective-permute-start | bytes 1327112 | tf_op jit(solution)/shard_map/ppermute | solution.py:425
  120.3 2.6 %collective-permute-start.26 = (bf16[1728,128]{1,0:T(8,128)(2,1)S(1)}, bf16[1728,128]{1,0:T(8,128)(2,1)S(1)}, u32[]{:S(2)}, u32[]{:S(2)}) collective-permute-start(bf16[1728,128]{1,0:T(8,128)(2,1)S(1)} %collective-permute-done.24.refs_1_), channel_id=1, source_target_pairs={{0,1},{1,0},{2,3},{3,2},{4,5},{5,4},{6,7},{7,6},{8,9},{9,8},{10,11... | collective-permute-start | bytes 1327112 | tf_op jit(solution)/shard_map/ppermute | solution.py:425
  120.3 2.6 %collective-permute-start.27 = (bf16[1728,128]{1,0:T(8,128)(2,1)S(1)}, bf16[1728,128]{1,0:T(8,128)(2,1)S(1)}, u32[]{:S(2)}, u32[]{:S(2)}) collective-permute-start(bf16[1728,128]{1,0:T(8,128)(2,1)S(1)} %collective-permute-done.25.refs_2_), channel_id=1, source_target_pairs={{0,1},{1,0},{2,3},{3,2},{4,5},{5,4},{6,7},{7,6},{8,9},{9,8},{10,11... | collective-permute-start | bytes 1327112 | tf_op jit(solution)/shard_map/ppermute | solution.py:425
